TPU v7x, 32 devices: a whole 2x2x4 slice. The times are simulated.
32 devices in a mesh: seq: 8 (over z, x), ctx: 4 (over y, core).
Axes of the slice: x: 2, y: 2, z: 4, core: 2. Of those that a mesh axis runs over, the one named last changes fastest.
Arguments:
- hidden_in: bfloat16 [2, 8, 256, 2048], P(None, 'seq', 'ctx'), may hold values from -6 to 6
- token_marks: int32 [2, 8, 256, 3], P(None, 'seq', 'ctx'), may hold values from 0 to 255, as said below
- out_grad: bfloat16 [2, 8, 256, 2048], P(None, 'seq', 'ctx'), may hold values from -6 to 6
- qkv_weight: bfloat16 [2048, 6144], P(('seq', 'ctx')), may hold values from -0.125 to 0.125
- proj_weight: bfloat16 [2048, 2048], P(('seq', 'ctx')), may hold values from -1 to 1
- gate_weight: bfloat16 [2048, 5461], P(('seq', 'ctx')), may hold values from -0.125 to 0.125
- up_weight: bfloat16 [2048, 5461], P(('seq', 'ctx')), may hold values from -0.125 to 0.125
- down_weight: bfloat16 [2048, 5461], P(('seq', 'ctx')), may hold values from -0.15625 to 0.15625
- first_gain: bfloat16 [2048], P(('seq', 'ctx')), may hold values from 0.25 to 1.75
- first_shift: bfloat16 [2048], P(('seq', 'ctx')), may hold values from -1.75 to 1.75
- second_gain: bfloat16 [2048], P(('seq', 'ctx')), may hold values from 0.25 to 1.75
- second_shift: bfloat16 [2048], P(('seq', 'ctx')), may hold values from -1.75 to 1.75
Outputs:
- layer_out: bfloat16 [2, 8, 256, 2048], P(None, 'seq', 'ctx')
- input_grad: bfloat16 [2, 8, 256, 2048], P(None, 'seq', 'ctx')
- qkv_grad: float32 [2048, 6144], P(('seq', 'ctx'))
- proj_grad: float32 [2048, 2048], P(('seq', 'ctx'))
- gate_grad: float32 [2048, 5461], P(('seq', 'ctx'))
- up_grad: float32 [2048, 5461], P(('seq', 'ctx'))
- down_grad: float32 [2048, 5461], P(('seq', 'ctx'))
- first_gain_grad: float32 [2048], P(('seq', 'ctx'))
- first_shift_grad: float32 [2048], P(('seq', 'ctx'))
- second_gain_grad: float32 [2048], P(('seq', 'ctx'))
- second_shift_grad: float32 [2048], P(('seq', 'ctx'))
Inputs may be any that keep to these rules, and one draw needn't show every extreme that they name: `token_marks`: within each row, segments are runs of positions and one starts at position 0. Column 0 is the first position of the token's segment; column 1 is the end of that segment's bidirectional prefix, from the segment's first position to one before the segment's end; column 2 is the token's position within its segment. Packed row 0 of micro-batch 0 is a single segment.
All inputs are finite; a program needn't handle non-finite values.
Results may differ from a plain program's by a relative error of at most 0.015.
Values may be sent and summed in bfloat16 or wider, within the bound.
A program may use at most 448 MiB of HBM per device.

v0:
```python
import math

import jax
import jax.numpy as jnp
from jax import lax
from jax.sharding import PartitionSpec as P

HEAD_DIM = 128


deep_alpha = 48.0**0.25
norm_eps = 1e-05
masked_score = -1e30


def layer_norm(values, gain_vec, shift_vec):
    center = values - jnp.mean(values, axis=-1, keepdims=True)
    spread = jnp.mean(center * center, axis=-1, keepdims=True)
    return center * lax.rsqrt(spread + norm_eps) * gain_vec + shift_vec


def geglu(gate_val, up_val):
    return jax.nn.gelu(gate_val, approximate=False) * up_val


def rotary_tables(positions, head_dim):
    exponent = jnp.arange(head_dim // 2, dtype=jnp.float32) * (2.0 / head_dim)
    angles = (
        positions.astype(jnp.float32)[:, None] * jnp.exp(-math.log(10000.0) * exponent)[None, :]
    )
    return (jnp.cos(angles), jnp.sin(angles))


def rotate(matrix, cosine, sine, head_dim):
    row_count = matrix.shape[0]
    split_view = matrix.reshape(row_count, -1, head_dim)
    half_dim = head_dim // 2
    front_half = split_view[..., :half_dim]
    back_half = split_view[..., half_dim:]
    cos_rows = cosine[:, None, :]
    sin_rows = sine[:, None, :]
    turned = jnp.concatenate(
        [
            front_half * cos_rows - back_half * sin_rows,
            back_half * cos_rows + front_half * sin_rows,
        ],
        axis=-1,
    )
    return turned.reshape(row_count, -1)


def heads_of(matrix, head_dim):
    return matrix.reshape(matrix.shape[0], -1, head_dim)


def contract_last(left_side, right_side):
    return lax.dot_general(
        left_side, right_side, (((1,), (1,)), ((), ())), preferred_element_type=jnp.float32
    )


def contract_first(left_side, right_side):
    return lax.dot_general(
        left_side, right_side, (((0,), (0,)), ((), ())), preferred_element_type=jnp.float32
    )


def allowed_mask(query_marks, key_marks, query_place, key_place):
    same_segment = query_marks[:, 0][:, None] == key_marks[:, 0][None, :]
    earlier = key_place[None, :] <= query_place[:, None]
    opened = (key_place < key_marks[:, 1])[None, :]
    return same_segment & (earlier | opened)


def masked_scores(queries, key_rows, allowed, head_dim):
    raw_scores = jnp.einsum(
        "qhd,khd->hqk",
        heads_of(queries, head_dim),
        heads_of(key_rows, head_dim),
        preferred_element_type=jnp.float32,
    )
    raw_scores = raw_scores * (1.0 / math.sqrt(head_dim))
    return jnp.where(allowed[None], raw_scores, masked_score)


def forward_micro(x_rows, local_marks, key_marks, attn_full, ffn_full, query_place, key_place):
    qkv_full, proj_full, gain_one, shift_one = attn_full
    gate_full, up_full, down_full, gain_two, shift_two = ffn_full
    model_width = x_rows.shape[1]
    head_dim = HEAD_DIM
    cosine, sine = rotary_tables(local_marks[:, 2], head_dim)
    mixed = jnp.dot(x_rows, qkv_full, preferred_element_type=jnp.float32)
    queries = rotate(mixed[:, :model_width], cosine, sine, head_dim).astype(jnp.bfloat16)
    key_part = rotate(mixed[:, model_width : 2 * model_width], cosine, sine, head_dim).astype(
        jnp.bfloat16
    )
    value_part = mixed[:, 2 * model_width :].astype(jnp.bfloat16)
    key_rows, value_rows = (
        lax.all_gather(key_part, "ctx", axis=0, tiled=True),
        lax.all_gather(value_part, "ctx", axis=0, tiled=True),
    )
    allowed = allowed_mask(local_marks, key_marks, query_place, key_place)
    scores = masked_scores(queries, key_rows, allowed, head_dim)
    row_top = jnp.max(scores, axis=-1, keepdims=True)
    exp_scores = jnp.exp(scores - row_top)
    exp_total = jnp.sum(exp_scores, axis=-1, keepdims=True)
    probs_low = (exp_scores / exp_total).astype(jnp.bfloat16)
    log_total = row_top + jnp.log(exp_total)
    context = jnp.einsum(
        "hqk,khd->qhd",
        probs_low,
        heads_of(value_rows, head_dim),
        preferred_element_type=jnp.float32,
    )
    context_low = context.reshape(x_rows.shape[0], model_width).astype(jnp.bfloat16)
    branch = jnp.dot(context_low, proj_full, preferred_element_type=jnp.float32)
    first_sum = deep_alpha * x_rows.astype(jnp.float32) + branch
    normed = layer_norm(
        first_sum, gain_one.astype(jnp.float32), shift_one.astype(jnp.float32)
    ).astype(jnp.bfloat16)
    gate_val = jnp.dot(normed, gate_full, preferred_element_type=jnp.float32)
    up_val = jnp.dot(normed, up_full, preferred_element_type=jnp.float32)
    active = geglu(gate_val, up_val).astype(jnp.bfloat16)
    second_sum = deep_alpha * normed.astype(jnp.float32) + contract_last(active, down_full)
    layer_rows = layer_norm(
        second_sum, gain_two.astype(jnp.float32), shift_two.astype(jnp.float32)
    ).astype(jnp.bfloat16)
    record = (
        x_rows,
        cosine,
        sine,
        queries,
        key_rows,
        value_rows,
        allowed,
        log_total,
        context_low,
        first_sum,
        normed,
        gate_val,
        up_val,
        active,
        second_sum,
    )
    return (layer_rows, record)


def ffn_backward(record, grad_rows, attn_weights, ffn_weights):
    first_sum, normed, gate_val, up_val, active, second_sum = record[9:]
    gain_one, shift_one = (attn_weights[2], attn_weights[3])
    gate_full, up_full, down_full, gain_two, shift_two = ffn_weights
    ignored_out, second_back = jax.vjp(
        layer_norm, second_sum, gain_two.astype(jnp.float32), shift_two.astype(jnp.float32)
    )
    d_second, gain_two_grad, shift_two_grad = second_back(grad_rows.astype(jnp.float32))
    down_low = d_second.astype(jnp.bfloat16)
    d_active = jnp.dot(down_low, down_full, preferred_element_type=jnp.float32)
    ignored_glu, glu_back = jax.vjp(geglu, gate_val, up_val)
    d_gate, d_up = glu_back(d_active)
    gate_low = d_gate.astype(jnp.bfloat16)
    up_low = d_up.astype(jnp.bfloat16)
    d_normed = (
        deep_alpha * d_second + contract_last(gate_low, gate_full) + contract_last(up_low, up_full)
    )
    ignored_first, first_back = jax.vjp(
        layer_norm, first_sum, gain_one.astype(jnp.float32), shift_one.astype(jnp.float32)
    )
    d_first, gain_one_grad, shift_one_grad = first_back(d_normed)
    return (
        d_first,
        (gain_one_grad, shift_one_grad),
        (normed, gate_low, up_low, down_low, active, gain_two_grad, shift_two_grad),
    )


def attn_backward(record, d_first, attn_weights):
    x_rows, cosine, sine, queries, key_rows, value_rows, allowed, log_total, context_low = record[
        :9
    ]
    qkv_full, proj_full = (attn_weights[0], attn_weights[1])
    head_dim = HEAD_DIM
    row_count = x_rows.shape[0]
    branch_low = d_first.astype(jnp.bfloat16)
    d_context = contract_last(branch_low, proj_full).astype(jnp.bfloat16)
    scores = masked_scores(queries, key_rows, allowed, head_dim)
    probs = jnp.exp(scores - log_total)
    probs_low = probs.astype(jnp.bfloat16)
    context_heads = heads_of(d_context, head_dim)
    d_probs = jnp.einsum(
        "qhd,khd->hqk",
        context_heads,
        heads_of(value_rows, head_dim),
        preferred_element_type=jnp.float32,
    )
    d_scores = (probs * (d_probs - jnp.sum(probs * d_probs, axis=-1, keepdims=True))).astype(
        jnp.bfloat16
    )
    score_scale = 1.0 / math.sqrt(head_dim)
    d_query = (
        jnp.einsum(
            "hqk,khd->qhd",
            d_scores,
            heads_of(key_rows, head_dim),
            preferred_element_type=jnp.float32,
        ).reshape(row_count, -1)
        * score_scale
    )
    d_keys = (
        jnp.einsum(
            "hqk,qhd->khd",
            d_scores,
            heads_of(queries, head_dim),
            preferred_element_type=jnp.float32,
        ).reshape(key_rows.shape[0], -1)
        * score_scale
    )
    d_values = jnp.einsum(
        "hqk,qhd->khd", probs_low, context_heads, preferred_element_type=jnp.float32
    ).reshape(key_rows.shape[0], -1)
    key_grad, value_grad = (
        lax.psum_scatter(
            d_keys.astype(jnp.bfloat16), "ctx", scatter_dimension=0, tiled=True
        ).astype(jnp.float32),
        lax.psum_scatter(
            d_values.astype(jnp.bfloat16), "ctx", scatter_dimension=0, tiled=True
        ).astype(jnp.float32),
    )
    d_mixed = jnp.concatenate(
        [
            rotate(d_query, cosine, -sine, head_dim),
            rotate(key_grad, cosine, -sine, head_dim),
            value_grad,
        ],
        axis=1,
    ).astype(jnp.bfloat16)
    d_input = deep_alpha * d_first + contract_last(d_mixed, qkv_full)
    return (d_input, (x_rows, d_mixed, context_low, branch_low))


def ffn_terms(piece_list):
    normed_all = jnp.concatenate([piece[0] for piece in piece_list], axis=0)
    gate_all = jnp.concatenate([piece[1] for piece in piece_list], axis=0)
    up_all = jnp.concatenate([piece[2] for piece in piece_list], axis=0)
    down_all = jnp.concatenate([piece[3] for piece in piece_list], axis=0)
    active_all = jnp.concatenate([piece[4] for piece in piece_list], axis=0)
    gain_sum = jnp.sum(jnp.stack([piece[5] for piece in piece_list]), axis=0)
    shift_sum = jnp.sum(jnp.stack([piece[6] for piece in piece_list]), axis=0)
    return (
        contract_first(normed_all, gate_all),
        contract_first(normed_all, up_all),
        contract_first(down_all, active_all),
        gain_sum,
        shift_sum,
    )


def attn_terms(piece_list, norm_list):
    x_all = jnp.concatenate([piece[0] for piece in piece_list], axis=0)
    mixed_all = jnp.concatenate([piece[1] for piece in piece_list], axis=0)
    context_all = jnp.concatenate([piece[2] for piece in piece_list], axis=0)
    branch_all = jnp.concatenate([piece[3] for piece in piece_list], axis=0)
    gain_sum = jnp.sum(jnp.stack([entry[0] for entry in norm_list]), axis=0)
    shift_sum = jnp.sum(jnp.stack([entry[1] for entry in norm_list]), axis=0)
    return (
        contract_first(x_all, mixed_all),
        contract_first(context_all, branch_all),
        gain_sum,
        shift_sum,
    )


def body(
    hidden_in,
    token_marks,
    out_grad,
    qkv_weight,
    proj_weight,
    gate_weight,
    up_weight,
    down_weight,
    first_gain,
    first_shift,
    second_gain,
    second_shift,
):
    micro_count = hidden_in.shape[0]
    pos_count = hidden_in.shape[2]
    row_length = pos_count * lax.axis_size("ctx")
    attn_full = (
        lax.all_gather(qkv_weight, ("seq", "ctx"), axis=0, tiled=True),
        lax.all_gather(proj_weight, ("seq", "ctx"), axis=0, tiled=True),
        lax.all_gather(first_gain, ("seq", "ctx"), axis=0, tiled=True),
        lax.all_gather(first_shift, ("seq", "ctx"), axis=0, tiled=True),
    )
    ffn_full = (
        lax.all_gather(gate_weight, ("seq", "ctx"), axis=0, tiled=True),
        lax.all_gather(up_weight, ("seq", "ctx"), axis=0, tiled=True),
        lax.all_gather(down_weight, ("seq", "ctx"), axis=0, tiled=True),
        lax.all_gather(second_gain, ("seq", "ctx"), axis=0, tiled=True),
        lax.all_gather(second_shift, ("seq", "ctx"), axis=0, tiled=True),
    )
    row_marks = lax.all_gather(token_marks, "ctx", axis=2, tiled=True)
    query_place = lax.axis_index("ctx") * pos_count + jnp.arange(pos_count, dtype=jnp.int32)
    key_place = jnp.arange(row_length, dtype=jnp.int32)
    layer_list = []
    records = []
    for micro_step in range(micro_count):
        layer_rows, record = forward_micro(
            hidden_in[micro_step, 0],
            token_marks[micro_step, 0],
            row_marks[micro_step, 0],
            attn_full,
            ffn_full,
            query_place,
            key_place,
        )
        layer_list.append(layer_rows)
        records.append(record)
    attn_back = (
        lax.all_gather(qkv_weight, ("seq", "ctx"), axis=0, tiled=True),
        lax.all_gather(proj_weight, ("seq", "ctx"), axis=0, tiled=True),
        lax.all_gather(first_gain, ("seq", "ctx"), axis=0, tiled=True),
        lax.all_gather(first_shift, ("seq", "ctx"), axis=0, tiled=True),
    )
    ffn_back = (
        lax.all_gather(gate_weight, ("seq", "ctx"), axis=0, tiled=True),
        lax.all_gather(up_weight, ("seq", "ctx"), axis=0, tiled=True),
        lax.all_gather(down_weight, ("seq", "ctx"), axis=0, tiled=True),
        lax.all_gather(second_gain, ("seq", "ctx"), axis=0, tiled=True),
        lax.all_gather(second_shift, ("seq", "ctx"), axis=0, tiled=True),
    )
    input_list = []
    for micro_step in range(micro_count):
        d_first, norm_grads, ffn_pieces = ffn_backward(
            records[micro_step], out_grad[micro_step, 0], attn_back, ffn_back
        )
        ffn_sums = ffn_terms([ffn_pieces])
        ffn_part = (
            lax.psum_scatter(ffn_sums[0], ("seq", "ctx"), scatter_dimension=0, tiled=True),
            lax.psum_scatter(ffn_sums[1], ("seq", "ctx"), scatter_dimension=0, tiled=True),
            lax.psum_scatter(ffn_sums[2], ("seq", "ctx"), scatter_dimension=0, tiled=True),
            lax.psum_scatter(ffn_sums[3], ("seq", "ctx"), scatter_dimension=0, tiled=True),
            lax.psum_scatter(ffn_sums[4], ("seq", "ctx"), scatter_dimension=0, tiled=True),
        )
        d_input, attn_pieces = attn_backward(records[micro_step], d_first, attn_back)
        attn_sums = attn_terms([attn_pieces], [norm_grads])
        attn_part = (
            lax.psum_scatter(attn_sums[0], ("seq", "ctx"), scatter_dimension=0, tiled=True),
            lax.psum_scatter(attn_sums[1], ("seq", "ctx"), scatter_dimension=0, tiled=True),
            lax.psum_scatter(attn_sums[2], ("seq", "ctx"), scatter_dimension=0, tiled=True),
            lax.psum_scatter(attn_sums[3], ("seq", "ctx"), scatter_dimension=0, tiled=True),
        )
        input_list.append(d_input)
        if micro_step == 0:
            ffn_total = ffn_part
            attn_total = attn_part
        else:
            ffn_total = tuple((running + arrived for running, arrived in zip(ffn_total, ffn_part)))
            attn_total = tuple(
                (running + arrived for running, arrived in zip(attn_total, attn_part))
            )
    layer_out = jnp.stack(layer_list)[:, None]
    input_grad = jnp.stack(input_list).astype(jnp.bfloat16)[:, None]
    return (
        layer_out,
        input_grad,
        attn_total[0],
        attn_total[1],
        ffn_total[0],
        ffn_total[1],
        ffn_total[2],
        attn_total[2],
        attn_total[3],
        ffn_total[3],
        ffn_total[4],
    )


def solution(mesh):
    in_specs = (
        P(None, "seq", "ctx", None),
        P(None, "seq", "ctx", None),
        P(None, "seq", "ctx", None),
        P(("seq", "ctx"), None),
        P(("seq", "ctx"), None),
        P(("seq", "ctx"), None),
        P(("seq", "ctx"), None),
        P(("seq", "ctx"), None),
        P(("seq", "ctx")),
        P(("seq", "ctx")),
        P(("seq", "ctx")),
        P(("seq", "ctx")),
    )
    out_specs = (
        P(None, "seq", "ctx", None),
        P(None, "seq", "ctx", None),
        P(("seq", "ctx"), None),
        P(("seq", "ctx"), None),
        P(("seq", "ctx"), None),
        P(("seq", "ctx"), None),
        P(("seq", "ctx"), None),
        P(("seq", "ctx")),
        P(("seq", "ctx")),
        P(("seq", "ctx")),
        P(("seq", "ctx")),
    )
    return jax.shard_map(body, mesh=mesh, in_specs=in_specs, out_specs=out_specs, check_vma=False)
```

profile of v0, /device:TPU:11, one launch (start us, length us, event | category | flops | bytes accessed | tf_op | source)
XLA Modules:
  0.0 3075.7 jit_solution(14366476990100240912)
XLA Ops:
  9.6 155.1 %all-gather.10.cloned.1.call-done = bf16[2048,6144]{1,0:T(8,128)(2,1)} async-done(((bf16[64,6144]{1,0:T(8,128)(2,1)}), bf16[2048,6144]{1,0:T(8,128)(2,1)}) %all-gather.10.cloned.1.call-update) | async-done | bytes 25165840 | tf_op jit(solution)/shard_map/all_gather | solution.py:290
  164.7 10.5 fusion.70
  178.2 10.9 fusion.74
  197.9 40.0 %all-reduce.9 = (bf16[2048]{0:T(1024)(128)(2,1)S(1)}, bf16[2048]{0:T(1024)(128)(2,1)S(1)}, bf16[2048]{0:T(1024)(128)(2,1)S(1)}, bf16[2048]{0:T(1024)(128)(2,1)S(1)}) all-reduce(bf16[2048]{0:T(1024)(128)(2,1)S(1)} %dynamic-update-slice.1, bf16[2048]{0:T(1024)(128)(2,1)S(1)} %dynamic-update-slice, ...), channel_id=1, replica_groups=mesh['seq'=8,'ctx'=4] {'seq','ctx'}, use_global_device_ids=true, to_apply=%add.1 | all-reduce | flops 8192 | bytes 32768
  237.9 7.1 all_gather.51
  247.7 2.7 copy.124
  253.1 59.5 %all-gather.16.cloned.1.call-done = bf16[2048,2048]{1,0:T(8,128)(2,1)} async-done(((bf16[64,2048]{1,0:T(8,128)(2,1)}), bf16[2048,2048]{1,0:T(8,128)(2,1)}) %all-gather.16.cloned.1.call-update) | async-done | bytes 8388624 | tf_op jit(solution)/shard_map/all_gather | solution.py:291
  312.6 5.1 fusion.122
  318.9 11.1 all-gather.12.cloned.1.call-done
  331.8 5.2 fusion.120
  338.1 134.6 %all-gather.18.cloned.1.call-done = bf16[2048,5461]{1,0:T(8,128)(2,1)} async-done(((bf16[64,5461]{1,0:T(8,128)(2,1)}), bf16[2048,5461]{1,0:T(8,128)(2,1)}) %all-gather.18.cloned.1.call-update) | async-done | bytes 22368272 | tf_op jit(solution)/shard_map/all_gather | solution.py:296
  472.8 10.6 fusion.126
  483.3 131.8 %all-gather.20.cloned.1.call-done = bf16[2048,5461]{1,0:T(8,128)(2,1)} async-done(((bf16[64,5461]{1,0:T(8,128)(2,1)}), bf16[2048,5461]{1,0:T(8,128)(2,1)}) %all-gather.20.cloned.1.call-update) | async-done | bytes 22368272 | tf_op jit(solution)/shard_map/all_gather | solution.py:297
  615.1 12.1 multiply_convert_fusion.4
  627.3 130.3 %all-gather.22.cloned.1.call-done = bf16[2048,5461]{1,0:T(8,128)(2,1)} async-done(((bf16[64,5461]{1,0:T(8,128)(2,1)}), bf16[2048,5461]{1,0:T(8,128)(2,1)}) %all-gather.22.cloned.1.call-update) | async-done | bytes 22368272 | tf_op jit(solution)/shard_map/all_gather | solution.py:298
  757.5 11.5 fusion.124
  769.3 9.7 fusion.125
  779.0 12.3 multiply_convert_fusion.5
  791.3 11.6 fusion.123
  806.3 12.1 multiply_convert_fusion.3
  818.4 13.2 convolution_add_fusion.7
  831.6 12.6 multiply_convert_fusion.2
  844.2 11.7 convolution_add_fusion.5
  856.0 12.3 convolution_add_fusion.4
  868.3 14.0 multiply_reduce_fusion.3
  882.3 2.4 fusion.105
  884.7 6.3 fusion.21
  896.8 6.1 fusion.20
  917.5 8.2 convolution_add_fusion.3
  930.1 18.5 reduce-scatter.12.cloned.1.call-done
  952.9 23.5 reduce-scatter.18.cloned.1.call-done
  977.4 26.9 reduce-scatter.14.cloned.1.call-done
  1005.3 19.9 fusion.72
  1025.3 33.2 %add_bitcast_fusion = f32[2048,6144]{0,1:T(8,128)} fusion(f32[6144,2048]{1,0:T(8,128)} %fusion.72, bf16[64,6144]{1,0:T(8,128)(2,1)S(1)} %constant_dynamic-update-slice_fusion.1, bf16[2,1,64,2048]{3,2,1,0:T(8,128)(2,1)S(1)} %copy-done.37), kind=kOutput, calls=%fused_computation | convolution fusion | flops 1623195648 | bytes 101711872 | tf_op jit(solution)/shard_map/dot_general | solution.py:63
  1058.5 49.2 %copy.163 = f32[2048,6144]{1,0:T(8,128)} copy(f32[2048,6144]{0,1:T(8,128)} %add_bitcast_fusion) | data formatting | bytes 100663296
  1108.9 18.0 fusion.102
  1126.9 29.1 convolution_add_fusion
  1157.2 17.9 fusion.128
  1175.1 28.8 convolution_add_fusion.1
  1205.1 27.4 fusion.127
  1232.6 39.9 %convolution_add_fusion.2 = f32[2048,5461]{1,0:T(8,128)} fusion(f32[2048,5461]{1,0:T(8,128)} %fusion.127, bf16[64,2048]{1,0:T(8,128)(2,1)S(1)} %copy-done.21, bf16[64,5461]{1,0:T(8,128)(2,1)S(1)} %copy-done.7), kind=kOutput, calls=%fused_computation.3 | convolution fusion | flops 1442752512 | bytes 90434176 | tf_op jit(solution)/shard_map/dot_general | solution.py:63
  1273.7 43.6 %all-reduce.8 = (f32[2048]{0:T(1024)S(1)}, f32[2048]{0:T(1024)S(1)}, f32[2048]{0:T(1024)S(1)}, f32[2048]{0:T(1024)S(1)}) all-reduce(f32[2048]{0:T(1024)S(1)} %add.269, f32[2048]{0:T(1024)S(1)} %add.270, f32[2048]{0:T(1024)S(1)} %add.271, f32[2048]{0:T(1024)S(1)} %add.272), channel_id=20, replica_groups=mesh['seq'=8,'ctx'=4] {'seq','ctx'}, use_global_device_ids=true, to_apply=%region_37.38.clone | all-reduce | flops 8192 | bytes 65536
  1320.6 12.7 fusion.2
  1333.3 12.8 fusion.3
  1347.0 279.9 %reduce-scatter.28.cloned.1.call-done = f32[64,6144]{1,0:T(8,128)} async-done(((f32[2048,6144]{1,0:T(8,128)}), f32[64,6144]{1,0:T(8,128)}) %reduce-scatter.28.cloned.1.call-update) | async-done | bytes 1572880
  1626.9 480.9 %reduce-scatter.26.cloned.1.call-done = f32[64,5461]{1,0:T(8,128)} async-done(((f32[2048,5461]{1,0:T(8,128)}), f32[64,5461]{1,0:T(8,128)}) %reduce-scatter.26.cloned.1.call-update) | async-done | bytes 1398032 | tf_op jit(solution)/shard_map/reduce_scatter | solution.py:341
  2107.8 480.3 %reduce-scatter.24.cloned.1.call-done = f32[64,5461]{1,0:T(8,128)} async-done(((f32[2048,5461]{1,0:T(8,128)}), f32[64,5461]{1,0:T(8,128)}) %reduce-scatter.24.cloned.1.call-update) | async-done | bytes 1398032 | tf_op jit(solution)/shard_map/reduce_scatter | solution.py:340
  2588.1 480.3 %reduce-scatter.22.cloned.1.call-done = f32[64,5461]{1,0:T(8,128)} async-done(((f32[2048,5461]{1,0:T(8,128)}), f32[64,5461]{1,0:T(8,128)}) %reduce-scatter.22.cloned.1.call-update) | async-done | bytes 1398032 | tf_op jit(solution)/shard_map/reduce_scatter | solution.py:339
  (326 shorter events, 65.8 us)
Async XLA Ops:
  7.2 157.6 %all-gather.10.cloned.1.call-start = ((), (), s32[]{:S(2)}) async-start(), calls=%async_computation.9 | async-start | bytes 25952256 | tf_op jit(solution)/shard_map/all_gather | solution.py:290
  7.9 237.8 %all-gather.26.cloned.1.call-start = ((), (), s32[]{:S(2)}) async-start(), calls=%async_computation.17 | async-start | bytes 1310720 | tf_op jit(solution)/shard_map/all_gather | solution.py:99
  9.6 166.3 %copy-start.64 = (f32[64,64]{1,0:T(8,128)}, f32[64,64]{1,0:T(8,128)S(1)}, u32[]{:S(2)}) copy-start(f32[64,64]{1,0:T(8,128)S(1)} %get-tuple-element.164) | copy-start | bytes 49156
  9.6 180.2 %copy-start.62 = (f32[64,64]{1,0:T(8,128)}, f32[64,64]{1,0:T(8,128)S(1)}, u32[]{:S(2)}) copy-start(f32[64,64]{1,0:T(8,128)S(1)} %get-tuple-element.159) | copy-start | bytes 49156
  177.3 73.1 %copy-start.44 = (bf16[64,16,64]{2,0,1:T(8,128)(2,1)}, bf16[64,16,64]{2,0,1:T(8,128)(2,1)S(1)}, u32[]{:S(2)}) copy-start(bf16[64,16,64]{2,0,1:T(8,128)(2,1)S(1)} %get-tuple-element.109) | copy-start | bytes 393220
  178.2 69.5 %all-gather.14.cloned.1.call-start = ((), (), s32[]{:S(2)}) async-start(), calls=%async_computation.11 | async-start | bytes 1310720 | tf_op jit(solution)/shard_map/all_gather | solution.py:99
  192.2 59.1 %all-gather.24.cloned.1.call-start = ((), (), s32[]{:S(2)}) async-start(), calls=%async_computation.16 | async-start | bytes 1310720 | tf_op jit(solution)/shard_map/all_gather | solution.py:100
  193.0 119.6 %all-gather.16.cloned.1.call-start = ((), (), s32[]{:S(2)}) async-start(), calls=%async_computation.12 | async-start | bytes 8650752 | tf_op jit(solution)/shard_map/all_gather | solution.py:291
  193.6 136.4 %all-gather.12.cloned.1.call-start = ((), (), s32[]{:S(2)}) async-start(), calls=%async_computation.10 | async-start | bytes 1310720 | tf_op jit(solution)/shard_map/all_gather | solution.py:100
  194.4 278.3 %all-gather.18.cloned.1.call-start = ((), (), s32[]{:S(2)}) async-start(), calls=%async_computation.13 | async-start | bytes 23248896 | tf_op jit(solution)/shard_map/all_gather | solution.py:296
  195.2 420.0 %all-gather.20.cloned.1.call-start = ((), (), s32[]{:S(2)}) async-start(), calls=%async_computation.14 | async-start | bytes 23248896 | tf_op jit(solution)/shard_map/all_gather | solution.py:297
  195.9 561.6 %all-gather.22.cloned.1.call-start = ((), (), s32[]{:S(2)}) async-start(), calls=%async_computation.15 | async-start | bytes 23248896 | tf_op jit(solution)/shard_map/all_gather | solution.py:298
  196.7 732.4 %reduce-scatter.16.cloned.1.call-start = ((), (), s32[]{:S(2)}) async-start(), calls=%async_computation.20 | async-start | bytes 1310720 | tf_op jit(solution)/shard_map/reduce_scatter | solution.py:221
  251.2 61.4 %copy-start.35 = (bf16[2,1,64,2048]{3,2,1,0:T(8,128)(2,1)S(1)}, bf16[2,1,64,2048]{3,2,1,0:T(8,128)(2,1)}, u32[]{:S(2)}) copy-start(bf16[2,1,64,2048]{3,2,1,0:T(8,128)(2,1)} %param.12) | copy-start | bytes 1572868
  253.0 64.7 %copy-start.42 = (bf16[16,8,8,128]{3,2,1,0:T(8,128)(2,1)}, bf16[16,8,8,128]{3,2,1,0:T(8,128)(2,1)S(1)}, u32[]{:S(2)}) copy-start(bf16[16,8,8,128]{3,2,1,0:T(8,128)(2,1)S(1)} %fusion.23) | copy-start | bytes 786436
  253.0 65.0 %copy-start.48 = (bf16[64,16,64]{2,0,1:T(8,128)(2,1)S(1)}, bf16[64,16,64]{2,0,1:T(8,128)(2,1)}, u32[]{:S(2)}) copy-start(bf16[64,16,64]{2,0,1:T(8,128)(2,1)} %get-tuple-element.105) | copy-start | bytes 393220
  253.1 65.0 %copy-start.50 = (bf16[64,16,64]{2,0,1:T(8,128)(2,1)S(1)}, bf16[64,16,64]{2,0,1:T(8,128)(2,1)}, u32[]{:S(2)}) copy-start(bf16[64,16,64]{2,0,1:T(8,128)(2,1)} %get-tuple-element.106) | copy-start | bytes 393220
  338.1 419.4 %copy-start.20 = (bf16[64,2048]{1,0:T(8,128)(2,1)}, bf16[64,2048]{1,0:T(8,128)(2,1)S(1)}, u32[]{:S(2)}) copy-start(bf16[64,2048]{1,0:T(8,128)(2,1)S(1)} %get-tuple-element.145) | copy-start | bytes 786436
  806.2 38.1 %copy-start = (f32[64,2048]{1,0:T(8,128)}, f32[64,2048]{1,0:T(8,128)S(1)}, u32[]{:S(2)}) copy-start(f32[64,2048]{1,0:T(8,128)S(1)} %get-tuple-element.88) | copy-start | bytes 1572868
  806.2 38.1 %copy-start.74 = (f32[64]{0:T(128)}, f32[64]{0:T(128)S(1)}, u32[]{:S(2)}) copy-start(f32[64]{0:T(128)S(1)} %negate_multiply_fusion.3) | copy-start | bytes 772
  818.4 13.2 copy-start.4
  818.4 49.9 %copy-start.8 = (bf16[64,5461]{1,0:T(8,128)(2,1)}, bf16[64,5461]{1,0:T(8,128)(2,1)S(1)}, u32[]{:S(2)}) copy-start(bf16[64,5461]{1,0:T(8,128)(2,1)S(1)} %get-tuple-element.93) | copy-start | bytes 2097028
  818.4 13.2 copy-start.29
  868.3 14.0 copy-start.38
  884.7 32.8 %copy-start.81 = (f32[64]{0:T(128)}, f32[64]{0:T(128)S(1)}, u32[]{:S(2)}) copy-start(f32[64]{0:T(128)S(1)} %negate_multiply_fusion.2) | copy-start | bytes 772
  896.7 52.0 %reduce-scatter.12.cloned.1.call-start = ((), (), s32[]{:S(2)}) async-start(), calls=%async_computation.18 | async-start | bytes 1310720 | tf_op jit(solution)/shard_map/reduce_scatter | solution.py:221
  896.7 18.4 copy-start.79
  908.8 67.6 %reduce-scatter.18.cloned.1.call-start = ((), (), s32[]{:S(2)}) async-start(), calls=%async_computation.21 | async-start | bytes 1310720 | tf_op jit(solution)/shard_map/reduce_scatter | solution.py:224
  912.8 91.6 %reduce-scatter.14.cloned.1.call-start = ((), (), s32[]{:S(2)}) async-start(), calls=%async_computation.19 | async-start | bytes 1310720 | tf_op jit(solution)/shard_map/reduce_scatter | solution.py:224
  914.9 432.1 %reduce-scatter.20.cloned.1.call-start = ((), (), s32[]{:S(2)}) async-start(), calls=%async_computation.22 | async-start | bytes 17301504 | tf_op jit(solution)/shard_map/reduce_scatter | solution.py:349
  925.8 701.1 %reduce-scatter.28.cloned.1.call-start = ((), (), s32[]{:S(2)}) async-start(), calls=%async_computation.26 | async-start | bytes 51904512
  952.6 52.7 %copy-start.37 = (bf16[2,1,64,2048]{3,2,1,0:T(8,128)(2,1)S(1)}, bf16[2,1,64,2048]{3,2,1,0:T(8,128)(2,1)}, u32[]{:S(2)}) copy-start(bf16[2,1,64,2048]{3,2,1,0:T(8,128)(2,1)} %param.12) | copy-start | bytes 1572868
  977.4 47.9 %copy-start.16 = (bf16[64,6144]{1,0:T(8,128)(2,1)}, bf16[64,6144]{1,0:T(8,128)(2,1)S(1)}, u32[]{:S(2)}) copy-start(bf16[64,6144]{1,0:T(8,128)(2,1)S(1)} %constant_dynamic-update-slice_fusion.1) | copy-start | bytes 2359300
  1005.3 19.9 copy-start.18
  1107.7 19.2 copy-start.1
  1107.7 19.2 copy-start.32
  1107.7 19.2 copy-start.75
  1107.7 1000.0 %reduce-scatter.26.cloned.1.call-start = ((), (), s32[]{:S(2)}) async-start(), calls=%async_computation.25 | async-start | bytes 46497792 | tf_op jit(solution)/shard_map/reduce_scatter | solution.py:341
  1156.1 19.0 copy-start.11
  1156.1 19.0 copy-start.21
  1156.1 1432.0 %reduce-scatter.24.cloned.1.call-start = ((), (), s32[]{:S(2)}) async-start(), calls=%async_computation.24 | async-start | bytes 46497792 | tf_op jit(solution)/shard_map/reduce_scatter | solution.py:340
  1203.9 28.7 copy-start.7
  1203.9 1864.5 %reduce-scatter.22.cloned.1.call-start = ((), (), s32[]{:S(2)}) async-start(), calls=%async_computation.23 | async-start | bytes 46497792 | tf_op jit(solution)/shard_map/reduce_scatter | solution.py:339
  1272.5 47.2 %copy-start.60 = (bf16[1,64,2048]{2,1,0:T(8,128)(2,1)S(1)}, bf16[1,64,2048]{2,1,0:T(8,128)(2,1)}, u32[]{:S(2)}) copy-start(bf16[1,64,2048]{2,1,0:T(8,128)(2,1)} %get-tuple-element.118) | copy-start | bytes 786436
  1272.5 47.2 %copy-start.61 = (bf16[1,64,2048]{2,1,0:T(8,128)(2,1)S(1)}, bf16[1,64,2048]{2,1,0:T(8,128)(2,1)}, u32[]{:S(2)}) copy-start(bf16[1,64,2048]{2,1,0:T(8,128)(2,1)} %get-tuple-element.119) | copy-start | bytes 786436
  1272.5 48.0 %copy-start.17 = (bf16[64,6144]{1,0:T(8,128)(2,1)S(1)}, bf16[64,6144]{1,0:T(8,128)(2,1)}, u32[]{:S(2)}) copy-start(bf16[64,6144]{1,0:T(8,128)(2,1)} %copy-done.16) | copy-start | bytes 2359300
  1272.5 48.0 %copy-start.26 = (f32[64,2048]{1,0:T(8,128)S(1)}, f32[64,2048]{1,0:T(8,128)}, u32[]{:S(2)}) copy-start(f32[64,2048]{1,0:T(8,128)} %copy-done.24) | copy-start | bytes 1572868
  1272.6 48.0 %copy-start.82 = (f32[64]{0:T(128)S(1)}, f32[64]{0:T(128)}, u32[]{:S(2)}) copy-start(f32[64]{0:T(128)} %copy-done.81) | copy-start | bytes 772
  (57 other events, 235.5 us)
Sparse Core Ops, SparseCore 0:
  10.9 153.8 all-gather.9
  178.3 16.5 all-gather.25
  197.1 16.7 all-gather.13
  215.9 16.8 all-gather.23
  235.5 77.0 all-gather.15
  314.6 15.3 all-gather.11
  332.8 139.8 all-gather.17
  475.6 139.4 all-gather.19
  618.0 139.4 all-gather.21
  896.8 23.8 reduce-scatter.15
  923.8 24.7 reduce-scatter.11
  951.6 24.7 reduce-scatter.17
  979.5 24.7 reduce-scatter.13
  1007.1 184.0 reduce-scatter.19
  1198.1 428.7 reduce-scatter.27
  1629.6 478.0 reduce-scatter.25
  2110.5 477.5 reduce-scatter.23
  2590.8 477.5 reduce-scatter.21
where the time goes:
time: 3090 us; the launch traced here: 3080 us
  waiting for transfers between devices  2420 us (78%)
  matrix products  451 us (15%)
  blocking collectives  90.7 us (3%)
  local copies, waits for them, and re-layouts  79.8 us (3%)
    reduce_scatter x1, waiting for transfers between devices, body(): lax.psum_scatter(ffn_sums[2], ('seq', 'ctx'), scatter_dimension=0, tiled=...  481 us
    reduce_scatter x1, waiting for transfers between devices, body(): lax.psum_scatter(ffn_sums[0], ('seq', 'ctx'), scatter_dimension=0, tiled=...  480 us
    reduce_scatter x1, waiting for transfers between devices, body(): lax.psum_scatter(ffn_sums[1], ('seq', 'ctx'), scatter_dimension=0, tiled=...  480 us
    unnamed x19, waiting for transfers between devices  283 us
    dot_general x10, matrix products, contract_first(): lax.dot_general(left_side, right_side, (((0,), (0,)), ((), ())), preferre...  225 us
    all_gather x1, waiting for transfers between devices, body(): lax.all_gather(qkv_weight, ('seq', 'ctx'), axis=0, tiled=True)  155 us
    all_gather x1, waiting for transfers between devices, body(): lax.all_gather(gate_weight, ('seq', 'ctx'), axis=0, tiled=True)  135 us
    all_gather x1, waiting for transfers between devices, body(): lax.all_gather(up_weight, ('seq', 'ctx'), axis=0, tiled=True)  132 us
  transfers between devices with their start and end apart: 18, of which 13 were waited for; matrix products, arithmetic and copies ran while one was open for 13% of the time, Pallas kernels for 0%

commit v1 on v0

v1 whole, which is shorter than its diff:
```python
import math

import jax
import jax.numpy as jnp
import numpy as np
from jax import lax
from jax.sharding import Mesh
from jax.sharding import PartitionSpec as P

HEAD_DIM = 128
LANES = 128

deep_alpha = 48.0**0.25
norm_eps = 1e-05
masked_score = -1e30

ALL = ("zo", "zi", "x", "y", "c")
HEAD_AXES = ("x", "y", "c")
UNIT_AXES = ("zi", "c")
HEAD_COPIES = ("zo", "zi")
UNIT_COPIES = ("zo", "x", "y")


def contract_last(left_side, right_side):
    return lax.dot_general(
        left_side, right_side, (((1,), (1,)), ((), ())), preferred_element_type=jnp.float32
    )


def contract_first(left_side, right_side):
    return lax.dot_general(
        left_side, right_side, (((0,), (0,)), ((), ())), preferred_element_type=jnp.float32
    )


def dot(left_side, right_side):
    return jnp.dot(left_side, right_side, preferred_element_type=jnp.float32)


def low(values):
    return values.astype(jnp.bfloat16)


def norm_parts(values):
    center = values - jnp.mean(values, axis=-1, keepdims=True)
    spread = jnp.mean(center * center, axis=-1, keepdims=True)
    inverse = lax.rsqrt(spread + norm_eps)
    return center * inverse, inverse


def norm_back(cotangent, hat, inverse, gain_vec):
    scaled = cotangent * gain_vec
    return (
        scaled
        - jnp.mean(scaled, axis=-1, keepdims=True)
        - hat * jnp.mean(scaled * hat, axis=-1, keepdims=True)
    ) * inverse


def rotary_tables(positions):
    half = HEAD_DIM // 2
    exponent = jnp.arange(half, dtype=jnp.float32) * (2.0 / HEAD_DIM)
    angles = positions.astype(jnp.float32)[..., None] * jnp.exp(-math.log(10000.0) * exponent)
    return (jnp.cos(angles), jnp.sin(angles))


def rotate(values, cosine, sine):
    half = HEAD_DIM // 2
    front, back = values[..., :half], values[..., half:]
    return jnp.concatenate(
        [front * cosine - back * sine, back * cosine + front * sine], axis=-1
    )


def gather(values, axes):
    return lax.all_gather(values, axes, axis=0, tiled=True)


def scatter_sum(values, axes):
    return lax.psum_scatter(values, axes, scatter_dimension=0, tiled=True)


def gelu_parts(value):
    phi = 0.5 * lax.erfc(-value * math.sqrt(0.5))
    density = jnp.exp(-0.5 * value * value) * (1.0 / math.sqrt(2.0 * math.pi))
    return value * phi, phi + value * density


def body(
    hidden_in,
    token_marks,
    out_grad,
    qkv_weight,
    proj_weight,
    gate_weight,
    up_weight,
    down_weight,
    first_gain,
    first_shift,
    second_gain,
    second_shift,
):
    micro_count, _, pos_count, width = hidden_in.shape
    rows_own = qkv_weight.shape[0]
    units = gate_weight.shape[1]
    head_ways = math.prod(lax.axis_size(name) for name in HEAD_AXES)
    unit_ways = math.prod(lax.axis_size(name) for name in UNIT_AXES)
    device_count = math.prod(lax.axis_size(name) for name in ALL)
    chunk_count = lax.axis_size("y") * lax.axis_size("c")
    row_length = pos_count * chunk_count
    x_size = lax.axis_size("x")
    own = micro_count * pos_count
    head_width = width // head_ways
    heads_here = head_width // HEAD_DIM
    unit_width = -(-units // (unit_ways * LANES)) * LANES
    unit_pad = unit_width * unit_ways - units

    small = jnp.stack([first_gain, first_shift, second_gain, second_shift])[None]
    small_all = gather(small, ALL).transpose(1, 0, 2).reshape(4, width).astype(jnp.float32)
    gain_one, shift_one, gain_two, shift_two = (small_all[i][None] for i in range(4))
    marks = gather(token_marks.reshape(1, micro_count, pos_count, 3), HEAD_AXES)

    qkv_parts = (
        qkv_weight.reshape(rows_own, 3, head_ways, head_width)
        .transpose(2, 0, 1, 3)
        .reshape(head_ways * rows_own, 3 * head_width)
    )
    qkv_here = gather(
        lax.all_to_all(qkv_parts, HEAD_AXES, split_axis=0, concat_axis=0, tiled=True), HEAD_COPIES
    )
    proj_full = gather(proj_weight, ALL)

    sizes = [lax.axis_size(name) for name in ALL]

    ffn = jnp.stack([gate_weight, up_weight, down_weight])
    ffn = jnp.pad(ffn, ((0, 0), (0, 0), (0, unit_pad)))
    ffn = (
        ffn.reshape(3, rows_own, unit_ways, unit_width)
        .transpose(2, 0, 1, 3)
        .reshape(unit_ways * 3, rows_own, unit_width)
    )
    ffn = lax.all_to_all(ffn, UNIT_AXES, split_axis=0, concat_axis=0, tiled=True)

    def unit_full(index):
        part = ffn.reshape(unit_ways, 3, rows_own, unit_width)[:, index]
        whole = gather(part, UNIT_COPIES)
        zo, zi, x, y, c = sizes
        return (
            whole.reshape(zo, x, y, zi, c, rows_own, unit_width)
            .transpose(0, 3, 1, 2, 4, 5, 6)
            .reshape(width, unit_width)
        )

    gate_here, up_here, down_here = (unit_full(index) for index in range(3))

    x_own = hidden_in.reshape(own, width)
    x_all = gather(x_own, HEAD_AXES)
    mixed = dot(x_all, qkv_here)

    def to_rows(values):
        inner = values.shape[1:]
        values = values.reshape((x_size, chunk_count, micro_count, pos_count) + inner)
        return jnp.swapaxes(values, 1, 2).reshape((x_size * micro_count, row_length) + inner)

    def from_rows(values):
        inner = values.shape[2:]
        values = values.reshape((x_size, micro_count, chunk_count, pos_count) + inner)
        return jnp.swapaxes(values, 1, 2).reshape((head_ways * own,) + inner)

    row_marks = to_rows(marks.reshape(head_ways * own, 3))
    cosine, sine = rotary_tables(row_marks[..., 2])
    cosine, sine = cosine[:, :, None, :], sine[:, :, None, :]
    mixed = to_rows(mixed).reshape(x_size * micro_count, row_length, 3, heads_here, HEAD_DIM)
    queries = low(rotate(mixed[:, :, 0], cosine, sine))
    key_rows = low(rotate(mixed[:, :, 1], cosine, sine))
    value_rows = low(mixed[:, :, 2])
    place = jnp.arange(row_length, dtype=jnp.int32)
    allowed = (row_marks[:, :, None, 0] == row_marks[:, None, :, 0]) & (
        (place[None, None, :] <= place[None, :, None])
        | (place[None, :] < row_marks[:, :, 1])[:, None, :]
    )
    score_scale = 1.0 / math.sqrt(HEAD_DIM)

    def pair(spec, left_side, right_side):
        return jnp.einsum(spec, left_side, right_side, preferred_element_type=jnp.float32)

    scores = pair("rqhd,rkhd->rhqk", queries, key_rows) * score_scale
    scores = jnp.where(allowed[:, None], scores, masked_score)
    exp_scores = jnp.exp(scores - jnp.max(scores, axis=-1, keepdims=True))
    probs = exp_scores / jnp.sum(exp_scores, axis=-1, keepdims=True)
    probs_low = low(probs)
    context = low(pair("rhqk,rkhd->rqhd", probs_low, value_rows))

    def heads_to_tokens(values):
        values = values.reshape(head_ways, own, head_width)
        values = lax.all_to_all(values, HEAD_AXES, split_axis=0, concat_axis=0, tiled=True)
        return values.transpose(1, 0, 2).reshape(own, width)

    def tokens_to_heads(values):
        values = values.reshape(own, head_ways, head_width).transpose(1, 0, 2)
        values = lax.all_to_all(values, HEAD_AXES, split_axis=0, concat_axis=0, tiled=True)
        return values.reshape(head_ways * own, head_width)

    context_own = heads_to_tokens(from_rows(context))
    first_sum = deep_alpha * x_own.astype(jnp.float32) + dot(context_own, proj_full)
    hat_one, inverse_one = norm_parts(first_sum)
    normed = low(hat_one * gain_one + shift_one)

    normed_all = gather(normed, UNIT_AXES)
    gate_val = dot(normed_all, gate_here)
    up_val = dot(normed_all, up_here)
    gelu_val, gelu_slope = gelu_parts(gate_val)
    active = low(gelu_val * up_val)
    down_val = scatter_sum(low(contract_last(active, down_here)), UNIT_AXES)
    second_sum = deep_alpha * normed.astype(jnp.float32) + down_val.astype(jnp.float32)
    hat_two, inverse_two = norm_parts(second_sum)
    layer_rows = low(hat_two * gain_two + shift_two)

    grad_own = out_grad.reshape(own, width).astype(jnp.float32)
    gain_two_grad = jnp.sum(grad_own * hat_two, axis=0)
    shift_two_grad = jnp.sum(grad_own, axis=0)
    d_second = norm_back(grad_own, hat_two, inverse_two, gain_two)
    down_low = gather(low(d_second), UNIT_AXES)
    d_active = dot(down_low, down_here)
    gate_low = low(d_active * up_val * gelu_slope)
    up_low = low(d_active * gelu_val)
    d_normed_part = low(contract_last(gate_low, gate_here) + contract_last(up_low, up_here))
    d_normed = deep_alpha * d_second + scatter_sum(d_normed_part, UNIT_AXES).astype(jnp.float32)

    def unit_grad(left_side, right_side):
        zo, zi, x, y, c = sizes
        part = low(contract_first(left_side, right_side))
        part = (
            part.reshape(zo, zi, x, y, c, rows_own, unit_width)
            .transpose(0, 2, 3, 1, 4, 5, 6)
            .reshape(width, unit_width)
        )
        part = scatter_sum(part, UNIT_COPIES).reshape(unit_ways, rows_own, unit_width)
        part = lax.all_to_all(part, UNIT_AXES, split_axis=0, concat_axis=0, tiled=True)
        part = part.transpose(1, 0, 2).reshape(rows_own, unit_ways * unit_width)
        return part[:, :units].astype(jnp.float32)

    down_grad = unit_grad(down_low, active)
    gate_grad = unit_grad(normed_all, gate_low)
    up_grad = unit_grad(normed_all, up_low)

    gain_one_grad = jnp.sum(d_normed * hat_one, axis=0)
    shift_one_grad = jnp.sum(d_normed, axis=0)
    d_first = norm_back(d_normed, hat_one, inverse_one, gain_one)
    branch_low = low(d_first)
    small_grads = jnp.stack([gain_one_grad, shift_one_grad, gain_two_grad, shift_two_grad])
    small_grads = small_grads.reshape(4, device_count, rows_own).transpose(1, 0, 2)
    small_grads = scatter_sum(small_grads, ALL)[0]

    proj_grad = scatter_sum(low(contract_first(context_own, branch_low)), ALL).astype(jnp.float32)
    d_context = to_rows(tokens_to_heads(low(contract_last(branch_low, proj_full))))
    d_context = d_context.reshape(x_size * micro_count, row_length, heads_here, HEAD_DIM)
    d_probs = pair("rqhd,rkhd->rhqk", d_context, value_rows)
    d_scores = low(probs * (d_probs - jnp.sum(probs * d_probs, axis=-1, keepdims=True)))
    d_query = pair("rhqk,rkhd->rqhd", d_scores, key_rows) * score_scale
    d_keys = pair("rhqk,rqhd->rkhd", d_scores, queries) * score_scale
    d_values = pair("rhqk,rqhd->rkhd", probs_low, d_context)
    d_mixed = low(
        jnp.stack(
            [rotate(d_query, cosine, -sine), rotate(d_keys, cosine, -sine), d_values], axis=2
        )
    )
    d_mixed = from_rows(d_mixed.reshape(x_size * micro_count, row_length, 3 * head_width))
    d_input = scatter_sum(low(contract_last(d_mixed, qkv_here)), HEAD_AXES).astype(jnp.float32)
    d_input = deep_alpha * d_first + d_input

    qkv_part = scatter_sum(low(contract_first(x_all, d_mixed)), HEAD_COPIES)
    qkv_part = lax.all_to_all(
        qkv_part.reshape(head_ways, rows_own, 3 * head_width),
        HEAD_AXES,
        split_axis=0,
        concat_axis=0,
        tiled=True,
    )
    qkv_grad = (
        qkv_part.reshape(head_ways, rows_own, 3, head_width)
        .transpose(1, 2, 0, 3)
        .reshape(rows_own, 3 * width)
        .astype(jnp.float32)
    )
    return (
        layer_rows.reshape(micro_count, 1, pos_count, width),
        low(d_input).reshape(micro_count, 1, pos_count, width),
        qkv_grad,
        proj_grad,
        gate_grad,
        up_grad,
        down_grad,
        small_grads[0],
        small_grads[1],
        small_grads[2],
        small_grads[3],
    )


def solution(mesh):
    seq_size, ctx_size = mesh.shape["seq"], mesh.shape["ctx"]
    cores, x_size = 2, 2
    zi_size = math.gcd(4, seq_size // x_size)
    zo_size = seq_size // (x_size * zi_size)
    devices = np.asarray(mesh.devices).reshape(
        zo_size, zi_size, x_size, ctx_size // cores, cores
    )
    inner = Mesh(devices, ALL)
    tokens = P(None, ("zo", "zi", "x"), ("y", "c"), None)
    matrix = P(ALL, None)
    vector = P(ALL)
    return jax.shard_map(
        body,
        mesh=inner,
        in_specs=(tokens,) * 3 + (matrix,) * 5 + (vector,) * 4,
        out_specs=(tokens,) * 2 + (matrix,) * 5 + (vector,) * 4,
        check_vma=False,
    )
```

time: 3090 us -> 1090 us (0.35)
  the two profiles are of different devices: /device:TPU:11 before, /device:TPU:0 now
where the time goes in v1:
time: 1090 us; the launch traced here: 1080 us
  waiting for transfers between devices  609 us (56%)
  blocking collectives  238 us (22%)
  matrix products  109 us (10%)
  local copies, waits for them, and re-layouts  62.4 us (6%)
  other arithmetic  25.4 us (2%)
  starting transfers between devices  22.2 us (2%)
  between operations  15.2 us (1%)
    reduce_scatter x8, waiting for transfers between devices, scatter_sum(): return lax.psum_scatter(values, axes, scatter_dimension=0, tiled=True)  322 us
    all_gather x8, waiting for transfers between devices, gather(): return lax.all_gather(values, axes, axis=0, tiled=True)  246 us
    all_to_all x1, blocking collectives, body(): lax.all_to_all(ffn, UNIT_AXES, split_axis=0, concat_axis=0, tiled=True)  110 us
    all_gather x2, blocking collectives, gather(): return lax.all_gather(values, axes, axis=0, tiled=True)  54.2 us
    dot_general x5, matrix products, dot(): return jnp.dot(left_side, right_side, preferred_element_type=jnp.float32)  40.4 us
    all_to_all x3, waiting for transfers between devices, unit_grad(): lax.all_to_all(part, UNIT_AXES, split_axis=0, concat_axis=0, tiled=True)  39.2 us
    unnamed x1, blocking collectives  38.2 us
    dot_general x5, matrix products, contract_first(): lax.dot_general(left_side, right_side, (((0,), (0,)), ((), ())), preferre...  31.4 us
  transfers between devices with their start and end apart: 21, of which 14 were waited for; matrix products, arithmetic and copies ran while one was open for 13% of the time, Pallas kernels for 0%

profile of v1, /device:TPU:0, one launch (start us, length us, event | category | flops | bytes accessed | tf_op | source)
XLA Modules:
  0.0 1080.9 jit_solution(17472272349894451296)
XLA Ops:
  9.9 17.0 %all_to_all.47 = bf16[8,64,768]{2,1,0:T(8,128)(2,1)} all-to-all(bf16[8,64,768]{2,1,0:T(8,128)(2,1)S(1)} %all_to_all.29), channel_id=1, replica_groups=mesh['zo'=1,'zi'=4,'x'=2,'y'=2,'c'=2] {'x','y','c'}, dimensions={0} | all-to-all | bytes 1572864 | tf_op jit(solution)/shard_map/all_to_all | solution.py:129
  30.1 109.8 %all_to_all.48 = bf16[24,64,768]{2,1,0:T(8,128)(2,1)S(1)} all-to-all(bf16[24,64,768]{2,1,0:T(8,128)(2,1)S(1)} %bitcast.211), channel_id=1, replica_groups=mesh['zo'=1,'zi'=4,'x'=2,'y'=2,'c'=2] {'zi','c'}, dimensions={0} | all-to-all | bytes 4718592 | tf_op jit(solution)/shard_map/all_to_all | solution.py:142
  142.1 9.0 all-gather
  151.2 3.1 fusion.46
  154.8 21.9 %all-gather.15.cloned.1.call-done = bf16[1024,2048]{1,0:T(8,128)(2,1)} async-done(((bf16[128,2048]{1,0:T(8,128)(2,1)}), bf16[1024,2048]{1,0:T(8,128)(2,1)}) %all-gather.15.cloned.1.call-update) | async-done | bytes 4194320 | tf_op jit(solution)/shard_map/all_gather | solution.py:76
  176.8 6.1 fusion.59
  183.2 2.8 reshape_reshape.16
  202.0 3.5 all-to-all-start.1
  205.6 45.2 %all-gather.5 = bf16[32,4,64]{2,1,0:T(4,128)(2,1)S(1)} all-gather(bf16[1,4,64]{2,1,0:T(4,128)(2,1)S(1)} %maximum_bitcast_fusion.3), channel_id=3, replica_groups=mesh['zo'=1,'zi'=4,'x'=2,'y'=2,'c'=2] {'zo','zi','x','y','c'}, dimensions={0}, use_global_device_ids=true | all-gather | bytes 16896 | tf_op jit(solution)/shard_map/all_gather | solution.py:76
  251.5 10.7 all-gather.19.cloned.1.call-done
  262.2 4.7 fusion.58
  268.4 38.6 %all-gather.25.cloned.1.call-done = bf16[32,1,64,768]{3,2,1,0:T(8,128)(2,1)} async-done(((bf16[8,1,64,768]{3,2,1,0:T(8,128)(2,1)}), bf16[32,1,64,768]{3,2,1,0:T(8,128)(2,1)}) %all-gather.25.cloned.1.call-update) | async-done | bytes 3145744 | tf_op jit(solution)/shard_map/all_gather | solution.py:76
  307.0 4.0 copy.165
  311.0 42.2 %all-gather.27.cloned.1.call-done = bf16[32,1,64,768]{3,2,1,0:T(8,128)(2,1)} async-done(((bf16[8,1,64,768]{3,2,1,0:T(8,128)(2,1)}), bf16[32,1,64,768]{3,2,1,0:T(8,128)(2,1)}) %all-gather.27.cloned.1.call-update) | async-done | bytes 3145744 | tf_op jit(solution)/shard_map/all_gather | solution.py:76
  353.1 3.9 copy.166
  357.1 42.2 %all-gather.29.cloned.1.call-done = bf16[32,1,64,768]{3,2,1,0:T(8,128)(2,1)} async-done(((bf16[8,1,64,768]{3,2,1,0:T(8,128)(2,1)}), bf16[32,1,64,768]{3,2,1,0:T(8,128)(2,1)}) %all-gather.29.cloned.1.call-update) | async-done | bytes 3145744 | tf_op jit(solution)/shard_map/all_gather | solution.py:76
  399.3 3.9 copy.167
  403.2 45.2 %all-gather.21.cloned.1.call-done = bf16[1024,2048]{1,0:T(8,128)(2,1)} async-done(((bf16[128,2048]{1,0:T(8,128)(2,1)}), bf16[1024,2048]{1,0:T(8,128)(2,1)}) %all-gather.21.cloned.1.call-update) | async-done | bytes 4194320 | tf_op jit(solution)/shard_map/all_gather | solution.py:76
  448.4 6.3 fusion.60
  454.7 12.5 %multiply_convert_fusion.1 = (bf16[1024,768]{1,0:T(8,128)(2,1)S(1)}, f32[1024,768]{1,0:T(8,128)}, f32[1024,768]{1,0:T(8,128)}, f32[1024,768]{1,0:T(8,128)}) fusion(f32[1024,768]{1,0:T(8,128)S(1)} %fusion.60, bf16[1024,2048]{1,0:T(8,128)(2,1)S(1)} %copy-done.32, bf16[2048,768]{1,0:T(8,128)(2,1)S(1)} %bitcast.223), kind=kOutput, calls=%fused_computation.25 | convolution fusion | flops 3273129984 | bytes 21495808 | tf_op jit(solution)/shard_map/dot_general | solution.py:37
  468.4 5.0 convolution_convert_fusion.2
  474.8 47.5 %reduce-scatter.9.cloned.1.call-done = bf16[128,2048]{1,0:T(8,128)(2,1)} async-done(((bf16[1024,2048]{1,0:T(8,128)(2,1)}), bf16[128,2048]{1,0:T(8,128)(2,1)}) %reduce-scatter.9.cloned.1.call-update) | async-done | bytes 524304 | tf_op jit(solution)/shard_map/reduce_scatter | solution.py:80
  529.1 45.1 %all-gather.23.cloned.1.call-done = bf16[1024,2048]{1,0:T(8,128)(2,1)} async-done(((bf16[128,2048]{1,0:T(8,128)(2,1)}), bf16[1024,2048]{1,0:T(8,128)(2,1)}) %all-gather.23.cloned.1.call-update) | async-done | bytes 4194320 | tf_op jit(solution)/shard_map/all_gather | solution.py:76
  574.1 10.8 multiply_convert_fusion
  584.9 3.4 fusion.61
  588.4 5.0 add_convert_fusion
  593.5 6.2 convolution_convert_fusion.3
  601.9 6.2 convolution_convert_fusion.4
  610.2 6.3 convolution_convert_fusion.5
  618.6 23.8 %reduce-scatter.11.cloned.1.call-done = bf16[128,2048]{1,0:T(8,128)(2,1)} async-done(((bf16[1024,2048]{1,0:T(8,128)(2,1)}), bf16[128,2048]{1,0:T(8,128)(2,1)}) %reduce-scatter.11.cloned.1.call-update) | async-done | bytes 524304 | tf_op jit(solution)/shard_map/reduce_scatter | solution.py:80
  642.4 3.0 multiply_reduce_fusion.1
  645.9 6.3 convolution_convert_fusion.7
  652.2 18.6 %all_to_all.49 = bf16[8,128,256]{2,1,0:T(8,128)(2,1)} all-to-all(bf16[8,128,256]{2,1,0:T(8,128)(2,1)S(1)} %bitcast.244), channel_id=1, replica_groups=mesh['zo'=1,'zi'=4,'x'=2,'y'=2,'c'=2] {'x','y','c'}, dimensions={0} | all-to-all | bytes 1048576 | tf_op jit(solution)/shard_map/all_to_all | solution.py:201
  681.4 2.8 copy.181
  684.1 5.0 convert_element_type.164
  691.8 7.1 fusion.18
  699.2 7.8 convolution_convert_fusion.1
  707.1 5.6 convolution_convert_fusion
  712.8 3.6 all-to-all-start.7
  716.3 23.8 %reduce-scatter.21.cloned.1.call-done = bf16[512,768]{1,0:T(8,128)(2,1)} async-done(((bf16[2048,768]{1,0:T(8,128)(2,1)}), bf16[512,768]{1,0:T(8,128)(2,1)}) %reduce-scatter.21.cloned.1.call-update) | async-done | bytes 786448 | tf_op jit(solution)/shard_map/reduce_scatter | solution.py:80
  740.1 4.6 all-to-all-start.6
  744.8 42.3 %reduce-scatter.19.cloned.1.call-done = bf16[512,768]{1,0:T(8,128)(2,1)} async-done(((bf16[2048,768]{1,0:T(8,128)(2,1)}), bf16[512,768]{1,0:T(8,128)(2,1)}) %reduce-scatter.19.cloned.1.call-update) | async-done | bytes 786448 | tf_op jit(solution)/shard_map/reduce_scatter | solution.py:80
  787.1 4.6 all-to-all-start.5
  793.7 39.2 %all-to-all-done.5 = bf16[8,64,768]{2,1,0:T(8,128)(2,1)S(1)} async-done(((bf16[8,64,768]{2,1,0:T(8,128)(2,1)}), bf16[8,64,768]{2,1,0:T(8,128)(2,1)S(1)}, u32[]{:S(2)}, u32[]{:S(2)}) %all-to-all-start.5) | async-done | bytes 786464 | tf_op jit(solution)/shard_map/all_to_all | solution.py:239
  836.7 38.2 %all-reduce.1 = f32[32,4,64]{2,1,0:T(4,128)S(1)} all-reduce(f32[32,4,64]{2,1,0:T(4,128)S(1)} %maximum_bitcast_fusion.2), channel_id=15, replica_groups=mesh['zo'=1,'zi'=4,'x'=2,'y'=2,'c'=2] {'zo','zi','x','y','c'}, use_global_device_ids=true, to_apply=%region_23.24.clone | all-reduce | flops 8192 | bytes 65536
  877.4 4.4 all-to-all-start.4
  882.3 37.5 %reduce-scatter.13.cloned.1.call-done = bf16[128,2048]{1,0:T(8,128)(2,1)} async-done(((bf16[1024,2048]{1,0:T(8,128)(2,1)}), bf16[128,2048]{1,0:T(8,128)(2,1)}) %reduce-scatter.13.cloned.1.call-update) | async-done | bytes 524304 | tf_op jit(solution)/shard_map/reduce_scatter | solution.py:80
  925.2 147.0 %reduce-scatter.17.cloned.1.call-done = bf16[64,2048]{1,0:T(8,128)(2,1)} async-done(((bf16[2048,2048]{1,0:T(8,128)(2,1)}), bf16[64,2048]{1,0:T(8,128)(2,1)}) %reduce-scatter.17.cloned.1.call-update) | async-done | bytes 262160 | tf_op jit(solution)/shard_map/reduce_scatter | solution.py:80
  (200 shorter events, 72.4 us)
Async XLA Ops:
  7.2 147.7 %all-gather.17.cloned.1.call-start = ((), (), s32[]{:S(2)}) async-start(), calls=%async_computation.17 | async-start | bytes 3932160 | tf_op jit(solution)/shard_map/all_gather | solution.py:76
  8.5 20.0 %copy-start.22 = (bf16[64,5461]{1,0:T(8,128)(2,1)S(1)}, bf16[64,5461]{1,0:T(8,128)(2,1)}, u32[]{:S(2)}) copy-start(bf16[64,5461]{1,0:T(8,128)(2,1)} %param.19) | copy-start | bytes 2097028
  8.5 20.0 %copy-start.23 = (bf16[64,5461]{1,0:T(8,128)(2,1)S(1)}, bf16[64,5461]{1,0:T(8,128)(2,1)}, u32[]{:S(2)}) copy-start(bf16[64,5461]{1,0:T(8,128)(2,1)} %param.18) | copy-start | bytes 2097028
  9.9 18.6 %copy-start.24 = (bf16[64,5461]{1,0:T(8,128)(2,1)S(1)}, bf16[64,5461]{1,0:T(8,128)(2,1)}, u32[]{:S(2)}) copy-start(bf16[64,5461]{1,0:T(8,128)(2,1)} %param.17) | copy-start | bytes 2097028
  27.0 149.8 %all-gather.15.cloned.1.call-start = ((), (), s32[]{:S(2)}) async-start(), calls=%async_computation.16 | async-start | bytes 4718592 | tf_op jit(solution)/shard_map/all_gather | solution.py:76
  27.7 234.5 %all-gather.19.cloned.1.call-start = ((), (), s32[]{:S(2)}) async-start(), calls=%async_computation.18 | async-start | bytes 8650752 | tf_op jit(solution)/shard_map/all_gather | solution.py:76
  28.4 278.6 %all-gather.25.cloned.1.call-start = ((), (), s32[]{:S(2)}) async-start(), calls=%async_computation.29 | async-start | bytes 3932160 | tf_op jit(solution)/shard_map/all_gather | solution.py:76
  139.9 2.1 copy-start.27
  141.4 211.7 %all-gather.27.cloned.1.call-start = ((), (), s32[]{:S(2)}) async-start(), calls=%async_computation.30 | async-start | bytes 3932160 | tf_op jit(solution)/shard_map/all_gather | solution.py:76
  142.0 257.3 %all-gather.29.cloned.1.call-start = ((), (), s32[]{:S(2)}) async-start(), calls=%async_computation.31 | async-start | bytes 3932160 | tf_op jit(solution)/shard_map/all_gather | solution.py:76
  187.9 6.5 copy-start.26
  191.9 5.2 copy-start.11
  191.9 5.2 copy-start.13
  192.0 5.2 copy-start.15
  192.0 5.2 copy-start.17
  197.1 8.4 copy-start.28
  197.2 8.4 copy-start.29
  197.2 8.4 copy-start.30
  197.2 8.4 copy-start.31
  197.2 65.0 %copy-start.19 = (bf16[2,1,64,2048]{3,2,1,0:T(8,128)(2,1)S(1)}, bf16[2,1,64,2048]{3,2,1,0:T(8,128)(2,1)}, u32[]{:S(2)}) copy-start(bf16[2,1,64,2048]{3,2,1,0:T(8,128)(2,1)} %param.12) | copy-start | bytes 1572868
  202.0 49.2 %all-to-all-start.1 = ((bf16[8,128,256]{2,1,0:T(8,128)(2,1)}), bf16[8,128,256]{2,1,0:T(8,128)(2,1)S(1)}, u32[]{:S(2)}, u32[]{:S(2)}) async-start(bf16[8,128,256]{2,1,0:T(8,128)(2,1)} %reshape_reshape.18), calls=%async_computation.1 | async-start | bytes 1048576 | tf_op jit(solution)/shard_map/all_to_all | solution.py:196
  205.5 242.8 %all-gather.21.cloned.1.call-start = ((), (), s32[]{:S(2)}) async-start(), calls=%async_computation.19 | async-start | bytes 4718592 | tf_op jit(solution)/shard_map/all_gather | solution.py:76
  268.3 253.9 %reduce-scatter.9.cloned.1.call-start = ((), (), s32[]{:S(2)}) async-start(), calls=%async_computation.20 | async-start | bytes 4718592 | tf_op jit(solution)/shard_map/reduce_scatter | solution.py:80
  448.4 6.3 copy-start.4
  448.4 6.3 copy-start.32
  454.6 12.6 %copy-start.33 = (f32[1024,768]{1,0:T(8,128)}, f32[1024,768]{1,0:T(8,128)S(1)}, u32[]{:S(2)}) copy-start(f32[1024,768]{1,0:T(8,128)S(1)} %fusion.60) | copy-start | bytes 9437188
  454.7 13.7 %copy-start.6 = (bf16[1,4,2,2,2,64,768]{6,5,4,3,2,1,0:T(8,128)(2,1)S(1)}, bf16[1,4,2,2,2,64,768]{6,5,4,3,2,1,0:T(8,128)(2,1)}, u32[]{:S(2)}) copy-start(bf16[1,4,2,2,2,64,768]{6,5,4,3,2,1,0:T(8,128)(2,1)} %copy.167) | copy-start | bytes 9437188
  473.4 100.7 %all-gather.23.cloned.1.call-start = ((), (), s32[]{:S(2)}) async-start(), calls=%async_computation.21 | async-start | bytes 4718592 | tf_op jit(solution)/shard_map/all_gather | solution.py:76
  522.3 3.1 copy-start
  528.6 113.8 %reduce-scatter.11.cloned.1.call-start = ((), (), s32[]{:S(2)}) async-start(), calls=%async_computation.22 | async-start | bytes 4718592 | tf_op jit(solution)/shard_map/reduce_scatter | solution.py:80
  574.1 10.8 %copy-start.3 = (bf16[1,4,2,2,2,64,768]{6,5,4,3,2,1,0:T(8,128)(2,1)S(1)}, bf16[1,4,2,2,2,64,768]{6,5,4,3,2,1,0:T(8,128)(2,1)}, u32[]{:S(2)}) copy-start(bf16[1,4,2,2,2,64,768]{6,5,4,3,2,1,0:T(8,128)(2,1)} %copy.165) | copy-start | bytes 9437188
  584.9 3.5 copy-start.34
  584.9 3.5 copy-start.35
  584.9 3.5 copy-start.5
  593.5 119.3 %reduce-scatter.23.cloned.1.call-start = ((), (), s32[]{:S(2)}) async-start(), calls=%async_computation.28 | async-start | bytes 3932160 | tf_op jit(solution)/shard_map/reduce_scatter | solution.py:80
  601.7 138.4 %reduce-scatter.21.cloned.1.call-start = ((), (), s32[]{:S(2)}) async-start(), calls=%async_computation.27 | async-start | bytes 3932160 | tf_op jit(solution)/shard_map/reduce_scatter | solution.py:80
  610.2 176.9 %reduce-scatter.19.cloned.1.call-start = ((), (), s32[]{:S(2)}) async-start(), calls=%async_computation.26 | async-start | bytes 3932160 | tf_op jit(solution)/shard_map/reduce_scatter | solution.py:80
  618.5 256.5 %reduce-scatter.15.cloned.1.call-start = ((), (), s32[]{:S(2)}) async-start(), calls=%async_computation.24 | async-start | bytes 3932160 | tf_op jit(solution)/shard_map/reduce_scatter | solution.py:80
  673.8 2.6 copy-start.20
  676.4 1.7 copy-start.12
  698.9 220.9 %reduce-scatter.13.cloned.1.call-start = ((), (), s32[]{:S(2)}) async-start(), calls=%async_computation.23 | async-start | bytes 4718592 | tf_op jit(solution)/shard_map/reduce_scatter | solution.py:80
  707.0 365.1 %reduce-scatter.17.cloned.1.call-start = ((), (), s32[]{:S(2)}) async-start(), calls=%async_computation.25 | async-start | bytes 8650752 | tf_op jit(solution)/shard_map/reduce_scatter | solution.py:80
  712.8 27.4 %all-to-all-start.7 = ((bf16[8,64,768]{2,1,0:T(8,128)(2,1)}), bf16[8,64,768]{2,1,0:T(8,128)(2,1)S(1)}, u32[]{:S(2)}, u32[]{:S(2)}) async-start(bf16[8,64,768]{2,1,0:T(8,128)(2,1)} %bitcast.250), calls=%async_computation.15 | async-start | bytes 1572864 | tf_op jit(solution)/shard_map/all_to_all | solution.py:239
  740.1 46.9 %all-to-all-start.6 = ((bf16[8,64,768]{2,1,0:T(8,128)(2,1)}), bf16[8,64,768]{2,1,0:T(8,128)(2,1)S(1)}, u32[]{:S(2)}, u32[]{:S(2)}) async-start(bf16[8,64,768]{2,1,0:T(8,128)(2,1)} %bitcast.251), calls=%async_computation.13 | async-start | bytes 1572864 | tf_op jit(solution)/shard_map/all_to_all | solution.py:239
  787.1 45.8 %all-to-all-start.5 = ((bf16[8,64,768]{2,1,0:T(8,128)(2,1)}), bf16[8,64,768]{2,1,0:T(8,128)(2,1)S(1)}, u32[]{:S(2)}, u32[]{:S(2)}) async-start(bf16[8,64,768]{2,1,0:T(8,128)(2,1)} %bitcast.249), calls=%async_computation.11 | async-start | bytes 1572864 | tf_op jit(solution)/shard_map/all_to_all | solution.py:239
  792.8 40.2 %copy-start.7 = (bf16[8,8,8,768]{3,2,0,1:T(8,128)(2,1)S(1)}, bf16[8,8,8,768]{3,2,0,1:T(8,128)(2,1)}, u32[]{:S(2)}) copy-start(bf16[8,8,8,768]{3,2,0,1:T(8,128)(2,1)} %copy.211) | copy-start | bytes 2359300
  793.7 40.4 %copy-start.8 = (bf16[8,8,8,768]{3,2,0,1:T(8,128)(2,1)S(1)}, bf16[8,8,8,768]{3,2,0,1:T(8,128)(2,1)}, u32[]{:S(2)}) copy-start(bf16[8,8,8,768]{3,2,0,1:T(8,128)(2,1)} %copy.210) | copy-start | bytes 2359300
  877.4 44.4 %all-to-all-start.4 = ((bf16[8,64,768]{2,1,0:T(8,128)(2,1)}), bf16[8,64,768]{2,1,0:T(8,128)(2,1)S(1)}, u32[]{:S(2)}, u32[]{:S(2)}) async-start(bf16[8,64,768]{2,1,0:T(8,128)(2,1)} %bitcast.56), calls=%async_computation.8 | async-start | bytes 1572864 | tf_op jit(solution)/shard_map/all_to_all | solution.py:273
  (10 other events, 11.9 us)
Sparse Core Ops, SparseCore 0:
  27.1 113.2 all-gather.16
  142.2 34.4 all-gather.14
  179.6 82.5 all-gather.18
  264.5 42.4 all-gather.24
  309.3 43.8 all-gather.26
  355.4 43.8 all-gather.28
  401.5 46.8 all-gather.20
  473.5 48.6 reduce-scatter.8
  528.7 45.3 all-gather.22
  593.6 48.7 reduce-scatter.10
  645.3 47.9 reduce-scatter.22
  696.2 43.8 reduce-scatter.20
  743.1 43.8 reduce-scatter.18
  789.2 70.6 reduce-scatter.14
  863.1 56.6 reduce-scatter.12
  921.9 150.1 reduce-scatter.16

commit v2 on v1

--- a/solution.py
+++ b/solution.py
@@ -4,6 +4,8 @@
 import jax.numpy as jnp
 import numpy as np
 from jax import lax
+from jax.experimental import pallas as pl
+from jax.experimental.pallas import tpu as pltpu
 from jax.sharding import Mesh
 from jax.sharding import PartitionSpec as P
 
@@ -84,6 +86,425 @@
     phi = 0.5 * lax.erfc(-value * math.sqrt(0.5))
     density = jnp.exp(-0.5 * value * value) * (1.0 / math.sqrt(2.0 * math.pi))
     return value * phi, phi + value * density
+
+
+MESH = pl.DeviceIdType.MESH
+
+
+class Wire:
+    def __init__(self, send_sems, recv_sems):
+        self.send_sems, self.recv_sems = send_sems, recv_sems
+        self.keys, self.sent = {}, []
+
+    def number(self, key):
+        return self.keys.setdefault(key, len(self.keys))
+
+    def copy(self, key, source, target, device):
+        index = self.number(key)
+        return pltpu.make_async_remote_copy(
+            src_ref=source,
+            dst_ref=target,
+            send_sem=self.send_sems.at[index],
+            recv_sem=self.recv_sems.at[index],
+            device_id=device,
+            device_id_type=MESH,
+        )
+
+    def send(self, key, source, target, device, when=None):
+        copy = self.copy(key, source, target, device)
+        if when is None:
+            copy.start()
+        else:
+            pl.when(when)(copy.start)
+        self.sent.append((copy, when))
+
+    def arrive(self, key, target, device, when=None):
+        copy = self.copy(key, target, target, device)
+        if when is None:
+            copy.wait_recv()
+        else:
+            pl.when(when)(copy.wait_recv)
+
+    def drain(self):
+        for copy, when in self.sent:
+            if when is None:
+                copy.wait_send()
+            else:
+                pl.when(when)(copy.wait_send)
+
+
+def flip(value, bit):
+    return 1 - value if bit else value
+
+
+def enter(devices):
+    barrier = pltpu.get_barrier_semaphore()
+    for device in devices:
+        pl.semaphore_signal(barrier, inc=1, device_id=device, device_id_type=MESH)
+    pl.semaphore_wait(barrier, len(devices))
+
+
+class Place:
+    def __init__(self):
+        self.zo, self.zi, self.x, self.y, self.c = (lax.axis_index(name) for name in ALL)
+        self.rank = self.x * 4 + self.y * 2 + self.c
+        self.unit = self.zi * 2 + self.c
+
+    def plane(self, delta):
+        dx, dy, dc = delta >> 2 & 1, delta >> 1 & 1, delta & 1
+        x, y, c = flip(self.x, dx), flip(self.y, dy), flip(self.c, dc)
+        return (self.zo, self.zi, x, y, c), x * 4 + y * 2 + c
+
+    def column(self, step):
+        other = lax.rem(self.unit + step + 8, 8)
+        return (self.zo, other // 2, self.x, self.y, lax.rem(other, 2)), other
+
+    def line(self, z):
+        return (self.zo, z, self.x, self.y, self.c)
+
+    def neighbours(self):
+        plane = [self.plane(delta)[0] for delta in range(1, 8)]
+        column = []
+        for dz in range(1, 4):
+            z = lax.rem(self.zi + dz, 4)
+            column += [(self.zo, z, self.x, self.y, core) for core in (0, 1)]
+        return plane + column
+
+
+def gather_kernel(qkv_in, ffn_in, x_in, qkv_out, ffn_out, x_out, send_sems, recv_sems, own_sems):
+    at = Place()
+    wire = Wire(send_sems, recv_sems)
+    enter(at.neighbours())
+    x_side, y_side, core_side = at.plane(4)[0], at.plane(2)[0], at.plane(1)[0]
+    half = x_in.shape[0] // 2
+
+    own = [
+        pltpu.make_async_copy(x_in, x_out.at[at.rank], own_sems.at[0]),
+        pltpu.make_async_copy(qkv_in.at[at.rank], qkv_out.at[at.zi, at.rank], own_sems.at[1]),
+        pltpu.make_async_copy(
+            ffn_in.at[at.unit], ffn_out.at[:, at.zi, at.x, at.y, at.c], own_sems.at[2]
+        ),
+    ]
+    for copy in own:
+        copy.start()
+
+    for step in (1, 7, 2, 6, 3, 5, 4):
+        device, other = at.column(step)
+        slot = ffn_out.at[:, at.zi, at.x, at.y, at.c]
+        wire.send(("f", step), ffn_in.at[other], slot, device)
+    for delta in range(1, 8):
+        device, other = at.plane(delta)
+        wire.send(("q", delta), qkv_in.at[other], qkv_out.at[at.zi, at.rank], device)
+    wire.send("xx", x_in, x_out.at[at.rank], x_side)
+    wire.send("xy", x_in, x_out.at[at.rank], y_side)
+    wire.send("xc0", x_in, x_out.at[at.rank], core_side)
+    for copy in own:
+        copy.wait()
+
+    def qkv_slot(z, delta):
+        return qkv_out.at[jnp.clip(z, 0, 3), at.plane(delta)[1]]
+
+    up, down = at.line(jnp.minimum(at.zi + 1, 3)), at.line(jnp.maximum(at.zi - 1, 0))
+
+    def qkv_hop(hop, delta):
+        below, above = qkv_slot(at.zi - hop, delta), qkv_slot(at.zi + hop, delta)
+        if hop == 0:
+            if delta:
+                wire.arrive(("q", delta), below, at.plane(delta)[0])
+        else:
+            wire.arrive(("up", hop - 1, delta), below, down, at.zi >= hop)
+            wire.arrive(("down", hop - 1, delta), above, up, at.zi <= 3 - hop)
+        if hop < 3:
+            wire.send(("up", hop, delta), below, below, up, (at.zi >= hop) & (at.zi < 3))
+            wire.send(("down", hop, delta), above, above, down, (at.zi <= 3 - hop) & (at.zi > 0))
+
+    def ffn_slot(step, x, y):
+        source = lax.rem(at.unit - step + 8, 8)
+        return ffn_out.at[:, source // 2, x, y, lax.rem(source, 2)]
+
+    def ffn_first(step):
+        slot = ffn_slot(step, at.x, at.y)
+        if step:
+            wire.arrive(("f", step), slot, at.column(-step)[0])
+        wire.send(("fx", step), slot, slot, x_side)
+        wire.send(("fy", step), slot, slot, y_side)
+
+    def ffn_second(step, turn):
+        from_x, from_y = ffn_slot(step, 1 - at.x, at.y), ffn_slot(step, at.x, 1 - at.y)
+        wire.arrive(("fx", step), from_x, x_side)
+        wire.arrive(("fy", step), from_y, y_side)
+        if turn % 2:
+            wire.send(("fd", step), from_x, from_x, y_side)
+        else:
+            wire.send(("fd", step), from_y, from_y, x_side)
+
+    from_x, from_y, from_xy = (at.plane(delta)[1] for delta in (4, 2, 6))
+    low_half, high_half = pl.ds(0, half), pl.ds(half, half)
+    ffn_first(0)
+    wire.arrive("xx", x_out.at[from_x], x_side)
+    wire.send("xd0", x_out.at[from_x, low_half], x_out.at[from_x, low_half], y_side)
+    wire.send("xc1", x_out.at[from_x], x_out.at[from_x], core_side)
+    wire.arrive("xy", x_out.at[from_y], y_side)
+    wire.send("xd1", x_out.at[from_y, high_half], x_out.at[from_y, high_half], x_side)
+    wire.send("xc2", x_out.at[from_y], x_out.at[from_y], core_side)
+    for delta in range(8):
+        qkv_hop(0, delta)
+    wire.arrive("xd0", x_out.at[from_xy, low_half], y_side)
+    wire.arrive("xd1", x_out.at[from_xy, high_half], x_side)
+    wire.send("xc3", x_out.at[from_xy], x_out.at[from_xy], core_side)
+
+    steps = (1, 7, 2, 6, 3, 5, 4)
+    ffn_second(0, 0)
+    for turn, step in enumerate(steps):
+        ffn_first(step)
+        qkv_hop(1, turn)
+        if turn >= 2:
+            ffn_second(steps[turn - 2], turn - 2 + 1)
+    qkv_hop(1, 7)
+    for delta in range(8):
+        qkv_hop(2, delta)
+        if delta < 2:
+            ffn_second(steps[5 + delta], 5 + delta + 1)
+    for delta in range(8):
+        qkv_hop(3, delta)
+    for index, delta in enumerate((1, 5, 3, 7)):
+        other = at.plane(delta)[1]
+        wire.arrive("xc%d" % index, x_out.at[other], core_side)
+    for step in range(8):
+        wire.arrive(("fd", step), ffn_slot(step, 1 - at.x, 1 - at.y), x_side)
+    wire.drain()
+
+
+def reduce_kernel(
+    qkv_in,
+    ffn_in,
+    qkv_out,
+    ffn_out,
+    first_in,
+    second_in,
+    second_sum,
+    total,
+    up_in,
+    down_in,
+    up_sum,
+    down_sum,
+    qkv_total,
+    send_sems,
+    recv_sems,
+    own_sems,
+):
+    at = Place()
+    wire = Wire(send_sems, recv_sems)
+    enter(at.neighbours())
+    x_side, y_side = at.plane(4)[0], at.plane(2)[0]
+    steps = (4, 3, 5, 2, 6, 1, 7, 0)
+
+    def add(*terms):
+        whole = terms[0].astype(jnp.float32)
+        for term in terms[1:]:
+            whole = whole + term.astype(jnp.float32)
+        return whole.astype(jnp.bfloat16)
+
+    def owner(step):
+        other = at.column(step)[1]
+        return other // 2, lax.rem(other, 2)
+
+    for turn, step in enumerate(steps):
+        z, c = owner(step)
+        if turn % 2:
+            wire.send(("a", step), ffn_in.at[:, z, 1 - at.x, :, c], first_in.at[step], x_side)
+        else:
+            wire.send(("a", step), ffn_in.at[:, z, :, 1 - at.y, c], first_in.at[step], y_side)
+
+    def ffn_second(step, turn):
+        z, c = owner(step)
+        if turn % 2:
+            wire.arrive(("a", step), first_in.at[step], x_side)
+            mine = ffn_in[:, z, at.x, 1 - at.y, c]
+            second_sum[step] = add(mine, first_in[step, :, 1 - at.y])
+            wire.send(("b", step), second_sum.at[step], second_in.at[step], y_side)
+        else:
+            wire.arrive(("a", step), first_in.at[step], y_side)
+            mine = ffn_in[:, z, 1 - at.x, at.y, c]
+            second_sum[step] = add(mine, first_in[step, :, 1 - at.x])
+            wire.send(("b", step), second_sum.at[step], second_in.at[step], x_side)
+
+    def ffn_last(step, turn):
+        z, c = owner(step)
+        near = at.y if turn % 2 else at.x
+        wire.arrive(("b", step), second_in.at[step], x_side)
+        total[step] = add(ffn_in[:, z, at.x, at.y, c], first_in[step, :, near], second_in[step])
+        if step:
+            wire.send(("c", step), total.at[step], ffn_out.at[at.unit], at.column(step)[0])
+        else:
+            pltpu.make_async_copy(total.at[0], ffn_out.at[at.unit], own_sems.at[0]).start()
+
+    pieces = 4
+    wide = 8 // pieces
+    up, down = at.line(jnp.minimum(at.zi + 1, 3)), at.line(jnp.maximum(at.zi - 1, 0))
+
+    def qkv_pass(goal, piece):
+        part = pl.ds(piece * wide, wide)
+
+        if goal > 0:
+
+            @pl.when(at.zi < goal)
+            def _():
+                @pl.when(at.zi == 0)
+                def _():
+                    up_sum[goal, part] = qkv_in[goal, part]
+
+                @pl.when(at.zi > 0)
+                def _():
+                    wire.arrive(("u", goal, piece), up_in.at[goal, part], down)
+                    up_sum[goal, part] = add(qkv_in[goal, part], up_in[goal, part])
+
+            wire.send(
+                ("u", goal, piece),
+                up_sum.at[goal, part],
+                up_in.at[goal, part],
+                up,
+                at.zi < goal,
+            )
+        back = 3 - goal
+        if back < 3:
+
+            @pl.when(at.zi > back)
+            def _():
+                @pl.when(at.zi == 3)
+                def _():
+                    down_sum[back, part] = qkv_in[back, part]
+
+                @pl.when(at.zi < 3)
+                def _():
+                    wire.arrive(("d", back, piece), down_in.at[back, part], up)
+                    down_sum[back, part] = add(qkv_in[back, part], down_in[back, part])
+
+            wire.send(
+                ("d", back, piece),
+                down_sum.at[back, part],
+                down_in.at[back, part],
+                down,
+                at.zi > back,
+            )
+
+    def qkv_last(piece):
+        part = pl.ds(piece * wide, wide)
+        for goal in range(4):
+
+            @pl.when(at.zi == goal)
+            def _():
+                terms = [qkv_in[goal, part]]
+                if goal > 0:
+                    wire.arrive(("u", goal, piece), up_in.at[goal, part], down)
+                    terms.append(up_in[goal, part])
+                if goal < 3:
+                    wire.arrive(("d", goal, piece), down_in.at[goal, part], up)
+                    terms.append(down_in[goal, part])
+                qkv_total[part] = add(*terms)
+
+    turn = 0
+    order = [(goal, piece) for goal in (3, 2, 1) for piece in range(pieces)]
+    for index, (goal, piece) in enumerate(order):
+        qkv_pass(goal, piece)
+        if index < 8:
+            ffn_second(steps[index], index)
+        if index >= 3 and index - 3 < 8:
+            ffn_last(steps[index - 3], index - 3)
+    for index in range(len(order) - 3, 8):
+        ffn_last(steps[index], index)
+    for piece in range(pieces):
+        qkv_last(piece)
+    own_qkv = pltpu.make_async_copy(
+        qkv_total.at[at.rank], qkv_out.at[at.rank], own_sems.at[1]
+    )
+    own_qkv.start()
+    for delta in range(1, 8):
+        device, other = at.plane(delta)
+        wire.send(("q", delta), qkv_total.at[other], qkv_out.at[at.rank], device)
+    own_qkv.wait()
+    pltpu.make_async_copy(total.at[0], ffn_out.at[at.unit], own_sems.at[0]).wait()
+    for delta in range(1, 8):
+        device, other = at.plane(delta)
+        wire.arrive(("q", delta), qkv_out.at[other], device)
+    for step in steps:
+        if step:
+            device, other = at.column(-step)
+            wire.arrive(("c", step), ffn_out.at[other], device)
+    wire.drain()
+
+
+ANY = pl.BlockSpec(memory_space=pl.ANY)
+VMEM = pl.BlockSpec(memory_space=pltpu.VMEM)
+
+
+def comm_params(number):
+    return pltpu.CompilerParams(
+        collective_id=number, has_side_effects=True, vmem_limit_bytes=63 * 2**20
+    )
+
+
+def gather_weights(qkv_parts, ffn_parts, x_own):
+    _, rows_own, qkv_width = qkv_parts.shape
+    unit_width = ffn_parts.shape[-1]
+    own, width = x_own.shape
+    low_type = jnp.bfloat16
+    return pl.pallas_call(
+        gather_kernel,
+        out_shape=(
+            jax.ShapeDtypeStruct((4, 8, rows_own, qkv_width), low_type),
+            jax.ShapeDtypeStruct((3, 4, 2, 2, 2, rows_own, unit_width), low_type),
+            jax.ShapeDtypeStruct((8, own, width), low_type),
+        ),
+        in_specs=[VMEM] * 3,
+        out_specs=(ANY,) * 3,
+        scratch_shapes=[
+            pltpu.SemaphoreType.DMA((100,)),
+            pltpu.SemaphoreType.DMA((100,)),
+            pltpu.SemaphoreType.DMA((3,)),
+        ],
+        compiler_params=comm_params(1),
+        cost_estimate=pl.CostEstimate(
+            flops=0, bytes_accessed=400_000_000, transcendentals=0
+        ),
+        name="gather_weights",
+    )(qkv_parts, ffn_parts, x_own)
+
+
+def reduce_grads(qkv_part, ffn_part):
+    _, _, rows_own, qkv_width = qkv_part.shape
+    unit_width = ffn_part.shape[-1]
+    low_type = jnp.bfloat16
+    block = (rows_own, unit_width)
+    line = (4, 8, rows_own, qkv_width)
+    return pl.pallas_call(
+        reduce_kernel,
+        out_shape=(
+            jax.ShapeDtypeStruct((8, rows_own, qkv_width), low_type),
+            jax.ShapeDtypeStruct((8, 3) + block, low_type),
+        ),
+        in_specs=[VMEM] * 2,
+        out_specs=(ANY,) * 2,
+        scratch_shapes=[
+            pltpu.VMEM((8, 3, 2) + block, low_type),
+            pltpu.VMEM((8, 3) + block, low_type),
+            pltpu.VMEM((8, 3) + block, low_type),
+            pltpu.VMEM((8, 3) + block, low_type),
+            pltpu.VMEM(line, low_type),
+            pltpu.VMEM(line, low_type),
+            pltpu.VMEM(line, low_type),
+            pltpu.VMEM(line, low_type),
+            pltpu.VMEM(line[1:], low_type),
+            pltpu.SemaphoreType.DMA((64,)),
+            pltpu.SemaphoreType.DMA((64,)),
+            pltpu.SemaphoreType.DMA((2,)),
+        ],
+        compiler_params=comm_params(2),
+        cost_estimate=pl.CostEstimate(
+            flops=0, bytes_accessed=400_000_000, transcendentals=0
+        ),
+        name="reduce_grads",
+    )(qkv_part, ffn_part)
 
 
 def body(
@@ -105,7 +526,6 @@
     units = gate_weight.shape[1]
     head_ways = math.prod(lax.axis_size(name) for name in HEAD_AXES)
     unit_ways = math.prod(lax.axis_size(name) for name in UNIT_AXES)
-    device_count = math.prod(lax.axis_size(name) for name in ALL)
     chunk_count = lax.axis_size("y") * lax.axis_size("c")
     row_length = pos_count * chunk_count
     x_size = lax.axis_size("x")
@@ -123,10 +543,7 @@
     qkv_parts = (
         qkv_weight.reshape(rows_own, 3, head_ways, head_width)
         .transpose(2, 0, 1, 3)
-        .reshape(head_ways * rows_own, 3 * head_width)
-    )
-    qkv_here = gather(
-        lax.all_to_all(qkv_parts, HEAD_AXES, split_axis=0, concat_axis=0, tiled=True), HEAD_COPIES
+        .reshape(head_ways, rows_own, 3 * head_width)
     )
     proj_full = gather(proj_weight, ALL)
 
@@ -134,27 +551,18 @@
 
     ffn = jnp.stack([gate_weight, up_weight, down_weight])
     ffn = jnp.pad(ffn, ((0, 0), (0, 0), (0, unit_pad)))
-    ffn = (
-        ffn.reshape(3, rows_own, unit_ways, unit_width)
-        .transpose(2, 0, 1, 3)
-        .reshape(unit_ways * 3, rows_own, unit_width)
-    )
-    ffn = lax.all_to_all(ffn, UNIT_AXES, split_axis=0, concat_axis=0, tiled=True)
-
-    def unit_full(index):
-        part = ffn.reshape(unit_ways, 3, rows_own, unit_width)[:, index]
-        whole = gather(part, UNIT_COPIES)
-        zo, zi, x, y, c = sizes
-        return (
-            whole.reshape(zo, x, y, zi, c, rows_own, unit_width)
-            .transpose(0, 3, 1, 2, 4, 5, 6)
-            .reshape(width, unit_width)
-        )
-
-    gate_here, up_here, down_here = (unit_full(index) for index in range(3))
+    ffn = ffn.reshape(3, rows_own, unit_ways, unit_width).transpose(2, 0, 1, 3)
 
     x_own = hidden_in.reshape(own, width)
-    x_all = gather(x_own, HEAD_AXES)
+    qkv_here, ffn, x_all = gather_weights(qkv_parts, ffn, x_own)
+    qkv_here = qkv_here.reshape(-1, 3 * head_width)
+    ffn = ffn.reshape(3, -1, unit_width)
+    x_all = x_all.reshape(-1, width)
+    if sizes[0] > 1:
+        qkv_here = gather(qkv_here, "zo")
+        ffn = lax.all_gather(ffn, "zo", axis=1, tiled=True)
+    gate_here, up_here, down_here = ffn[0], ffn[1], ffn[2]
+
     mixed = dot(x_all, qkv_here)
 
     def to_rows(values):
@@ -227,30 +635,23 @@
     d_normed_part = low(contract_last(gate_low, gate_here) + contract_last(up_low, up_here))
     d_normed = deep_alpha * d_second + scatter_sum(d_normed_part, UNIT_AXES).astype(jnp.float32)
 
-    def unit_grad(left_side, right_side):
-        zo, zi, x, y, c = sizes
-        part = low(contract_first(left_side, right_side))
-        part = (
-            part.reshape(zo, zi, x, y, c, rows_own, unit_width)
-            .transpose(0, 2, 3, 1, 4, 5, 6)
-            .reshape(width, unit_width)
-        )
-        part = scatter_sum(part, UNIT_COPIES).reshape(unit_ways, rows_own, unit_width)
-        part = lax.all_to_all(part, UNIT_AXES, split_axis=0, concat_axis=0, tiled=True)
-        part = part.transpose(1, 0, 2).reshape(rows_own, unit_ways * unit_width)
-        return part[:, :units].astype(jnp.float32)
-
-    down_grad = unit_grad(down_low, active)
-    gate_grad = unit_grad(normed_all, gate_low)
-    up_grad = unit_grad(normed_all, up_low)
+    ffn_part = jnp.stack(
+        [
+            low(contract_first(normed_all, gate_low)),
+            low(contract_first(normed_all, up_low)),
+            low(contract_first(down_low, active)),
+        ]
+    )
 
     gain_one_grad = jnp.sum(d_normed * hat_one, axis=0)
     shift_one_grad = jnp.sum(d_normed, axis=0)
     d_first = norm_back(d_normed, hat_one, inverse_one, gain_one)
     branch_low = low(d_first)
     small_grads = jnp.stack([gain_one_grad, shift_one_grad, gain_two_grad, shift_two_grad])
-    small_grads = small_grads.reshape(4, device_count, rows_own).transpose(1, 0, 2)
-    small_grads = scatter_sum(small_grads, ALL)[0]
+    place_own = lax.axis_index(ALL) * rows_own
+    small_grads = gather(small_grads[None], ALL)
+    small_grads = lax.dynamic_slice_in_dim(small_grads, place_own, rows_own, axis=2)
+    small_grads = jnp.sum(small_grads, axis=0)
 
     proj_grad = scatter_sum(low(contract_first(context_own, branch_low)), ALL).astype(jnp.float32)
     d_context = to_rows(tokens_to_heads(low(contract_last(branch_low, proj_full))))
@@ -269,19 +670,23 @@
     d_input = scatter_sum(low(contract_last(d_mixed, qkv_here)), HEAD_AXES).astype(jnp.float32)
     d_input = deep_alpha * d_first + d_input
 
-    qkv_part = scatter_sum(low(contract_first(x_all, d_mixed)), HEAD_COPIES)
-    qkv_part = lax.all_to_all(
-        qkv_part.reshape(head_ways, rows_own, 3 * head_width),
-        HEAD_AXES,
-        split_axis=0,
-        concat_axis=0,
-        tiled=True,
+    qkv_part = low(contract_first(x_all, d_mixed))
+    if sizes[0] > 1:
+        qkv_part = scatter_sum(qkv_part, "zo")
+        ffn_part = lax.psum_scatter(ffn_part, "zo", scatter_dimension=1, tiled=True)
+    qkv_part, ffn_part = reduce_grads(
+        qkv_part.reshape(4, 8, rows_own, 3 * head_width),
+        ffn_part.reshape(3, 4, 2, 2, 2, rows_own, unit_width),
     )
     qkv_grad = (
         qkv_part.reshape(head_ways, rows_own, 3, head_width)
         .transpose(1, 2, 0, 3)
         .reshape(rows_own, 3 * width)
         .astype(jnp.float32)
+    )
+    ffn_part = ffn_part.transpose(1, 2, 0, 3).reshape(3, rows_own, unit_ways * unit_width)
+    gate_grad, up_grad, down_grad = (
+        ffn_part[index, :, :units].astype(jnp.float32) for index in range(3)
     )
     return (
         layer_rows.reshape(micro_count, 1, pos_count, width),

time: 1090 us -> 827 us (0.76)
  waiting for transfers between devices: 609 us -> 214 us
  Pallas kernels: 0 us -> 337 us
  blocking collectives: 238 us -> 51.4 us
  starting transfers between devices: 22.2 us -> 8.33 us
    pallas_call x0 -> x2, Pallas kernels: none -> 337 us  [the longest x1 186 us: reduce_grads(): pl.pallas_call(reduce_kernel, out_shape=(jax.ShapeDtypeStruct((8, rows_ow...]
    reduce_scatter x8 -> x4, waiting for transfers between devices: 322 us -> 125 us  [scatter_sum(): return lax.psum_scatter(values, axes, scatter_dimension=0, tiled=True)]
    all_gather x8 -> x4, waiting for transfers between devices: 246 us -> 80.8 us  [gather(): return lax.all_gather(values, axes, axis=0, tiled=True)]
    all_to_all x3 -> x0, blocking collectives: 145 us -> none  [the longest x1 110 us: body(): lax.all_to_all(ffn, UNIT_AXES, split_axis=0, concat_axis=0, tiled=True)]
    unnamed x1 -> x0, blocking collectives: 38.2 us -> none
    all_to_all x4 -> x1, waiting for transfers between devices: 39.2 us -> 7.92 us  [tokens_to_heads(): lax.all_to_all(values, HEAD_AXES, split_axis=0, concat_axis=0, tiled=True)]
    all_to_all x4 -> x1, starting transfers between devices: 17.3 us -> 3.65 us  [tokens_to_heads(): lax.all_to_all(values, HEAD_AXES, split_axis=0, concat_axis=0, tiled=True)]
    transpose x5 -> x0, local copies, waits for them, and re-layouts: 12.5 us -> none  [the longest x3 11.8 us: unit_full(): return whole.reshape(zo, x, y, zi, c, rows_own, unit_width).transpose(0,...]
  transfers between devices with their start and end apart: 21 -> 10, of which waited for: 14 -> 6; matrix products, arithmetic and copies ran while one was open for 13% -> 14% of each run, Pallas kernels for 0% -> 41%
where the time goes in v2:
time: 827 us; the launch traced here: 817 us
  Pallas kernels  337 us (41%)
  waiting for transfers between devices  214 us (26%)
  matrix products  106 us (13%)
  local copies, waits for them, and re-layouts  52.1 us (6%)
  blocking collectives  51.4 us (6%)
  other arithmetic  32.2 us (4%)
  between operations  15.3 us (2%)
  starting transfers between devices  8.33 us (1%)
    pallas_call x1, Pallas kernels, reduce_grads(): pl.pallas_call(reduce_kernel, out_shape=(jax.ShapeDtypeStruct((8, rows_ow...  186 us
    pallas_call x1, Pallas kernels, gather_weights(): pl.pallas_call(gather_kernel, out_shape=(jax.ShapeDtypeStruct((4, 8, rows...  152 us
    reduce_scatter x4, waiting for transfers between devices, scatter_sum(): return lax.psum_scatter(values, axes, scatter_dimension=0, tiled=True)  125 us
    all_gather x4, waiting for transfers between devices, gather(): return lax.all_gather(values, axes, axis=0, tiled=True)  80.8 us
    all_gather x2, blocking collectives, gather(): return lax.all_gather(values, axes, axis=0, tiled=True)  51.4 us
    dot_general x5, matrix products, dot(): return jnp.dot(left_side, right_side, preferred_element_type=jnp.float32)  40.5 us
    dot_general x5, matrix products, contract_first(): lax.dot_general(left_side, right_side, (((0,), (0,)), ((), ())), preferre...  30.8 us
    dot_general x5, matrix products, contract_last(): lax.dot_general(left_side, right_side, (((1,), (1,)), ((), ())), preferre...  25.1 us
  transfers between devices with their start and end apart: 10, of which 6 were waited for; matrix products, arithmetic and copies ran while one was open for 14% of the time, Pallas kernels for 41%

profile of v2, /device:TPU:0, one launch (start us, length us, event | category | flops | bytes accessed | tf_op | source)
XLA Modules:
  0.0 817.1 jit_solution(2320364578786380738)
XLA Ops:
  7.9 10.7 %all-gather = s32[16,1,64,3]{2,1,3,0:T(1,128)S(1)} all-gather(s32[2,1,64,3]{2,1,3,0:T(1,128)} %param.13), channel_id=2, replica_groups=mesh['zo'=1,'zi'=4,'x'=2,'y'=2,'c'=2] {'x','y','c'}, dimensions={0}, use_global_device_ids=true | all-gather | bytes 13824 | tf_op jit(solution)/shard_map/all_gather | solution.py:78
  20.5 1.7 reshape.212.qkv_in
  22.4 1.7 copy.154
  24.2 151.7 %gather_weights.1 = (bf16[4,8,64,768]{3,2,1,0:T(8,128)(2,1)}, bf16[3,4,2,2,2,64,768]{6,5,4,3,2,1,0:T(8,128)(2,1)}, bf16[8,128,2048]{2,1,0:T(8,128)(2,1)}) custom-call(bf16[8,64,768]{2,1,0:T(8,128)(2,1)} %reshape.212.qkv_in, bf16[8,3,64,768]{3,2,1,0:T(8,128)(2,1)} %bitcast.196, bf16[128,2048]{1,0:T(8,128)(2,1)} %bitcast.215), custom_call_target="tpu_custom_call" | custom-call | bytes 400000000 | tf_op jit(solution)/shard_map/gather_weights/pallas_call | solution.py:452
  175.9 6.2 convolution_bitcast_fusion
  182.3 2.8 reshape_reshape.16
  185.2 2.5 slice.121
  187.7 2.0 copy.143
  190.2 3.0 fusion.48
  195.0 2.5 fusion.59
  197.5 2.7 fusion.23
  203.4 3.5 all-to-all-start
  207.2 40.7 %all-gather.3 = bf16[32,4,64]{2,1,0:T(4,128)(2,1)S(1)} all-gather(bf16[1,4,64]{2,1,0:T(4,128)(2,1)S(1)} %maximum_bitcast_fusion.3), channel_id=3, replica_groups=mesh['zo'=1,'zi'=4,'x'=2,'y'=2,'c'=2] {'zo','zi','x','y','c'}, dimensions={0}, use_global_device_ids=true | all-gather | bytes 16896 | tf_op jit(solution)/shard_map/all_gather | solution.py:78
  248.6 4.7 fusion.60
  254.7 7.3 fusion.57
  262.0 35.8 %all-gather.12.cloned.1.call-done = bf16[1024,2048]{1,0:T(8,128)(2,1)} async-done(((bf16[128,2048]{1,0:T(8,128)(2,1)}), bf16[1024,2048]{1,0:T(8,128)(2,1)}) %all-gather.12.cloned.1.call-update) | async-done | bytes 4194320 | tf_op jit(solution)/shard_map/all_gather | solution.py:78
  297.8 6.3 fusion.61
  304.1 12.5 %multiply_convert_fusion.1 = (bf16[1024,768]{1,0:T(8,128)(2,1)S(1)}, f32[1024,768]{1,0:T(8,128)}, f32[1024,768]{1,0:T(8,128)}, f32[1024,768]{1,0:T(8,128)}) fusion(f32[1024,768]{1,0:T(8,128)S(1)} %fusion.61, bf16[1024,2048]{1,0:T(8,128)(2,1)S(1)} %copy-done.32, bf16[2048,768]{1,0:T(8,128)(2,1)S(1)} %bitcast.203), kind=kOutput, calls=%fused_computation.25 | convolution fusion | flops 3273129984 | bytes 21495808 | tf_op jit(solution)/shard_map/dot_general | solution.py:39
  317.8 5.0 convolution_convert_fusion.2
  324.2 47.5 %reduce-scatter.5.cloned.1.call-done = bf16[128,2048]{1,0:T(8,128)(2,1)} async-done(((bf16[1024,2048]{1,0:T(8,128)(2,1)}), bf16[128,2048]{1,0:T(8,128)(2,1)}) %reduce-scatter.5.cloned.1.call-update) | async-done | bytes 524304 | tf_op jit(solution)/shard_map/reduce_scatter | solution.py:82
  375.6 2.5 fusion.55
  378.6 45.0 %all-gather.14.cloned.1.call-done = bf16[1024,2048]{1,0:T(8,128)(2,1)} async-done(((bf16[128,2048]{1,0:T(8,128)(2,1)}), bf16[1024,2048]{1,0:T(8,128)(2,1)}) %all-gather.14.cloned.1.call-update) | async-done | bytes 4194320 | tf_op jit(solution)/shard_map/all_gather | solution.py:78
  423.6 10.8 %multiply_convert_fusion = (bf16[1024,768]{1,0:T(8,128)(2,1)S(1)}, bf16[1024,768]{1,0:T(8,128)(2,1)S(1)}) fusion(f32[1024,768]{1,0:T(8,128)} %get-tuple-element.79, f32[1024,768]{1,0:T(8,128)} %get-tuple-element.80, f32[1024,768]{1,0:T(8,128)} %copy-done.35, f32[1024,768]{1,0:T(8,128)} %get-tuple-element.117, ...), kind=kOutput, calls=%fused_computation.24 | convolution fusion | flops 3229089792 | bytes 23068672 | tf_op jit(solution)/shard_map/dot_general | solution.py:39
  434.4 3.4 fusion.62
  437.9 5.1 add_convert_fusion
  443.0 48.8 %reduce-scatter.7.cloned.1.call-done = bf16[128,2048]{1,0:T(8,128)(2,1)} async-done(((bf16[1024,2048]{1,0:T(8,128)(2,1)}), bf16[128,2048]{1,0:T(8,128)(2,1)}) %reduce-scatter.7.cloned.1.call-update) | async-done | bytes 524304 | tf_op jit(solution)/shard_map/reduce_scatter | solution.py:82
  491.8 3.0 multiply_reduce_fusion.1
  495.4 6.6 convolution_convert_fusion.7
  502.8 3.7 all-to-all-start.1
  507.4 7.9 all-to-all-done.1
  519.2 2.6 multiply_reduce_fusion
  526.7 2.8 copy.122
  529.5 4.9 convert_element_type.170
  537.2 5.0 convolution_convert_fusion.1
  542.3 5.7 convolution_convert_fusion
  548.0 6.5 convolution_convert_fusion.3
  554.5 5.1 convolution_convert_fusion.4
  559.7 4.9 convolution_convert_fusion.5
  564.6 6.9 pad_maximum_fusion.ffn_in
  571.5 8.6 %convolution_convert_fusion.6 = bf16[2048,768]{1,0:T(8,128)(2,1)} fusion(bf16[1024,2048]{1,0:T(8,128)(2,1)} %bitcast.240, bf16[1024,768]{1,0:T(8,128)(2,1)} %bitcast.222), kind=kOutput, calls=%fused_computation.15 | convolution fusion | flops 3222798336 | bytes 8912896 | tf_op jit(solution)/shard_map/dot_general | solution.py:33
  580.1 185.8 %reduce_grads.1 = (bf16[8,64,768]{2,1,0:T(8,128)(2,1)}, bf16[8,3,64,768]{3,2,1,0:T(8,128)(2,1)}) custom-call(bf16[4,8,64,768]{3,2,1,0:T(8,128)(2,1)} %bitcast.213, bf16[3,4,2,2,2,64,768]{6,5,4,3,2,1,0:T(8,128)(2,1)} %pad_maximum_fusion.ffn_in), custom_call_target="tpu_custom_call" | custom-call | bytes 400000000 | tf_op jit(solution)/shard_map/reduce_grads/pallas_call | solution.py:480
  765.8 2.0 copy.146
  767.9 1.8 reshape.231
  769.8 2.5 copy.124
  773.9 2.1 fusion.36
  777.5 2.0 add_convert_fusion.1
  779.4 28.6 %reduce-scatter.11.cloned.1.call-done = bf16[64,2048]{1,0:T(8,128)(2,1)} async-done(((bf16[2048,2048]{1,0:T(8,128)(2,1)}), bf16[64,2048]{1,0:T(8,128)(2,1)}) %reduce-scatter.11.cloned.1.call-update) | async-done | bytes 262160 | tf_op jit(solution)/shard_map/reduce_scatter | solution.py:82
  808.0 1.8 convert_element_type.183
  (160 shorter events, 34.7 us)
Async XLA Ops:
  7.2 15.0 %copy-start.23 = (bf16[64,5461]{1,0:T(8,128)(2,1)S(1)}, bf16[64,5461]{1,0:T(8,128)(2,1)}, u32[]{:S(2)}) copy-start(bf16[64,5461]{1,0:T(8,128)(2,1)} %param.19) | copy-start | bytes 2097028
  7.2 15.0 %copy-start.24 = (bf16[64,5461]{1,0:T(8,128)(2,1)S(1)}, bf16[64,5461]{1,0:T(8,128)(2,1)}, u32[]{:S(2)}) copy-start(bf16[64,5461]{1,0:T(8,128)(2,1)} %param.18) | copy-start | bytes 2097028
  7.2 15.0 %copy-start.25 = (bf16[64,5461]{1,0:T(8,128)(2,1)S(1)}, bf16[64,5461]{1,0:T(8,128)(2,1)}, u32[]{:S(2)}) copy-start(bf16[64,5461]{1,0:T(8,128)(2,1)} %param.17) | copy-start | bytes 2097028
  7.2 241.4 %all-gather.10.cloned.1.call-start = ((), (), s32[]{:S(2)}) async-start(), calls=%async_computation.6 | async-start | bytes 8650752 | tf_op jit(solution)/shard_map/all_gather | solution.py:78
  185.2 8.0 copy-start.3
  195.0 5.3 copy-start.12
  195.0 5.3 copy-start.14
  195.0 5.2 copy-start.16
  195.0 2.5 copy-start.27
  200.3 6.9 copy-start.28
  200.3 6.9 copy-start.29
  200.3 6.9 copy-start.30
  200.3 6.9 copy-start.31
  200.3 48.3 %copy-start.18 = (bf16[2,1,64,2048]{3,2,1,0:T(8,128)(2,1)S(1)}, bf16[2,1,64,2048]{3,2,1,0:T(8,128)(2,1)}, u32[]{:S(2)}) copy-start(bf16[2,1,64,2048]{3,2,1,0:T(8,128)(2,1)} %param.12) | copy-start | bytes 1572868
  203.4 44.9 %all-to-all-start = ((bf16[8,128,256]{2,1,0:T(8,128)(2,1)}), bf16[8,128,256]{2,1,0:T(8,128)(2,1)S(1)}, u32[]{:S(2)}, u32[]{:S(2)}) async-start(bf16[8,128,256]{2,1,0:T(8,128)(2,1)} %reshape_reshape.18), calls=%async_computation | async-start | bytes 1048576 | tf_op jit(solution)/shard_map/all_to_all | solution.py:604
  206.9 90.9 %all-gather.12.cloned.1.call-start = ((), (), s32[]{:S(2)}) async-start(), calls=%async_computation.7 | async-start | bytes 4718592 | tf_op jit(solution)/shard_map/all_gather | solution.py:78
  254.7 117.1 %reduce-scatter.5.cloned.1.call-start = ((), (), s32[]{:S(2)}) async-start(), calls=%async_computation.8 | async-start | bytes 4718592 | tf_op jit(solution)/shard_map/reduce_scatter | solution.py:82
  297.8 6.3 copy-start.7
  297.8 6.3 copy-start.32
  304.1 12.5 %copy-start.35 = (f32[1024,768]{1,0:T(8,128)}, f32[1024,768]{1,0:T(8,128)S(1)}, u32[]{:S(2)}) copy-start(f32[1024,768]{1,0:T(8,128)S(1)} %fusion.61) | copy-start | bytes 9437188
  304.1 13.7 %copy-start.10 = (bf16[1,4,2,2,2,64,768]{6,5,4,3,2,1,0:T(8,128)(2,1)S(1)}, bf16[1,4,2,2,2,64,768]{6,5,4,3,2,1,0:T(8,128)(2,1)}, u32[]{:S(2)}) copy-start(bf16[1,4,2,2,2,64,768]{6,5,4,3,2,1,0:T(8,128)(2,1)} %get-tuple-element.81) | copy-start | bytes 9437188
  316.6 1.2 copy-start.40
  322.9 100.7 %all-gather.14.cloned.1.call-start = ((), (), s32[]{:S(2)}) async-start(), calls=%async_computation.9 | async-start | bytes 4718592 | tf_op jit(solution)/shard_map/all_gather | solution.py:78
  371.8 3.1 copy-start.2
  378.1 113.8 %reduce-scatter.7.cloned.1.call-start = ((), (), s32[]{:S(2)}) async-start(), calls=%async_computation.10 | async-start | bytes 4718592 | tf_op jit(solution)/shard_map/reduce_scatter | solution.py:82
  423.5 10.8 %copy-start.9 = (bf16[1,4,2,2,2,64,768]{6,5,4,3,2,1,0:T(8,128)(2,1)S(1)}, bf16[1,4,2,2,2,64,768]{6,5,4,3,2,1,0:T(8,128)(2,1)}, u32[]{:S(2)}) copy-start(bf16[1,4,2,2,2,64,768]{6,5,4,3,2,1,0:T(8,128)(2,1)} %get-tuple-element.83) | copy-start | bytes 9437188
  434.3 3.5 copy-start.36
  434.4 3.5 copy-start.38
  434.4 3.5 copy-start.8
  495.4 46.9 %copy-start = (f32[128,2048]{1,0:T(8,128)}, f32[128,2048]{1,0:T(8,128)S(1)}, u32[]{:S(2)}) copy-start(f32[128,2048]{1,0:T(8,128)S(1)} %subtract_multiply_fusion) | copy-start | bytes 3145732
  502.8 12.5 %all-to-all-start.1 = ((bf16[8,128,256]{2,1,0:T(8,128)(2,1)}), bf16[8,128,256]{2,1,0:T(8,128)(2,1)S(1)}, u32[]{:S(2)}, u32[]{:S(2)}) async-start(bf16[8,128,256]{2,1,0:T(8,128)(2,1)} %bitcast.193), calls=%async_computation.3 | async-start | bytes 1048576 | tf_op jit(solution)/shard_map/all_to_all | solution.py:609
  506.5 269.5 %all-gather.16.cloned.1.call-start = ((), (), s32[]{:S(2)}) async-start(), calls=%async_computation.13 | async-start | bytes 1081344 | tf_op jit(solution)/shard_map/all_gather | solution.py:78
  507.2 270.3 %reduce-scatter.9.cloned.1.call-start = ((), (), s32[]{:S(2)}) async-start(), calls=%async_computation.11 | async-start | bytes 4718592 | tf_op jit(solution)/shard_map/reduce_scatter | solution.py:82
  519.2 2.6 copy-start.20
  521.7 1.0 copy-start.15
  521.7 1.2 copy-start.17
  521.8 1.7 copy-start.13
  522.9 1.3 copy-start.6
  522.9 1.3 copy-start.11
  525.0 1.0 copy-start.26
  534.4 2.8 copy-start.34
  536.1 1.1 copy-start.21
  542.2 265.8 %reduce-scatter.11.cloned.1.call-start = ((), (), s32[]{:S(2)}) async-start(), calls=%async_computation.12 | async-start | bytes 8650752 | tf_op jit(solution)/shard_map/reduce_scatter | solution.py:82
  548.0 6.5 copy-start.33
  548.0 6.5 copy-start.39
  554.5 5.2 copy-start.37
  765.8 2.1 copy-start.22
  773.9 3.6 copy-start.1
  (3 other events, 2.8 us)
Sparse Core Ops, SparseCore 0:
  10.9 120.3 all-gather.9
  254.8 42.9 all-gather.11
  323.0 48.7 reduce-scatter.4
  378.2 45.3 all-gather.13
  443.1 48.7 reduce-scatter.6
  509.9 52.6 all-gather.15
  565.9 67.1 reduce-scatter.8
  635.4 172.5 reduce-scatter.10

commit v3 on v2

--- a/solution.py
+++ b/solution.py
@@ -96,26 +96,34 @@
         self.send_sems, self.recv_sems = send_sems, recv_sems
         self.keys, self.sent = {}, []
 
-    def number(self, key):
-        return self.keys.setdefault(key, len(self.keys))
-
-    def copy(self, key, source, target, device):
-        index = self.number(key)
+    def number(self, key, span=1):
+        if key not in self.keys:
+            self.keys[key] = sum(size for _, size in self.keys.values()), span
+        return self.keys[key][0]
+
+    def copy(self, key, source, target, device, slot=0, span=1, recv=None):
+        send = self.number(key, span)
+        receive = send if recv is None else self.number(recv)
         return pltpu.make_async_remote_copy(
             src_ref=source,
             dst_ref=target,
-            send_sem=self.send_sems.at[index],
-            recv_sem=self.recv_sems.at[index],
+            send_sem=self.send_sems.at[send],
+            recv_sem=self.recv_sems.at[receive + slot],
             device_id=device,
             device_id_type=MESH,
         )
 
-    def send(self, key, source, target, device, when=None):
-        copy = self.copy(key, source, target, device)
+    def send(self, key, source, target, device, when=None, recv=None):
+        copy = self.copy(key, source, target, device, recv=recv)
         if when is None:
             copy.start()
         else:
             pl.when(when)(copy.start)
+        self.sent.append((copy, when))
+
+    def send_to_slot(self, key, source, target, device, slot, span, when):
+        copy = self.copy(key, source, target, device, slot, span)
+        pl.when(when)(copy.start)
         self.sent.append((copy, when))
 
     def arrive(self, key, target, device, when=None):
@@ -124,6 +132,9 @@
             copy.wait_recv()
         else:
             pl.when(when)(copy.wait_recv)
+
+    def arrive_slot(self, key, target, device, slot, span, when):
+        pl.when(when)(self.copy(key, target, target, device, slot, span).wait_recv)
 
     def drain(self):
         for copy, when in self.sent:
@@ -171,7 +182,21 @@
         return plane + column
 
 
-def gather_kernel(qkv_in, ffn_in, x_in, qkv_out, ffn_out, x_out, send_sems, recv_sems, own_sems):
+def gather_kernel(
+    qkv_in,
+    ffn_in,
+    proj_in,
+    x_in,
+    small_in,
+    qkv_out,
+    ffn_out,
+    proj_out,
+    x_out,
+    small_out,
+    send_sems,
+    recv_sems,
+    own_sems,
+):
     at = Place()
     wire = Wire(send_sems, recv_sems)
     enter(at.neighbours())
@@ -184,9 +209,25 @@
         pltpu.make_async_copy(
             ffn_in.at[at.unit], ffn_out.at[:, at.zi, at.x, at.y, at.c], own_sems.at[2]
         ),
+        pltpu.make_async_copy(small_in, small_out.at[at.zi, at.rank], own_sems.at[3]),
     ]
     for copy in own:
         copy.start()
+
+    chunk = at.y * 2 + at.c
+    holder = at.zi * 2 + at.x
+    proj_home = at.rank // 2
+    proj_first = at.rank == holder
+    proj_own = pltpu.make_async_copy(proj_in, proj_out.at[chunk], own_sems.at[4])
+    pl.when(proj_first)(proj_own.start)
+
+    def small_first():
+        for delta in range(1, 8):
+            device, _ = at.plane(delta)
+            slot = small_out.at[at.zi, at.rank]
+            wire.send(("s", delta), small_in, slot, device)
+
+    small_first()
 
     for step in (1, 7, 2, 6, 3, 5, 4):
         device, other = at.column(step)
@@ -195,11 +236,42 @@
     for delta in range(1, 8):
         device, other = at.plane(delta)
         wire.send(("q", delta), qkv_in.at[other], qkv_out.at[at.zi, at.rank], device)
+    holder_device = (at.zo, at.zi, holder // 4, lax.rem(holder // 2, 2), lax.rem(holder, 2))
+    wire.send_to_slot("p", proj_in, proj_out.at[chunk], holder_device, chunk, 4, at.rank != holder)
     wire.send("xx", x_in, x_out.at[at.rank], x_side)
     wire.send("xy", x_in, x_out.at[at.rank], y_side)
     wire.send("xc0", x_in, x_out.at[at.rank], core_side)
     for copy in own:
         copy.wait()
+    pl.when(proj_first)(proj_own.wait)
+
+    def small_second():
+        for delta in range(1, 8):
+            device, other = at.plane(delta)
+            wire.arrive(("s", delta), small_out.at[at.zi, other], device)
+        for dz in range(1, 4):
+            device = at.line(lax.rem(at.zi + dz, 4))
+            wire.send(("t", dz), small_out.at[at.zi], small_out.at[at.zi], device)
+
+    def small_last():
+        for dz in range(1, 4):
+            z = lax.rem(at.zi - dz + 4, 4)
+            wire.arrive(("t", dz), small_out.at[z], at.line(z))
+
+    def proj_start():
+        for slot in range(4):
+            source = (at.zo, at.zi, lax.rem(at.rank, 2), slot // 2, slot % 2)
+            mine = (at.zi == proj_home) & ((chunk != slot) | (at.rank != holder))
+            wire.arrive_slot("p", proj_out.at[slot], source, slot, 4, mine)
+        wire.send("pu0", proj_out, proj_out, up, (at.zi == proj_home) & (at.zi < 3))
+        wire.send("pd0", proj_out, proj_out, down, (at.zi == proj_home) & (at.zi > 0))
+
+    def proj_relay():
+        above, below = at.zi > proj_home, at.zi < proj_home
+        wire.arrive("pu0", proj_out, down, above)
+        wire.arrive("pd0", proj_out, up, below)
+        wire.send("pu1", proj_out, proj_out, up, above & (at.zi < 3), recv="pu0")
+        wire.send("pd1", proj_out, proj_out, down, below & (at.zi > 0), recv="pd0")
 
     def qkv_slot(z, delta):
         return qkv_out.at[jnp.clip(z, 0, 3), at.plane(delta)[1]]
@@ -247,8 +319,10 @@
     wire.arrive("xy", x_out.at[from_y], y_side)
     wire.send("xd1", x_out.at[from_y, high_half], x_out.at[from_y, high_half], x_side)
     wire.send("xc2", x_out.at[from_y], x_out.at[from_y], core_side)
+    small_second()
     for delta in range(8):
         qkv_hop(0, delta)
+    proj_start()
     wire.arrive("xd0", x_out.at[from_xy, low_half], y_side)
     wire.arrive("xd1", x_out.at[from_xy, high_half], x_side)
     wire.send("xc3", x_out.at[from_xy], x_out.at[from_xy], core_side)
@@ -261,6 +335,7 @@
         if turn >= 2:
             ffn_second(steps[turn - 2], turn - 2 + 1)
     qkv_hop(1, 7)
+    proj_relay()
     for delta in range(8):
         qkv_hop(2, delta)
         if delta < 2:
@@ -272,14 +347,25 @@
         wire.arrive("xc%d" % index, x_out.at[other], core_side)
     for step in range(8):
         wire.arrive(("fd", step), ffn_slot(step, 1 - at.x, 1 - at.y), x_side)
+    small_last()
     wire.drain()
 
 
 def reduce_kernel(
     qkv_in,
     ffn_in,
+    proj_in,
+    small_in,
     qkv_out,
     ffn_out,
+    proj_out,
+    small_out,
+    proj_below,
+    proj_above,
+    proj_sum,
+    small_plane,
+    small_mid,
+    small_line,
     first_in,
     second_in,
     second_sum,
@@ -309,6 +395,29 @@
         other = at.column(step)[1]
         return other // 2, lax.rem(other, 2)
 
+    for delta in range(1, 8):
+        device, other = at.plane(delta)
+        wire.send(("s", delta), small_in.at[other], small_plane.at[at.rank], device)
+
+    def small_second():
+        whole = small_in[at.rank]
+        for delta in range(1, 8):
+            device, other = at.plane(delta)
+            wire.arrive(("s", delta), small_plane.at[other], device)
+            whole = whole + small_plane[other]
+        small_mid[...] = whole
+        for dz in range(1, 4):
+            z = lax.rem(at.zi + dz, 4)
+            wire.send(("t", dz), small_mid.at[z], small_line.at[at.zi], at.line(z))
+
+    def small_last():
+        whole = small_mid[at.zi]
+        for dz in range(1, 4):
+            z = lax.rem(at.zi - dz + 4, 4)
+            wire.arrive(("t", dz), small_line.at[z], at.line(z))
+            whole = whole + small_line[z]
+        small_out[...] = whole
+
     for turn, step in enumerate(steps):
         z, c = owner(step)
         if turn % 2:
@@ -388,6 +497,73 @@
                 at.zi > back,
             )
 
+    proj_home = at.rank // 2
+
+    def each_rows(step, count, function):
+        @pl.loop(0, count // step)
+        def _(index):
+            function(pl.ds(pl.multiple_of(index * step, step), step))
+
+    def proj_add(out, *terms):
+        for slot in range(4):
+
+            def rows(part):
+                out[slot, part] = add(*(term[slot, part] for term in terms))
+
+            each_rows(16, proj_in.shape[1], rows)
+
+    def proj_pass():
+        ends = (at.zi == 0) | (at.zi == 3)
+        below, above = at.zi < proj_home, at.zi > proj_home
+        wire.send("pu0", proj_in, proj_below, up, below & ends)
+        wire.send("pd0", proj_in, proj_above, down, above & ends)
+
+    def proj_climb():
+        below, above = at.zi < proj_home, at.zi > proj_home
+
+        def climb():
+            wire.arrive("pu0", proj_below, down)
+            proj_add(proj_sum, proj_in, proj_below)
+
+        def descend():
+            wire.arrive("pd0", proj_above, up)
+            proj_add(proj_sum, proj_in, proj_above)
+
+        pl.when(below & (at.zi > 0))(climb)
+        pl.when(above & (at.zi < 3))(descend)
+        wire.send("pu1", proj_sum, proj_below, up, below & (at.zi > 0), recv="pu0")
+        wire.send("pd1", proj_sum, proj_above, down, above & (at.zi < 3), recv="pd0")
+
+    holder = at.zi * 2 + at.x
+    chunk = at.y * 2 + at.c
+    holder_device = (at.zo, at.zi, holder // 4, lax.rem(holder // 2, 2), lax.rem(holder, 2))
+
+    def proj_last():
+        home = at.zi == proj_home
+
+        def first():
+            wire.arrive("pu0", proj_below, down)
+            proj_add(proj_sum, proj_in, proj_below)
+
+        def only():
+            wire.arrive("pd0", proj_above, up)
+            proj_add(proj_sum, proj_in, proj_above)
+
+        def both():
+            wire.arrive("pd0", proj_above, up)
+            proj_add(proj_sum, proj_sum, proj_above)
+
+        pl.when(home & (at.zi > 0))(first)
+        pl.when(home & (at.zi == 0))(only)
+        pl.when(home & (at.zi > 0) & (at.zi < 3))(both)
+        for slot in range(4):
+            target = (at.zo, at.zi, lax.rem(at.rank, 2), slot // 2, slot % 2)
+            other = (chunk != slot) | (at.rank != holder)
+            wire.send(("o", slot), proj_sum.at[slot], proj_out, target, home & other, recv="o")
+        own = pltpu.make_async_copy(proj_sum.at[chunk], proj_out, own_sems.at[2])
+        pl.when(home & (at.rank == holder))(own.start)
+        pl.when(home & (at.rank == holder))(own.wait)
+
     def qkv_last(piece):
         part = pl.ds(piece * wide, wide)
         for goal in range(4):
@@ -403,16 +579,20 @@
                     terms.append(down_in[goal, part])
                 qkv_total[part] = add(*terms)
 
-    turn = 0
+    proj_pass()
     order = [(goal, piece) for goal in (3, 2, 1) for piece in range(pieces)]
     for index, (goal, piece) in enumerate(order):
         qkv_pass(goal, piece)
+        if index == 4:
+            proj_climb()
         if index < 8:
             ffn_second(steps[index], index)
         if index >= 3 and index - 3 < 8:
             ffn_last(steps[index - 3], index - 3)
     for index in range(len(order) - 3, 8):
         ffn_last(steps[index], index)
+    small_second()
+    proj_last()
     for piece in range(pieces):
         qkv_last(piece)
     own_qkv = pltpu.make_async_copy(
@@ -431,6 +611,8 @@
         if step:
             device, other = at.column(-step)
             wire.arrive(("c", step), ffn_out.at[other], device)
+    small_last()
+    wire.arrive("o", proj_out, holder_device, at.rank != holder)
     wire.drain()
 
 
@@ -444,7 +626,7 @@
     )
 
 
-def gather_weights(qkv_parts, ffn_parts, x_own):
+def gather_weights(qkv_parts, ffn_parts, proj_own, x_own, small):
     _, rows_own, qkv_width = qkv_parts.shape
     unit_width = ffn_parts.shape[-1]
     own, width = x_own.shape
@@ -454,38 +636,50 @@
         out_shape=(
             jax.ShapeDtypeStruct((4, 8, rows_own, qkv_width), low_type),
             jax.ShapeDtypeStruct((3, 4, 2, 2, 2, rows_own, unit_width), low_type),
+            jax.ShapeDtypeStruct((4, rows_own, width), low_type),
             jax.ShapeDtypeStruct((8, own, width), low_type),
+            jax.ShapeDtypeStruct((4, 8) + small.shape, small.dtype),
         ),
-        in_specs=[VMEM] * 3,
-        out_specs=(ANY,) * 3,
+        in_specs=[VMEM] * 5,
+        out_specs=(ANY,) * 5,
         scratch_shapes=[
-            pltpu.SemaphoreType.DMA((100,)),
-            pltpu.SemaphoreType.DMA((100,)),
-            pltpu.SemaphoreType.DMA((3,)),
+            pltpu.SemaphoreType.DMA((128,)),
+            pltpu.SemaphoreType.DMA((128,)),
+            pltpu.SemaphoreType.DMA((5,)),
         ],
         compiler_params=comm_params(1),
         cost_estimate=pl.CostEstimate(
             flops=0, bytes_accessed=400_000_000, transcendentals=0
         ),
         name="gather_weights",
-    )(qkv_parts, ffn_parts, x_own)
-
-
-def reduce_grads(qkv_part, ffn_part):
+    )(qkv_parts, ffn_parts, proj_own, x_own, small)
+
+
+def reduce_grads(qkv_part, ffn_part, proj_part, small_part):
     _, _, rows_own, qkv_width = qkv_part.shape
     unit_width = ffn_part.shape[-1]
+    width = proj_part.shape[-1]
     low_type = jnp.bfloat16
     block = (rows_own, unit_width)
     line = (4, 8, rows_own, qkv_width)
+    small_shape = small_part.shape[1:]
     return pl.pallas_call(
         reduce_kernel,
         out_shape=(
             jax.ShapeDtypeStruct((8, rows_own, qkv_width), low_type),
             jax.ShapeDtypeStruct((8, 3) + block, low_type),
+            jax.ShapeDtypeStruct((rows_own, width), low_type),
+            jax.ShapeDtypeStruct(small_shape[1:], small_part.dtype),
         ),
-        in_specs=[VMEM] * 2,
-        out_specs=(ANY,) * 2,
+        in_specs=[VMEM] * 4,
+        out_specs=(ANY,) * 3 + (VMEM,),
         scratch_shapes=[
+            pltpu.VMEM((4, rows_own, width), low_type),
+            pltpu.VMEM((4, rows_own, width), low_type),
+            pltpu.VMEM((4, rows_own, width), low_type),
+            pltpu.VMEM(small_part.shape, small_part.dtype),
+            pltpu.VMEM(small_shape, small_part.dtype),
+            pltpu.VMEM(small_shape, small_part.dtype),
             pltpu.VMEM((8, 3, 2) + block, low_type),
             pltpu.VMEM((8, 3) + block, low_type),
             pltpu.VMEM((8, 3) + block, low_type),
@@ -495,19 +689,145 @@
             pltpu.VMEM(line, low_type),
             pltpu.VMEM(line, low_type),
             pltpu.VMEM(line[1:], low_type),
-            pltpu.SemaphoreType.DMA((64,)),
-            pltpu.SemaphoreType.DMA((64,)),
-            pltpu.SemaphoreType.DMA((2,)),
+            pltpu.SemaphoreType.DMA((96,)),
+            pltpu.SemaphoreType.DMA((96,)),
+            pltpu.SemaphoreType.DMA((3,)),
         ],
         compiler_params=comm_params(2),
         cost_estimate=pl.CostEstimate(
             flops=0, bytes_accessed=400_000_000, transcendentals=0
         ),
         name="reduce_grads",
-    )(qkv_part, ffn_part)
-
-
-def body(
+    )(qkv_part, ffn_part, proj_part, small_part)
+
+
+def add_rows(out, *terms):
+    step = 16
+
+    @pl.loop(0, out.shape[0] // step)
+    def _(index):
+        part = pl.ds(pl.multiple_of(index * step, step), step)
+        whole = terms[0][part].astype(jnp.float32)
+        for term in terms[1:]:
+            whole = whole + term[part].astype(jnp.float32)
+        out[part] = whole.astype(out.dtype)
+
+
+def plane_scatter_kernel(part, out, core_in, core_sum, side_in, side_sum, last_in, ss, rs):
+    at = Place()
+    wire = Wire(ss, rs)
+    x_side, y_side, core_side = at.plane(4)[0], at.plane(2)[0], at.plane(1)[0]
+    enter([x_side, y_side, core_side])
+    half = out.shape[1] // 2
+    halves = (pl.ds(0, half), pl.ds(half, half))
+    order = ((1, 1), (1, 0), (0, 1), (0, 0))
+
+    def place(dx, dy):
+        return flip(at.x, dx), flip(at.y, dy)
+
+    for dx, dy in order:
+        x, y = place(dx, dy)
+        other = x * 4 + y * 2 + 1 - at.c
+        wire.send(("c", dx, dy), part.at[other], core_in.at[dx * 2 + dy], core_side)
+    for dx, dy in order:
+        x, y = place(dx, dy)
+        mine = x * 4 + y * 2 + at.c
+        slot = dx * 2 + dy
+        wire.arrive(("c", dx, dy), core_in.at[slot], core_side)
+        add_rows(core_sum.at[slot], part.at[mine], core_in.at[slot])
+        if dx:
+            source = core_sum.at[slot, :, halves[0]]
+            wire.send(("a", dy), source, side_in.at[0, dy], x_side)
+        if dy:
+            source = core_sum.at[slot, :, halves[1]]
+            wire.send(("b", dx), source, side_in.at[1, dx], y_side)
+    wire.arrive(("a", 1), side_in.at[0, 1], x_side)
+    add_rows(side_sum.at[0], core_sum.at[1, :, halves[0]], side_in.at[0, 1])
+    wire.send("y", side_sum.at[0], last_in.at[0], y_side)
+    wire.arrive(("b", 1), side_in.at[1, 1], y_side)
+    add_rows(side_sum.at[1], core_sum.at[2, :, halves[1]], side_in.at[1, 1])
+    wire.send("x", side_sum.at[1], last_in.at[1], x_side)
+    wire.arrive(("a", 0), side_in.at[0, 0], x_side)
+    wire.arrive(("b", 0), side_in.at[1, 0], y_side)
+    wire.arrive("y", last_in.at[0], y_side)
+    add_rows(
+        out.at[:, halves[0]], core_sum.at[0, :, halves[0]], side_in.at[0, 0], last_in.at[0]
+    )
+    wire.arrive("x", last_in.at[1], x_side)
+    add_rows(
+        out.at[:, halves[1]], core_sum.at[0, :, halves[1]], side_in.at[1, 0], last_in.at[1]
+    )
+    wire.drain()
+
+
+def plane_scatter(part, number):
+    _, own, width = part.shape
+    low_type = part.dtype
+    return pl.pallas_call(
+        plane_scatter_kernel,
+        out_shape=jax.ShapeDtypeStruct((own, width), jnp.float32),
+        in_specs=[VMEM],
+        out_specs=VMEM,
+        scratch_shapes=[
+            pltpu.VMEM((4, own, width), low_type),
+            pltpu.VMEM((4, own, width), low_type),
+            pltpu.VMEM((2, 2, own, width // 2), low_type),
+            pltpu.VMEM((2, own, width // 2), low_type),
+            pltpu.VMEM((2, own, width // 2), low_type),
+            pltpu.SemaphoreType.DMA((16,)),
+            pltpu.SemaphoreType.DMA((16,)),
+        ],
+        compiler_params=comm_params(number),
+        name="plane_scatter_%d" % number,
+    )(part)
+
+
+def plane_gather_kernel(own_in, out, ss, rs, own_sem):
+    at = Place()
+    wire = Wire(ss, rs)
+    x_side, y_side, core_side = at.plane(4)[0], at.plane(2)[0], at.plane(1)[0]
+    enter([x_side, y_side, core_side])
+    half = own_in.shape[0] // 2
+    mine = out.at[at.rank]
+    wire.send("x", own_in, mine, x_side)
+    wire.send("y", own_in, mine, y_side)
+    wire.send("c0", own_in, mine, core_side)
+    own = pltpu.make_async_copy(own_in, mine, own_sem)
+    own.start()
+    from_x, from_y, from_xy = (at.plane(delta)[1] for delta in (4, 2, 6))
+    low_half, high_half = pl.ds(0, half), pl.ds(half, half)
+    wire.arrive("x", out.at[from_x], x_side)
+    wire.send("d0", out.at[from_x, low_half], out.at[from_x, low_half], y_side)
+    wire.send("c1", out.at[from_x], out.at[from_x], core_side)
+    wire.arrive("y", out.at[from_y], y_side)
+    wire.send("d1", out.at[from_y, high_half], out.at[from_y, high_half], x_side)
+    wire.send("c2", out.at[from_y], out.at[from_y], core_side)
+    wire.arrive("d0", out.at[from_xy, low_half], y_side)
+    wire.arrive("d1", out.at[from_xy, high_half], x_side)
+    wire.send("c3", out.at[from_xy], out.at[from_xy], core_side)
+    own.wait()
+    for index, delta in enumerate((1, 5, 3, 7)):
+        wire.arrive("c%d" % index, out.at[at.plane(delta)[1]], core_side)
+    wire.drain()
+
+
+def plane_gather(own_block, number):
+    return pl.pallas_call(
+        plane_gather_kernel,
+        out_shape=jax.ShapeDtypeStruct((8,) + own_block.shape, own_block.dtype),
+        in_specs=[VMEM],
+        out_specs=VMEM,
+        scratch_shapes=[
+            pltpu.SemaphoreType.DMA((16,)),
+            pltpu.SemaphoreType.DMA((16,)),
+            pltpu.SemaphoreType.DMA,
+        ],
+        compiler_params=comm_params(number),
+        name="plane_gather_%d" % number,
+    )(own_block)
+
+
+def group_body(
     hidden_in,
     token_marks,
     out_grad,
@@ -529,39 +849,40 @@
     chunk_count = lax.axis_size("y") * lax.axis_size("c")
     row_length = pos_count * chunk_count
     x_size = lax.axis_size("x")
+    marks_own = token_marks.astype(jnp.float32)
     own = micro_count * pos_count
     head_width = width // head_ways
     heads_here = head_width // HEAD_DIM
     unit_width = -(-units // (unit_ways * LANES)) * LANES
     unit_pad = unit_width * unit_ways - units
-
-    small = jnp.stack([first_gain, first_shift, second_gain, second_shift])[None]
-    small_all = gather(small, ALL).transpose(1, 0, 2).reshape(4, width).astype(jnp.float32)
-    gain_one, shift_one, gain_two, shift_two = (small_all[i][None] for i in range(4))
-    marks = gather(token_marks.reshape(1, micro_count, pos_count, 3), HEAD_AXES)
+    x_own = hidden_in.reshape(own, width)
+
+    params = jnp.stack([first_gain, first_shift, second_gain, second_shift])
+    small = jnp.concatenate([params.astype(jnp.float32).ravel(), marks_own.ravel()])
+    small = jnp.pad(small, (0, -small.size % (8 * LANES))).reshape(-1, LANES)
 
     qkv_parts = (
         qkv_weight.reshape(rows_own, 3, head_ways, head_width)
         .transpose(2, 0, 1, 3)
         .reshape(head_ways, rows_own, 3 * head_width)
     )
-    proj_full = gather(proj_weight, ALL)
-
-    sizes = [lax.axis_size(name) for name in ALL]
-
     ffn = jnp.stack([gate_weight, up_weight, down_weight])
     ffn = jnp.pad(ffn, ((0, 0), (0, 0), (0, unit_pad)))
     ffn = ffn.reshape(3, rows_own, unit_ways, unit_width).transpose(2, 0, 1, 3)
 
-    x_own = hidden_in.reshape(own, width)
-    qkv_here, ffn, x_all = gather_weights(qkv_parts, ffn, x_own)
+    qkv_here, ffn, proj_here, x_all, small = gather_weights(
+        qkv_parts, ffn, proj_weight, x_own, small
+    )
     qkv_here = qkv_here.reshape(-1, 3 * head_width)
     ffn = ffn.reshape(3, -1, unit_width)
     x_all = x_all.reshape(-1, width)
-    if sizes[0] > 1:
-        qkv_here = gather(qkv_here, "zo")
-        ffn = lax.all_gather(ffn, "zo", axis=1, tiled=True)
+    proj_here = proj_here.reshape(head_width, width)
     gate_here, up_here, down_here = ffn[0], ffn[1], ffn[2]
+    small = small.reshape(unit_ways * 4, -1)
+    params = small[:, : 4 * rows_own].reshape(-1, 4, rows_own).transpose(1, 0, 2)
+    gain_one, shift_one, gain_two, shift_two = params.reshape(4, 1, width)
+    marks = small.reshape(4, head_ways, -1)[lax.axis_index("zi")]
+    marks = marks[:, 4 * rows_own : 4 * rows_own + own * 3].astype(jnp.int32)
 
     mixed = dot(x_all, qkv_here)
 
@@ -599,18 +920,9 @@
     probs_low = low(probs)
     context = low(pair("rhqk,rkhd->rqhd", probs_low, value_rows))
 
-    def heads_to_tokens(values):
-        values = values.reshape(head_ways, own, head_width)
-        values = lax.all_to_all(values, HEAD_AXES, split_axis=0, concat_axis=0, tiled=True)
-        return values.transpose(1, 0, 2).reshape(own, width)
-
-    def tokens_to_heads(values):
-        values = values.reshape(own, head_ways, head_width).transpose(1, 0, 2)
-        values = lax.all_to_all(values, HEAD_AXES, split_axis=0, concat_axis=0, tiled=True)
-        return values.reshape(head_ways * own, head_width)
-
-    context_own = heads_to_tokens(from_rows(context))
-    first_sum = deep_alpha * x_own.astype(jnp.float32) + dot(context_own, proj_full)
+    context = from_rows(context).reshape(-1, head_width)
+    branch = plane_scatter(low(dot(context, proj_here)).reshape(head_ways, own, width), 4)
+    first_sum = deep_alpha * x_own.astype(jnp.float32) + branch
     hat_one, inverse_one = norm_parts(first_sum)
     normed = low(hat_one * gain_one + shift_one)
 
@@ -648,13 +960,13 @@
     d_first = norm_back(d_normed, hat_one, inverse_one, gain_one)
     branch_low = low(d_first)
     small_grads = jnp.stack([gain_one_grad, shift_one_grad, gain_two_grad, shift_two_grad])
-    place_own = lax.axis_index(ALL) * rows_own
-    small_grads = gather(small_grads[None], ALL)
-    small_grads = lax.dynamic_slice_in_dim(small_grads, place_own, rows_own, axis=2)
-    small_grads = jnp.sum(small_grads, axis=0)
-
-    proj_grad = scatter_sum(low(contract_first(context_own, branch_low)), ALL).astype(jnp.float32)
-    d_context = to_rows(tokens_to_heads(low(contract_last(branch_low, proj_full))))
+    small_grads = small_grads.reshape(4, 4, head_ways, rows_own).transpose(2, 1, 0, 3)
+    small_grads = small_grads.reshape(head_ways, 4, 4 * rows_own // LANES, LANES)
+    small_grads = jnp.pad(small_grads, ((0, 0), (0, 0), (0, -small_grads.shape[2] % 8), (0, 0)))
+
+    branch_all = plane_gather(branch_low, 5).reshape(-1, width)
+    proj_part = low(contract_first(context, branch_all)).reshape(4, rows_own, width)
+    d_context = to_rows(low(contract_last(branch_all, proj_here)))
     d_context = d_context.reshape(x_size * micro_count, row_length, heads_here, HEAD_DIM)
     d_probs = pair("rqhd,rkhd->rhqk", d_context, value_rows)
     d_scores = low(probs * (d_probs - jnp.sum(probs * d_probs, axis=-1, keepdims=True)))
@@ -667,17 +979,18 @@
         )
     )
     d_mixed = from_rows(d_mixed.reshape(x_size * micro_count, row_length, 3 * head_width))
-    d_input = scatter_sum(low(contract_last(d_mixed, qkv_here)), HEAD_AXES).astype(jnp.float32)
+    d_input = low(contract_last(d_mixed, qkv_here)).reshape(head_ways, own, width)
+    d_input = plane_scatter(d_input, 6)
     d_input = deep_alpha * d_first + d_input
 
     qkv_part = low(contract_first(x_all, d_mixed))
-    if sizes[0] > 1:
-        qkv_part = scatter_sum(qkv_part, "zo")
-        ffn_part = lax.psum_scatter(ffn_part, "zo", scatter_dimension=1, tiled=True)
-    qkv_part, ffn_part = reduce_grads(
+    qkv_part, ffn_part, proj_part, small_grads = reduce_grads(
         qkv_part.reshape(4, 8, rows_own, 3 * head_width),
         ffn_part.reshape(3, 4, 2, 2, 2, rows_own, unit_width),
-    )
+        proj_part,
+        small_grads,
+    )
+    small_grads = small_grads.ravel()[: 4 * rows_own].reshape(4, rows_own)
     qkv_grad = (
         qkv_part.reshape(head_ways, rows_own, 3, head_width)
         .transpose(1, 2, 0, 3)
@@ -692,7 +1005,7 @@
         layer_rows.reshape(micro_count, 1, pos_count, width),
         low(d_input).reshape(micro_count, 1, pos_count, width),
         qkv_grad,
-        proj_grad,
+        proj_part.astype(jnp.float32),
         gate_grad,
         up_grad,
         down_grad,
@@ -701,6 +1014,40 @@
         small_grads[2],
         small_grads[3],
     )
+
+
+def body(hidden_in, token_marks, out_grad, *weights):
+    joined = lax.axis_size("zo")
+    if joined == 1:
+        return group_body(hidden_in, token_marks, out_grad, *weights)
+    rows = weights[0].shape[0]
+    width = hidden_in.shape[-1]
+    groups = width // (joined * rows)
+    group_place = lax.axis_index(ALL[1:])
+
+    def inward(values):
+        shape = values.shape
+        values = values.reshape(shape[:-1] + (joined, groups, rows))
+        return jnp.swapaxes(values, -3, -2).reshape(shape)
+
+    def outward(values):
+        shape = values.shape
+        values = values.reshape(shape[:-1] + (groups, joined, rows))
+        return jnp.swapaxes(values, -3, -2).reshape(shape)
+
+    proj = gather(weights[1], ALL)
+    proj = inward(lax.dynamic_slice_in_dim(proj, group_place * joined * rows, joined * rows))
+    weights = [gather(weight, "zo") for weight in weights]
+    weights[1] = proj
+    outs = list(group_body(inward(hidden_in), token_marks, inward(out_grad), *weights))
+    outs[:2] = outward(outs[0]), outward(outs[1])
+    proj_grad = jnp.zeros((width, width), jnp.float32)
+    proj_grad = lax.dynamic_update_slice_in_dim(
+        proj_grad, outward(outs[3]), group_place * joined * rows, 0
+    )
+    outs[2:] = [scatter_sum(grad, "zo") for grad in outs[2:]]
+    outs[3] = scatter_sum(proj_grad, ALL)
+    return tuple(outs)
 
 
 def solution(mesh):

time: 827 us -> 780 us (0.943)
  the two profiles are of different devices: /device:TPU:0 before, /device:TPU:1 now
where the time goes in v3:
time: 780 us; the launch traced here: 769 us
  Pallas kernels  419 us (54%)
  waiting for transfers between devices  152 us (19%)
  matrix products  102 us (13%)
  local copies, waits for them, and re-layouts  43.6 us (6%)
  other arithmetic  37.6 us (5%)
  between operations  15 us (2%)
    pallas_call x1, Pallas kernels, reduce_grads(): pl.pallas_call(reduce_kernel, out_shape=(jax.ShapeDtypeStruct((8, rows_ow...  177 us
    pallas_call x1, Pallas kernels, gather_weights(): pl.pallas_call(gather_kernel, out_shape=(jax.ShapeDtypeStruct((4, 8, rows...  132 us
    all_gather x2, waiting for transfers between devices, gather(): return lax.all_gather(values, axes, axis=0, tiled=True)  86.3 us
    pallas_call x2, Pallas kernels, plane_scatter(): pl.pallas_call(plane_scatter_kernel, out_shape=jax.ShapeDtypeStruct((own,...  81.3 us
    reduce_scatter x2, waiting for transfers between devices, scatter_sum(): return lax.psum_scatter(values, axes, scatter_dimension=0, tiled=True)  65.2 us
    dot_general x5, matrix products, dot(): return jnp.dot(left_side, right_side, preferred_element_type=jnp.float32)  40.4 us
    dot_general x5, matrix products, contract_first(): lax.dot_general(left_side, right_side, (((0,), (0,)), ((), ())), preferre...  30 us
    pallas_call x1, Pallas kernels, plane_gather(): pl.pallas_call(plane_gather_kernel, out_shape=jax.ShapeDtypeStruct((8,) +...  28.7 us
  transfers between devices with their start and end apart: 4, of which 4 were waited for; matrix products, arithmetic and copies ran while one was open for 4% of the time, Pallas kernels for 0%

profile of v3, /device:TPU:1, one launch (start us, length us, event | category | flops | bytes accessed | tf_op | source)
XLA Modules:
  0.0 769.3 jit_solution(16140437719090889981)
XLA Ops:
  7.2 1.8 fusion.19
  9.1 1.8 copy.131
  11.4 1.7 reshape.258.qkv_in
  14.2 132.0 %gather_weights.1 = (bf16[4,8,64,768]{3,2,1,0:T(8,128)(2,1)}, bf16[3,4,2,2,2,64,768]{6,5,4,3,2,1,0:T(8,128)(2,1)}, bf16[4,64,2048]{2,1,0:T(8,128)(2,1)}, bf16[8,128,2048]{2,1,0:T(8,128)(2,1)}, f32[4,8,8,128]{3,2,1,0:T(8,128)}) custom-call(bf16[8,64,768]{2,1,0:T(8,128)(2,1)} %reshape.258.qkv_in, bf16[8,3,64,768]{3,2,1,0:T(8,128)(2,1)} %bitcast.207, ...), custom_call_target="tpu_custom_call" | custom-call | bytes 400000000 | tf_op jit(solution)/shard_map/gather_weights/pallas_call | solution.py:634
  147.9 6.2 convolution_bitcast_fusion
  154.4 2.8 reshape_reshape.16
  157.2 1.7 fusion.63
  158.9 1.6 slice.118
  161.8 3.0 fusion.50
  166.1 2.5 fusion.64
  168.6 2.9 fusion.23
  171.5 2.0 copy.76
  173.5 1.6 copy.77
  175.1 4.6 convolution_convert_fusion
  179.7 55.2 %plane_scatter_4.1 = f32[128,2048]{1,0:T(8,128)} custom-call(bf16[8,128,2048]{2,1,0:T(8,128)(2,1)} %bitcast.206), custom_call_target="tpu_custom_call" | custom-call | tf_op jit(solution)/shard_map/plane_scatter_4/pallas_call | solution.py:766
  238.3 6.7 fusion.62
  245.0 38.6 %all-gather.3.cloned.1.call-done = bf16[1024,2048]{1,0:T(8,128)(2,1)} async-done(((bf16[128,2048]{1,0:T(8,128)(2,1)}), bf16[1024,2048]{1,0:T(8,128)(2,1)}) %all-gather.3.cloned.1.call-update) | async-done | bytes 4194320 | tf_op jit(solution)/shard_map/all_gather | solution.py:78
  283.6 6.3 fusion.65
  290.0 12.6 %multiply_convert_fusion.1 = (bf16[1024,768]{1,0:T(8,128)(2,1)S(1)}, f32[1024,768]{1,0:T(8,128)}, f32[1024,768]{1,0:T(8,128)}, f32[1024,768]{1,0:T(8,128)}) fusion(f32[1024,768]{1,0:T(8,128)S(1)} %fusion.65, bf16[1024,2048]{1,0:T(8,128)(2,1)S(1)} %copy-done.32, bf16[2048,768]{1,0:T(8,128)(2,1)S(1)} %bitcast.219), kind=kOutput, calls=%fused_computation.25 | convolution fusion | flops 3273129984 | bytes 21495808 | tf_op jit(solution)/shard_map/dot_general | solution.py:39
  303.7 5.0 convolution_convert_fusion.2
  310.1 45.3 %reduce-scatter.3.cloned.1.call-done = bf16[128,2048]{1,0:T(8,128)(2,1)} async-done(((bf16[1024,2048]{1,0:T(8,128)(2,1)}), bf16[128,2048]{1,0:T(8,128)(2,1)}) %reduce-scatter.3.cloned.1.call-update) | async-done | bytes 524304 | tf_op jit(solution)/shard_map/reduce_scatter | solution.py:82
  359.2 2.5 fusion.58
  361.7 47.7 %all-gather.5.cloned.1.call-done = bf16[1024,2048]{1,0:T(8,128)(2,1)} async-done(((bf16[128,2048]{1,0:T(8,128)(2,1)}), bf16[1024,2048]{1,0:T(8,128)(2,1)}) %all-gather.5.cloned.1.call-update) | async-done | bytes 4194320 | tf_op jit(solution)/shard_map/all_gather | solution.py:78
  409.4 10.8 %multiply_convert_fusion = (bf16[1024,768]{1,0:T(8,128)(2,1)S(1)}, bf16[1024,768]{1,0:T(8,128)(2,1)S(1)}) fusion(f32[1024,768]{1,0:T(8,128)} %get-tuple-element.78, f32[1024,768]{1,0:T(8,128)} %get-tuple-element.79, f32[1024,768]{1,0:T(8,128)} %copy-done.35, f32[1024,768]{1,0:T(8,128)} %get-tuple-element.116, ...), kind=kOutput, calls=%fused_computation.24 | convolution fusion | flops 3229089792 | bytes 23068672 | tf_op jit(solution)/shard_map/dot_general | solution.py:39
  420.3 3.4 fusion.66
  423.7 5.3 add_convert_fusion
  429.2 8.1 %convolution_convert_fusion.5 = bf16[2048,768]{1,0:T(8,128)(2,1)} fusion(bf16[1024,2048]{1,0:T(8,128)(2,1)} %all-gather.3.cloned.1.call-done, bf16[1024,768]{1,0:T(8,128)(2,1)} %copy-done.38), kind=kOutput, calls=%fused_computation.14 | convolution fusion | flops 3222798336 | bytes 8912896 | tf_op jit(solution)/shard_map/dot_general | solution.py:33
  437.4 4.9 convolution_convert_fusion.4
  442.3 4.9 convolution_convert_fusion.3
  447.2 8.5 %pad_maximum_fusion.ffn_in = bf16[3,4,2,2,2,64,768]{6,5,4,3,2,1,0:T(8,128)(2,1)} fusion(bf16[1,4,2,2,2,64,768]{6,5,4,3,2,1,0:T(8,128)(2,1)} %bitcast.227, bf16[1,4,2,2,2,64,768]{6,5,4,3,2,1,0:T(8,128)(2,1)} %bitcast.226, bf16[1,4,2,2,2,64,768]{6,5,4,3,2,1,0:T(8,128)(2,1)} %bitcast.225), kind=kLoop, calls=%fused_computation.1 | loop fusion | flops 9437184 | bytes 18874368 | tf_op jit(solution)/shard_map/stack | solution.py:950
  455.7 20.0 %reduce-scatter.5.cloned.1.call-done = bf16[128,2048]{1,0:T(8,128)(2,1)} async-done(((bf16[1024,2048]{1,0:T(8,128)(2,1)}), bf16[128,2048]{1,0:T(8,128)(2,1)}) %reduce-scatter.5.cloned.1.call-update) | async-done | bytes 524304 | tf_op jit(solution)/shard_map/reduce_scatter | solution.py:82
  475.6 3.0 multiply_reduce_fusion.1
  478.7 1.7 fusion.59
  480.3 28.7 %plane_gather_5.1 = bf16[8,128,2048]{2,1,0:T(8,128)(2,1)} custom-call(bf16[128,2048]{1,0:T(8,128)(2,1)} %get-tuple-element.74.own_in), custom_call_target="tpu_custom_call" | custom-call | tf_op jit(solution)/shard_map/plane_gather_5/pallas_call | solution.py:815
  509.1 4.7 convolution_convert_fusion.7
  516.0 2.0 reshape_reshape.20
  517.9 2.0 copy.87
  519.9 1.9 multiply_reduce_fusion
  525.8 1.9 subtract_convert_fusion.1
  528.9 1.6 copy.90
  532.4 7.3 convolution_convert_fusion.6
  539.8 177.1 %reduce_grads.1 = (bf16[8,64,768]{2,1,0:T(8,128)(2,1)}, bf16[8,3,64,768]{3,2,1,0:T(8,128)(2,1)}, bf16[64,2048]{1,0:T(8,128)(2,1)}, f32[8,128]{1,0:T(8,128)}) custom-call(bf16[4,8,64,768]{3,2,1,0:T(8,128)(2,1)} %bitcast.229, bf16[3,4,2,2,2,64,768]{6,5,4,3,2,1,0:T(8,128)(2,1)} %pad_maximum_fusion.ffn_in, bf16[4,64,2048]{2,1,0:T(8,128)(2,1)} %bitcast.240, ...), custom_call_target="tpu_custom_call" | custom-call | bytes 400000000 | tf_op jit(solution)/shard_map/reduce_grads/pallas_call | solution.py:666
  716.8 1.9 copy.112
  718.8 2.1 fusion.36
  723.0 1.6 copy.116
  726.8 6.9 convolution_convert_fusion.1
  733.6 26.1 %plane_scatter_6.1 = f32[128,2048]{1,0:T(8,128)} custom-call(bf16[8,128,2048]{2,1,0:T(8,128)(2,1)} %bitcast.213), custom_call_target="tpu_custom_call" | custom-call | tf_op jit(solution)/shard_map/plane_scatter_6/pallas_call | solution.py:766
  759.8 2.5 add_convert_fusion.1
  (162 shorter events, 29.6 us)
Async XLA Ops:
  7.2 276.5 %all-gather.3.cloned.1.call-start = ((), (), s32[]{:S(2)}) async-start(), calls=%async_computation.2 | async-start | bytes 4718592 | tf_op jit(solution)/shard_map/all_gather | solution.py:78
  9.0 1.8 copy-start.21
  10.8 2.3 copy-start.27
  10.8 2.6 copy-start.28
  10.8 2.6 copy-start.29
  10.8 2.6 copy-start.30
  10.8 2.6 copy-start.31
  157.2 3.3 copy-start.24
  166.0 5.4 copy-start.8
  166.1 5.4 copy-start.10
  166.1 5.4 copy-start.12
  166.1 5.4 copy-start.14
  175.1 4.6 copy-start.3
  238.3 117.1 %reduce-scatter.3.cloned.1.call-start = ((), (), s32[]{:S(2)}) async-start(), calls=%async_computation.3 | async-start | bytes 4718592 | tf_op jit(solution)/shard_map/reduce_scatter | solution.py:82
  283.6 6.3 copy-start.4
  283.6 6.3 copy-start.32
  289.9 12.6 %copy-start.35 = (f32[1024,768]{1,0:T(8,128)}, f32[1024,768]{1,0:T(8,128)S(1)}, u32[]{:S(2)}) copy-start(f32[1024,768]{1,0:T(8,128)S(1)} %fusion.65) | copy-start | bytes 9437188
  290.0 13.7 %copy-start.7 = (bf16[1,4,2,2,2,64,768]{6,5,4,3,2,1,0:T(8,128)(2,1)S(1)}, bf16[1,4,2,2,2,64,768]{6,5,4,3,2,1,0:T(8,128)(2,1)}, u32[]{:S(2)}) copy-start(bf16[1,4,2,2,2,64,768]{6,5,4,3,2,1,0:T(8,128)(2,1)} %get-tuple-element.82) | copy-start | bytes 9437188
  302.5 1.1 copy-start.39
  308.7 1.0 copy-start.1
  308.7 100.7 %all-gather.5.cloned.1.call-start = ((), (), s32[]{:S(2)}) async-start(), calls=%async_computation.4 | async-start | bytes 4718592 | tf_op jit(solution)/shard_map/all_gather | solution.py:78
  355.3 3.1 copy-start
  361.7 114.0 %reduce-scatter.5.cloned.1.call-start = ((), (), s32[]{:S(2)}) async-start(), calls=%async_computation.5 | async-start | bytes 4718592 | tf_op jit(solution)/shard_map/reduce_scatter | solution.py:82
  409.4 10.8 %copy-start.6 = (bf16[1,4,2,2,2,64,768]{6,5,4,3,2,1,0:T(8,128)(2,1)S(1)}, bf16[1,4,2,2,2,64,768]{6,5,4,3,2,1,0:T(8,128)(2,1)}, u32[]{:S(2)}) copy-start(bf16[1,4,2,2,2,64,768]{6,5,4,3,2,1,0:T(8,128)(2,1)} %get-tuple-element.84) | copy-start | bytes 9437188
  420.2 3.5 copy-start.38
  420.2 3.5 copy-start.36
  420.2 3.5 copy-start.5
  429.2 8.1 %copy-start.33 = (bf16[1024,2048]{1,0:T(8,128)(2,1)S(1)}, bf16[1024,2048]{1,0:T(8,128)(2,1)}, u32[]{:S(2)}) copy-start(bf16[1024,2048]{1,0:T(8,128)(2,1)} %all-gather.3.cloned.1.call-done) | copy-start | bytes 12582916
  429.2 8.1 %copy-start.37 = (bf16[1024,768]{1,0:T(8,128)(2,1)S(1)}, bf16[1024,768]{1,0:T(8,128)(2,1)}, u32[]{:S(2)}) copy-start(bf16[1024,768]{1,0:T(8,128)(2,1)} %copy-done.36) | copy-start | bytes 4718596
  437.3 4.9 copy-start.34
  437.3 4.9 copy-start.40
  509.1 4.8 copy-start.2
  509.1 4.8 copy-start.20
  515.1 4.8 copy-start.16
  519.9 1.9 copy-start.17
  521.7 1.1 copy-start.13
  521.8 1.2 copy-start.15
  521.8 1.7 copy-start.9
  521.8 1.7 copy-start.11
  523.0 1.3 copy-start.23
  527.7 1.0 copy-start.25
  531.7 8.1 %copy-start.18 = (bf16[2,4,2,64,768]{4,3,2,1,0:T(8,128)(2,1)}, bf16[2,4,2,64,768]{4,3,2,1,0:T(8,128)(2,1)S(1)}, u32[]{:S(2)}) copy-start(bf16[2,4,2,64,768]{4,3,2,1,0:T(8,128)(2,1)S(1)} %copy.91) | copy-start | bytes 4718596
  718.8 2.1 copy-start.22
  722.1 2.6 copy-start.26
  723.0 3.7 copy-start.19
Sparse Core Ops, SparseCore 0:
  238.4 45.1 all-gather.2
  308.9 46.4 reduce-scatter.2
  361.8 47.5 all-gather.4
  429.2 46.4 reduce-scatter.4

commit v4 on v3

--- a/solution.py
+++ b/solution.py
@@ -169,6 +169,9 @@
     def column(self, step):
         other = lax.rem(self.unit + step + 8, 8)
         return (self.zo, other // 2, self.x, self.y, lax.rem(other, 2)), other
+
+    def ends(self):
+        return self.line(jnp.minimum(self.zi + 1, 3)), self.line(jnp.maximum(self.zi - 1, 0))
 
     def line(self, z):
         return (self.zo, z, self.x, self.y, self.c)
@@ -348,271 +351,6 @@
     for step in range(8):
         wire.arrive(("fd", step), ffn_slot(step, 1 - at.x, 1 - at.y), x_side)
     small_last()
-    wire.drain()
-
-
-def reduce_kernel(
-    qkv_in,
-    ffn_in,
-    proj_in,
-    small_in,
-    qkv_out,
-    ffn_out,
-    proj_out,
-    small_out,
-    proj_below,
-    proj_above,
-    proj_sum,
-    small_plane,
-    small_mid,
-    small_line,
-    first_in,
-    second_in,
-    second_sum,
-    total,
-    up_in,
-    down_in,
-    up_sum,
-    down_sum,
-    qkv_total,
-    send_sems,
-    recv_sems,
-    own_sems,
-):
-    at = Place()
-    wire = Wire(send_sems, recv_sems)
-    enter(at.neighbours())
-    x_side, y_side = at.plane(4)[0], at.plane(2)[0]
-    steps = (4, 3, 5, 2, 6, 1, 7, 0)
-
-    def add(*terms):
-        whole = terms[0].astype(jnp.float32)
-        for term in terms[1:]:
-            whole = whole + term.astype(jnp.float32)
-        return whole.astype(jnp.bfloat16)
-
-    def owner(step):
-        other = at.column(step)[1]
-        return other // 2, lax.rem(other, 2)
-
-    for delta in range(1, 8):
-        device, other = at.plane(delta)
-        wire.send(("s", delta), small_in.at[other], small_plane.at[at.rank], device)
-
-    def small_second():
-        whole = small_in[at.rank]
-        for delta in range(1, 8):
-            device, other = at.plane(delta)
-            wire.arrive(("s", delta), small_plane.at[other], device)
-            whole = whole + small_plane[other]
-        small_mid[...] = whole
-        for dz in range(1, 4):
-            z = lax.rem(at.zi + dz, 4)
-            wire.send(("t", dz), small_mid.at[z], small_line.at[at.zi], at.line(z))
-
-    def small_last():
-        whole = small_mid[at.zi]
-        for dz in range(1, 4):
-            z = lax.rem(at.zi - dz + 4, 4)
-            wire.arrive(("t", dz), small_line.at[z], at.line(z))
-            whole = whole + small_line[z]
-        small_out[...] = whole
-
-    for turn, step in enumerate(steps):
-        z, c = owner(step)
-        if turn % 2:
-            wire.send(("a", step), ffn_in.at[:, z, 1 - at.x, :, c], first_in.at[step], x_side)
-        else:
-            wire.send(("a", step), ffn_in.at[:, z, :, 1 - at.y, c], first_in.at[step], y_side)
-
-    def ffn_second(step, turn):
-        z, c = owner(step)
-        if turn % 2:
-            wire.arrive(("a", step), first_in.at[step], x_side)
-            mine = ffn_in[:, z, at.x, 1 - at.y, c]
-            second_sum[step] = add(mine, first_in[step, :, 1 - at.y])
-            wire.send(("b", step), second_sum.at[step], second_in.at[step], y_side)
-        else:
-            wire.arrive(("a", step), first_in.at[step], y_side)
-            mine = ffn_in[:, z, 1 - at.x, at.y, c]
-            second_sum[step] = add(mine, first_in[step, :, 1 - at.x])
-            wire.send(("b", step), second_sum.at[step], second_in.at[step], x_side)
-
-    def ffn_last(step, turn):
-        z, c = owner(step)
-        near = at.y if turn % 2 else at.x
-        wire.arrive(("b", step), second_in.at[step], x_side)
-        total[step] = add(ffn_in[:, z, at.x, at.y, c], first_in[step, :, near], second_in[step])
-        if step:
-            wire.send(("c", step), total.at[step], ffn_out.at[at.unit], at.column(step)[0])
-        else:
-            pltpu.make_async_copy(total.at[0], ffn_out.at[at.unit], own_sems.at[0]).start()
-
-    pieces = 4
-    wide = 8 // pieces
-    up, down = at.line(jnp.minimum(at.zi + 1, 3)), at.line(jnp.maximum(at.zi - 1, 0))
-
-    def qkv_pass(goal, piece):
-        part = pl.ds(piece * wide, wide)
-
-        if goal > 0:
-
-            @pl.when(at.zi < goal)
-            def _():
-                @pl.when(at.zi == 0)
-                def _():
-                    up_sum[goal, part] = qkv_in[goal, part]
-
-                @pl.when(at.zi > 0)
-                def _():
-                    wire.arrive(("u", goal, piece), up_in.at[goal, part], down)
-                    up_sum[goal, part] = add(qkv_in[goal, part], up_in[goal, part])
-
-            wire.send(
-                ("u", goal, piece),
-                up_sum.at[goal, part],
-                up_in.at[goal, part],
-                up,
-                at.zi < goal,
-            )
-        back = 3 - goal
-        if back < 3:
-
-            @pl.when(at.zi > back)
-            def _():
-                @pl.when(at.zi == 3)
-                def _():
-                    down_sum[back, part] = qkv_in[back, part]
-
-                @pl.when(at.zi < 3)
-                def _():
-                    wire.arrive(("d", back, piece), down_in.at[back, part], up)
-                    down_sum[back, part] = add(qkv_in[back, part], down_in[back, part])
-
-            wire.send(
-                ("d", back, piece),
-                down_sum.at[back, part],
-                down_in.at[back, part],
-                down,
-                at.zi > back,
-            )
-
-    proj_home = at.rank // 2
-
-    def each_rows(step, count, function):
-        @pl.loop(0, count // step)
-        def _(index):
-            function(pl.ds(pl.multiple_of(index * step, step), step))
-
-    def proj_add(out, *terms):
-        for slot in range(4):
-
-            def rows(part):
-                out[slot, part] = add(*(term[slot, part] for term in terms))
-
-            each_rows(16, proj_in.shape[1], rows)
-
-    def proj_pass():
-        ends = (at.zi == 0) | (at.zi == 3)
-        below, above = at.zi < proj_home, at.zi > proj_home
-        wire.send("pu0", proj_in, proj_below, up, below & ends)
-        wire.send("pd0", proj_in, proj_above, down, above & ends)
-
-    def proj_climb():
-        below, above = at.zi < proj_home, at.zi > proj_home
-
-        def climb():
-            wire.arrive("pu0", proj_below, down)
-            proj_add(proj_sum, proj_in, proj_below)
-
-        def descend():
-            wire.arrive("pd0", proj_above, up)
-            proj_add(proj_sum, proj_in, proj_above)
-
-        pl.when(below & (at.zi > 0))(climb)
-        pl.when(above & (at.zi < 3))(descend)
-        wire.send("pu1", proj_sum, proj_below, up, below & (at.zi > 0), recv="pu0")
-        wire.send("pd1", proj_sum, proj_above, down, above & (at.zi < 3), recv="pd0")
-
-    holder = at.zi * 2 + at.x
-    chunk = at.y * 2 + at.c
-    holder_device = (at.zo, at.zi, holder // 4, lax.rem(holder // 2, 2), lax.rem(holder, 2))
-
-    def proj_last():
-        home = at.zi == proj_home
-
-        def first():
-            wire.arrive("pu0", proj_below, down)
-            proj_add(proj_sum, proj_in, proj_below)
-
-        def only():
-            wire.arrive("pd0", proj_above, up)
-            proj_add(proj_sum, proj_in, proj_above)
-
-        def both():
-            wire.arrive("pd0", proj_above, up)
-            proj_add(proj_sum, proj_sum, proj_above)
-
-        pl.when(home & (at.zi > 0))(first)
-        pl.when(home & (at.zi == 0))(only)
-        pl.when(home & (at.zi > 0) & (at.zi < 3))(both)
-        for slot in range(4):
-            target = (at.zo, at.zi, lax.rem(at.rank, 2), slot // 2, slot % 2)
-            other = (chunk != slot) | (at.rank != holder)
-            wire.send(("o", slot), proj_sum.at[slot], proj_out, target, home & other, recv="o")
-        own = pltpu.make_async_copy(proj_sum.at[chunk], proj_out, own_sems.at[2])
-        pl.when(home & (at.rank == holder))(own.start)
-        pl.when(home & (at.rank == holder))(own.wait)
-
-    def qkv_last(piece):
-        part = pl.ds(piece * wide, wide)
-        for goal in range(4):
-
-            @pl.when(at.zi == goal)
-            def _():
-                terms = [qkv_in[goal, part]]
-                if goal > 0:
-                    wire.arrive(("u", goal, piece), up_in.at[goal, part], down)
-                    terms.append(up_in[goal, part])
-                if goal < 3:
-                    wire.arrive(("d", goal, piece), down_in.at[goal, part], up)
-                    terms.append(down_in[goal, part])
-                qkv_total[part] = add(*terms)
-
-    proj_pass()
-    order = [(goal, piece) for goal in (3, 2, 1) for piece in range(pieces)]
-    for index, (goal, piece) in enumerate(order):
-        qkv_pass(goal, piece)
-        if index == 4:
-            proj_climb()
-        if index < 8:
-            ffn_second(steps[index], index)
-        if index >= 3 and index - 3 < 8:
-            ffn_last(steps[index - 3], index - 3)
-    for index in range(len(order) - 3, 8):
-        ffn_last(steps[index], index)
-    small_second()
-    proj_last()
-    for piece in range(pieces):
-        qkv_last(piece)
-    own_qkv = pltpu.make_async_copy(
-        qkv_total.at[at.rank], qkv_out.at[at.rank], own_sems.at[1]
-    )
-    own_qkv.start()
-    for delta in range(1, 8):
-        device, other = at.plane(delta)
-        wire.send(("q", delta), qkv_total.at[other], qkv_out.at[at.rank], device)
-    own_qkv.wait()
-    pltpu.make_async_copy(total.at[0], ffn_out.at[at.unit], own_sems.at[0]).wait()
-    for delta in range(1, 8):
-        device, other = at.plane(delta)
-        wire.arrive(("q", delta), qkv_out.at[other], device)
-    for step in steps:
-        if step:
-            device, other = at.column(-step)
-            wire.arrive(("c", step), ffn_out.at[other], device)
-    small_last()
-    wire.arrive("o", proj_out, holder_device, at.rank != holder)
     wire.drain()
 
 
@@ -655,54 +393,8 @@
     )(qkv_parts, ffn_parts, proj_own, x_own, small)
 
 
-def reduce_grads(qkv_part, ffn_part, proj_part, small_part):
-    _, _, rows_own, qkv_width = qkv_part.shape
-    unit_width = ffn_part.shape[-1]
-    width = proj_part.shape[-1]
-    low_type = jnp.bfloat16
-    block = (rows_own, unit_width)
-    line = (4, 8, rows_own, qkv_width)
-    small_shape = small_part.shape[1:]
-    return pl.pallas_call(
-        reduce_kernel,
-        out_shape=(
-            jax.ShapeDtypeStruct((8, rows_own, qkv_width), low_type),
-            jax.ShapeDtypeStruct((8, 3) + block, low_type),
-            jax.ShapeDtypeStruct((rows_own, width), low_type),
-            jax.ShapeDtypeStruct(small_shape[1:], small_part.dtype),
-        ),
-        in_specs=[VMEM] * 4,
-        out_specs=(ANY,) * 3 + (VMEM,),
-        scratch_shapes=[
-            pltpu.VMEM((4, rows_own, width), low_type),
-            pltpu.VMEM((4, rows_own, width), low_type),
-            pltpu.VMEM((4, rows_own, width), low_type),
-            pltpu.VMEM(small_part.shape, small_part.dtype),
-            pltpu.VMEM(small_shape, small_part.dtype),
-            pltpu.VMEM(small_shape, small_part.dtype),
-            pltpu.VMEM((8, 3, 2) + block, low_type),
-            pltpu.VMEM((8, 3) + block, low_type),
-            pltpu.VMEM((8, 3) + block, low_type),
-            pltpu.VMEM((8, 3) + block, low_type),
-            pltpu.VMEM(line, low_type),
-            pltpu.VMEM(line, low_type),
-            pltpu.VMEM(line, low_type),
-            pltpu.VMEM(line, low_type),
-            pltpu.VMEM(line[1:], low_type),
-            pltpu.SemaphoreType.DMA((96,)),
-            pltpu.SemaphoreType.DMA((96,)),
-            pltpu.SemaphoreType.DMA((3,)),
-        ],
-        compiler_params=comm_params(2),
-        cost_estimate=pl.CostEstimate(
-            flops=0, bytes_accessed=400_000_000, transcendentals=0
-        ),
-        name="reduce_grads",
-    )(qkv_part, ffn_part, proj_part, small_part)
-
-
 def add_rows(out, *terms):
-    step = 16
+    step = 32
 
     @pl.loop(0, out.shape[0] // step)
     def _(index):
@@ -713,11 +405,61 @@
         out[part] = whole.astype(out.dtype)
 
 
-def plane_scatter_kernel(part, out, core_in, core_sum, side_in, side_sum, last_in, ss, rs):
-    at = Place()
-    wire = Wire(ss, rs)
+def column_scatter_flow(at, wire, part, out, core_in, core_sum, up_in, down_in, up_sum, down_sum):
+    core_side = at.plane(1)[0]
+    up, down = at.ends()
+    for goal in (3, 0, 2, 1):
+        source = part.at[goal * 2 + 1 - at.c]
+        wire.send(("rc", goal), source, core_in.at[goal], core_side)
+    yield
+    for goal in (3, 0, 2, 1):
+        wire.arrive(("rc", goal), core_in.at[goal], core_side)
+        add_rows(core_sum.at[goal], part.at[goal * 2 + at.c], core_in.at[goal])
+        source = core_sum.at[goal]
+        if goal > 0:
+            wire.send(("ru", goal), source, up_in.at[goal], up, at.zi == 0)
+        if goal < 3:
+            wire.send(("rd", goal), source, down_in.at[goal], down, at.zi == 3)
+
+    def climb(goal):
+        wire.arrive(("ru", goal), up_in.at[goal], down)
+        add_rows(up_sum.at[goal], core_sum.at[goal], up_in.at[goal])
+
+    def descend(goal):
+        wire.arrive(("rd", goal), down_in.at[goal], up)
+        add_rows(down_sum.at[goal], core_sum.at[goal], down_in.at[goal])
+
+    for goal in (3, 2):
+        yield
+        back = 3 - goal
+        passing = (at.zi > 0) & (at.zi < goal)
+        pl.when(passing)(lambda: climb(goal))
+        key = "ru", goal
+        wire.send(("ru2", goal), up_sum.at[goal], up_in.at[goal], up, passing, recv=key)
+        passing = (at.zi < 3) & (at.zi > back)
+        pl.when(passing)(lambda: descend(back))
+        key = "rd", back
+        wire.send(("rd2", back), down_sum.at[back], down_in.at[back], down, passing, recv=key)
+    yield
+    add_rows(out, core_sum.at[at.zi])
+
+    def last(key, source, device):
+        wire.arrive(key, source, device)
+        add_rows(out, out, source)
+
+    for goal in range(4):
+        if goal > 0:
+            pl.when(at.zi == goal)(lambda: last(("ru", goal), up_in.at[goal], down))
+        if goal < 3:
+            pl.when(at.zi == goal)(lambda: last(("rd", goal), down_in.at[goal], up))
+
+
+def column_scratch(own, width):
+    return [pltpu.VMEM((4, own, width), jnp.bfloat16)] * 6
+
+
+def plane_scatter_flow(at, wire, part, out, core_in, core_sum, side_in, side_sum, last_in):
     x_side, y_side, core_side = at.plane(4)[0], at.plane(2)[0], at.plane(1)[0]
-    enter([x_side, y_side, core_side])
     half = out.shape[1] // 2
     halves = (pl.ds(0, half), pl.ds(half, half))
     order = ((1, 1), (1, 0), (0, 1), (0, 0))
@@ -729,6 +471,7 @@
         x, y = place(dx, dy)
         other = x * 4 + y * 2 + 1 - at.c
         wire.send(("c", dx, dy), part.at[other], core_in.at[dx * 2 + dy], core_side)
+    yield
     for dx, dy in order:
         x, y = place(dx, dy)
         mine = x * 4 + y * 2 + at.c
@@ -737,94 +480,532 @@
         add_rows(core_sum.at[slot], part.at[mine], core_in.at[slot])
         if dx:
             source = core_sum.at[slot, :, halves[0]]
-            wire.send(("a", dy), source, side_in.at[0, dy], x_side)
+            wire.send(("sa", dy), source, side_in.at[0, dy], x_side)
         if dy:
             source = core_sum.at[slot, :, halves[1]]
-            wire.send(("b", dx), source, side_in.at[1, dx], y_side)
-    wire.arrive(("a", 1), side_in.at[0, 1], x_side)
+            wire.send(("sb", dx), source, side_in.at[1, dx], y_side)
+    yield
+    wire.arrive(("sa", 1), side_in.at[0, 1], x_side)
     add_rows(side_sum.at[0], core_sum.at[1, :, halves[0]], side_in.at[0, 1])
-    wire.send("y", side_sum.at[0], last_in.at[0], y_side)
-    wire.arrive(("b", 1), side_in.at[1, 1], y_side)
+    wire.send("sy", side_sum.at[0], last_in.at[0], y_side)
+    wire.arrive(("sb", 1), side_in.at[1, 1], y_side)
     add_rows(side_sum.at[1], core_sum.at[2, :, halves[1]], side_in.at[1, 1])
-    wire.send("x", side_sum.at[1], last_in.at[1], x_side)
-    wire.arrive(("a", 0), side_in.at[0, 0], x_side)
-    wire.arrive(("b", 0), side_in.at[1, 0], y_side)
-    wire.arrive("y", last_in.at[0], y_side)
-    add_rows(
-        out.at[:, halves[0]], core_sum.at[0, :, halves[0]], side_in.at[0, 0], last_in.at[0]
-    )
-    wire.arrive("x", last_in.at[1], x_side)
-    add_rows(
-        out.at[:, halves[1]], core_sum.at[0, :, halves[1]], side_in.at[1, 0], last_in.at[1]
-    )
+    wire.send("sx", side_sum.at[1], last_in.at[1], x_side)
+    yield
+    wire.arrive(("sa", 0), side_in.at[0, 0], x_side)
+    wire.arrive(("sb", 0), side_in.at[1, 0], y_side)
+    wire.arrive("sy", last_in.at[0], y_side)
+    terms = core_sum.at[0, :, halves[0]], side_in.at[0, 0], last_in.at[0]
+    add_rows(out.at[:, halves[0]], *terms)
+    wire.arrive("sx", last_in.at[1], x_side)
+    terms = core_sum.at[0, :, halves[1]], side_in.at[1, 0], last_in.at[1]
+    add_rows(out.at[:, halves[1]], *terms)
+
+
+def plane_scratch(own, width):
+    return [
+        pltpu.VMEM((4, own, width), jnp.bfloat16),
+        pltpu.VMEM((4, own, width), jnp.bfloat16),
+        pltpu.VMEM((2, 2, own, width // 2), jnp.bfloat16),
+        pltpu.VMEM((2, own, width // 2), jnp.bfloat16),
+        pltpu.VMEM((2, own, width // 2), jnp.bfloat16),
+    ]
+
+
+def plane_gather_flow(at, wire, own_in, out, own_sem):
+    x_side, y_side, core_side = at.plane(4)[0], at.plane(2)[0], at.plane(1)[0]
+    half = own_in.shape[0] // 2
+    mine = out.at[at.rank]
+    wire.send("gx", own_in, mine, x_side)
+    wire.send("gy", own_in, mine, y_side)
+    wire.send("gc0", own_in, mine, core_side)
+    own = pltpu.make_async_copy(own_in, mine, own_sem)
+    own.start()
+    yield
+    from_x, from_y, from_xy = (at.plane(delta)[1] for delta in (4, 2, 6))
+    low_half, high_half = pl.ds(0, half), pl.ds(half, half)
+    wire.arrive("gx", out.at[from_x], x_side)
+    wire.send("gd0", out.at[from_x, low_half], out.at[from_x, low_half], y_side)
+    wire.send("gc1", out.at[from_x], out.at[from_x], core_side)
+    wire.arrive("gy", out.at[from_y], y_side)
+    wire.send("gd1", out.at[from_y, high_half], out.at[from_y, high_half], x_side)
+    wire.send("gc2", out.at[from_y], out.at[from_y], core_side)
+    yield
+    wire.arrive("gd0", out.at[from_xy, low_half], y_side)
+    wire.arrive("gd1", out.at[from_xy, high_half], x_side)
+    wire.send("gc3", out.at[from_xy], out.at[from_xy], core_side)
+    own.wait()
+    for index, delta in enumerate((1, 5, 3, 7)):
+        wire.arrive("gc%d" % index, out.at[at.plane(delta)[1]], core_side)
+
+
+def close_units_kernel(
+    gate_in,
+    raise_in,
+    lower_in,
+    part,
+    d_second,
+    hat,
+    inverse,
+    gain,
+    ffn_out,
+    branch_out,
+    d_first,
+    norm_out,
+    first_in,
+    second_sum,
+    second_in,
+    total,
+    d_normed,
+    branch_low,
+    core_in,
+    core_sum,
+    up_in,
+    down_in,
+    up_sum,
+    down_sum,
+    send_sems,
+    recv_sems,
+    own_sems,
+):
+    at = Place()
+    wire = Wire(send_sems, recv_sems)
+    enter(at.neighbours())
+    x_side, y_side = at.plane(4)[0], at.plane(2)[0]
+    steps = (4, 3, 5, 2, 6, 1, 7, 0)
+    sources = gate_in, raise_in, lower_in
+
+    def owner(step):
+        other = at.column(step)[1]
+        return other // 2, lax.rem(other, 2)
+
+    def ffn_first(turn):
+        step = steps[turn]
+        z, c = owner(step)
+        for index, source in enumerate(sources):
+            if turn % 2:
+                block, device = source.at[z, 1 - at.x, :, c], x_side
+            else:
+                block, device = source.at[z, :, 1 - at.y, c], y_side
+            wire.send(("a", step, index), block, first_in.at[step, index], device)
+
+    def ffn_second(turn):
+        step = steps[turn]
+        z, c = owner(step)
+        for index, source in enumerate(sources):
+            if turn % 2:
+                wire.arrive(("a", step, index), first_in.at[step, index], x_side)
+                terms = source.at[z, at.x, 1 - at.y, c], first_in.at[step, index, 1 - at.y]
+            else:
+                wire.arrive(("a", step, index), first_in.at[step, index], y_side)
+                terms = source.at[z, 1 - at.x, at.y, c], first_in.at[step, index, 1 - at.x]
+            add_rows(second_sum.at[step, index], *terms)
+        wire.send(
+            ("b", step), second_sum.at[step], second_in.at[step], y_side if turn % 2 else x_side
+        )
+
+    own_total = pltpu.make_async_copy(total.at[0], ffn_out.at[at.unit], own_sems.at[0])
+
+    def ffn_last(turn):
+        step = steps[turn]
+        z, c = owner(step)
+        near = at.y if turn % 2 else at.x
+        wire.arrive(("b", step), second_in.at[step], x_side)
+        for index, source in enumerate(sources):
+            add_rows(
+                total.at[step, index],
+                source.at[z, at.x, at.y, c],
+                first_in.at[step, index, near],
+                second_in.at[step, index],
+            )
+        if step:
+            wire.send(("f", step), total.at[step], ffn_out.at[at.unit], at.column(step)[0])
+        else:
+            own_total.start()
+
+    def norm_rows():
+        count = 16
+        norm_out[...] = jnp.zeros_like(norm_out)
+
+        @pl.loop(0, hat.shape[0] // count)
+        def _(index):
+            rows = pl.ds(pl.multiple_of(index * count, count), count)
+            cotangent = deep_alpha * d_second[rows] + d_normed[rows]
+            near = hat[rows]
+            result = norm_back(cotangent, near, inverse[rows], gain[...])
+            d_first[rows] = result
+            branch_low[rows] = result.astype(jnp.bfloat16)
+            along = cotangent * near
+            norm_out[0] += along[:8] + along[8:]
+            norm_out[1] += cotangent[:8] + cotangent[8:]
+
+    scatter = column_scatter_flow(
+        at, wire, part, d_normed, core_in, core_sum, up_in, down_in, up_sum, down_sum
+    )
+    next(scatter)
+    for turn in range(5):
+        ffn_first(turn)
+    next(scatter)
+    next(scatter)
+    ffn_second(0)
+    ffn_second(1)
+    next(scatter)
+    ffn_second(2)
+    ffn_last(0)
+    for _ in scatter:
+        pass
+    norm_rows()
+    spread = plane_gather_flow(at, wire, branch_low, branch_out, own_sems.at[1])
+    next(spread)
+    for turn in range(5, 8):
+        ffn_first(turn)
+    ffn_last(1)
+    ffn_second(3)
+    ffn_second(4)
+    next(spread)
+    ffn_last(2)
+    ffn_last(3)
+    ffn_second(5)
+    ffn_last(4)
+    next(spread, None)
+    ffn_second(6)
+    ffn_second(7)
+    for _ in spread:
+        pass
+    for turn in range(5, 8):
+        ffn_last(turn)
+    own_total.wait()
+    for step in steps:
+        if step:
+            device, other = at.column(-step)
+            wire.arrive(("f", step), ffn_out.at[other], device)
+    wire.drain()
+
+
+def close_units(grads, part, d_second, hat, inverse, gain):
+    rows_own, unit_width = grads[0].shape[-2:]
+    _, own, width = part.shape
+    low_type = jnp.bfloat16
+    block = (rows_own, unit_width)
+    return pl.pallas_call(
+        close_units_kernel,
+        out_shape=(
+            jax.ShapeDtypeStruct((8, 3) + block, low_type),
+            jax.ShapeDtypeStruct((8, own, width), low_type),
+            jax.ShapeDtypeStruct((own, width), jnp.float32),
+            jax.ShapeDtypeStruct((2, 8, width), jnp.float32),
+        ),
+        in_specs=[VMEM] * 8,
+        out_specs=(ANY, ANY, VMEM, VMEM),
+        scratch_shapes=[
+            pltpu.VMEM((8, 3, 2) + block, low_type),
+            pltpu.VMEM((8, 3) + block, low_type),
+            pltpu.VMEM((8, 3) + block, low_type),
+            pltpu.VMEM((8, 3) + block, low_type),
+            pltpu.VMEM((own, width), jnp.float32),
+            pltpu.VMEM((own, width), low_type),
+        ]
+        + column_scratch(own, width)
+        + [
+            pltpu.SemaphoreType.DMA((80,)),
+            pltpu.SemaphoreType.DMA((80,)),
+            pltpu.SemaphoreType.DMA((2,)),
+        ],
+        compiler_params=comm_params(3),
+        name="close_units",
+    )(*grads, part, d_second, hat, inverse, gain)
+
+
+def close_heads_kernel(
+    qkv_in,
+    proj_in,
+    small_in,
+    part,
+    qkv_out,
+    proj_out,
+    small_out,
+    d_input,
+    proj_below,
+    proj_above,
+    proj_sum,
+    small_plane,
+    small_mid,
+    small_line,
+    up_in,
+    down_in,
+    up_sum,
+    down_sum,
+    qkv_total,
+    core_in,
+    core_sum,
+    side_in,
+    side_sum,
+    last_in,
+    send_sems,
+    recv_sems,
+    own_sems,
+):
+    at = Place()
+    wire = Wire(send_sems, recv_sems)
+    enter(at.neighbours())
+    scatter = plane_scatter_flow(
+        at, wire, part, d_input, core_in, core_sum, side_in, side_sum, last_in
+    )
+    next(scatter)
+
+    def add(*terms):
+        whole = terms[0].astype(jnp.float32)
+        for term in terms[1:]:
+            whole = whole + term.astype(jnp.float32)
+        return whole.astype(jnp.bfloat16)
+
+    for delta in range(1, 8):
+        device, other = at.plane(delta)
+        wire.send(("s", delta), small_in.at[other], small_plane.at[at.rank], device)
+
+    def small_second():
+        whole = small_in[at.rank]
+        for delta in range(1, 8):
+            device, other = at.plane(delta)
+            wire.arrive(("s", delta), small_plane.at[other], device)
+            whole = whole + small_plane[other]
+        small_mid[...] = whole
+        for dz in range(1, 4):
+            z = lax.rem(at.zi + dz, 4)
+            wire.send(("t", dz), small_mid.at[z], small_line.at[at.zi], at.line(z))
+
+    def small_last():
+        whole = small_mid[at.zi]
+        for dz in range(1, 4):
+            z = lax.rem(at.zi - dz + 4, 4)
+            wire.arrive(("t", dz), small_line.at[z], at.line(z))
+            whole = whole + small_line[z]
+        small_out[...] = whole
+
+    pieces = 4
+    wide = 8 // pieces
+    up, down = at.line(jnp.minimum(at.zi + 1, 3)), at.line(jnp.maximum(at.zi - 1, 0))
+
+    def qkv_pass(goal, piece):
+        part = pl.ds(piece * wide, wide)
+
+        if goal > 0:
+
+            @pl.when(at.zi < goal)
+            def _():
+                @pl.when(at.zi == 0)
+                def _():
+                    up_sum[goal, part] = qkv_in[goal, part]
+
+                @pl.when(at.zi > 0)
+                def _():
+                    wire.arrive(("u", goal, piece), up_in.at[goal, part], down)
+                    up_sum[goal, part] = add(qkv_in[goal, part], up_in[goal, part])
+
+            wire.send(
+                ("u", goal, piece),
+                up_sum.at[goal, part],
+                up_in.at[goal, part],
+                up,
+                at.zi < goal,
+            )
+        back = 3 - goal
+        if back < 3:
+
+            @pl.when(at.zi > back)
+            def _():
+                @pl.when(at.zi == 3)
+                def _():
+                    down_sum[back, part] = qkv_in[back, part]
+
+                @pl.when(at.zi < 3)
+                def _():
+                    wire.arrive(("d", back, piece), down_in.at[back, part], up)
+                    down_sum[back, part] = add(qkv_in[back, part], down_in[back, part])
+
+            wire.send(
+                ("d", back, piece),
+                down_sum.at[back, part],
+                down_in.at[back, part],
+                down,
+                at.zi > back,
+            )
+
+    proj_home = at.rank // 2
+
+    def each_rows(step, count, function):
+        @pl.loop(0, count // step)
+        def _(index):
+            function(pl.ds(pl.multiple_of(index * step, step), step))
+
+    def proj_add(out, *terms):
+        for slot in range(4):
+
+            def rows(part):
+                out[slot, part] = add(*(term[slot, part] for term in terms))
+
+            each_rows(16, proj_in.shape[1], rows)
+
+    def proj_pass():
+        ends = (at.zi == 0) | (at.zi == 3)
+        below, above = at.zi < proj_home, at.zi > proj_home
+        wire.send("pu0", proj_in, proj_below, up, below & ends)
+        wire.send("pd0", proj_in, proj_above, down, above & ends)
+
+    def proj_climb():
+        below, above = at.zi < proj_home, at.zi > proj_home
+
+        def climb():
+            wire.arrive("pu0", proj_below, down)
+            proj_add(proj_sum, proj_in, proj_below)
+
+        def descend():
+            wire.arrive("pd0", proj_above, up)
+            proj_add(proj_sum, proj_in, proj_above)
+
+        pl.when(below & (at.zi > 0))(climb)
+        pl.when(above & (at.zi < 3))(descend)
+        wire.send("pu1", proj_sum, proj_below, up, below & (at.zi > 0), recv="pu0")
+        wire.send("pd1", proj_sum, proj_above, down, above & (at.zi < 3), recv="pd0")
+
+    holder = at.zi * 2 + at.x
+    chunk = at.y * 2 + at.c
+    holder_device = (at.zo, at.zi, holder // 4, lax.rem(holder // 2, 2), lax.rem(holder, 2))
+
+    def proj_last():
+        home = at.zi == proj_home
+
+        def first():
+            wire.arrive("pu0", proj_below, down)
+            proj_add(proj_sum, proj_in, proj_below)
+
+        def only():
+            wire.arrive("pd0", proj_above, up)
+            proj_add(proj_sum, proj_in, proj_above)
+
+        def both():
+            wire.arrive("pd0", proj_above, up)
+            proj_add(proj_sum, proj_sum, proj_above)
+
+        pl.when(home & (at.zi > 0))(first)
+        pl.when(home & (at.zi == 0))(only)
+        pl.when(home & (at.zi > 0) & (at.zi < 3))(both)
+        for slot in range(4):
+            target = (at.zo, at.zi, lax.rem(at.rank, 2), slot // 2, slot % 2)
+            other = (chunk != slot) | (at.rank != holder)
+            wire.send(("o", slot), proj_sum.at[slot], proj_out, target, home & other, recv="o")
+        own = pltpu.make_async_copy(proj_sum.at[chunk], proj_out, own_sems.at[2])
+        pl.when(home & (at.rank == holder))(own.start)
+        pl.when(home & (at.rank == holder))(own.wait)
+
+    def qkv_last(piece):
+        part = pl.ds(piece * wide, wide)
+        for goal in range(4):
+
+            @pl.when(at.zi == goal)
+            def _():
+                terms = [qkv_in[goal, part]]
+                if goal > 0:
+                    wire.arrive(("u", goal, piece), up_in.at[goal, part], down)
+                    terms.append(up_in[goal, part])
+                if goal < 3:
+                    wire.arrive(("d", goal, piece), down_in.at[goal, part], up)
+                    terms.append(down_in[goal, part])
+                qkv_total[part] = add(*terms)
+
+    for piece in range(pieces):
+        qkv_pass(3, piece)
+    proj_pass()
+    next(scatter)
+    small_second()
+    for piece in range(pieces):
+        qkv_pass(2, piece)
+    next(scatter)
+    for _ in scatter:
+        pass
+    proj_climb()
+    for piece in range(pieces):
+        qkv_pass(1, piece)
+    proj_last()
+    for piece in range(pieces):
+        qkv_last(piece)
+    own_qkv = pltpu.make_async_copy(
+        qkv_total.at[at.rank], qkv_out.at[at.rank], own_sems.at[1]
+    )
+    own_qkv.start()
+    for delta in range(1, 8):
+        device, other = at.plane(delta)
+        wire.send(("q", delta), qkv_total.at[other], qkv_out.at[at.rank], device)
+    own_qkv.wait()
+    for delta in range(1, 8):
+        device, other = at.plane(delta)
+        wire.arrive(("q", delta), qkv_out.at[other], device)
+    small_last()
+    wire.arrive("o", proj_out, holder_device, at.rank != holder)
+    wire.drain()
+
+
+def close_heads(qkv_part, proj_part, small_part, part):
+    _, _, rows_own, qkv_width = qkv_part.shape
+    _, own, width = part.shape
+    low_type = jnp.bfloat16
+    line = (4, 8, rows_own, qkv_width)
+    small_shape = small_part.shape[1:]
+    return pl.pallas_call(
+        close_heads_kernel,
+        out_shape=(
+            jax.ShapeDtypeStruct((8, rows_own, qkv_width), low_type),
+            jax.ShapeDtypeStruct((rows_own, width), low_type),
+            jax.ShapeDtypeStruct(small_shape[1:], small_part.dtype),
+            jax.ShapeDtypeStruct((own, width), jnp.float32),
+        ),
+        in_specs=[VMEM] * 4,
+        out_specs=(ANY, ANY, VMEM, VMEM),
+        scratch_shapes=[
+            pltpu.VMEM((4, rows_own, width), low_type),
+            pltpu.VMEM((4, rows_own, width), low_type),
+            pltpu.VMEM((4, rows_own, width), low_type),
+            pltpu.VMEM(small_part.shape, small_part.dtype),
+            pltpu.VMEM(small_shape, small_part.dtype),
+            pltpu.VMEM(small_shape, small_part.dtype),
+            pltpu.VMEM(line, low_type),
+            pltpu.VMEM(line, low_type),
+            pltpu.VMEM(line, low_type),
+            pltpu.VMEM(line, low_type),
+            pltpu.VMEM(line[1:], low_type),
+        ]
+        + plane_scratch(own, width)
+        + [
+            pltpu.SemaphoreType.DMA((80,)),
+            pltpu.SemaphoreType.DMA((80,)),
+            pltpu.SemaphoreType.DMA((3,)),
+        ],
+        compiler_params=comm_params(2),
+        name="close_heads",
+    )(qkv_part, proj_part, small_part, part)
+
+
+def plane_scatter_kernel(part, out, *rest):
+    at = Place()
+    wire = Wire(*rest[-2:])
+    enter([at.plane(delta)[0] for delta in (4, 2, 1)])
+    for _ in plane_scatter_flow(at, wire, part, out, *rest[:-2]):
+        pass
     wire.drain()
 
 
 def plane_scatter(part, number):
     _, own, width = part.shape
-    low_type = part.dtype
     return pl.pallas_call(
         plane_scatter_kernel,
         out_shape=jax.ShapeDtypeStruct((own, width), jnp.float32),
         in_specs=[VMEM],
         out_specs=VMEM,
-        scratch_shapes=[
-            pltpu.VMEM((4, own, width), low_type),
-            pltpu.VMEM((4, own, width), low_type),
-            pltpu.VMEM((2, 2, own, width // 2), low_type),
-            pltpu.VMEM((2, own, width // 2), low_type),
-            pltpu.VMEM((2, own, width // 2), low_type),
-            pltpu.SemaphoreType.DMA((16,)),
-            pltpu.SemaphoreType.DMA((16,)),
-        ],
+        scratch_shapes=plane_scratch(own, width)
+        + [pltpu.SemaphoreType.DMA((16,)), pltpu.SemaphoreType.DMA((16,))],
         compiler_params=comm_params(number),
         name="plane_scatter_%d" % number,
     )(part)
-
-
-def plane_gather_kernel(own_in, out, ss, rs, own_sem):
-    at = Place()
-    wire = Wire(ss, rs)
-    x_side, y_side, core_side = at.plane(4)[0], at.plane(2)[0], at.plane(1)[0]
-    enter([x_side, y_side, core_side])
-    half = own_in.shape[0] // 2
-    mine = out.at[at.rank]
-    wire.send("x", own_in, mine, x_side)
-    wire.send("y", own_in, mine, y_side)
-    wire.send("c0", own_in, mine, core_side)
-    own = pltpu.make_async_copy(own_in, mine, own_sem)
-    own.start()
-    from_x, from_y, from_xy = (at.plane(delta)[1] for delta in (4, 2, 6))
-    low_half, high_half = pl.ds(0, half), pl.ds(half, half)
-    wire.arrive("x", out.at[from_x], x_side)
-    wire.send("d0", out.at[from_x, low_half], out.at[from_x, low_half], y_side)
-    wire.send("c1", out.at[from_x], out.at[from_x], core_side)
-    wire.arrive("y", out.at[from_y], y_side)
-    wire.send("d1", out.at[from_y, high_half], out.at[from_y, high_half], x_side)
-    wire.send("c2", out.at[from_y], out.at[from_y], core_side)
-    wire.arrive("d0", out.at[from_xy, low_half], y_side)
-    wire.arrive("d1", out.at[from_xy, high_half], x_side)
-    wire.send("c3", out.at[from_xy], out.at[from_xy], core_side)
-    own.wait()
-    for index, delta in enumerate((1, 5, 3, 7)):
-        wire.arrive("c%d" % index, out.at[at.plane(delta)[1]], core_side)
-    wire.drain()
-
-
-def plane_gather(own_block, number):
-    return pl.pallas_call(
-        plane_gather_kernel,
-        out_shape=jax.ShapeDtypeStruct((8,) + own_block.shape, own_block.dtype),
-        in_specs=[VMEM],
-        out_specs=VMEM,
-        scratch_shapes=[
-            pltpu.SemaphoreType.DMA((16,)),
-            pltpu.SemaphoreType.DMA((16,)),
-            pltpu.SemaphoreType.DMA,
-        ],
-        compiler_params=comm_params(number),
-        name="plane_gather_%d" % number,
-    )(own_block)
 
 
 def group_body(
@@ -945,26 +1126,31 @@
     gate_low = low(d_active * up_val * gelu_slope)
     up_low = low(d_active * gelu_val)
     d_normed_part = low(contract_last(gate_low, gate_here) + contract_last(up_low, up_here))
-    d_normed = deep_alpha * d_second + scatter_sum(d_normed_part, UNIT_AXES).astype(jnp.float32)
-
-    ffn_part = jnp.stack(
-        [
-            low(contract_first(normed_all, gate_low)),
-            low(contract_first(normed_all, up_low)),
-            low(contract_first(down_low, active)),
-        ]
-    )
-
-    gain_one_grad = jnp.sum(d_normed * hat_one, axis=0)
-    shift_one_grad = jnp.sum(d_normed, axis=0)
-    d_first = norm_back(d_normed, hat_one, inverse_one, gain_one)
-    branch_low = low(d_first)
+
+    def unit_grad(left_side, right_side):
+        part = low(contract_first(left_side, right_side))
+        return part.reshape(4, 2, 2, 2, rows_own, unit_width)
+
+    ffn_grads = (
+        unit_grad(normed_all, gate_low),
+        unit_grad(normed_all, up_low),
+        unit_grad(down_low, active),
+    )
+    ffn_part, branch_all, d_first, norm_grads = close_units(
+        ffn_grads,
+        d_normed_part.reshape(unit_ways, own, width),
+        d_second,
+        hat_one,
+        inverse_one,
+        gain_one,
+    )
+    gain_one_grad, shift_one_grad = jnp.sum(norm_grads, axis=1)
+    branch_all = branch_all.reshape(-1, width)
     small_grads = jnp.stack([gain_one_grad, shift_one_grad, gain_two_grad, shift_two_grad])
     small_grads = small_grads.reshape(4, 4, head_ways, rows_own).transpose(2, 1, 0, 3)
     small_grads = small_grads.reshape(head_ways, 4, 4 * rows_own // LANES, LANES)
     small_grads = jnp.pad(small_grads, ((0, 0), (0, 0), (0, -small_grads.shape[2] % 8), (0, 0)))
 
-    branch_all = plane_gather(branch_low, 5).reshape(-1, width)
     proj_part = low(contract_first(context, branch_all)).reshape(4, rows_own, width)
     d_context = to_rows(low(contract_last(branch_all, proj_here)))
     d_context = d_context.reshape(x_size * micro_count, row_length, heads_here, HEAD_DIM)
@@ -980,16 +1166,11 @@
     )
     d_mixed = from_rows(d_mixed.reshape(x_size * micro_count, row_length, 3 * head_width))
     d_input = low(contract_last(d_mixed, qkv_here)).reshape(head_ways, own, width)
-    d_input = plane_scatter(d_input, 6)
+    qkv_part = low(contract_first(x_all, d_mixed))
+    qkv_part, proj_part, small_grads, d_input = close_heads(
+        qkv_part.reshape(4, 8, rows_own, 3 * head_width), proj_part, small_grads, d_input
+    )
     d_input = deep_alpha * d_first + d_input
-
-    qkv_part = low(contract_first(x_all, d_mixed))
-    qkv_part, ffn_part, proj_part, small_grads = reduce_grads(
-        qkv_part.reshape(4, 8, rows_own, 3 * head_width),
-        ffn_part.reshape(3, 4, 2, 2, 2, rows_own, unit_width),
-        proj_part,
-        small_grads,
-    )
     small_grads = small_grads.ravel()[: 4 * rows_own].reshape(4, rows_own)
     qkv_grad = (
         qkv_part.reshape(head_ways, rows_own, 3, head_width)

time: 780 us -> 780 us (level)
  the two profiles are of different devices: /device:TPU:1 before, /device:TPU:6 now
where the time goes in v4:
time: 780 us; the launch traced here: 770 us
  Pallas kernels  464 us (59%)
  waiting for transfers between devices  133 us (17%)
  matrix products  95.6 us (12%)
  local copies, waits for them, and re-layouts  39.9 us (5%)
  other arithmetic  23.6 us (3%)
  between operations  14.7 us (2%)
    pallas_call x1, Pallas kernels, gather_weights(): pl.pallas_call(gather_kernel, out_shape=(jax.ShapeDtypeStruct((4, 8, rows...  161 us
    pallas_call x1, Pallas kernels, close_heads(): pl.pallas_call(close_heads_kernel, out_shape=(jax.ShapeDtypeStruct((8, ro...  149 us
    pallas_call x1, Pallas kernels, close_units(): pl.pallas_call(close_units_kernel, out_shape=(jax.ShapeDtypeStruct((8, 3)...  131 us
    all_gather x2, waiting for transfers between devices, gather(): return lax.all_gather(values, axes, axis=0, tiled=True)  85 us
    reduce_scatter x1, waiting for transfers between devices, scatter_sum(): return lax.psum_scatter(values, axes, scatter_dimension=0, tiled=True)  47.5 us
    dot_general x5, matrix products, dot(): return jnp.dot(left_side, right_side, preferred_element_type=jnp.float32)  40.4 us
    dot_general x5, matrix products, contract_last(): lax.dot_general(left_side, right_side, (((1,), (1,)), ((), ())), preferre...  24.6 us
    pallas_call x1, Pallas kernels, plane_scatter(): pl.pallas_call(plane_scatter_kernel, out_shape=jax.ShapeDtypeStruct((own,...  23.1 us
  transfers between devices with their start and end apart: 3, of which 3 were waited for; matrix products, arithmetic and copies ran while one was open for 1% of the time, Pallas kernels for 0%

profile of v4, /device:TPU:6, one launch (start us, length us, event | category | flops | bytes accessed | tf_op | source)
XLA Modules:
  0.0 770.3 jit_solution(772663237040347275)
XLA Ops:
  7.2 1.8 fusion.19
  9.1 1.7 copy.134
  11.3 1.7 reshape.265.qkv_in
  14.1 160.9 %gather_weights.1 = (bf16[4,8,64,768]{3,2,1,0:T(8,128)(2,1)}, bf16[3,4,2,2,2,64,768]{6,5,4,3,2,1,0:T(8,128)(2,1)}, bf16[4,64,2048]{2,1,0:T(8,128)(2,1)}, bf16[8,128,2048]{2,1,0:T(8,128)(2,1)}, f32[4,8,8,128]{3,2,1,0:T(8,128)}) custom-call(bf16[8,64,768]{2,1,0:T(8,128)(2,1)} %reshape.265.qkv_in, bf16[8,3,64,768]{3,2,1,0:T(8,128)(2,1)} %bitcast.209, ...), custom_call_target="tpu_custom_call" | custom-call | bytes 400000000 | tf_op jit(solution)/shard_map/gather_weights/pallas_call | solution.py:372
  176.6 6.2 convolution_bitcast_fusion
  183.1 2.8 reshape_reshape.16
  185.9 1.7 fusion.64
  187.7 1.6 slice.119
  189.9 3.0 fusion.51
  194.2 2.5 fusion.65
  196.7 2.7 fusion.23
  199.4 1.3 copy.78
  201.3 4.6 convolution_convert_fusion
  205.9 23.1 %plane_scatter_4.1 = f32[128,2048]{1,0:T(8,128)} custom-call(bf16[8,128,2048]{2,1,0:T(8,128)(2,1)} %bitcast.208), custom_call_target="tpu_custom_call" | custom-call | tf_op jit(solution)/shard_map/plane_scatter_4/pallas_call | solution.py:999
  229.0 1.5 fusion.48
  230.6 1.5 multiply_reduce_fusion.2
  232.6 1.5 add_convert_fusion.5
  234.1 5.9 fusion.63
  240.0 41.1 %all-gather.3.cloned.1.call-done = bf16[1024,2048]{1,0:T(8,128)(2,1)} async-done(((bf16[128,2048]{1,0:T(8,128)(2,1)}), bf16[1024,2048]{1,0:T(8,128)(2,1)}) %all-gather.3.cloned.1.call-update) | async-done | bytes 4194320 | tf_op jit(solution)/shard_map/all_gather | solution.py:78
  281.1 6.3 fusion.66
  287.5 12.5 %multiply_convert_fusion.1 = (bf16[1024,768]{1,0:T(8,128)(2,1)S(1)}, f32[1024,768]{1,0:T(8,128)}, f32[1024,768]{1,0:T(8,128)}, f32[1024,768]{1,0:T(8,128)}) fusion(f32[1024,768]{1,0:T(8,128)S(1)} %fusion.66, bf16[1024,2048]{1,0:T(8,128)(2,1)S(1)} %copy-done.37, bf16[2048,768]{1,0:T(8,128)(2,1)S(1)} %bitcast.221), kind=kOutput, calls=%fused_computation.24 | convolution fusion | flops 3273129984 | bytes 21495808 | tf_op jit(solution)/shard_map/dot_general | solution.py:39
  300.0 1.1 copy-done.42
  301.1 5.0 convolution_convert_fusion.2
  307.6 47.5 %reduce-scatter.2.cloned.1.call-done = bf16[128,2048]{1,0:T(8,128)(2,1)} async-done(((bf16[1024,2048]{1,0:T(8,128)(2,1)}), bf16[128,2048]{1,0:T(8,128)(2,1)}) %reduce-scatter.2.cloned.1.call-update) | async-done | bytes 524304 | tf_op jit(solution)/shard_map/reduce_scatter | solution.py:82
  355.1 1.4 fusion.35
  356.4 1.4 multiply_reduce_fusion.1
  357.8 1.6 fusion.31
  359.4 1.9 fusion.60
  362.9 43.9 %all-gather.5.cloned.1.call-done = bf16[1024,2048]{1,0:T(8,128)(2,1)} async-done(((bf16[128,2048]{1,0:T(8,128)(2,1)}), bf16[1024,2048]{1,0:T(8,128)(2,1)}) %all-gather.5.cloned.1.call-update) | async-done | bytes 4194320 | tf_op jit(solution)/shard_map/all_gather | solution.py:78
  406.9 10.8 %multiply_convert_fusion = (bf16[1024,768]{1,0:T(8,128)(2,1)S(1)}, bf16[1024,768]{1,0:T(8,128)(2,1)S(1)}) fusion(f32[1024,768]{1,0:T(8,128)} %get-tuple-element.81, f32[1024,768]{1,0:T(8,128)} %get-tuple-element.82, f32[1024,768]{1,0:T(8,128)} %copy-done.41, f32[1024,768]{1,0:T(8,128)} %get-tuple-element.122, ...), kind=kOutput, calls=%fused_computation.23 | convolution fusion | flops 3229089792 | bytes 23068672 | tf_op jit(solution)/shard_map/dot_general | solution.py:39
  417.7 3.4 fusion.67
  421.2 5.3 add_convert_fusion
  426.5 5.0 convolution_convert_fusion.4
  431.4 4.9 convolution_convert_fusion.5
  436.4 4.9 convolution_convert_fusion.6
  441.3 130.9 %close_units.1 = (bf16[8,3,64,768]{3,2,1,0:T(8,128)(2,1)}, bf16[8,128,2048]{2,1,0:T(8,128)(2,1)}, f32[128,2048]{1,0:T(8,128)}, f32[2,8,2048]{2,1,0:T(8,128)}) custom-call(bf16[4,2,2,2,64,768]{5,4,3,2,1,0:T(8,128)(2,1)} %bitcast.229, bf16[4,2,2,2,64,768]{5,4,3,2,1,0:T(8,128)(2,1)} %bitcast.228, bf16[4,2,2,2,64,768]{5,4,3,2,1,0:T(8,128)(2,1)} %bitcast.227, ...), custom_call_target="tpu_custom_call" | custom-call | tf_op jit(solution)/shard_map/close_units/pallas_call | solution.py:690
  572.2 3.8 convolution_convert_fusion.10
  576.6 1.0 copy-done.23
  577.6 1.5 multiply_reduce_fusion
  582.7 1.3 copy-done.39
  584.0 2.2 convolution_convert_fusion.7
  587.8 1.6 copy.93
  591.4 7.0 convolution_convert_fusion.1
  598.4 5.2 convolution_convert_fusion.3
  603.6 148.8 %close_heads.1 = (bf16[8,64,768]{2,1,0:T(8,128)(2,1)}, bf16[64,2048]{1,0:T(8,128)(2,1)}, f32[8,128]{1,0:T(8,128)}, f32[128,2048]{1,0:T(8,128)}) custom-call(bf16[4,8,64,768]{3,2,1,0:T(8,128)(2,1)} %bitcast.231, bf16[4,64,2048]{2,1,0:T(8,128)(2,1)} %bitcast.241, f32[8,4,8,128]{3,2,1,0:T(8,128)} %pad.14.small_in, bf16[8,128,2048]{2,1,0:T(8,128)(2,1)} %bitcast.218), custom_call_target="tpu_custom_call" | custom-call | tf_op jit(solution)/shard_map/close_heads/pallas_call | solution.py:954
  752.3 2.5 reshape.298
  755.8 1.6 copy.119
  759.9 2.1 fusion.36
  (161 shorter events, 21.9 us)
Async XLA Ops:
  7.2 274.0 %all-gather.3.cloned.1.call-start = ((), (), s32[]{:S(2)}) async-start(), calls=%async_computation.1 | async-start | bytes 4718592 | tf_op jit(solution)/shard_map/all_gather | solution.py:78
  9.0 1.7 copy-start.26
  10.7 2.3 copy-start.31
  10.7 2.6 copy-start.32
  10.7 2.6 copy-start.33
  10.7 2.6 copy-start.34
  10.7 2.6 copy-start.35
  185.9 3.3 copy-start.28
  189.7 7.0 copy-start.27
  192.9 1.3 copy-start.4
  194.1 5.3 copy-start.15
  194.1 5.3 copy-start.17
  194.2 5.2 copy-start.19
  194.2 5.2 copy-start.21
  201.3 4.6 copy-start.7
  205.9 23.1 %copy-start.3 = (bf16[2,1,64,2048]{3,2,1,0:T(8,128)(2,1)S(1)}, bf16[2,1,64,2048]{3,2,1,0:T(8,128)(2,1)}, u32[]{:S(2)}) copy-start(bf16[2,1,64,2048]{3,2,1,0:T(8,128)(2,1)} %param.12) | copy-start | bytes 1572868
  229.0 3.5 copy-start.1
  234.1 121.0 %reduce-scatter.2.cloned.1.call-start = ((), (), s32[]{:S(2)}) async-start(), calls=%async_computation.2 | async-start | bytes 4718592 | tf_op jit(solution)/shard_map/reduce_scatter | solution.py:82
  240.0 47.4 %copy-start.9 = (bf16[1,4,2,2,2,64,768]{6,5,4,3,2,1,0:T(8,128)(2,1)}, bf16[1,4,2,2,2,64,768]{6,5,4,3,2,1,0:T(8,128)(2,1)S(1)}, u32[]{:S(2)}) copy-start(bf16[1,4,2,2,2,64,768]{6,5,4,3,2,1,0:T(8,128)(2,1)S(1)} %get-tuple-element.86) | copy-start | bytes 9437188
  281.1 6.3 copy-start.37
  287.4 12.6 %copy-start.41 = (f32[1024,768]{1,0:T(8,128)}, f32[1024,768]{1,0:T(8,128)S(1)}, u32[]{:S(2)}) copy-start(f32[1024,768]{1,0:T(8,128)S(1)} %fusion.66) | copy-start | bytes 9437188
  287.4 13.7 %copy-start.12 = (bf16[1,4,2,2,2,64,768]{6,5,4,3,2,1,0:T(8,128)(2,1)S(1)}, bf16[1,4,2,2,2,64,768]{6,5,4,3,2,1,0:T(8,128)(2,1)}, u32[]{:S(2)}) copy-start(bf16[1,4,2,2,2,64,768]{6,5,4,3,2,1,0:T(8,128)(2,1)} %get-tuple-element.85) | copy-start | bytes 9437188
  300.0 1.1 copy-start.42
  306.2 1.0 copy-start.6
  306.2 48.9 %copy-start = (bf16[128,2048]{1,0:T(8,128)(2,1)S(1)}, bf16[128,2048]{1,0:T(8,128)(2,1)}, u32[]{:S(2)}) copy-start(bf16[128,2048]{1,0:T(8,128)(2,1)} %get-tuple-element.83) | copy-start | bytes 1572868
  306.2 100.7 %all-gather.5.cloned.1.call-start = ((), (), s32[]{:S(2)}) async-start(), calls=%async_computation.3 | async-start | bytes 4718592 | tf_op jit(solution)/shard_map/all_gather | solution.py:78
  355.1 4.3 copy-start.2
  406.9 10.8 %copy-start.11 = (bf16[1,4,2,2,2,64,768]{6,5,4,3,2,1,0:T(8,128)(2,1)S(1)}, bf16[1,4,2,2,2,64,768]{6,5,4,3,2,1,0:T(8,128)(2,1)}, u32[]{:S(2)}) copy-start(bf16[1,4,2,2,2,64,768]{6,5,4,3,2,1,0:T(8,128)(2,1)} %get-tuple-element.87) | copy-start | bytes 9437188
  417.7 3.5 copy-start.10
  421.1 5.3 copy-start.40
  421.1 5.3 copy-start.43
  426.5 5.0 copy-start.38
  576.0 1.6 copy-start.23
  579.1 1.0 copy-start.20
  579.2 1.2 copy-start.22
  579.2 1.7 copy-start.16
  579.2 1.7 copy-start.18
  581.6 1.0 copy-start.8
  581.6 2.4 copy-start.39
  584.0 2.3 copy-start.5
  584.0 2.3 copy-start.14
  589.5 0.9 copy-start.30
  591.4 7.0 copy-start.36
  754.9 2.6 copy-start.29
  755.8 3.8 copy-start.13
  759.8 2.1 copy-start.24
  759.9 2.8 copy-start.25
Sparse Core Ops, SparseCore 0:
  234.2 46.9 all-gather.2
  306.3 48.7 reduce-scatter.1
  361.5 45.3 all-gather.4

commit v5 on v4

--- a/solution.py
+++ b/solution.py
@@ -175,6 +175,12 @@
 
     def line(self, z):
         return (self.zo, z, self.x, self.y, self.c)
+
+    def column_neighbours(self):
+        return [self.line(z) for z in self.others()] + [self.plane(1)[0]]
+
+    def others(self):
+        return [lax.rem(self.zi + step, 4) for step in (1, 2, 3)]
 
     def neighbours(self):
         plane = [self.plane(delta)[0] for delta in range(1, 8)]
@@ -405,28 +411,30 @@
         out[part] = whole.astype(out.dtype)
 
 
-def column_scatter_flow(at, wire, part, out, core_in, core_sum, up_in, down_in, up_sum, down_sum):
+def column_scatter_flow(
+    at, wire, tag, part, out, core_in, core_sum, up_in, down_in, up_sum, down_sum
+):
     core_side = at.plane(1)[0]
     up, down = at.ends()
     for goal in (3, 0, 2, 1):
         source = part.at[goal * 2 + 1 - at.c]
-        wire.send(("rc", goal), source, core_in.at[goal], core_side)
+        wire.send(("rc", tag, goal), source, core_in.at[goal], core_side)
     yield
     for goal in (3, 0, 2, 1):
-        wire.arrive(("rc", goal), core_in.at[goal], core_side)
+        wire.arrive(("rc", tag, goal), core_in.at[goal], core_side)
         add_rows(core_sum.at[goal], part.at[goal * 2 + at.c], core_in.at[goal])
         source = core_sum.at[goal]
         if goal > 0:
-            wire.send(("ru", goal), source, up_in.at[goal], up, at.zi == 0)
+            wire.send(("ru", tag, goal), source, up_in.at[goal], up, at.zi == 0)
         if goal < 3:
-            wire.send(("rd", goal), source, down_in.at[goal], down, at.zi == 3)
+            wire.send(("rd", tag, goal), source, down_in.at[goal], down, at.zi == 3)
 
     def climb(goal):
-        wire.arrive(("ru", goal), up_in.at[goal], down)
+        wire.arrive(("ru", tag, goal), up_in.at[goal], down)
         add_rows(up_sum.at[goal], core_sum.at[goal], up_in.at[goal])
 
     def descend(goal):
-        wire.arrive(("rd", goal), down_in.at[goal], up)
+        wire.arrive(("rd", tag, goal), down_in.at[goal], up)
         add_rows(down_sum.at[goal], core_sum.at[goal], down_in.at[goal])
 
     for goal in (3, 2):
@@ -434,12 +442,12 @@
         back = 3 - goal
         passing = (at.zi > 0) & (at.zi < goal)
         pl.when(passing)(lambda: climb(goal))
-        key = "ru", goal
-        wire.send(("ru2", goal), up_sum.at[goal], up_in.at[goal], up, passing, recv=key)
+        key = "ru", tag, goal
+        wire.send(("ru2", tag, goal), up_sum.at[goal], up_in.at[goal], up, passing, recv=key)
         passing = (at.zi < 3) & (at.zi > back)
         pl.when(passing)(lambda: descend(back))
-        key = "rd", back
-        wire.send(("rd2", back), down_sum.at[back], down_in.at[back], down, passing, recv=key)
+        key = "rd", tag, back
+        wire.send(("rd2", tag, back), down_sum.at[back], down_in.at[back], down, passing, recv=key)
     yield
     add_rows(out, core_sum.at[at.zi])
 
@@ -449,9 +457,43 @@
 
     for goal in range(4):
         if goal > 0:
-            pl.when(at.zi == goal)(lambda: last(("ru", goal), up_in.at[goal], down))
+            pl.when(at.zi == goal)(lambda: last(("ru", tag, goal), up_in.at[goal], down))
         if goal < 3:
-            pl.when(at.zi == goal)(lambda: last(("rd", goal), down_in.at[goal], up))
+            pl.when(at.zi == goal)(lambda: last(("rd", tag, goal), down_in.at[goal], up))
+
+
+def column_gather_flow(at, wire, tag, own_in, out, own_sem):
+    core_side = at.plane(1)[0]
+    up, down = at.ends()
+
+    def slot(z, c):
+        return out.at[jnp.clip(z, 0, 3) * 2 + c]
+
+    mine = slot(at.zi, at.c)
+    wire.send(("gu", tag, 0), own_in, mine, up, at.zi < 3)
+    wire.send(("gd", tag, 0), own_in, mine, down, at.zi > 0)
+    wire.send(("gc", tag), own_in, mine, core_side)
+    own = pltpu.make_async_copy(own_in, mine, own_sem)
+    own.start()
+    for hop in (1, 2, 3):
+        yield
+        below, above = slot(at.zi - hop, at.c), slot(at.zi + hop, at.c)
+        has_below, has_above = at.zi >= hop, at.zi <= 3 - hop
+        wire.arrive(("gu", tag, hop - 1), below, down, has_below)
+        if hop < 3:
+            wire.send(("gu", tag, hop), below, below, up, has_below & (at.zi < 3))
+        wire.send(("gcu", tag, hop), below, below, core_side, has_below)
+        wire.arrive(("gd", tag, hop - 1), above, up, has_above)
+        if hop < 3:
+            wire.send(("gd", tag, hop), above, above, down, has_above & (at.zi > 0))
+        wire.send(("gcd", tag, hop), above, above, core_side, has_above)
+    yield
+    own.wait()
+    wire.arrive(("gc", tag), slot(at.zi, 1 - at.c), core_side)
+    for hop in (1, 2, 3):
+        below, above = slot(at.zi - hop, 1 - at.c), slot(at.zi + hop, 1 - at.c)
+        wire.arrive(("gcu", tag, hop), below, core_side, at.zi >= hop)
+        wire.arrive(("gcd", tag, hop), above, core_side, at.zi <= 3 - hop)
 
 
 def column_scratch(own, width):
@@ -537,6 +579,115 @@
     own.wait()
     for index, delta in enumerate((1, 5, 3, 7)):
         wire.arrive("gc%d" % index, out.at[at.plane(delta)[1]], core_side)
+
+
+def turn_kernel(
+    part,
+    normed,
+    out_grad,
+    gain,
+    shift,
+    layer_out,
+    d_second,
+    down_out,
+    norm_out,
+    second,
+    down_low,
+    core_in,
+    core_sum,
+    up_in,
+    down_in,
+    up_sum,
+    down_sum,
+    send_sems,
+    recv_sems,
+    own_sems,
+):
+    at = Place()
+    wire = Wire(send_sems, recv_sems)
+    enter(at.column_neighbours())
+    half = normed.shape[0] // 2
+    scratch = core_in, core_sum, up_in, down_in, up_sum, down_sum
+
+    def norm_rows(start):
+        count = 16
+
+        @pl.loop(0, half // count)
+        def _(index):
+            rows = pl.ds(pl.multiple_of(start + index * count, count), count)
+            whole = deep_alpha * normed[rows].astype(jnp.float32) + second[rows]
+            near, inverse = norm_parts(whole)
+            layer_out[rows] = (near * gain[...] + shift[...]).astype(jnp.bfloat16)
+            cotangent = out_grad[rows].astype(jnp.float32)
+            result = norm_back(cotangent, near, inverse, gain[...])
+            d_second[rows] = result
+            down_low[rows] = result.astype(jnp.bfloat16)
+            along = cotangent * near
+            norm_out[0] += along[:8] + along[8:]
+            norm_out[1] += cotangent[:8] + cotangent[8:]
+
+    scatters, gathers = [], []
+    for index in range(2):
+        rows = pl.ds(index * half, half)
+        views = [ref.at[:, rows] for ref in scratch]
+        scatters.append(
+            column_scatter_flow(at, wire, index, part.at[:, rows], second.at[rows], *views)
+        )
+        gathers.append(
+            column_gather_flow(
+                at, wire, index, down_low.at[rows], down_out.at[:, rows], own_sems.at[index]
+            )
+        )
+    norm_out[...] = jnp.zeros_like(norm_out)
+    for flow in scatters:
+        next(flow)
+    for flow in scatters:
+        next(flow)
+    for _ in scatters[0]:
+        pass
+    norm_rows(0)
+    next(gathers[0])
+    next(scatters[1])
+    next(gathers[0])
+    for _ in scatters[1]:
+        pass
+    norm_rows(half)
+    next(gathers[1])
+    next(gathers[0])
+    next(gathers[1])
+    next(gathers[0])
+    for flow in gathers[::-1]:
+        for _ in flow:
+            pass
+    wire.drain()
+
+
+def turn(part, normed, out_grad, gain, shift):
+    _, own, width = part.shape
+    low_type = jnp.bfloat16
+    return pl.pallas_call(
+        turn_kernel,
+        out_shape=(
+            jax.ShapeDtypeStruct((own, width), low_type),
+            jax.ShapeDtypeStruct((own, width), jnp.float32),
+            jax.ShapeDtypeStruct((8, own, width), low_type),
+            jax.ShapeDtypeStruct((2, 8, width), jnp.float32),
+        ),
+        in_specs=[VMEM] * 5,
+        out_specs=(VMEM, VMEM, ANY, VMEM),
+        scratch_shapes=[
+            pltpu.VMEM((own, width), jnp.float32),
+            pltpu.VMEM((own, width), low_type),
+        ]
+        + column_scratch(own, width)
+        + [
+            pltpu.SemaphoreType.DMA((72,)),
+            pltpu.SemaphoreType.DMA((72,)),
+            pltpu.SemaphoreType.DMA((2,)),
+        ],
+        compiler_params=comm_params(5),
+        name="turn",
+    )(part, normed, out_grad, gain, shift)
 
 
 def close_units_kernel(
@@ -640,7 +791,7 @@
             norm_out[1] += cotangent[:8] + cotangent[8:]
 
     scatter = column_scatter_flow(
-        at, wire, part, d_normed, core_in, core_sum, up_in, down_in, up_sum, down_sum
+        at, wire, 0, part, d_normed, core_in, core_sum, up_in, down_in, up_sum, down_sum
     )
     next(scatter)
     for turn in range(5):
@@ -648,28 +799,28 @@
     next(scatter)
     next(scatter)
     ffn_second(0)
+    ffn_first(5)
     ffn_second(1)
+    ffn_first(6)
     next(scatter)
     ffn_second(2)
-    ffn_last(0)
+    ffn_first(7)
+    ffn_second(3)
     for _ in scatter:
         pass
     norm_rows()
     spread = plane_gather_flow(at, wire, branch_low, branch_out, own_sems.at[1])
     next(spread)
-    for turn in range(5, 8):
-        ffn_first(turn)
+    ffn_last(0)
     ffn_last(1)
-    ffn_second(3)
     ffn_second(4)
+    ffn_last(2)
+    ffn_second(5)
+    ffn_last(3)
     next(spread)
-    ffn_last(2)
-    ffn_last(3)
-    ffn_second(5)
-    ffn_last(4)
-    next(spread, None)
     ffn_second(6)
     ffn_second(7)
+    ffn_last(4)
     for _ in spread:
         pass
     for turn in range(5, 8):
@@ -833,40 +984,32 @@
 
     proj_home = at.rank // 2
 
-    def each_rows(step, count, function):
-        @pl.loop(0, count // step)
-        def _(index):
-            function(pl.ds(pl.multiple_of(index * step, step), step))
-
-    def proj_add(out, *terms):
-        for slot in range(4):
-
-            def rows(part):
-                out[slot, part] = add(*(term[slot, part] for term in terms))
-
-            each_rows(16, proj_in.shape[1], rows)
-
-    def proj_pass():
-        ends = (at.zi == 0) | (at.zi == 3)
-        below, above = at.zi < proj_home, at.zi > proj_home
-        wire.send("pu0", proj_in, proj_below, up, below & ends)
-        wire.send("pd0", proj_in, proj_above, down, above & ends)
-
-    def proj_climb():
-        below, above = at.zi < proj_home, at.zi > proj_home
+    def proj_add(slot, *terms):
+        add_rows(proj_sum.at[slot], *(term.at[slot] for term in terms))
+
+    below, above = at.zi < proj_home, at.zi > proj_home
+    ends = (at.zi == 0) | (at.zi == 3)
+
+    def proj_pass(slot):
+        under, over = proj_below.at[slot], proj_above.at[slot]
+        wire.send(("pu", slot), proj_in.at[slot], under, up, below & ends)
+        wire.send(("pd", slot), proj_in.at[slot], over, down, above & ends)
 
         def climb():
-            wire.arrive("pu0", proj_below, down)
-            proj_add(proj_sum, proj_in, proj_below)
+            wire.arrive(("pu", slot), under, down)
+            proj_add(slot, proj_in, proj_below)
 
         def descend():
-            wire.arrive("pd0", proj_above, up)
-            proj_add(proj_sum, proj_in, proj_above)
+            wire.arrive(("pd", slot), over, up)
+            proj_add(slot, proj_in, proj_above)
 
         pl.when(below & (at.zi > 0))(climb)
         pl.when(above & (at.zi < 3))(descend)
-        wire.send("pu1", proj_sum, proj_below, up, below & (at.zi > 0), recv="pu0")
-        wire.send("pd1", proj_sum, proj_above, down, above & (at.zi < 3), recv="pd0")
+        source = proj_sum.at[slot]
+        key = "pu", slot
+        wire.send(("pu2", slot), source, under, up, below & (at.zi > 0), recv=key)
+        key = "pd", slot
+        wire.send(("pd2", slot), source, over, down, above & (at.zi < 3), recv=key)
 
     holder = at.zi * 2 + at.x
     chunk = at.y * 2 + at.c
@@ -874,23 +1017,24 @@
 
     def proj_last():
         home = at.zi == proj_home
-
-        def first():
-            wire.arrive("pu0", proj_below, down)
-            proj_add(proj_sum, proj_in, proj_below)
-
-        def only():
-            wire.arrive("pd0", proj_above, up)
-            proj_add(proj_sum, proj_in, proj_above)
-
-        def both():
-            wire.arrive("pd0", proj_above, up)
-            proj_add(proj_sum, proj_sum, proj_above)
-
-        pl.when(home & (at.zi > 0))(first)
-        pl.when(home & (at.zi == 0))(only)
-        pl.when(home & (at.zi > 0) & (at.zi < 3))(both)
         for slot in range(4):
+            under, over = proj_below.at[slot], proj_above.at[slot]
+
+            def first():
+                wire.arrive(("pu", slot), under, down)
+                proj_add(slot, proj_in, proj_below)
+
+            def only():
+                wire.arrive(("pd", slot), over, up)
+                proj_add(slot, proj_in, proj_above)
+
+            def both():
+                wire.arrive(("pd", slot), over, up)
+                proj_add(slot, proj_sum, proj_above)
+
+            pl.when(home & (at.zi > 0))(first)
+            pl.when(home & (at.zi == 0))(only)
+            pl.when(home & (at.zi > 0) & (at.zi < 3))(both)
             target = (at.zo, at.zi, lax.rem(at.rank, 2), slot // 2, slot % 2)
             other = (chunk != slot) | (at.rank != holder)
             wire.send(("o", slot), proj_sum.at[slot], proj_out, target, home & other, recv="o")
@@ -915,15 +1059,16 @@
 
     for piece in range(pieces):
         qkv_pass(3, piece)
-    proj_pass()
+        if piece == 0:
+            next(scatter)
+    for slot in range(4):
+        proj_pass(slot)
     next(scatter)
     small_second()
     for piece in range(pieces):
         qkv_pass(2, piece)
-    next(scatter)
     for _ in scatter:
         pass
-    proj_climb()
     for piece in range(pieces):
         qkv_pass(1, piece)
     proj_last()
@@ -1112,16 +1257,12 @@
     up_val = dot(normed_all, up_here)
     gelu_val, gelu_slope = gelu_parts(gate_val)
     active = low(gelu_val * up_val)
-    down_val = scatter_sum(low(contract_last(active, down_here)), UNIT_AXES)
-    second_sum = deep_alpha * normed.astype(jnp.float32) + down_val.astype(jnp.float32)
-    hat_two, inverse_two = norm_parts(second_sum)
-    layer_rows = low(hat_two * gain_two + shift_two)
-
-    grad_own = out_grad.reshape(own, width).astype(jnp.float32)
-    gain_two_grad = jnp.sum(grad_own * hat_two, axis=0)
-    shift_two_grad = jnp.sum(grad_own, axis=0)
-    d_second = norm_back(grad_own, hat_two, inverse_two, gain_two)
-    down_low = gather(low(d_second), UNIT_AXES)
+    down_part = low(contract_last(active, down_here)).reshape(unit_ways, own, width)
+    layer_rows, d_second, down_low, norm_grads = turn(
+        down_part, normed, out_grad.reshape(own, width), gain_two, shift_two
+    )
+    gain_two_grad, shift_two_grad = jnp.sum(norm_grads, axis=1)
+    down_low = down_low.reshape(-1, width)
     d_active = dot(down_low, down_here)
     gate_low = low(d_active * up_val * gelu_slope)
     up_low = low(d_active * gelu_val)

time: 780 us -> 720 us (0.923)
  the two profiles are of different devices: /device:TPU:6 before, /device:TPU:21 now
where the time goes in v5:
time: 720 us; the launch traced here: 710 us
  Pallas kernels  505 us (70%)
  matrix products  92.1 us (13%)
  local copies, waits for them, and re-layouts  41.2 us (6%)
  waiting for transfers between devices  39.1 us (5%)
  other arithmetic  17.2 us (2%)
  between operations  15.1 us (2%)
    pallas_call x1, Pallas kernels, gather_weights(): pl.pallas_call(gather_kernel, out_shape=(jax.ShapeDtypeStruct((4, 8, rows...  140 us
    pallas_call x1, Pallas kernels, close_units(): pl.pallas_call(close_units_kernel, out_shape=(jax.ShapeDtypeStruct((8, 3)...  123 us
    pallas_call x1, Pallas kernels, close_heads(): pl.pallas_call(close_heads_kernel, out_shape=(jax.ShapeDtypeStruct((8, ro...  116 us
    pallas_call x1, Pallas kernels, turn(): pl.pallas_call(turn_kernel, out_shape=(jax.ShapeDtypeStruct((own, width),...  84.4 us
    pallas_call x1, Pallas kernels, plane_scatter(): pl.pallas_call(plane_scatter_kernel, out_shape=jax.ShapeDtypeStruct((own,...  41.9 us
    all_gather x1, waiting for transfers between devices, gather(): return lax.all_gather(values, axes, axis=0, tiled=True)  39.1 us
    dot_general x5, matrix products, dot(): return jnp.dot(left_side, right_side, preferred_element_type=jnp.float32)  33.8 us
    dot_general x5, matrix products, contract_first(): lax.dot_general(left_side, right_side, (((0,), (0,)), ((), ())), preferre...  25.4 us
  transfers between devices with their start and end apart: 1, of which 1 were waited for; matrix products, arithmetic and copies ran while one was open for 1% of the time, Pallas kernels for 0%

profile of v5, /device:TPU:21, one launch (start us, length us, event | category | flops | bytes accessed | tf_op | source)
XLA Modules:
  0.0 710.0 jit_solution(2800294253847619472)
XLA Ops:
  7.2 1.8 fusion.19
  9.1 1.7 copy.134
  11.4 1.7 reshape.233.qkv_in
  14.1 140.3 %gather_weights.1 = (bf16[4,8,64,768]{3,2,1,0:T(8,128)(2,1)}, bf16[3,4,2,2,2,64,768]{6,5,4,3,2,1,0:T(8,128)(2,1)}, bf16[4,64,2048]{2,1,0:T(8,128)(2,1)}, bf16[8,128,2048]{2,1,0:T(8,128)(2,1)}, f32[4,8,8,128]{3,2,1,0:T(8,128)}) custom-call(bf16[8,64,768]{2,1,0:T(8,128)(2,1)} %reshape.233.qkv_in, bf16[8,3,64,768]{3,2,1,0:T(8,128)(2,1)} %bitcast.195, ...), custom_call_target="tpu_custom_call" | custom-call | bytes 400000000 | tf_op jit(solution)/shard_map/gather_weights/pallas_call | solution.py:378
  154.5 0.9 reshape_reshape.17
  156.1 6.2 convolution_bitcast_fusion
  162.6 2.8 reshape_reshape.16
  165.4 1.7 fusion.54
  167.2 1.6 slice.120
  169.4 3.0 fusion.43
  172.8 0.8 subtract_convert_fusion.3
  173.7 2.6 fusion.55
  176.2 2.7 fusion.23
  179.0 1.3 copy.78
  180.8 4.6 convolution_convert_fusion
  185.5 41.9 %plane_scatter_4.1 = f32[128,2048]{1,0:T(8,128)} custom-call(bf16[8,128,2048]{2,1,0:T(8,128)(2,1)} %bitcast.194), custom_call_target="tpu_custom_call" | custom-call | tf_op jit(solution)/shard_map/plane_scatter_4/pallas_call | solution.py:1144
  227.4 1.5 fusion.40
  229.0 1.5 multiply_reduce_fusion.1
  230.9 1.5 add_convert_fusion.4
  235.2 6.0 fusion.53
  241.2 39.1 %all-gather.2.cloned.1.call-done = bf16[1024,2048]{1,0:T(8,128)(2,1)} async-done(((bf16[128,2048]{1,0:T(8,128)(2,1)}), bf16[1024,2048]{1,0:T(8,128)(2,1)}) %all-gather.2.cloned.1.call-update) | async-done | bytes 4194320 | tf_op jit(solution)/shard_map/all_gather | solution.py:78
  280.2 6.3 fusion.56
  286.6 12.6 %multiply_convert_fusion.1 = (bf16[1024,768]{1,0:T(8,128)(2,1)S(1)}, f32[1024,768]{1,0:T(8,128)}, f32[1024,768]{1,0:T(8,128)}, f32[1024,768]{1,0:T(8,128)}) fusion(f32[1024,768]{1,0:T(8,128)S(1)} %fusion.56, bf16[1024,2048]{1,0:T(8,128)(2,1)S(1)} %copy-done.37, bf16[2048,768]{1,0:T(8,128)(2,1)S(1)} %bitcast.208), kind=kOutput, calls=%fused_computation.24 | convolution fusion | flops 3273129984 | bytes 21495808 | tf_op jit(solution)/shard_map/dot_general | solution.py:39
  299.2 5.1 convolution_convert_fusion.2
  304.3 84.4 %turn.1 = (bf16[128,2048]{1,0:T(8,128)(2,1)}, f32[128,2048]{1,0:T(8,128)}, bf16[8,128,2048]{2,1,0:T(8,128)(2,1)}, f32[2,8,2048]{2,1,0:T(8,128)}) custom-call(bf16[8,128,2048]{2,1,0:T(8,128)(2,1)} %bitcast.203, bf16[128,2048]{1,0:T(8,128)(2,1)} %get-tuple-element.85.normed, bf16[128,2048]{1,0:T(8,128)(2,1)} %bitcast.233, f32[1,2048]{1,0:T(1,128)} %unstack.29.gain, ...), custom_call_target="tpu_custom_call" | custom-call | tf_op jit(solution)/shard_map/turn/pallas_call | solution.py:668
  388.7 8.0 %convolution_convert_fusion.4 = bf16[2048,768]{1,0:T(8,128)(2,1)} fusion(bf16[1024,2048]{1,0:T(8,128)(2,1)} %bitcast.249, bf16[1024,768]{1,0:T(8,128)(2,1)} %copy-done.46), kind=kOutput, calls=%fused_computation.12 | convolution fusion | flops 3222798336 | bytes 8912896 | tf_op jit(solution)/shard_map/dot_general | solution.py:33
  396.8 1.5 copy-done.45
  398.3 4.0 multiply_convert_fusion
  402.4 3.4 fusion.57
  405.8 5.1 add_convert_fusion
  411.0 5.0 convolution_convert_fusion.5
  415.9 5.0 convolution_convert_fusion.6
  420.9 122.9 %close_units.1 = (bf16[8,3,64,768]{3,2,1,0:T(8,128)(2,1)}, bf16[8,128,2048]{2,1,0:T(8,128)(2,1)}, f32[128,2048]{1,0:T(8,128)}, f32[2,8,2048]{2,1,0:T(8,128)}) custom-call(bf16[4,2,2,2,64,768]{5,4,3,2,1,0:T(8,128)(2,1)} %bitcast.216, bf16[4,2,2,2,64,768]{5,4,3,2,1,0:T(8,128)(2,1)} %bitcast.215, bf16[4,2,2,2,64,768]{5,4,3,2,1,0:T(8,128)(2,1)} %bitcast.212, ...), custom_call_target="tpu_custom_call" | custom-call | tf_op jit(solution)/shard_map/close_units/pallas_call | solution.py:841
  543.8 3.8 convolution_convert_fusion.10
  548.2 1.0 copy-done.21
  549.2 1.5 multiply_reduce_fusion
  554.2 1.3 copy-done.39
  555.6 2.2 convolution_convert_fusion.7
  559.4 1.6 copy.93
  563.1 7.0 convolution_convert_fusion.1
  570.1 5.2 convolution_convert_fusion.3
  575.2 115.7 %close_heads.1 = (bf16[8,64,768]{2,1,0:T(8,128)(2,1)}, bf16[64,2048]{1,0:T(8,128)(2,1)}, f32[8,128]{1,0:T(8,128)}, f32[128,2048]{1,0:T(8,128)}) custom-call(bf16[4,8,64,768]{3,2,1,0:T(8,128)(2,1)} %bitcast.218, bf16[4,64,2048]{2,1,0:T(8,128)(2,1)} %bitcast.228, f32[8,4,8,128]{3,2,1,0:T(8,128)} %pad.14.small_in, bf16[8,128,2048]{2,1,0:T(8,128)(2,1)} %bitcast.205), custom_call_target="tpu_custom_call" | custom-call | tf_op jit(solution)/shard_map/close_heads/pallas_call | solution.py:1099
  691.0 2.5 reshape.269
  693.5 0.9 copy.96
  694.4 1.6 copy.119
  696.0 0.8 convert_element_type.158
  698.5 2.2 fusion.28
  701.2 0.9 add_convert_fusion.1
  (152 shorter events, 17.9 us)
Async XLA Ops:
  7.2 273.1 %all-gather.2.cloned.1.call-start = ((), (), s32[]{:S(2)}) async-start(), calls=%async_computation | async-start | bytes 4718592 | tf_op jit(solution)/shard_map/all_gather | solution.py:78
  9.0 1.7 copy-start.24
  10.8 2.3 copy-start.31
  10.8 2.6 copy-start.32
  10.8 2.6 copy-start.33
  10.8 2.6 copy-start.34
  10.8 2.6 copy-start.35
  165.4 3.3 copy-start.27
  169.2 7.1 copy-start.25
  172.4 1.3 copy-start.2
  173.6 5.3 copy-start.13
  173.7 5.3 copy-start.15
  173.7 5.3 copy-start.17
  173.7 5.3 copy-start.19
  180.8 4.6 copy-start.4
  185.5 41.9 %copy-start.1 = (bf16[2,1,64,2048]{3,2,1,0:T(8,128)(2,1)S(1)}, bf16[2,1,64,2048]{3,2,1,0:T(8,128)(2,1)}, u32[]{:S(2)}) copy-start(bf16[2,1,64,2048]{3,2,1,0:T(8,128)(2,1)} %param.12) | copy-start | bytes 1572868
  227.4 3.5 copy-start
  241.2 45.4 %copy-start.6 = (bf16[1,4,2,2,2,64,768]{6,5,4,3,2,1,0:T(8,128)(2,1)}, bf16[1,4,2,2,2,64,768]{6,5,4,3,2,1,0:T(8,128)(2,1)S(1)}, u32[]{:S(2)}) copy-start(bf16[1,4,2,2,2,64,768]{6,5,4,3,2,1,0:T(8,128)(2,1)S(1)} %get-tuple-element.88) | copy-start | bytes 9437188
  280.2 6.3 copy-start.37
  286.5 12.7 %copy-start.41 = (f32[1024,768]{1,0:T(8,128)}, f32[1024,768]{1,0:T(8,128)S(1)}, u32[]{:S(2)}) copy-start(f32[1024,768]{1,0:T(8,128)S(1)} %fusion.56) | copy-start | bytes 9437188
  286.6 12.6 %copy-start.9 = (bf16[1,4,2,2,2,64,768]{6,5,4,3,2,1,0:T(8,128)(2,1)S(1)}, bf16[1,4,2,2,2,64,768]{6,5,4,3,2,1,0:T(8,128)(2,1)}, u32[]{:S(2)}) copy-start(bf16[1,4,2,2,2,64,768]{6,5,4,3,2,1,0:T(8,128)(2,1)} %get-tuple-element.87) | copy-start | bytes 9437188
  299.2 5.1 copy-start.46
  388.7 8.1 %copy-start.10 = (bf16[1,4,2,2,2,64,768]{6,5,4,3,2,1,0:T(8,128)(2,1)S(1)}, bf16[1,4,2,2,2,64,768]{6,5,4,3,2,1,0:T(8,128)(2,1)}, u32[]{:S(2)}) copy-start(bf16[1,4,2,2,2,64,768]{6,5,4,3,2,1,0:T(8,128)(2,1)} %get-tuple-element.87) | copy-start | bytes 9437188
  388.7 8.1 %copy-start.40 = (bf16[8,128,2048]{2,1,0:T(8,128)(2,1)S(1)}, bf16[8,128,2048]{2,1,0:T(8,128)(2,1)}, u32[]{:S(2)}) copy-start(bf16[8,128,2048]{2,1,0:T(8,128)(2,1)} %get-tuple-element.34) | copy-start | bytes 12582916
  388.7 8.1 %copy-start.42 = (f32[1024,768]{1,0:T(8,128)S(1)}, f32[1024,768]{1,0:T(8,128)}, u32[]{:S(2)}) copy-start(f32[1024,768]{1,0:T(8,128)} %copy-done.41) | copy-start | bytes 9437188
  388.7 8.1 %copy-start.43 = (f32[1024,768]{1,0:T(8,128)S(1)}, f32[1024,768]{1,0:T(8,128)}, u32[]{:S(2)}) copy-start(f32[1024,768]{1,0:T(8,128)} %get-tuple-element.83) | copy-start | bytes 9437188
  388.7 8.1 %copy-start.44 = (f32[1024,768]{1,0:T(8,128)S(1)}, f32[1024,768]{1,0:T(8,128)}, u32[]{:S(2)}) copy-start(f32[1024,768]{1,0:T(8,128)} %get-tuple-element.84) | copy-start | bytes 9437188
  388.7 9.5 %copy-start.45 = (f32[1024,768]{1,0:T(8,128)S(1)}, f32[1024,768]{1,0:T(8,128)}, u32[]{:S(2)}) copy-start(f32[1024,768]{1,0:T(8,128)} %get-tuple-element.123) | copy-start | bytes 9437188
  398.3 4.1 copy-start.8
  402.3 3.5 copy-start.7
  405.8 5.1 copy-start.38
  547.6 1.6 copy-start.21
  550.7 1.0 copy-start.18
  550.7 1.2 copy-start.20
  550.8 1.7 copy-start.14
  550.8 1.7 copy-start.16
  553.2 1.0 copy-start.5
  553.2 2.4 copy-start.39
  555.6 2.3 copy-start.3
  555.6 2.3 copy-start.12
  561.0 0.9 copy-start.30
  561.1 1.0 copy-start.29
  563.1 7.0 copy-start.36
  693.5 2.6 copy-start.28
  694.4 3.8 copy-start.11
  698.5 2.3 copy-start.22
  698.5 2.8 copy-start.23
  698.5 3.7 copy-start.26
Sparse Core Ops, SparseCore 0:
  232.6 47.6 all-gather.1

commit v6 on v5

--- a/solution.py
+++ b/solution.py
@@ -161,6 +161,13 @@
         self.rank = self.x * 4 + self.y * 2 + self.c
         self.unit = self.zi * 2 + self.c
 
+    def head_home(self):
+        return self.y + self.c * (3 - 2 * self.y)
+
+    def holder(self):
+        y, c = lax.rem((self.zi + 1) // 2, 2), self.zi // 2
+        return (self.zo, self.zi, self.x, y, c), self.x * 4 + y * 2 + c
+
     def plane(self, delta):
         dx, dy, dc = delta >> 2 & 1, delta >> 1 & 1, delta & 1
         x, y, c = flip(self.x, dx), flip(self.y, dy), flip(self.c, dc)
@@ -191,7 +198,53 @@
         return plane + column
 
 
-def gather_kernel(
+def unit_gather_flow(at, wire, ffn_in, ffn_out, own_sem):
+    x_side, y_side = at.plane(4)[0], at.plane(2)[0]
+    steps = (1, 7, 2, 6, 3, 5, 4)
+    mine = ffn_out.at[:, at.zi, at.x, at.y, at.c]
+    own = pltpu.make_async_copy(ffn_in.at[at.unit], mine, own_sem)
+    own.start()
+    for step in (4, 3, 5, 2, 6, 1, 7):
+        device, other = at.column(step)
+        wire.send(("f", step), ffn_in.at[other], mine, device)
+    own.wait()
+
+    def slot(step, x, y):
+        source = lax.rem(at.unit - step + 8, 8)
+        return ffn_out.at[:, source // 2, x, y, lax.rem(source, 2)]
+
+    def first(step):
+        here = slot(step, at.x, at.y)
+        if step:
+            wire.arrive(("f", step), here, at.column(-step)[0])
+        wire.send(("fx", step), here, here, x_side)
+        wire.send(("fy", step), here, here, y_side)
+
+    def second(step, turn):
+        from_x, from_y = slot(step, 1 - at.x, at.y), slot(step, at.x, 1 - at.y)
+        wire.arrive(("fx", step), from_x, x_side)
+        wire.arrive(("fy", step), from_y, y_side)
+        if turn % 2:
+            wire.send(("fd", step), from_x, from_x, y_side)
+        else:
+            wire.send(("fd", step), from_y, from_y, x_side)
+
+    yield
+    first(0)
+    for turn, step in enumerate(steps):
+        yield
+        first(step)
+        if turn >= 1:
+            second(((0,) + steps)[turn - 1], turn - 1)
+    yield
+    second(steps[5], 6)
+    second(steps[6], 7)
+    yield
+    for step in (0,) + steps:
+        wire.arrive(("fd", step), slot(step, 1 - at.x, 1 - at.y), x_side)
+
+
+def open_heads_kernel(
     qkv_in,
     ffn_in,
     proj_in,
@@ -209,50 +262,30 @@
     at = Place()
     wire = Wire(send_sems, recv_sems)
     enter(at.neighbours())
-    x_side, y_side, core_side = at.plane(4)[0], at.plane(2)[0], at.plane(1)[0]
-    half = x_in.shape[0] // 2
-
+    up, down = at.ends()
+    chunk = at.y * 2 + at.c
+    holder_device, holder = at.holder()
+    proj_home = at.head_home()
     own = [
-        pltpu.make_async_copy(x_in, x_out.at[at.rank], own_sems.at[0]),
         pltpu.make_async_copy(qkv_in.at[at.rank], qkv_out.at[at.zi, at.rank], own_sems.at[1]),
-        pltpu.make_async_copy(
-            ffn_in.at[at.unit], ffn_out.at[:, at.zi, at.x, at.y, at.c], own_sems.at[2]
-        ),
         pltpu.make_async_copy(small_in, small_out.at[at.zi, at.rank], own_sems.at[3]),
     ]
     for copy in own:
         copy.start()
-
-    chunk = at.y * 2 + at.c
-    holder = at.zi * 2 + at.x
-    proj_home = at.rank // 2
-    proj_first = at.rank == holder
-    proj_own = pltpu.make_async_copy(proj_in, proj_out.at[chunk], own_sems.at[4])
-    pl.when(proj_first)(proj_own.start)
-
-    def small_first():
-        for delta in range(1, 8):
-            device, _ = at.plane(delta)
-            slot = small_out.at[at.zi, at.rank]
-            wire.send(("s", delta), small_in, slot, device)
-
-    small_first()
-
-    for step in (1, 7, 2, 6, 3, 5, 4):
-        device, other = at.column(step)
-        slot = ffn_out.at[:, at.zi, at.x, at.y, at.c]
-        wire.send(("f", step), ffn_in.at[other], slot, device)
     for delta in range(1, 8):
         device, other = at.plane(delta)
         wire.send(("q", delta), qkv_in.at[other], qkv_out.at[at.zi, at.rank], device)
-    holder_device = (at.zo, at.zi, holder // 4, lax.rem(holder // 2, 2), lax.rem(holder, 2))
     wire.send_to_slot("p", proj_in, proj_out.at[chunk], holder_device, chunk, 4, at.rank != holder)
-    wire.send("xx", x_in, x_out.at[at.rank], x_side)
-    wire.send("xy", x_in, x_out.at[at.rank], y_side)
-    wire.send("xc0", x_in, x_out.at[at.rank], core_side)
+    proj_own = pltpu.make_async_copy(proj_in, proj_out.at[chunk], own_sems.at[4])
+    pl.when(at.rank == holder)(proj_own.start)
+    for delta in range(1, 8):
+        device, _ = at.plane(delta)
+        wire.send(("s", delta), small_in, small_out.at[at.zi, at.rank], device)
+    spread = plane_gather_flow(at, wire, x_in, x_out, own_sems.at[0])
+    next(spread)
     for copy in own:
         copy.wait()
-    pl.when(proj_first)(proj_own.wait)
+    pl.when(at.rank == holder)(proj_own.wait)
 
     def small_second():
         for delta in range(1, 8):
@@ -267,25 +300,27 @@
             z = lax.rem(at.zi - dz + 4, 4)
             wire.arrive(("t", dz), small_out.at[z], at.line(z))
 
-    def proj_start():
-        for slot in range(4):
-            source = (at.zo, at.zi, lax.rem(at.rank, 2), slot // 2, slot % 2)
-            mine = (at.zi == proj_home) & ((chunk != slot) | (at.rank != holder))
-            wire.arrive_slot("p", proj_out.at[slot], source, slot, 4, mine)
-        wire.send("pu0", proj_out, proj_out, up, (at.zi == proj_home) & (at.zi < 3))
-        wire.send("pd0", proj_out, proj_out, down, (at.zi == proj_home) & (at.zi > 0))
-
-    def proj_relay():
+    def proj_start(slot):
+        block = proj_out.at[slot]
+        source = (at.zo, at.zi, at.x, slot // 2, slot % 2)
+        home = at.zi == proj_home
+        mine = home & ((chunk != slot) | (at.rank != holder))
+        wire.arrive_slot("p", block, source, slot, 4, mine)
+        wire.send(("pu", slot), block, block, up, home & (at.zi < 3))
+        wire.send(("pd", slot), block, block, down, home & (at.zi > 0))
+
+    def proj_relay(slot):
+        block = proj_out.at[slot]
         above, below = at.zi > proj_home, at.zi < proj_home
-        wire.arrive("pu0", proj_out, down, above)
-        wire.arrive("pd0", proj_out, up, below)
-        wire.send("pu1", proj_out, proj_out, up, above & (at.zi < 3), recv="pu0")
-        wire.send("pd1", proj_out, proj_out, down, below & (at.zi > 0), recv="pd0")
+        wire.arrive(("pu", slot), block, down, above)
+        wire.arrive(("pd", slot), block, up, below)
+        key = "pu", slot
+        wire.send(("pu2", slot), block, block, up, above & (at.zi < 3), recv=key)
+        key = "pd", slot
+        wire.send(("pd2", slot), block, block, down, below & (at.zi > 0), recv=key)
 
     def qkv_slot(z, delta):
         return qkv_out.at[jnp.clip(z, 0, 3), at.plane(delta)[1]]
-
-    up, down = at.line(jnp.minimum(at.zi + 1, 3)), at.line(jnp.maximum(at.zi - 1, 0))
 
     def qkv_hop(hop, delta):
         below, above = qkv_slot(at.zi - hop, delta), qkv_slot(at.zi + hop, delta)
@@ -299,64 +334,91 @@
             wire.send(("up", hop, delta), below, below, up, (at.zi >= hop) & (at.zi < 3))
             wire.send(("down", hop, delta), above, above, down, (at.zi <= 3 - hop) & (at.zi > 0))
 
-    def ffn_slot(step, x, y):
-        source = lax.rem(at.unit - step + 8, 8)
-        return ffn_out.at[:, source // 2, x, y, lax.rem(source, 2)]
-
-    def ffn_first(step):
-        slot = ffn_slot(step, at.x, at.y)
-        if step:
-            wire.arrive(("f", step), slot, at.column(-step)[0])
-        wire.send(("fx", step), slot, slot, x_side)
-        wire.send(("fy", step), slot, slot, y_side)
-
-    def ffn_second(step, turn):
-        from_x, from_y = ffn_slot(step, 1 - at.x, at.y), ffn_slot(step, at.x, 1 - at.y)
-        wire.arrive(("fx", step), from_x, x_side)
-        wire.arrive(("fy", step), from_y, y_side)
-        if turn % 2:
-            wire.send(("fd", step), from_x, from_x, y_side)
-        else:
-            wire.send(("fd", step), from_y, from_y, x_side)
-
-    from_x, from_y, from_xy = (at.plane(delta)[1] for delta in (4, 2, 6))
-    low_half, high_half = pl.ds(0, half), pl.ds(half, half)
-    ffn_first(0)
-    wire.arrive("xx", x_out.at[from_x], x_side)
-    wire.send("xd0", x_out.at[from_x, low_half], x_out.at[from_x, low_half], y_side)
-    wire.send("xc1", x_out.at[from_x], x_out.at[from_x], core_side)
-    wire.arrive("xy", x_out.at[from_y], y_side)
-    wire.send("xd1", x_out.at[from_y, high_half], x_out.at[from_y, high_half], x_side)
-    wire.send("xc2", x_out.at[from_y], x_out.at[from_y], core_side)
-    small_second()
     for delta in range(8):
         qkv_hop(0, delta)
-    proj_start()
-    wire.arrive("xd0", x_out.at[from_xy, low_half], y_side)
-    wire.arrive("xd1", x_out.at[from_xy, high_half], x_side)
-    wire.send("xc3", x_out.at[from_xy], x_out.at[from_xy], core_side)
-
-    steps = (1, 7, 2, 6, 3, 5, 4)
-    ffn_second(0, 0)
-    for turn, step in enumerate(steps):
-        ffn_first(step)
-        qkv_hop(1, turn)
-        if turn >= 2:
-            ffn_second(steps[turn - 2], turn - 2 + 1)
-    qkv_hop(1, 7)
-    proj_relay()
+    units = unit_gather_flow(at, wire, ffn_in, ffn_out, own_sems.at[2])
+    for slot in range(4):
+        proj_start(slot)
+    next(units)
+    next(spread)
+    small_second()
+    next(units)
+    for _ in spread:
+        pass
+    for delta in range(8):
+        qkv_hop(1, delta)
+        if delta % 2:
+            proj_relay(delta // 2)
+            next(units)
     for delta in range(8):
         qkv_hop(2, delta)
-        if delta < 2:
-            ffn_second(steps[5 + delta], 5 + delta + 1)
+        if delta % 2:
+            next(units)
     for delta in range(8):
         qkv_hop(3, delta)
-    for index, delta in enumerate((1, 5, 3, 7)):
-        other = at.plane(delta)[1]
-        wire.arrive("xc%d" % index, x_out.at[other], core_side)
-    for step in range(8):
-        wire.arrive(("fd", step), ffn_slot(step, 1 - at.x, 1 - at.y), x_side)
+    for _ in units:
+        pass
     small_last()
+    wire.drain()
+
+
+def open_units_kernel(
+    part,
+    x_own,
+    gain,
+    shift,
+    ffn_in,
+    normed,
+    hat,
+    inverse_out,
+    normed_all,
+    ffn_out,
+    branch,
+    *rest,
+):
+    at = Place()
+    *scratch, send_sems, recv_sems, own_sems = rest
+    wire = Wire(send_sems, recv_sems)
+    enter(at.neighbours())
+
+    def norm_rows():
+        count = 16
+
+        @pl.loop(0, x_own.shape[0] // count)
+        def _(index):
+            rows = pl.ds(pl.multiple_of(index * count, count), count)
+            whole = deep_alpha * x_own[rows].astype(jnp.float32) + branch[rows]
+            near, inverse = norm_parts(whole)
+            hat[rows] = near
+            inverse_out[rows] = jnp.broadcast_to(inverse, (count, LANES))
+            normed[rows] = (near * gain[...] + shift[...]).astype(jnp.bfloat16)
+
+    scatter = plane_scatter_flow(at, wire, part, branch, *scratch)
+    units = unit_gather_flow(at, wire, ffn_in, ffn_out, own_sems.at[0])
+    next(scatter)
+    next(units)
+    next(scatter)
+    next(scatter)
+    next(units)
+    for _ in scatter:
+        pass
+    norm_rows()
+    spread = column_gather_flow(at, wire, 0, normed, normed_all, own_sems.at[1])
+    next(spread)
+    next(units)
+    next(units)
+    next(spread)
+    next(units)
+    next(units)
+    next(spread)
+    next(units)
+    next(units)
+    next(spread)
+    next(units)
+    for _ in spread:
+        pass
+    for _ in units:
+        pass
     wire.drain()
 
 
@@ -370,16 +432,16 @@
     )
 
 
-def gather_weights(qkv_parts, ffn_parts, proj_own, x_own, small):
+def open_heads(qkv_parts, ffn_parts, proj_own, x_own, small):
     _, rows_own, qkv_width = qkv_parts.shape
-    unit_width = ffn_parts.shape[-1]
+    _, matrices, _, unit_width = ffn_parts.shape
     own, width = x_own.shape
     low_type = jnp.bfloat16
     return pl.pallas_call(
-        gather_kernel,
+        open_heads_kernel,
         out_shape=(
             jax.ShapeDtypeStruct((4, 8, rows_own, qkv_width), low_type),
-            jax.ShapeDtypeStruct((3, 4, 2, 2, 2, rows_own, unit_width), low_type),
+            jax.ShapeDtypeStruct((matrices, 4, 2, 2, 2, rows_own, unit_width), low_type),
             jax.ShapeDtypeStruct((4, rows_own, width), low_type),
             jax.ShapeDtypeStruct((8, own, width), low_type),
             jax.ShapeDtypeStruct((4, 8) + small.shape, small.dtype),
@@ -387,16 +449,40 @@
         in_specs=[VMEM] * 5,
         out_specs=(ANY,) * 5,
         scratch_shapes=[
-            pltpu.SemaphoreType.DMA((128,)),
-            pltpu.SemaphoreType.DMA((128,)),
+            pltpu.SemaphoreType.DMA((136,)),
+            pltpu.SemaphoreType.DMA((136,)),
             pltpu.SemaphoreType.DMA((5,)),
         ],
         compiler_params=comm_params(1),
-        cost_estimate=pl.CostEstimate(
-            flops=0, bytes_accessed=400_000_000, transcendentals=0
+        name="open_heads",
+    )(qkv_parts, ffn_parts, proj_own, x_own, small)
+
+
+def open_units(part, x_own, gain, shift, ffn_parts):
+    _, matrices, rows_own, unit_width = ffn_parts.shape
+    own, width = x_own.shape
+    low_type = jnp.bfloat16
+    return pl.pallas_call(
+        open_units_kernel,
+        out_shape=(
+            jax.ShapeDtypeStruct((own, width), low_type),
+            jax.ShapeDtypeStruct((own, width), jnp.float32),
+            jax.ShapeDtypeStruct((own, LANES), jnp.float32),
+            jax.ShapeDtypeStruct((8, own, width), low_type),
+            jax.ShapeDtypeStruct((matrices, 4, 2, 2, 2, rows_own, unit_width), low_type),
         ),
-        name="gather_weights",
-    )(qkv_parts, ffn_parts, proj_own, x_own, small)
+        in_specs=[VMEM] * 5,
+        out_specs=(VMEM, VMEM, VMEM, ANY, ANY),
+        scratch_shapes=[pltpu.VMEM((own, width), jnp.float32)]
+        + plane_scratch(own, width)
+        + [
+            pltpu.SemaphoreType.DMA((64,)),
+            pltpu.SemaphoreType.DMA((64,)),
+            pltpu.SemaphoreType.DMA((2,)),
+        ],
+        compiler_params=comm_params(4),
+        name="open_units",
+    )(part, x_own, gain, shift, ffn_parts)
 
 
 def add_rows(out, *terms):
@@ -783,7 +869,7 @@
             rows = pl.ds(pl.multiple_of(index * count, count), count)
             cotangent = deep_alpha * d_second[rows] + d_normed[rows]
             near = hat[rows]
-            result = norm_back(cotangent, near, inverse[rows], gain[...])
+            result = norm_back(cotangent, near, inverse[rows, :1], gain[...])
             d_first[rows] = result
             branch_low[rows] = result.astype(jnp.bfloat16)
             along = cotangent * near
@@ -982,7 +1068,7 @@
                 at.zi > back,
             )
 
-    proj_home = at.rank // 2
+    proj_home = at.head_home()
 
     def proj_add(slot, *terms):
         add_rows(proj_sum.at[slot], *(term.at[slot] for term in terms))
@@ -1011,9 +1097,8 @@
         key = "pd", slot
         wire.send(("pd2", slot), source, over, down, above & (at.zi < 3), recv=key)
 
-    holder = at.zi * 2 + at.x
     chunk = at.y * 2 + at.c
-    holder_device = (at.zo, at.zi, holder // 4, lax.rem(holder // 2, 2), lax.rem(holder, 2))
+    holder_device, holder = at.holder()
 
     def proj_last():
         home = at.zi == proj_home
@@ -1035,7 +1120,7 @@
             pl.when(home & (at.zi > 0))(first)
             pl.when(home & (at.zi == 0))(only)
             pl.when(home & (at.zi > 0) & (at.zi < 3))(both)
-            target = (at.zo, at.zi, lax.rem(at.rank, 2), slot // 2, slot % 2)
+            target = (at.zo, at.zi, at.x, slot // 2, slot % 2)
             other = (chunk != slot) | (at.rank != holder)
             wire.send(("o", slot), proj_sum.at[slot], proj_out, target, home & other, recv="o")
         own = pltpu.make_async_copy(proj_sum.at[chunk], proj_out, own_sems.at[2])
@@ -1130,29 +1215,6 @@
     )(qkv_part, proj_part, small_part, part)
 
 
-def plane_scatter_kernel(part, out, *rest):
-    at = Place()
-    wire = Wire(*rest[-2:])
-    enter([at.plane(delta)[0] for delta in (4, 2, 1)])
-    for _ in plane_scatter_flow(at, wire, part, out, *rest[:-2]):
-        pass
-    wire.drain()
-
-
-def plane_scatter(part, number):
-    _, own, width = part.shape
-    return pl.pallas_call(
-        plane_scatter_kernel,
-        out_shape=jax.ShapeDtypeStruct((own, width), jnp.float32),
-        in_specs=[VMEM],
-        out_specs=VMEM,
-        scratch_shapes=plane_scratch(own, width)
-        + [pltpu.SemaphoreType.DMA((16,)), pltpu.SemaphoreType.DMA((16,))],
-        compiler_params=comm_params(number),
-        name="plane_scatter_%d" % number,
-    )(part)
-
-
 def group_body(
     hidden_in,
     token_marks,
@@ -1187,23 +1249,23 @@
     small = jnp.concatenate([params.astype(jnp.float32).ravel(), marks_own.ravel()])
     small = jnp.pad(small, (0, -small.size % (8 * LANES))).reshape(-1, LANES)
 
-    qkv_parts = (
-        qkv_weight.reshape(rows_own, 3, head_ways, head_width)
-        .transpose(2, 0, 1, 3)
-        .reshape(head_ways, rows_own, 3 * head_width)
-    )
-    ffn = jnp.stack([gate_weight, up_weight, down_weight])
-    ffn = jnp.pad(ffn, ((0, 0), (0, 0), (0, unit_pad)))
-    ffn = ffn.reshape(3, rows_own, unit_ways, unit_width).transpose(2, 0, 1, 3)
-
-    qkv_here, ffn, proj_here, x_all, small = gather_weights(
-        qkv_parts, ffn, proj_weight, x_own, small
+    qkv_parts = qkv_weight.reshape(rows_own, 3, 4, 2, head_width)
+    qkv_parts = jnp.stack([qkv_parts[:, :, home] for home in (0, 3, 1, 2)])
+    qkv_parts = qkv_parts.transpose(3, 0, 1, 2, 4).reshape(head_ways, rows_own, 3 * head_width)
+
+    def unit_parts(*matrices):
+        parts = jnp.stack(matrices)
+        parts = jnp.pad(parts, ((0, 0), (0, 0), (0, unit_pad)))
+        parts = parts.reshape(len(matrices), rows_own, unit_ways, unit_width)
+        return parts.transpose(2, 0, 1, 3)
+
+    qkv_here, gate_here, proj_here, x_all, small = open_heads(
+        qkv_parts, unit_parts(gate_weight), proj_weight, x_own, small
     )
     qkv_here = qkv_here.reshape(-1, 3 * head_width)
-    ffn = ffn.reshape(3, -1, unit_width)
+    gate_here = gate_here.reshape(-1, unit_width)
     x_all = x_all.reshape(-1, width)
     proj_here = proj_here.reshape(head_width, width)
-    gate_here, up_here, down_here = ffn[0], ffn[1], ffn[2]
     small = small.reshape(unit_ways * 4, -1)
     params = small[:, : 4 * rows_own].reshape(-1, 4, rows_own).transpose(1, 0, 2)
     gain_one, shift_one, gain_two, shift_two = params.reshape(4, 1, width)
@@ -1247,12 +1309,13 @@
     context = low(pair("rhqk,rkhd->rqhd", probs_low, value_rows))
 
     context = from_rows(context).reshape(-1, head_width)
-    branch = plane_scatter(low(dot(context, proj_here)).reshape(head_ways, own, width), 4)
-    first_sum = deep_alpha * x_own.astype(jnp.float32) + branch
-    hat_one, inverse_one = norm_parts(first_sum)
-    normed = low(hat_one * gain_one + shift_one)
-
-    normed_all = gather(normed, UNIT_AXES)
+    branch_part = low(dot(context, proj_here)).reshape(head_ways, own, width)
+    normed, hat_one, inverse_one, normed_all, ffn = open_units(
+        branch_part, x_own, gain_one, shift_one, unit_parts(up_weight, down_weight)
+    )
+    normed_all = normed_all.reshape(-1, width)
+    up_here, down_here = ffn.reshape(2, -1, unit_width)
+
     gate_val = dot(normed_all, gate_here)
     up_val = dot(normed_all, up_here)
     gelu_val, gelu_slope = gelu_parts(gate_val)
@@ -1313,12 +1376,9 @@
     )
     d_input = deep_alpha * d_first + d_input
     small_grads = small_grads.ravel()[: 4 * rows_own].reshape(4, rows_own)
-    qkv_grad = (
-        qkv_part.reshape(head_ways, rows_own, 3, head_width)
-        .transpose(1, 2, 0, 3)
-        .reshape(rows_own, 3 * width)
-        .astype(jnp.float32)
-    )
+    qkv_grad = qkv_part.reshape(2, 4, rows_own, 3, head_width)
+    qkv_grad = jnp.stack([qkv_grad[:, place] for place in (0, 2, 3, 1)])
+    qkv_grad = qkv_grad.transpose(2, 3, 0, 1, 4).reshape(rows_own, 3 * width).astype(jnp.float32)
     ffn_part = ffn_part.transpose(1, 2, 0, 3).reshape(3, rows_own, unit_ways * unit_width)
     gate_grad, up_grad, down_grad = (
         ffn_part[index, :, :units].astype(jnp.float32) for index in range(3)

time: 720 us -> 687 us (0.954)
  the two profiles are of different devices: /device:TPU:21 before, /device:TPU:11 now
where the time goes in v6:
time: 687 us; the launch traced here: 677 us
  Pallas kernels  507 us (74%)
  matrix products  100 us (15%)
  local copies, waits for them, and re-layouts  50.6 us (7%)
  other arithmetic  16.8 us (2%)
    pallas_call x1, Pallas kernels, close_units(): pl.pallas_call(close_units_kernel, out_shape=(jax.ShapeDtypeStruct((8, 3)...  126 us
    pallas_call x1, Pallas kernels, open_units(): pl.pallas_call(open_units_kernel, out_shape=(jax.ShapeDtypeStruct((own, w...  103 us
    pallas_call x1, Pallas kernels, close_heads(): pl.pallas_call(close_heads_kernel, out_shape=(jax.ShapeDtypeStruct((8, ro...  96.1 us
    pallas_call x1, Pallas kernels, turn(): pl.pallas_call(turn_kernel, out_shape=(jax.ShapeDtypeStruct((own, width),...  93.3 us
    pallas_call x1, Pallas kernels, open_heads(): pl.pallas_call(open_heads_kernel, out_shape=(jax.ShapeDtypeStruct((4, 8,...  89.1 us
    dot_general x5, matrix products, dot(): return jnp.dot(left_side, right_side, preferred_element_type=jnp.float32)  41.5 us
    dot_general x5, matrix products, contract_first(): lax.dot_general(left_side, right_side, (((0,), (0,)), ((), ())), preferre...  27.5 us
    dot_general x5, matrix products, contract_last(): lax.dot_general(left_side, right_side, (((1,), (1,)), ((), ())), preferre...  22.5 us

profile of v6, /device:TPU:11, one launch (start us, length us, event | category | flops | bytes accessed | tf_op | source)
XLA Modules:
  0.0 676.9 jit_solution(10110489311104549226)
XLA Ops:
  3.1 2.6 reshape.211
  6.7 0.9 maximum_bitcast_fusion
  7.7 1.7 reshape.212.qkv_in
  9.4 0.9 copy.164
  10.5 1.3 copy.161
  11.8 89.1 %open_heads.1 = (bf16[4,8,64,768]{3,2,1,0:T(8,128)(2,1)}, bf16[1,4,2,2,2,64,768]{6,5,4,3,2,1,0:T(8,128)(2,1)}, bf16[4,64,2048]{2,1,0:T(8,128)(2,1)}, bf16[8,128,2048]{2,1,0:T(8,128)(2,1)}, f32[4,8,8,128]{3,2,1,0:T(8,128)}) custom-call(bf16[8,64,768]{2,1,0:T(8,128)(2,1)} %reshape.212.qkv_in, bf16[8,1,64,768]{3,2,1,0:T(8,128)(2,1)} %bitcast.229, ...), custom_call_target="tpu_custom_call" | custom-call | tf_op jit(solution)/shard_map/open_heads/pallas_call | solution.py:440
  101.9 0.9 reshape_reshape.17
  107.0 3.1 fusion.40
  110.1 6.2 convolution_bitcast_fusion
  116.6 2.8 reshape_reshape.16
  119.4 2.4 slice.143
  121.7 1.7 fusion.50
  123.5 2.2 copy.137
  127.6 2.5 fusion.52
  130.0 2.9 fusion.21
  132.9 2.0 copy.92
  135.0 1.6 copy.93
  136.6 4.7 convolution_convert_fusion
  141.2 102.6 %open_units.1 = (bf16[128,2048]{1,0:T(8,128)(2,1)}, f32[128,2048]{1,0:T(8,128)}, f32[128,128]{1,0:T(8,128)}, bf16[8,128,2048]{2,1,0:T(8,128)(2,1)}, bf16[2,4,2,2,2,64,768]{6,5,4,3,2,1,0:T(8,128)(2,1)}) custom-call(bf16[8,128,2048]{2,1,0:T(8,128)(2,1)} %bitcast.213, bf16[128,2048]{1,0:T(8,128)(2,1)} %bitcast.237, f32[1,2048]{1,0:T(1,128)} %unstack.41.gain, ...), custom_call_target="tpu_custom_call" | custom-call | tf_op jit(solution)/shard_map/open_units/pallas_call | solution.py:465
  243.8 6.3 fusion.53
  250.9 1.0 copy-done.33
  251.9 3.5 copy-done.27
  255.4 12.4 %multiply_convert_fusion.1 = (bf16[1024,768]{1,0:T(8,128)(2,1)S(1)}, f32[1024,768]{1,0:T(8,128)}, f32[1024,768]{1,0:T(8,128)}, f32[1024,768]{1,0:T(8,128)}) fusion(f32[1024,768]{1,0:T(8,128)S(1)} %fusion.53, bf16[1024,2048]{1,0:T(8,128)(2,1)S(1)} %bitcast.264, bf16[2048,768]{1,0:T(8,128)(2,1)S(1)} %bitcast.231), kind=kOutput, calls=%fused_computation.23 | convolution fusion | flops 3273129984 | bytes 21495808 | tf_op jit(solution)/shard_map/dot_general | solution.py:39
  267.9 5.0 convolution_convert_fusion.2
  272.9 93.3 %turn.1 = (bf16[128,2048]{1,0:T(8,128)(2,1)}, f32[128,2048]{1,0:T(8,128)}, bf16[8,128,2048]{2,1,0:T(8,128)(2,1)}, f32[2,8,2048]{2,1,0:T(8,128)}) custom-call(bf16[8,128,2048]{2,1,0:T(8,128)(2,1)} %bitcast.221, bf16[128,2048]{1,0:T(8,128)(2,1)} %get-tuple-element.40.normed, bf16[128,2048]{1,0:T(8,128)(2,1)} %bitcast.249, f32[1,2048]{1,0:T(1,128)} %unstack.49.gain, ...), custom_call_target="tpu_custom_call" | custom-call | tf_op jit(solution)/shard_map/turn/pallas_call | solution.py:754
  366.3 11.9 %multiply_convert_fusion = (bf16[1024,768]{1,0:T(8,128)(2,1)S(1)}, bf16[1024,768]{1,0:T(8,128)(2,1)}) fusion(f32[1024,768]{1,0:T(8,128)} %get-tuple-element.93, f32[1024,768]{1,0:T(8,128)} %get-tuple-element.94, f32[1024,768]{1,0:T(8,128)} %copy-done.33, f32[1024,768]{1,0:T(8,128)} %get-tuple-element.135, bf16[1024,2048]{1,0:T(8,128)(2,1)} %bitcast.266, ...), kind=kOutput, calls=%fused_computation.22 | convolution fusion | flops 3229089792 | bytes 23068672 | tf_op jit(solution)/shard_map/dot_general | solution.py:39
  378.2 5.0 convolution_convert_fusion.4
  383.3 7.5 %convolution_convert_fusion.5 = bf16[2048,768]{1,0:T(8,128)(2,1)} fusion(bf16[1024,2048]{1,0:T(8,128)(2,1)} %bitcast.263, bf16[1024,768]{1,0:T(8,128)(2,1)S(1)} %get-tuple-element.97), kind=kOutput, calls=%fused_computation.9 | convolution fusion | flops 3222798336 | bytes 8912896 | tf_op jit(solution)/shard_map/dot_general | solution.py:33
  390.8 5.0 convolution_convert_fusion.6
  395.9 3.4 fusion.54
  399.4 5.1 add_convert_fusion
  404.5 126.3 %close_units.1 = (bf16[8,3,64,768]{3,2,1,0:T(8,128)(2,1)}, bf16[8,128,2048]{2,1,0:T(8,128)(2,1)}, f32[128,2048]{1,0:T(8,128)}, f32[2,8,2048]{2,1,0:T(8,128)}) custom-call(bf16[4,2,2,2,64,768]{5,4,3,2,1,0:T(8,128)(2,1)} %bitcast.227, bf16[4,2,2,2,64,768]{5,4,3,2,1,0:T(8,128)(2,1)} %bitcast.226, bf16[4,2,2,2,64,768]{5,4,3,2,1,0:T(8,128)(2,1)} %bitcast.225, ...), custom_call_target="tpu_custom_call" | custom-call | tf_op jit(solution)/shard_map/close_units/pallas_call | solution.py:927
  530.8 3.9 convolution_convert_fusion.10
  534.7 2.2 convolution_convert_fusion.7
  537.8 2.0 reshape_reshape.20
  539.8 2.0 copy.104
  542.8 1.6 fusion.22
  549.0 1.6 copy.107
  550.6 1.0 convert_element_type.140
  551.7 7.7 %convolution_convert_fusion.3 = bf16[2048,768]{1,0:T(8,128)(2,1)} fusion(bf16[1024,2048]{1,0:T(8,128)(2,1)} %bitcast.261, bf16[1024,768]{1,0:T(8,128)(2,1)S(1)} %bitcast.241), kind=kOutput, calls=%fused_computation.7 | convolution fusion | flops 3222798336 | bytes 8912896 | tf_op jit(solution)/shard_map/dot_general | solution.py:33
  559.4 5.0 convolution_convert_fusion.1
  564.4 96.1 %close_heads.1 = (bf16[8,64,768]{2,1,0:T(8,128)(2,1)}, bf16[64,2048]{1,0:T(8,128)(2,1)}, f32[8,128]{1,0:T(8,128)}, f32[128,2048]{1,0:T(8,128)}) custom-call(bf16[4,8,64,768]{3,2,1,0:T(8,128)(2,1)} %bitcast.228, bf16[4,64,2048]{2,1,0:T(8,128)(2,1)} %bitcast.245, f32[8,4,8,128]{3,2,1,0:T(8,128)} %pad.19.small_in, bf16[8,128,2048]{2,1,0:T(8,128)(2,1)} %bitcast.222), custom_call_target="tpu_custom_call" | custom-call | tf_op jit(solution)/shard_map/close_heads/pallas_call | solution.py:1184
  660.5 2.5 add_convert_fusion.1
  664.3 1.8 convert_element_type.148
  668.0 1.2 copy.113
  669.2 2.4 reshape.249
  671.6 1.9 copy.140
  673.6 2.1 fusion.26
  (130 shorter events, 22.0 us)
Async XLA Ops:
  6.3 3.1 copy-start.19
  6.7 3.6 copy-start.20
  6.7 3.6 copy-start.21
  123.4 2.4 copy-start.1
  125.7 1.0 copy-start.8
  127.5 5.4 copy-start.9
  127.5 5.4 copy-start.11
  127.5 5.4 copy-start.13
  127.5 5.4 copy-start.15
  136.6 4.7 copy-start.2
  243.8 6.3 copy-start
  250.2 1.8 copy-start.33
  250.2 5.3 copy-start.27
  250.9 16.9 %copy-start.4 = (bf16[1,4,2,2,2,64,768]{6,5,4,3,2,1,0:T(8,128)(2,1)}, bf16[1,4,2,2,2,64,768]{6,5,4,3,2,1,0:T(8,128)(2,1)S(1)}, u32[]{:S(2)}) copy-start(bf16[1,4,2,2,2,64,768]{6,5,4,3,2,1,0:T(8,128)(2,1)S(1)} %get-tuple-element.96) | copy-start | bytes 9437188
  250.9 16.9 %copy-start.6 = (bf16[1,4,2,2,2,64,768]{6,5,4,3,2,1,0:T(8,128)(2,1)}, bf16[1,4,2,2,2,64,768]{6,5,4,3,2,1,0:T(8,128)(2,1)S(1)}, u32[]{:S(2)}) copy-start(bf16[1,4,2,2,2,64,768]{6,5,4,3,2,1,0:T(8,128)(2,1)S(1)} %get-tuple-element.95) | copy-start | bytes 9437188
  267.9 5.1 copy-start.35
  366.3 12.0 %copy-start.29 = (bf16[8,128,2048]{2,1,0:T(8,128)(2,1)S(1)}, bf16[8,128,2048]{2,1,0:T(8,128)(2,1)}, u32[]{:S(2)}) copy-start(bf16[8,128,2048]{2,1,0:T(8,128)(2,1)} %get-tuple-element.42) | copy-start | bytes 12582916
  366.3 11.9 %copy-start.36 = (bf16[1024,768]{1,0:T(8,128)(2,1)S(1)}, bf16[1024,768]{1,0:T(8,128)(2,1)}, u32[]{:S(2)}) copy-start(bf16[1024,768]{1,0:T(8,128)(2,1)} %copy-done.35) | copy-start | bytes 4718596
  378.2 5.0 copy-start.26
  383.3 7.6 %copy-start.28 = (bf16[8,128,2048]{2,1,0:T(8,128)(2,1)S(1)}, bf16[8,128,2048]{2,1,0:T(8,128)(2,1)}, u32[]{:S(2)}) copy-start(bf16[8,128,2048]{2,1,0:T(8,128)(2,1)} %get-tuple-element.37) | copy-start | bytes 12582916
  383.3 7.6 %copy-start.34 = (bf16[1024,768]{1,0:T(8,128)(2,1)S(1)}, bf16[1024,768]{1,0:T(8,128)(2,1)}, u32[]{:S(2)}) copy-start(bf16[1024,768]{1,0:T(8,128)(2,1)} %get-tuple-element.98) | copy-start | bytes 4718596
  390.8 5.0 copy-start.32
  395.9 3.5 copy-start.5
  530.7 4.0 copy-start.3
  530.8 4.0 copy-start.30
  537.0 4.8 copy-start.25
  537.0 5.8 copy-start.17
  542.8 1.6 copy-start.23
  542.8 1.6 copy-start.24
  544.9 1.0 copy-start.14
  544.9 1.2 copy-start.16
  544.9 1.7 copy-start.10
  544.9 1.7 copy-start.12
  546.1 1.3 copy-start.7
  551.7 7.7 %copy-start.31 = (bf16[4,8,64,768]{3,2,1,0:T(8,128)(2,1)S(1)}, bf16[4,8,64,768]{3,2,1,0:T(8,128)(2,1)}, u32[]{:S(2)}) copy-start(bf16[4,8,64,768]{3,2,1,0:T(8,128)(2,1)} %get-tuple-element.34) | copy-start | bytes 9437188
  660.5 5.6 copy-start.18
  673.5 2.1 copy-start.22

commit v7 on v6

--- a/solution.py
+++ b/solution.py
@@ -362,17 +362,39 @@
     wire.drain()
 
 
+def turned(values, cosine, sine):
+    return values * cosine + pltpu.roll(values, HEAD_DIM // 2, 1) * sine
+
+
+def row_place(rank, micro):
+    piece = rank % 4
+    return (rank // 4) * 2 + micro, piece
+
+
 def open_units_kernel(
-    part,
+    x_all,
+    qkv,
+    proj,
+    cosine,
+    sine,
+    start_query,
+    start_key,
+    end_key,
     x_own,
     gain,
     shift,
     ffn_in,
+    queries,
+    key_rows,
+    value_rows,
+    probs_out,
+    context,
     normed,
     hat,
     inverse_out,
     normed_all,
     ffn_out,
+    part,
     branch,
     *rest,
 ):
@@ -380,11 +402,62 @@
     *scratch, send_sems, recv_sems, own_sems = rest
     wire = Wire(send_sems, recv_sems)
     enter(at.neighbours())
+    own = x_own.shape[0]
+    pos = own // 2
+    length = 4 * pos
+    heads = context.shape[-1] // HEAD_DIM
+    wide = heads * HEAD_DIM
+
+    def project():
+        @pl.loop(0, 8)
+        def _(rank):
+            mixed = dot(x_all[rank], qkv[...])
+            for micro in range(2):
+                row, piece = row_place(rank, micro)
+                place = pl.ds(pl.multiple_of(piece * pos, pos), pos)
+                near = mixed[micro * pos : (micro + 1) * pos]
+                cos, sin = cosine[row, place], sine[row, place]
+                for head in range(heads):
+                    cols = pl.ds(head * HEAD_DIM, HEAD_DIM)
+                    for kind, target in enumerate((queries, key_rows, value_rows)):
+                        first = kind * wide + head * HEAD_DIM
+                        values = near[:, first : first + HEAD_DIM]
+                        if kind < 2:
+                            values = turned(values, cos, sin)
+                        target[row, place, cols] = values.astype(jnp.bfloat16)
+
+    def attend():
+        scale = 1.0 / math.sqrt(HEAD_DIM)
+        here = lax.broadcasted_iota(jnp.int32, (length, length), 0)
+        there = lax.broadcasted_iota(jnp.int32, (length, length), 1)
+
+        @pl.loop(0, 4)
+        def _(row):
+            bound = end_key[row].astype(jnp.int32)
+            seen = (start_query[row] == start_key[row]) & ((there <= here) | (there < bound))
+            for head in range(heads):
+                cols = pl.ds(head * HEAD_DIM, HEAD_DIM)
+                scores = contract_last(queries[row, :, cols], key_rows[row, :, cols]) * scale
+                scores = jnp.where(seen, scores, masked_score)
+                scores = jnp.exp(scores - jnp.max(scores, axis=-1, keepdims=True))
+                probs = scores / jnp.sum(scores, axis=-1, keepdims=True)
+                probs_out[row, head] = probs
+                result = dot(probs.astype(jnp.bfloat16), value_rows[row, :, cols])
+                result = result.astype(jnp.bfloat16)
+                for piece in range(4):
+                    target = pl.ds(pl.multiple_of((row % 2) * pos, pos), pos)
+                    source = result[piece * pos : (piece + 1) * pos]
+                    context[(row // 2) * 4 + piece, target, cols] = source
+
+    def branch_parts():
+        @pl.loop(0, 8)
+        def _(rank):
+            part[rank] = dot(context[rank], proj[...]).astype(jnp.bfloat16)
 
     def norm_rows():
         count = 16
 
-        @pl.loop(0, x_own.shape[0] // count)
+        @pl.loop(0, own // count)
         def _(index):
             rows = pl.ds(pl.multiple_of(index * count, count), count)
             whole = deep_alpha * x_own[rows].astype(jnp.float32) + branch[rows]
@@ -395,11 +468,18 @@
 
     scatter = plane_scatter_flow(at, wire, part, branch, *scratch)
     units = unit_gather_flow(at, wire, ffn_in, ffn_out, own_sems.at[0])
+    next(units)
+    next(units)
+    project()
+    next(units)
+    next(units)
+    attend()
+    next(units)
+    branch_parts()
     next(scatter)
     next(units)
     next(scatter)
     next(scatter)
-    next(units)
     for _ in scatter:
         pass
     norm_rows()
@@ -409,14 +489,9 @@
     next(units)
     next(spread)
     next(units)
-    next(units)
     next(spread)
-    next(units)
-    next(units)
-    next(spread)
-    next(units)
     for _ in spread:
-        pass
+        next(units, None)
     for _ in units:
         pass
     wire.drain()
@@ -458,22 +533,33 @@
     )(qkv_parts, ffn_parts, proj_own, x_own, small)
 
 
-def open_units(part, x_own, gain, shift, ffn_parts):
+def open_units(x_all, qkv, proj, tables, x_own, gain, shift, ffn_parts):
     _, matrices, rows_own, unit_width = ffn_parts.shape
     own, width = x_own.shape
+    head_width = proj.shape[0]
+    length = 2 * own
     low_type = jnp.bfloat16
+    rows = jax.ShapeDtypeStruct((4, length, head_width), low_type)
     return pl.pallas_call(
         open_units_kernel,
         out_shape=(
+            rows,
+            rows,
+            rows,
+            jax.ShapeDtypeStruct((4, head_width // HEAD_DIM, length, length), jnp.float32),
+            jax.ShapeDtypeStruct((8, own, head_width), low_type),
             jax.ShapeDtypeStruct((own, width), low_type),
             jax.ShapeDtypeStruct((own, width), jnp.float32),
             jax.ShapeDtypeStruct((own, LANES), jnp.float32),
             jax.ShapeDtypeStruct((8, own, width), low_type),
             jax.ShapeDtypeStruct((matrices, 4, 2, 2, 2, rows_own, unit_width), low_type),
         ),
-        in_specs=[VMEM] * 5,
-        out_specs=(VMEM, VMEM, VMEM, ANY, ANY),
-        scratch_shapes=[pltpu.VMEM((own, width), jnp.float32)]
+        in_specs=[VMEM] * 12,
+        out_specs=(VMEM,) * 8 + (ANY, ANY),
+        scratch_shapes=[
+            pltpu.VMEM((8, own, width), low_type),
+            pltpu.VMEM((own, width), jnp.float32),
+        ]
         + plane_scratch(own, width)
         + [
             pltpu.SemaphoreType.DMA((64,)),
@@ -482,7 +568,7 @@
         ],
         compiler_params=comm_params(4),
         name="open_units",
-    )(part, x_own, gain, shift, ffn_parts)
+    )(x_all, qkv, proj, *tables, x_own, gain, shift, ffn_parts)
 
 
 def add_rows(out, *terms):
@@ -692,13 +778,14 @@
     at = Place()
     wire = Wire(send_sems, recv_sems)
     enter(at.column_neighbours())
-    half = normed.shape[0] // 2
+    pieces = 4
+    height = normed.shape[0] // pieces
     scratch = core_in, core_sum, up_in, down_in, up_sum, down_sum
 
     def norm_rows(start):
         count = 16
 
-        @pl.loop(0, half // count)
+        @pl.loop(0, height // count)
         def _(index):
             rows = pl.ds(pl.multiple_of(start + index * count, count), count)
             whole = deep_alpha * normed[rows].astype(jnp.float32) + second[rows]
@@ -713,8 +800,8 @@
             norm_out[1] += cotangent[:8] + cotangent[8:]
 
     scatters, gathers = [], []
-    for index in range(2):
-        rows = pl.ds(index * half, half)
+    for index in range(pieces):
+        rows = pl.ds(index * height, height)
         views = [ref.at[:, rows] for ref in scratch]
         scatters.append(
             column_scatter_flow(at, wire, index, part.at[:, rows], second.at[rows], *views)
@@ -729,20 +816,16 @@
         next(flow)
     for flow in scatters:
         next(flow)
-    for _ in scatters[0]:
-        pass
-    norm_rows(0)
-    next(gathers[0])
-    next(scatters[1])
-    next(gathers[0])
-    for _ in scatters[1]:
-        pass
-    norm_rows(half)
-    next(gathers[1])
-    next(gathers[0])
-    next(gathers[1])
-    next(gathers[0])
-    for flow in gathers[::-1]:
+    for index in range(pieces):
+        for _ in scatters[index]:
+            for flow in gathers[:index]:
+                next(flow, None)
+        norm_rows(index * height)
+        next(gathers[index])
+    for _ in range(4):
+        for flow in gathers:
+            next(flow, None)
+    for flow in gathers:
         for _ in flow:
             pass
     wire.drain()
@@ -767,9 +850,9 @@
         ]
         + column_scratch(own, width)
         + [
-            pltpu.SemaphoreType.DMA((72,)),
-            pltpu.SemaphoreType.DMA((72,)),
-            pltpu.SemaphoreType.DMA((2,)),
+            pltpu.SemaphoreType.DMA((112,)),
+            pltpu.SemaphoreType.DMA((112,)),
+            pltpu.SemaphoreType.DMA((4,)),
         ],
         compiler_params=comm_params(5),
         name="turn",
@@ -1270,9 +1353,7 @@
     params = small[:, : 4 * rows_own].reshape(-1, 4, rows_own).transpose(1, 0, 2)
     gain_one, shift_one, gain_two, shift_two = params.reshape(4, 1, width)
     marks = small.reshape(4, head_ways, -1)[lax.axis_index("zi")]
-    marks = marks[:, 4 * rows_own : 4 * rows_own + own * 3].astype(jnp.int32)
-
-    mixed = dot(x_all, qkv_here)
+    marks = marks[:, 4 * rows_own : 4 * rows_own + own * 3]
 
     def to_rows(values):
         inner = values.shape[1:]
@@ -1286,33 +1367,37 @@
 
     row_marks = to_rows(marks.reshape(head_ways * own, 3))
     cosine, sine = rotary_tables(row_marks[..., 2])
+    tables = (
+        jnp.concatenate([cosine, cosine], axis=-1),
+        jnp.concatenate([-sine, sine], axis=-1),
+        row_marks[:, :, :1],
+        row_marks[:, None, :, 0],
+        row_marks[:, None, :, 1],
+    )
+    queries, key_rows, value_rows, probs, context, normed, hat_one, inverse_one, normed_all, ffn = (
+        open_units(
+            x_all.reshape(head_ways, own, width),
+            qkv_here,
+            proj_here,
+            tables,
+            x_own,
+            gain_one,
+            shift_one,
+            unit_parts(up_weight, down_weight),
+        )
+    )
+    rows_shape = (x_size * micro_count, row_length, heads_here, HEAD_DIM)
+    queries, key_rows, value_rows = (
+        values.reshape(rows_shape) for values in (queries, key_rows, value_rows)
+    )
+    probs_low = low(probs)
+    context = context.reshape(-1, head_width)
     cosine, sine = cosine[:, :, None, :], sine[:, :, None, :]
-    mixed = to_rows(mixed).reshape(x_size * micro_count, row_length, 3, heads_here, HEAD_DIM)
-    queries = low(rotate(mixed[:, :, 0], cosine, sine))
-    key_rows = low(rotate(mixed[:, :, 1], cosine, sine))
-    value_rows = low(mixed[:, :, 2])
-    place = jnp.arange(row_length, dtype=jnp.int32)
-    allowed = (row_marks[:, :, None, 0] == row_marks[:, None, :, 0]) & (
-        (place[None, None, :] <= place[None, :, None])
-        | (place[None, :] < row_marks[:, :, 1])[:, None, :]
-    )
     score_scale = 1.0 / math.sqrt(HEAD_DIM)
 
     def pair(spec, left_side, right_side):
         return jnp.einsum(spec, left_side, right_side, preferred_element_type=jnp.float32)
 
-    scores = pair("rqhd,rkhd->rhqk", queries, key_rows) * score_scale
-    scores = jnp.where(allowed[:, None], scores, masked_score)
-    exp_scores = jnp.exp(scores - jnp.max(scores, axis=-1, keepdims=True))
-    probs = exp_scores / jnp.sum(exp_scores, axis=-1, keepdims=True)
-    probs_low = low(probs)
-    context = low(pair("rhqk,rkhd->rqhd", probs_low, value_rows))
-
-    context = from_rows(context).reshape(-1, head_width)
-    branch_part = low(dot(context, proj_here)).reshape(head_ways, own, width)
-    normed, hat_one, inverse_one, normed_all, ffn = open_units(
-        branch_part, x_own, gain_one, shift_one, unit_parts(up_weight, down_weight)
-    )
     normed_all = normed_all.reshape(-1, width)
     up_here, down_here = ffn.reshape(2, -1, unit_width)
 

time: 687 us -> 696 us (1.013)
  Pallas kernels: 507 us -> 543 us
  matrix products: 100 us -> 84.8 us
  local copies, waits for them, and re-layouts: 50.6 us -> 40.3 us
    pallas_call x1, Pallas kernels: 103 us -> 124 us  [open_units(): pl.pallas_call(open_units_kernel, out_shape=(rows, rows, rows, jax.ShapeD...]
    pallas_call x1, Pallas kernels: 93.3 us -> 107 us  [turn(): pl.pallas_call(turn_kernel, out_shape=(jax.ShapeDtypeStruct((own, width),...]
    dot_general x5 -> x3, matrix products: 41.5 us -> 30.7 us  [dot(): return jnp.dot(left_side, right_side, preferred_element_type=jnp.float32)]
where the time goes in v7:
time: 696 us; the launch traced here: 686 us
  Pallas kernels  543 us (78%)
  matrix products  84.8 us (12%)
  local copies, waits for them, and re-layouts  40.3 us (6%)
  other arithmetic  16.7 us (2%)
    pallas_call x1, Pallas kernels, close_units(): pl.pallas_call(close_units_kernel, out_shape=(jax.ShapeDtypeStruct((8, 3)...  127 us
    pallas_call x1, Pallas kernels, open_units(): pl.pallas_call(open_units_kernel, out_shape=(rows, rows, rows, jax.ShapeD...  124 us
    pallas_call x1, Pallas kernels, turn(): pl.pallas_call(turn_kernel, out_shape=(jax.ShapeDtypeStruct((own, width),...  107 us
    pallas_call x1, Pallas kernels, close_heads(): pl.pallas_call(close_heads_kernel, out_shape=(jax.ShapeDtypeStruct((8, ro...  96.5 us
    pallas_call x1, Pallas kernels, open_heads(): pl.pallas_call(open_heads_kernel, out_shape=(jax.ShapeDtypeStruct((4, 8,...  89.1 us
    dot_general x3, matrix products, dot(): return jnp.dot(left_side, right_side, preferred_element_type=jnp.float32)  30.7 us
    dot_general x5, matrix products, contract_first(): lax.dot_general(left_side, right_side, (((0,), (0,)), ((), ())), preferre...  29.8 us
    dot_general x5, matrix products, contract_last(): lax.dot_general(left_side, right_side, (((1,), (1,)), ((), ())), preferre...  22.6 us

profile of v7, /device:TPU:11, one launch (start us, length us, event | category | flops | bytes accessed | tf_op | source)
XLA Modules:
  0.0 686.3 jit_solution(16098960758520524303)
XLA Ops:
  3.1 2.6 reshape.180
  6.7 0.9 maximum_bitcast_fusion
  7.6 1.7 reshape.181.qkv_in
  9.3 0.9 copy.167
  10.5 1.3 copy.166
  11.8 89.1 %open_heads.1 = (bf16[4,8,64,768]{3,2,1,0:T(8,128)(2,1)}, bf16[1,4,2,2,2,64,768]{6,5,4,3,2,1,0:T(8,128)(2,1)}, bf16[4,64,2048]{2,1,0:T(8,128)(2,1)}, bf16[8,128,2048]{2,1,0:T(8,128)(2,1)}, f32[4,8,8,128]{3,2,1,0:T(8,128)}) custom-call(bf16[8,64,768]{2,1,0:T(8,128)(2,1)} %reshape.181.qkv_in, bf16[8,1,64,768]{3,2,1,0:T(8,128)(2,1)} %bitcast.208, ...), custom_call_target="tpu_custom_call" | custom-call | tf_op jit(solution)/shard_map/open_heads/pallas_call | solution.py:515
  100.9 0.9 copy.169
  101.8 0.9 reshape_reshape.10
  107.1 1.0 copy.112.start_query
  108.1 1.9 fusion.28
  110.0 1.0 pad_maximum_fusion.2.sine
  111.2 0.9 copy.119
  112.1 1.0 pad_maximum_fusion.1.cosine
  113.1 123.5 %open_units.1 = (bf16[4,256,256]{2,1,0:T(8,128)(2,1)}, bf16[4,256,256]{2,1,0:T(8,128)(2,1)}, bf16[4,256,256]{2,1,0:T(8,128)(2,1)}, f32[4,2,256,256]{3,2,1,0:T(8,...) custom-call(bf16[8,128,2048]{2,1,0:T(8,128)(2,1)} %get-tuple-element, ...), custom_call_target="tpu_custom_call" | custom-call | tf_op jit(solution)/shard_map/open_units/pallas_call | solution.py:543
  236.6 1.2 copy.136
  237.8 2.2 copy.137
  240.0 6.3 fusion.33
  246.4 0.7 fusion.31
  247.1 1.0 copy-done.20
  248.1 3.5 copy-done.16
  251.6 12.4 %multiply_convert_fusion.1 = (bf16[1024,768]{1,0:T(8,128)(2,1)S(1)}, f32[1024,768]{1,0:T(8,128)}, f32[1024,768]{1,0:T(8,128)}, f32[1024,768]{1,0:T(8,128)}) fusion(f32[1024,768]{1,0:T(8,128)S(1)} %fusion.33, bf16[1024,2048]{1,0:T(8,128)(2,1)S(1)} %bitcast.244, bf16[2048,768]{1,0:T(8,128)(2,1)S(1)} %bitcast.212), kind=kOutput, calls=%fused_computation.21 | convolution fusion | flops 3273129984 | bytes 21495808 | tf_op jit(solution)/shard_map/dot_general | solution.py:39
  264.1 5.0 convolution_convert_fusion.1
  269.1 106.6 %turn.1 = (bf16[128,2048]{1,0:T(8,128)(2,1)}, f32[128,2048]{1,0:T(8,128)}, bf16[8,128,2048]{2,1,0:T(8,128)(2,1)}, f32[2,8,2048]{2,1,0:T(8,128)}) custom-call(bf16[8,128,2048]{2,1,0:T(8,128)(2,1)} %bitcast.201, bf16[128,2048]{1,0:T(8,128)(2,1)} %get-tuple-element.45.normed, bf16[128,2048]{1,0:T(8,128)(2,1)} %bitcast.230, f32[1,2048]{1,0:T(1,128)} %unstack.49.gain, ...), custom_call_target="tpu_custom_call" | custom-call | tf_op jit(solution)/shard_map/turn/pallas_call | solution.py:837
  375.8 11.9 %multiply_convert_fusion = (bf16[1024,768]{1,0:T(8,128)(2,1)S(1)}, bf16[1024,768]{1,0:T(8,128)(2,1)}) fusion(f32[1024,768]{1,0:T(8,128)} %get-tuple-element.114, f32[1024,768]{1,0:T(8,128)} %get-tuple-element.115, f32[1024,768]{1,0:T(8,128)} %copy-done.20, f32[1024,768]{1,0:T(8,128)} %get-tuple-element.148, bf16[1024,2048]{1,0:T(8,128)(2,1)} %bitcast.246, ...), kind=kOutput, calls=%fused_computation.20 | convolution fusion | flops 3229089792 | bytes 23068672 | tf_op jit(solution)/shard_map/dot_general | solution.py:39
  387.7 5.0 convolution_convert_fusion.3
  392.8 7.6 %convolution_convert_fusion.4 = bf16[2048,768]{1,0:T(8,128)(2,1)} fusion(bf16[1024,2048]{1,0:T(8,128)(2,1)} %bitcast.243, bf16[1024,768]{1,0:T(8,128)(2,1)S(1)} %get-tuple-element.118), kind=kOutput, calls=%fused_computation.7 | convolution fusion | flops 3222798336 | bytes 8912896 | tf_op jit(solution)/shard_map/dot_general | solution.py:33
  400.4 5.1 convolution_convert_fusion.5
  405.5 3.4 fusion.34
  408.9 5.1 add_convert_fusion
  414.1 127.2 %close_units.1 = (bf16[8,3,64,768]{3,2,1,0:T(8,128)(2,1)}, bf16[8,128,2048]{2,1,0:T(8,128)(2,1)}, f32[128,2048]{1,0:T(8,128)}, f32[2,8,2048]{2,1,0:T(8,128)}) custom-call(bf16[4,2,2,2,64,768]{5,4,3,2,1,0:T(8,128)(2,1)} %bitcast.206, bf16[4,2,2,2,64,768]{5,4,3,2,1,0:T(8,128)(2,1)} %bitcast.205, bf16[4,2,2,2,64,768]{5,4,3,2,1,0:T(8,128)(2,1)} %bitcast.204, ...), custom_call_target="tpu_custom_call" | custom-call | tf_op jit(solution)/shard_map/close_units/pallas_call | solution.py:1010
  541.2 3.8 convolution_convert_fusion.7
  545.1 0.9 reshape_reshape.12
  546.0 1.3 copy.122
  547.9 0.7 pad_maximum_fusion.3
  550.0 4.5 fusion.16
  557.7 2.2 copy.123
  559.9 0.8 convert_element_type.112
  560.8 7.7 %convolution_convert_fusion.2 = bf16[2048,768]{1,0:T(8,128)(2,1)} fusion(bf16[1024,2048]{1,0:T(8,128)(2,1)} %bitcast.199, bf16[1024,768]{1,0:T(8,128)(2,1)S(1)} %bitcast.223), kind=kOutput, calls=%fused_computation.5 | convolution fusion | flops 3222798336 | bytes 8912896 | tf_op jit(solution)/shard_map/dot_general | solution.py:33
  568.5 5.2 convolution_convert_fusion
  573.7 96.5 %close_heads.1 = (bf16[8,64,768]{2,1,0:T(8,128)(2,1)}, bf16[64,2048]{1,0:T(8,128)(2,1)}, f32[8,128]{1,0:T(8,128)}, f32[128,2048]{1,0:T(8,128)}) custom-call(bf16[4,8,64,768]{3,2,1,0:T(8,128)(2,1)} %bitcast.207, bf16[4,64,2048]{2,1,0:T(8,128)(2,1)} %bitcast.203, f32[8,4,8,128]{3,2,1,0:T(8,128)} %pad.19.small_in, bf16[8,128,2048]{2,1,0:T(8,128)(2,1)} %bitcast.202), custom_call_target="tpu_custom_call" | custom-call | tf_op jit(solution)/shard_map/close_heads/pallas_call | solution.py:1267
  670.3 2.5 add_convert_fusion.1
  674.1 1.8 convert_element_type.120
  676.6 0.9 convert_bitcast_fusion
  677.5 1.2 copy.130
  678.7 2.4 reshape.219
  681.1 1.9 copy.149
  683.1 2.1 fusion.22
  685.2 0.8 copy.172
  (100 shorter events, 15.4 us)
Async XLA Ops:
  6.2 3.1 copy-start.9
  6.6 3.6 copy-start.10
  6.7 3.6 copy-start.11
  237.8 8.5 %slice-start = ((s8[6291456]{0:T(1024)(128)(4,1)}), s8[2097152]{0:T(1024)(128)(4,1)S(1)}, s32[]{:S(2)}) async-start(s8[6291456]{0:T(1024)(128)(4,1)} %bitcast.194), calls=%async_computation | async-start | bytes 4194304
  240.0 6.3 slice-start.1
  246.4 1.8 copy-start.20
  246.4 5.3 copy-start.16
  247.1 17.0 %copy-start.2 = (bf16[1,4,2,2,2,64,768]{6,5,4,3,2,1,0:T(8,128)(2,1)}, bf16[1,4,2,2,2,64,768]{6,5,4,3,2,1,0:T(8,128)(2,1)S(1)}, u32[]{:S(2)}) copy-start(bf16[1,4,2,2,2,64,768]{6,5,4,3,2,1,0:T(8,128)(2,1)S(1)} %get-tuple-element.117) | copy-start | bytes 9437188
  247.1 16.9 %copy-start.4 = (bf16[1,4,2,2,2,64,768]{6,5,4,3,2,1,0:T(8,128)(2,1)}, bf16[1,4,2,2,2,64,768]{6,5,4,3,2,1,0:T(8,128)(2,1)S(1)}, u32[]{:S(2)}) copy-start(bf16[1,4,2,2,2,64,768]{6,5,4,3,2,1,0:T(8,128)(2,1)S(1)} %get-tuple-element.116) | copy-start | bytes 9437188
  264.1 5.0 copy-start.22
  375.8 12.0 %copy-start.18 = (bf16[8,128,2048]{2,1,0:T(8,128)(2,1)S(1)}, bf16[8,128,2048]{2,1,0:T(8,128)(2,1)}, u32[]{:S(2)}) copy-start(bf16[8,128,2048]{2,1,0:T(8,128)(2,1)} %get-tuple-element.47) | copy-start | bytes 12582916
  375.8 11.9 %copy-start.23 = (bf16[1024,768]{1,0:T(8,128)(2,1)S(1)}, bf16[1024,768]{1,0:T(8,128)(2,1)}, u32[]{:S(2)}) copy-start(bf16[1024,768]{1,0:T(8,128)(2,1)} %copy-done.22) | copy-start | bytes 4718596
  387.7 5.0 copy-start.15
  392.8 7.6 %copy-start.17 = (bf16[8,128,2048]{2,1,0:T(8,128)(2,1)S(1)}, bf16[8,128,2048]{2,1,0:T(8,128)(2,1)}, u32[]{:S(2)}) copy-start(bf16[8,128,2048]{2,1,0:T(8,128)(2,1)} %get-tuple-element.42) | copy-start | bytes 12582916
  392.8 7.6 %copy-start.21 = (bf16[1024,768]{1,0:T(8,128)(2,1)S(1)}, bf16[1024,768]{1,0:T(8,128)(2,1)}, u32[]{:S(2)}) copy-start(bf16[1024,768]{1,0:T(8,128)(2,1)} %get-tuple-element.119) | copy-start | bytes 4718596
  400.4 5.1 copy-start.19
  405.5 3.5 copy-start.3
  545.0 2.3 copy-start.14
  545.0 4.6 copy-start
  548.9 1.1 copy-start.6
  550.0 4.5 copy-start.12
  555.1 1.0 copy-start.5
  556.2 0.9 copy-start.7
  560.8 7.7 %copy-start.1 = (bf16[4,8,64,768]{3,2,1,0:T(8,128)(2,1)S(1)}, bf16[4,8,64,768]{3,2,1,0:T(8,128)(2,1)}, u32[]{:S(2)}) copy-start(bf16[4,8,64,768]{3,2,1,0:T(8,128)(2,1)} %get-tuple-element.39) | copy-start | bytes 9437188
  670.3 5.6 copy-start.8
  683.0 2.1 copy-start.13

commit v8 on v7

--- a/solution.py
+++ b/solution.py
@@ -454,46 +454,58 @@
         def _(rank):
             part[rank] = dot(context[rank], proj[...]).astype(jnp.bfloat16)
 
-    def norm_rows():
+    pieces = 4
+    height = own // pieces
+
+    def norm_rows(start):
         count = 16
 
-        @pl.loop(0, own // count)
+        @pl.loop(0, height // count)
         def _(index):
-            rows = pl.ds(pl.multiple_of(index * count, count), count)
+            rows = pl.ds(pl.multiple_of(start + index * count, count), count)
             whole = deep_alpha * x_own[rows].astype(jnp.float32) + branch[rows]
             near, inverse = norm_parts(whole)
             hat[rows] = near
             inverse_out[rows] = jnp.broadcast_to(inverse, (count, LANES))
             normed[rows] = (near * gain[...] + shift[...]).astype(jnp.bfloat16)
 
-    scatter = plane_scatter_flow(at, wire, part, branch, *scratch)
+    core_in, core_sum, side_in, side_sum, last_in = scratch
+    scatters, gathers = [], []
+    for index in range(pieces):
+        rows = pl.ds(index * height, height)
+        views = [core_in.at[:, rows], core_sum.at[:, rows], side_in.at[:, :, rows]]
+        views += [side_sum.at[:, rows], last_in.at[:, rows]]
+        scatters.append(
+            plane_scatter_flow(at, wire, index, part.at[:, rows], branch.at[rows], *views)
+        )
+        sem = own_sems.at[1 + index]
+        gathers.append(
+            column_gather_flow(at, wire, index, normed.at[rows], normed_all.at[:, rows], sem)
+        )
     units = unit_gather_flow(at, wire, ffn_in, ffn_out, own_sems.at[0])
     next(units)
     next(units)
     project()
     next(units)
-    next(units)
     attend()
     next(units)
     branch_parts()
-    next(scatter)
-    next(units)
-    next(scatter)
-    next(scatter)
-    for _ in scatter:
-        pass
-    norm_rows()
-    spread = column_gather_flow(at, wire, 0, normed, normed_all, own_sems.at[1])
-    next(spread)
-    next(units)
-    next(units)
-    next(spread)
-    next(units)
-    next(spread)
-    for _ in spread:
+    for stage in range(3):
+        for flow in scatters:
+            next(flow)
+    for index in range(pieces + 3):
+        if index < pieces:
+            for _ in scatters[index]:
+                pass
+            norm_rows(index * height)
+            next(gathers[index])
+        for lag in (1, 2, 3):
+            if 0 <= index - lag < pieces:
+                next(gathers[index - lag], None)
         next(units, None)
-    for _ in units:
-        pass
+    for flow in gathers + [units]:
+        for _ in flow:
+            pass
     wire.drain()
 
 
@@ -562,9 +574,9 @@
         ]
         + plane_scratch(own, width)
         + [
-            pltpu.SemaphoreType.DMA((64,)),
-            pltpu.SemaphoreType.DMA((64,)),
-            pltpu.SemaphoreType.DMA((2,)),
+            pltpu.SemaphoreType.DMA((136,)),
+            pltpu.SemaphoreType.DMA((136,)),
+            pltpu.SemaphoreType.DMA((5,)),
         ],
         compiler_params=comm_params(4),
         name="open_units",
@@ -595,11 +607,12 @@
     for goal in (3, 0, 2, 1):
         wire.arrive(("rc", tag, goal), core_in.at[goal], core_side)
         add_rows(core_sum.at[goal], part.at[goal * 2 + at.c], core_in.at[goal])
-        source = core_sum.at[goal]
-        if goal > 0:
-            wire.send(("ru", tag, goal), source, up_in.at[goal], up, at.zi == 0)
-        if goal < 3:
-            wire.send(("rd", tag, goal), source, down_in.at[goal], down, at.zi == 3)
+        for rising in {3: (3,), 2: (2,), 1: (1,)}.get(goal, ()):
+            key = "ru", tag, rising
+            wire.send(key, core_sum.at[rising], up_in.at[rising], up, at.zi == 0)
+        for falling in {0: (0,), 1: (1, 2)}.get(goal, ()):
+            key = "rd", tag, falling
+            wire.send(key, core_sum.at[falling], down_in.at[falling], down, at.zi == 3)
 
     def climb(goal):
         wire.arrive(("ru", tag, goal), up_in.at[goal], down)
@@ -609,17 +622,26 @@
         wire.arrive(("rd", tag, goal), down_in.at[goal], up)
         add_rows(down_sum.at[goal], core_sum.at[goal], down_in.at[goal])
 
-    for goal in (3, 2):
-        yield
-        back = 3 - goal
-        passing = (at.zi > 0) & (at.zi < goal)
-        pl.when(passing)(lambda: climb(goal))
+    def rise(goal, z):
+        pl.when(at.zi == z)(lambda: climb(goal))
         key = "ru", tag, goal
-        wire.send(("ru2", tag, goal), up_sum.at[goal], up_in.at[goal], up, passing, recv=key)
-        passing = (at.zi < 3) & (at.zi > back)
-        pl.when(passing)(lambda: descend(back))
-        key = "rd", tag, back
-        wire.send(("rd2", tag, back), down_sum.at[back], down_in.at[back], down, passing, recv=key)
+        target = up_in.at[goal]
+        wire.send(("ru2", tag, goal), up_sum.at[goal], target, up, at.zi == z, recv=key)
+
+    def fall(goal, z):
+        pl.when(at.zi == z)(lambda: descend(goal))
+        key = "rd", tag, goal
+        target = down_in.at[goal]
+        wire.send(("rd2", tag, goal), down_sum.at[goal], target, down, at.zi == z, recv=key)
+
+    yield
+    rise(3, 1)
+    fall(0, 2)
+    yield
+    rise(3, 2)
+    fall(0, 1)
+    rise(2, 1)
+    fall(1, 2)
     yield
     add_rows(out, core_sum.at[at.zi])
 
@@ -672,7 +694,9 @@
     return [pltpu.VMEM((4, own, width), jnp.bfloat16)] * 6
 
 
-def plane_scatter_flow(at, wire, part, out, core_in, core_sum, side_in, side_sum, last_in):
+def plane_scatter_flow(
+    at, wire, tag, part, out, core_in, core_sum, side_in, side_sum, last_in
+):
     x_side, y_side, core_side = at.plane(4)[0], at.plane(2)[0], at.plane(1)[0]
     half = out.shape[1] // 2
     halves = (pl.ds(0, half), pl.ds(half, half))
@@ -684,34 +708,34 @@
     for dx, dy in order:
         x, y = place(dx, dy)
         other = x * 4 + y * 2 + 1 - at.c
-        wire.send(("c", dx, dy), part.at[other], core_in.at[dx * 2 + dy], core_side)
+        wire.send(("c", tag, dx, dy), part.at[other], core_in.at[dx * 2 + dy], core_side)
     yield
     for dx, dy in order:
         x, y = place(dx, dy)
         mine = x * 4 + y * 2 + at.c
         slot = dx * 2 + dy
-        wire.arrive(("c", dx, dy), core_in.at[slot], core_side)
+        wire.arrive(("c", tag, dx, dy), core_in.at[slot], core_side)
         add_rows(core_sum.at[slot], part.at[mine], core_in.at[slot])
         if dx:
             source = core_sum.at[slot, :, halves[0]]
-            wire.send(("sa", dy), source, side_in.at[0, dy], x_side)
+            wire.send(("sa", tag, dy), source, side_in.at[0, dy], x_side)
         if dy:
             source = core_sum.at[slot, :, halves[1]]
-            wire.send(("sb", dx), source, side_in.at[1, dx], y_side)
+            wire.send(("sb", tag, dx), source, side_in.at[1, dx], y_side)
     yield
-    wire.arrive(("sa", 1), side_in.at[0, 1], x_side)
+    wire.arrive(("sa", tag, 1), side_in.at[0, 1], x_side)
     add_rows(side_sum.at[0], core_sum.at[1, :, halves[0]], side_in.at[0, 1])
-    wire.send("sy", side_sum.at[0], last_in.at[0], y_side)
-    wire.arrive(("sb", 1), side_in.at[1, 1], y_side)
+    wire.send(("sy", tag), side_sum.at[0], last_in.at[0], y_side)
+    wire.arrive(("sb", tag, 1), side_in.at[1, 1], y_side)
     add_rows(side_sum.at[1], core_sum.at[2, :, halves[1]], side_in.at[1, 1])
-    wire.send("sx", side_sum.at[1], last_in.at[1], x_side)
+    wire.send(("sx", tag), side_sum.at[1], last_in.at[1], x_side)
     yield
-    wire.arrive(("sa", 0), side_in.at[0, 0], x_side)
-    wire.arrive(("sb", 0), side_in.at[1, 0], y_side)
-    wire.arrive("sy", last_in.at[0], y_side)
+    wire.arrive(("sa", tag, 0), side_in.at[0, 0], x_side)
+    wire.arrive(("sb", tag, 0), side_in.at[1, 0], y_side)
+    wire.arrive(("sy", tag), last_in.at[0], y_side)
     terms = core_sum.at[0, :, halves[0]], side_in.at[0, 0], last_in.at[0]
     add_rows(out.at[:, halves[0]], *terms)
-    wire.arrive("sx", last_in.at[1], x_side)
+    wire.arrive(("sx", tag), last_in.at[1], x_side)
     terms = core_sum.at[0, :, halves[1]], side_in.at[1, 0], last_in.at[1]
     add_rows(out.at[:, halves[1]], *terms)
 
@@ -778,7 +802,7 @@
     at = Place()
     wire = Wire(send_sems, recv_sems)
     enter(at.column_neighbours())
-    pieces = 4
+    pieces = 2
     height = normed.shape[0] // pieces
     scratch = core_in, core_sum, up_in, down_in, up_sum, down_sum
 
@@ -816,15 +840,15 @@
         next(flow)
     for flow in scatters:
         next(flow)
-    for index in range(pieces):
-        for _ in scatters[index]:
-            for flow in gathers[:index]:
-                next(flow, None)
-        norm_rows(index * height)
-        next(gathers[index])
-    for _ in range(4):
-        for flow in gathers:
-            next(flow, None)
+    for index in range(pieces + 3):
+        if index < pieces:
+            for _ in scatters[index]:
+                pass
+            norm_rows(index * height)
+            next(gathers[index])
+        for lag in (1, 2, 3):
+            if 0 <= index - lag < pieces:
+                next(gathers[index - lag], None)
     for flow in gathers:
         for _ in flow:
             pass
@@ -1069,7 +1093,7 @@
     wire = Wire(send_sems, recv_sems)
     enter(at.neighbours())
     scatter = plane_scatter_flow(
-        at, wire, part, d_input, core_in, core_sum, side_in, side_sum, last_in
+        at, wire, 0, part, d_input, core_in, core_sum, side_in, side_sum, last_in
     )
     next(scatter)
 
@@ -1106,50 +1130,43 @@
     wide = 8 // pieces
     up, down = at.line(jnp.minimum(at.zi + 1, 3)), at.line(jnp.maximum(at.zi - 1, 0))
 
-    def qkv_pass(goal, piece):
+    def qkv_rise(goal, piece, low_z, high_z):
         part = pl.ds(piece * wide, wide)
-
-        if goal > 0:
-
-            @pl.when(at.zi < goal)
-            def _():
-                @pl.when(at.zi == 0)
-                def _():
-                    up_sum[goal, part] = qkv_in[goal, part]
-
-                @pl.when(at.zi > 0)
-                def _():
-                    wire.arrive(("u", goal, piece), up_in.at[goal, part], down)
-                    up_sum[goal, part] = add(qkv_in[goal, part], up_in[goal, part])
-
+        here = (at.zi >= low_z) & (at.zi <= high_z)
+        source = up_sum.at[goal, part]
+
+        def climb():
+            wire.arrive(("u", goal, piece), up_in.at[goal, part], down)
+            up_sum[goal, part] = add(qkv_in[goal, part], up_in[goal, part])
+
+        key = "u", goal, piece
+        if low_z == 0:
+            first = qkv_in.at[goal, part]
+            wire.send(("u0", goal, piece), first, up_in.at[goal, part], up, at.zi == 0, recv=key)
+        if high_z > 0:
+            here = here & (at.zi > 0)
+            pl.when(here)(climb)
+            wire.send(key, source, up_in.at[goal, part], up, here)
+
+    def qkv_fall(goal, piece, low_z, high_z):
+        part = pl.ds(piece * wide, wide)
+        here = (at.zi >= low_z) & (at.zi <= high_z)
+        source = down_sum.at[goal, part]
+
+        def descend():
+            wire.arrive(("d", goal, piece), down_in.at[goal, part], up)
+            down_sum[goal, part] = add(qkv_in[goal, part], down_in[goal, part])
+
+        key = "d", goal, piece
+        if high_z == 3:
+            first = qkv_in.at[goal, part]
             wire.send(
-                ("u", goal, piece),
-                up_sum.at[goal, part],
-                up_in.at[goal, part],
-                up,
-                at.zi < goal,
+                ("d0", goal, piece), first, down_in.at[goal, part], down, at.zi == 3, recv=key
             )
-        back = 3 - goal
-        if back < 3:
-
-            @pl.when(at.zi > back)
-            def _():
-                @pl.when(at.zi == 3)
-                def _():
-                    down_sum[back, part] = qkv_in[back, part]
-
-                @pl.when(at.zi < 3)
-                def _():
-                    wire.arrive(("d", back, piece), down_in.at[back, part], up)
-                    down_sum[back, part] = add(qkv_in[back, part], down_in[back, part])
-
-            wire.send(
-                ("d", back, piece),
-                down_sum.at[back, part],
-                down_in.at[back, part],
-                down,
-                at.zi > back,
-            )
+        if low_z < 3:
+            here = here & (at.zi < 3)
+            pl.when(here)(descend)
+            wire.send(key, source, down_in.at[goal, part], down, here)
 
     proj_home = at.head_home()
 
@@ -1226,19 +1243,25 @@
                 qkv_total[part] = add(*terms)
 
     for piece in range(pieces):
-        qkv_pass(3, piece)
+        qkv_rise(3, piece, 0, 1)
+        qkv_fall(0, piece, 2, 3)
         if piece == 0:
             next(scatter)
+    for piece in range(pieces):
+        qkv_rise(3, piece, 2, 2)
+        qkv_fall(0, piece, 1, 1)
     for slot in range(4):
         proj_pass(slot)
     next(scatter)
     small_second()
     for piece in range(pieces):
-        qkv_pass(2, piece)
+        qkv_rise(2, piece, 0, 1)
+        qkv_fall(1, piece, 2, 3)
     for _ in scatter:
         pass
     for piece in range(pieces):
-        qkv_pass(1, piece)
+        qkv_rise(1, piece, 0, 0)
+        qkv_fall(2, piece, 3, 3)
     proj_last()
     for piece in range(pieces):
         qkv_last(piece)
@@ -1289,8 +1312,8 @@
         ]
         + plane_scratch(own, width)
         + [
-            pltpu.SemaphoreType.DMA((80,)),
-            pltpu.SemaphoreType.DMA((80,)),
+            pltpu.SemaphoreType.DMA((112,)),
+            pltpu.SemaphoreType.DMA((112,)),
             pltpu.SemaphoreType.DMA((3,)),
         ],
         compiler_params=comm_params(2),

time: 696 us -> 656 us (0.943)
  Pallas kernels: 543 us -> 503 us
    pallas_call x1, Pallas kernels: 107 us -> 88.1 us  [turn(): pl.pallas_call(turn_kernel, out_shape=(jax.ShapeDtypeStruct((own, width),...]
    pallas_call x1, Pallas kernels: 127 us -> 114 us  [close_units(): pl.pallas_call(close_units_kernel, out_shape=(jax.ShapeDtypeStruct((8, 3)...]
where the time goes in v8:
time: 656 us; the launch traced here: 646 us
  Pallas kernels  503 us (77%)
  matrix products  84.8 us (13%)
  local copies, waits for them, and re-layouts  40.3 us (6%)
  other arithmetic  16.7 us (3%)
    pallas_call x1, Pallas kernels, open_units(): pl.pallas_call(open_units_kernel, out_shape=(rows, rows, rows, jax.ShapeD...  117 us
    pallas_call x1, Pallas kernels, close_units(): pl.pallas_call(close_units_kernel, out_shape=(jax.ShapeDtypeStruct((8, 3)...  114 us
    pallas_call x1, Pallas kernels, close_heads(): pl.pallas_call(close_heads_kernel, out_shape=(jax.ShapeDtypeStruct((8, ro...  95 us
    pallas_call x1, Pallas kernels, open_heads(): pl.pallas_call(open_heads_kernel, out_shape=(jax.ShapeDtypeStruct((4, 8,...  89.1 us
    pallas_call x1, Pallas kernels, turn(): pl.pallas_call(turn_kernel, out_shape=(jax.ShapeDtypeStruct((own, width),...  88.1 us
    dot_general x3, matrix products, dot(): return jnp.dot(left_side, right_side, preferred_element_type=jnp.float32)  30.6 us
    dot_general x5, matrix products, contract_first(): lax.dot_general(left_side, right_side, (((0,), (0,)), ((), ())), preferre...  29.8 us
    dot_general x5, matrix products, contract_last(): lax.dot_general(left_side, right_side, (((1,), (1,)), ((), ())), preferre...  22.6 us

profile of v8, /device:TPU:11, one launch (start us, length us, event | category | flops | bytes accessed | tf_op | source)
XLA Modules:
  0.0 646.1 jit_solution(16932738862526585103)
XLA Ops:
  3.1 2.6 reshape.180
  6.7 0.9 maximum_bitcast_fusion
  7.6 1.7 reshape.181.qkv_in
  9.3 0.9 copy.167
  10.5 1.3 copy.166
  11.8 89.1 %open_heads.1 = (bf16[4,8,64,768]{3,2,1,0:T(8,128)(2,1)}, bf16[1,4,2,2,2,64,768]{6,5,4,3,2,1,0:T(8,128)(2,1)}, bf16[4,64,2048]{2,1,0:T(8,128)(2,1)}, bf16[8,128,2048]{2,1,0:T(8,128)(2,1)}, f32[4,8,8,128]{3,2,1,0:T(8,128)}) custom-call(bf16[8,64,768]{2,1,0:T(8,128)(2,1)} %reshape.181.qkv_in, bf16[8,1,64,768]{3,2,1,0:T(8,128)(2,1)} %bitcast.208, ...), custom_call_target="tpu_custom_call" | custom-call | tf_op jit(solution)/shard_map/open_heads/pallas_call | solution.py:527
  100.9 0.9 copy.169
  101.8 0.9 reshape_reshape.10
  107.1 1.0 copy.112.start_query
  108.1 1.9 fusion.28
  110.0 1.0 pad_maximum_fusion.2.sine
  111.2 0.9 copy.119
  112.1 1.0 pad_maximum_fusion.1.cosine
  113.1 116.6 %open_units.1 = (bf16[4,256,256]{2,1,0:T(8,128)(2,1)}, bf16[4,256,256]{2,1,0:T(8,128)(2,1)}, bf16[4,256,256]{2,1,0:T(8,128)(2,1)}, f32[4,2,256,256]{3,2,1,0:T(8,...) custom-call(bf16[8,128,2048]{2,1,0:T(8,128)(2,1)} %get-tuple-element, ...), custom_call_target="tpu_custom_call" | custom-call | tf_op jit(solution)/shard_map/open_units/pallas_call | solution.py:555
  229.7 1.2 copy.136
  231.0 2.2 copy.137
  233.1 6.3 fusion.33
  239.5 0.7 fusion.31
  240.2 1.0 copy-done.20
  241.2 3.5 copy-done.16
  244.7 12.4 %multiply_convert_fusion.1 = (bf16[1024,768]{1,0:T(8,128)(2,1)S(1)}, f32[1024,768]{1,0:T(8,128)}, f32[1024,768]{1,0:T(8,128)}, f32[1024,768]{1,0:T(8,128)}) fusion(f32[1024,768]{1,0:T(8,128)S(1)} %fusion.33, bf16[1024,2048]{1,0:T(8,128)(2,1)S(1)} %bitcast.244, bf16[2048,768]{1,0:T(8,128)(2,1)S(1)} %bitcast.212), kind=kOutput, calls=%fused_computation.21 | convolution fusion | flops 3273129984 | bytes 21495808 | tf_op jit(solution)/shard_map/dot_general | solution.py:39
  257.2 5.0 convolution_convert_fusion.1
  262.2 88.1 %turn.1 = (bf16[128,2048]{1,0:T(8,128)(2,1)}, f32[128,2048]{1,0:T(8,128)}, bf16[8,128,2048]{2,1,0:T(8,128)(2,1)}, f32[2,8,2048]{2,1,0:T(8,128)}) custom-call(bf16[8,128,2048]{2,1,0:T(8,128)(2,1)} %bitcast.201, bf16[128,2048]{1,0:T(8,128)(2,1)} %get-tuple-element.45.normed, bf16[128,2048]{1,0:T(8,128)(2,1)} %bitcast.230, f32[1,2048]{1,0:T(1,128)} %unstack.49.gain, ...), custom_call_target="tpu_custom_call" | custom-call | tf_op jit(solution)/shard_map/turn/pallas_call | solution.py:861
  350.3 11.9 %multiply_convert_fusion = (bf16[1024,768]{1,0:T(8,128)(2,1)S(1)}, bf16[1024,768]{1,0:T(8,128)(2,1)}) fusion(f32[1024,768]{1,0:T(8,128)} %get-tuple-element.114, f32[1024,768]{1,0:T(8,128)} %get-tuple-element.115, f32[1024,768]{1,0:T(8,128)} %copy-done.20, f32[1024,768]{1,0:T(8,128)} %get-tuple-element.148, bf16[1024,2048]{1,0:T(8,128)(2,1)} %bitcast.246, ...), kind=kOutput, calls=%fused_computation.20 | convolution fusion | flops 3229089792 | bytes 23068672 | tf_op jit(solution)/shard_map/dot_general | solution.py:39
  362.3 5.0 convolution_convert_fusion.3
  367.3 7.6 %convolution_convert_fusion.4 = bf16[2048,768]{1,0:T(8,128)(2,1)} fusion(bf16[1024,2048]{1,0:T(8,128)(2,1)} %bitcast.243, bf16[1024,768]{1,0:T(8,128)(2,1)S(1)} %get-tuple-element.118), kind=kOutput, calls=%fused_computation.7 | convolution fusion | flops 3222798336 | bytes 8912896 | tf_op jit(solution)/shard_map/dot_general | solution.py:33
  374.9 5.1 convolution_convert_fusion.5
  380.0 3.4 fusion.34
  383.5 5.1 add_convert_fusion
  388.6 114.0 %close_units.1 = (bf16[8,3,64,768]{3,2,1,0:T(8,128)(2,1)}, bf16[8,128,2048]{2,1,0:T(8,128)(2,1)}, f32[128,2048]{1,0:T(8,128)}, f32[2,8,2048]{2,1,0:T(8,128)}) custom-call(bf16[4,2,2,2,64,768]{5,4,3,2,1,0:T(8,128)(2,1)} %bitcast.206, bf16[4,2,2,2,64,768]{5,4,3,2,1,0:T(8,128)(2,1)} %bitcast.205, bf16[4,2,2,2,64,768]{5,4,3,2,1,0:T(8,128)(2,1)} %bitcast.204, ...), custom_call_target="tpu_custom_call" | custom-call | tf_op jit(solution)/shard_map/close_units/pallas_call | solution.py:1034
  502.6 3.8 convolution_convert_fusion.7
  506.4 0.9 reshape_reshape.12
  507.3 1.3 copy.122
  509.3 0.7 pad_maximum_fusion.3
  511.3 4.5 fusion.16
  519.1 2.2 copy.123
  521.2 0.8 convert_element_type.112
  522.1 7.7 %convolution_convert_fusion.2 = bf16[2048,768]{1,0:T(8,128)(2,1)} fusion(bf16[1024,2048]{1,0:T(8,128)(2,1)} %bitcast.199, bf16[1024,768]{1,0:T(8,128)(2,1)S(1)} %bitcast.223), kind=kOutput, calls=%fused_computation.5 | convolution fusion | flops 3222798336 | bytes 8912896 | tf_op jit(solution)/shard_map/dot_general | solution.py:33
  529.8 5.2 convolution_convert_fusion
  535.1 95.0 %close_heads.1 = (bf16[8,64,768]{2,1,0:T(8,128)(2,1)}, bf16[64,2048]{1,0:T(8,128)(2,1)}, f32[8,128]{1,0:T(8,128)}, f32[128,2048]{1,0:T(8,128)}) custom-call(bf16[4,8,64,768]{3,2,1,0:T(8,128)(2,1)} %bitcast.207, bf16[4,64,2048]{2,1,0:T(8,128)(2,1)} %bitcast.203, f32[8,4,8,128]{3,2,1,0:T(8,128)} %pad.19.small_in, bf16[8,128,2048]{2,1,0:T(8,128)(2,1)} %bitcast.202), custom_call_target="tpu_custom_call" | custom-call | tf_op jit(solution)/shard_map/close_heads/pallas_call | solution.py:1290
  630.0 2.5 add_convert_fusion.1
  633.9 1.8 convert_element_type.120
  636.4 0.9 convert_bitcast_fusion
  637.3 1.2 copy.130
  638.5 2.4 reshape.219
  640.9 1.9 copy.149
  642.8 2.1 fusion.22
  645.0 0.8 copy.172
  (100 shorter events, 15.5 us)
Async XLA Ops:
  6.2 3.1 copy-start.9
  6.6 3.6 copy-start.10
  6.7 3.6 copy-start.11
  230.9 8.5 %slice-start = ((s8[6291456]{0:T(1024)(128)(4,1)}), s8[2097152]{0:T(1024)(128)(4,1)S(1)}, s32[]{:S(2)}) async-start(s8[6291456]{0:T(1024)(128)(4,1)} %bitcast.194), calls=%async_computation | async-start | bytes 4194304
  233.1 6.3 slice-start.1
  239.5 1.8 copy-start.20
  239.5 5.3 copy-start.16
  240.2 17.0 %copy-start.2 = (bf16[1,4,2,2,2,64,768]{6,5,4,3,2,1,0:T(8,128)(2,1)}, bf16[1,4,2,2,2,64,768]{6,5,4,3,2,1,0:T(8,128)(2,1)S(1)}, u32[]{:S(2)}) copy-start(bf16[1,4,2,2,2,64,768]{6,5,4,3,2,1,0:T(8,128)(2,1)S(1)} %get-tuple-element.117) | copy-start | bytes 9437188
  240.2 16.9 %copy-start.4 = (bf16[1,4,2,2,2,64,768]{6,5,4,3,2,1,0:T(8,128)(2,1)}, bf16[1,4,2,2,2,64,768]{6,5,4,3,2,1,0:T(8,128)(2,1)S(1)}, u32[]{:S(2)}) copy-start(bf16[1,4,2,2,2,64,768]{6,5,4,3,2,1,0:T(8,128)(2,1)S(1)} %get-tuple-element.116) | copy-start | bytes 9437188
  257.2 5.0 copy-start.22
  350.3 12.0 %copy-start.18 = (bf16[8,128,2048]{2,1,0:T(8,128)(2,1)S(1)}, bf16[8,128,2048]{2,1,0:T(8,128)(2,1)}, u32[]{:S(2)}) copy-start(bf16[8,128,2048]{2,1,0:T(8,128)(2,1)} %get-tuple-element.47) | copy-start | bytes 12582916
  350.3 11.9 %copy-start.23 = (bf16[1024,768]{1,0:T(8,128)(2,1)S(1)}, bf16[1024,768]{1,0:T(8,128)(2,1)}, u32[]{:S(2)}) copy-start(bf16[1024,768]{1,0:T(8,128)(2,1)} %copy-done.22) | copy-start | bytes 4718596
  362.3 5.0 copy-start.15
  367.3 7.6 %copy-start.17 = (bf16[8,128,2048]{2,1,0:T(8,128)(2,1)S(1)}, bf16[8,128,2048]{2,1,0:T(8,128)(2,1)}, u32[]{:S(2)}) copy-start(bf16[8,128,2048]{2,1,0:T(8,128)(2,1)} %get-tuple-element.42) | copy-start | bytes 12582916
  367.3 7.6 %copy-start.21 = (bf16[1024,768]{1,0:T(8,128)(2,1)S(1)}, bf16[1024,768]{1,0:T(8,128)(2,1)}, u32[]{:S(2)}) copy-start(bf16[1024,768]{1,0:T(8,128)(2,1)} %get-tuple-element.119) | copy-start | bytes 4718596
  374.9 5.1 copy-start.19
  380.0 3.5 copy-start.3
  506.3 2.3 copy-start.14
  506.3 4.6 copy-start
  510.2 1.1 copy-start.6
  511.3 4.5 copy-start.12
  516.4 1.0 copy-start.5
  517.5 0.9 copy-start.7
  522.1 7.7 %copy-start.1 = (bf16[4,8,64,768]{3,2,1,0:T(8,128)(2,1)S(1)}, bf16[4,8,64,768]{3,2,1,0:T(8,128)(2,1)}, u32[]{:S(2)}) copy-start(bf16[4,8,64,768]{3,2,1,0:T(8,128)(2,1)} %get-tuple-element.39) | copy-start | bytes 9437188
  630.0 5.6 copy-start.8
  642.8 2.1 copy-start.13

commit v9 on v8

--- a/solution.py
+++ b/solution.py
@@ -83,7 +83,7 @@
 
 
 def gelu_parts(value):
-    phi = 0.5 * lax.erfc(-value * math.sqrt(0.5))
+    phi = 0.5 + 0.5 * lax.erf(value * math.sqrt(0.5))
     density = jnp.exp(-0.5 * value * value) * (1.0 / math.sqrt(2.0 * math.pi))
     return value * phi, phi + value * density
 
@@ -204,7 +204,7 @@
     mine = ffn_out.at[:, at.zi, at.x, at.y, at.c]
     own = pltpu.make_async_copy(ffn_in.at[at.unit], mine, own_sem)
     own.start()
-    for step in (4, 3, 5, 2, 6, 1, 7):
+    for step in steps:
         device, other = at.column(step)
         wire.send(("f", step), ffn_in.at[other], mine, device)
     own.wait()
@@ -892,10 +892,19 @@
     hat,
     inverse,
     gain,
+    proj,
+    queries,
+    key_rows,
+    value_rows,
+    probs_in,
+    cosine,
+    sine,
     ffn_out,
     branch_out,
+    d_mixed,
     d_first,
     norm_out,
+    d_context,
     first_in,
     second_sum,
     second_in,
@@ -982,6 +991,42 @@
             along = cotangent * near
             norm_out[0] += along[:8] + along[8:]
             norm_out[1] += cotangent[:8] + cotangent[8:]
+
+    pos = hat.shape[0] // 2
+    wide = proj.shape[0]
+    heads = wide // HEAD_DIM
+    scale = 1.0 / math.sqrt(HEAD_DIM)
+
+    def pull():
+        @pl.loop(0, 8)
+        def _(rank):
+            result = contract_last(branch_out[rank], proj[...]).astype(jnp.bfloat16)
+            for micro in range(2):
+                row, piece = row_place(rank, micro)
+                place = pl.ds(pl.multiple_of(piece * pos, pos), pos)
+                d_context[row, place] = result[micro * pos : (micro + 1) * pos]
+
+    def attend_back(first, last):
+        @pl.loop(first, last)
+        def _(row):
+            cos, sin = cosine[row], -sine[row]
+            target = pl.ds(pl.multiple_of((row % 2) * pos, pos), pos)
+            for head in range(heads):
+                cols = pl.ds(head * HEAD_DIM, HEAD_DIM)
+                probs, above = probs_in[row, head], d_context[row, :, cols]
+                d_probs = contract_last(above, value_rows[row, :, cols])
+                along = jnp.sum(probs * d_probs, axis=-1, keepdims=True)
+                d_scores = (probs * (d_probs - along)).astype(jnp.bfloat16)
+                d_query = dot(d_scores, key_rows[row, :, cols]) * scale
+                d_keys = contract_first(d_scores, queries[row, :, cols]) * scale
+                d_values = contract_first(probs.astype(jnp.bfloat16), above)
+                results = turned(d_query, cos, sin), turned(d_keys, cos, sin), d_values
+                for kind, result in enumerate(results):
+                    result = result.astype(jnp.bfloat16)
+                    place = pl.ds(kind * wide + head * HEAD_DIM, HEAD_DIM)
+                    for piece in range(4):
+                        source = result[piece * pos : (piece + 1) * pos]
+                        d_mixed[(row // 2) * 4 + piece, target, place] = source
 
     scatter = column_scatter_flow(
         at, wire, 0, part, d_normed, core_in, core_sum, up_in, down_in, up_sum, down_sum
@@ -1016,8 +1061,12 @@
     ffn_last(4)
     for _ in spread:
         pass
-    for turn in range(5, 8):
-        ffn_last(turn)
+    pull()
+    ffn_last(5)
+    attend_back(0, 2)
+    ffn_last(6)
+    attend_back(2, 4)
+    ffn_last(7)
     own_total.wait()
     for step in steps:
         if step:
@@ -1026,22 +1075,25 @@
     wire.drain()
 
 
-def close_units(grads, part, d_second, hat, inverse, gain):
+def close_units(grads, part, d_second, hat, inverse, gain, *heads):
     rows_own, unit_width = grads[0].shape[-2:]
     _, own, width = part.shape
     low_type = jnp.bfloat16
+    head_width = heads[0].shape[0]
     block = (rows_own, unit_width)
     return pl.pallas_call(
         close_units_kernel,
         out_shape=(
             jax.ShapeDtypeStruct((8, 3) + block, low_type),
             jax.ShapeDtypeStruct((8, own, width), low_type),
+            jax.ShapeDtypeStruct((8, own, 3 * head_width), low_type),
             jax.ShapeDtypeStruct((own, width), jnp.float32),
             jax.ShapeDtypeStruct((2, 8, width), jnp.float32),
         ),
-        in_specs=[VMEM] * 8,
-        out_specs=(ANY, ANY, VMEM, VMEM),
+        in_specs=[VMEM] * 15,
+        out_specs=(ANY, VMEM, VMEM, VMEM, VMEM),
         scratch_shapes=[
+            pltpu.VMEM((4, 2 * own, head_width), low_type),
             pltpu.VMEM((8, 3, 2) + block, low_type),
             pltpu.VMEM((8, 3) + block, low_type),
             pltpu.VMEM((8, 3) + block, low_type),
@@ -1057,7 +1109,7 @@
         ],
         compiler_params=comm_params(3),
         name="close_units",
-    )(*grads, part, d_second, hat, inverse, gain)
+    )(*grads, part, d_second, hat, inverse, gain, *heads)
 
 
 def close_heads_kernel(
@@ -1409,18 +1461,7 @@
             unit_parts(up_weight, down_weight),
         )
     )
-    rows_shape = (x_size * micro_count, row_length, heads_here, HEAD_DIM)
-    queries, key_rows, value_rows = (
-        values.reshape(rows_shape) for values in (queries, key_rows, value_rows)
-    )
-    probs_low = low(probs)
     context = context.reshape(-1, head_width)
-    cosine, sine = cosine[:, :, None, :], sine[:, :, None, :]
-    score_scale = 1.0 / math.sqrt(HEAD_DIM)
-
-    def pair(spec, left_side, right_side):
-        return jnp.einsum(spec, left_side, right_side, preferred_element_type=jnp.float32)
-
     normed_all = normed_all.reshape(-1, width)
     up_here, down_here = ffn.reshape(2, -1, unit_width)
 
@@ -1448,14 +1489,21 @@
         unit_grad(normed_all, up_low),
         unit_grad(down_low, active),
     )
-    ffn_part, branch_all, d_first, norm_grads = close_units(
+    ffn_part, branch_all, d_mixed, d_first, norm_grads = close_units(
         ffn_grads,
         d_normed_part.reshape(unit_ways, own, width),
         d_second,
         hat_one,
         inverse_one,
         gain_one,
-    )
+        proj_here,
+        queries,
+        key_rows,
+        value_rows,
+        probs,
+        *tables[:2],
+    )
+    d_mixed = d_mixed.reshape(-1, 3 * head_width)
     gain_one_grad, shift_one_grad = jnp.sum(norm_grads, axis=1)
     branch_all = branch_all.reshape(-1, width)
     small_grads = jnp.stack([gain_one_grad, shift_one_grad, gain_two_grad, shift_two_grad])
@@ -1464,19 +1512,6 @@
     small_grads = jnp.pad(small_grads, ((0, 0), (0, 0), (0, -small_grads.shape[2] % 8), (0, 0)))
 
     proj_part = low(contract_first(context, branch_all)).reshape(4, rows_own, width)
-    d_context = to_rows(low(contract_last(branch_all, proj_here)))
-    d_context = d_context.reshape(x_size * micro_count, row_length, heads_here, HEAD_DIM)
-    d_probs = pair("rqhd,rkhd->rhqk", d_context, value_rows)
-    d_scores = low(probs * (d_probs - jnp.sum(probs * d_probs, axis=-1, keepdims=True)))
-    d_query = pair("rhqk,rkhd->rqhd", d_scores, key_rows) * score_scale
-    d_keys = pair("rhqk,rqhd->rkhd", d_scores, queries) * score_scale
-    d_values = pair("rhqk,rqhd->rkhd", probs_low, d_context)
-    d_mixed = low(
-        jnp.stack(
-            [rotate(d_query, cosine, -sine), rotate(d_keys, cosine, -sine), d_values], axis=2
-        )
-    )
-    d_mixed = from_rows(d_mixed.reshape(x_size * micro_count, row_length, 3 * head_width))
     d_input = low(contract_last(d_mixed, qkv_here)).reshape(head_ways, own, width)
     qkv_part = low(contract_first(x_all, d_mixed))
     qkv_part, proj_part, small_grads, d_input = close_heads(

time: 656 us -> 612 us (0.933)
  Pallas kernels: 503 us -> 487 us
  matrix products: 84.8 us -> 70 us
  local copies, waits for them, and re-layouts: 40.3 us -> 29.6 us
    pallas_call x1, Pallas kernels: 117 us -> 100 us  [open_units(): pl.pallas_call(open_units_kernel, out_shape=(rows, rows, rows, jax.ShapeD...]
    pallas_call x1, Pallas kernels: 114 us -> 124 us  [close_units(): pl.pallas_call(close_units_kernel, out_shape=(jax.ShapeDtypeStruct((8, 3)...]
    dot_general x3, matrix products: 30.6 us -> 21.2 us  [dot(): return jnp.dot(left_side, right_side, preferred_element_type=jnp.float32)]
    pallas_call x1, Pallas kernels: 88.1 us -> 81.2 us  [turn(): pl.pallas_call(turn_kernel, out_shape=(jax.ShapeDtypeStruct((own, width),...]
    dot_general x5 -> x4, matrix products: 22.6 us -> 18.6 us  [contract_last(): lax.dot_general(left_side, right_side, (((1,), (1,)), ((), ())), preferre...]
where the time goes in v9:
time: 612 us; the launch traced here: 603 us
  Pallas kernels  487 us (80%)
  matrix products  70 us (11%)
  local copies, waits for them, and re-layouts  29.6 us (5%)
  other arithmetic  14.4 us (2%)
    pallas_call x1, Pallas kernels, close_units(): pl.pallas_call(close_units_kernel, out_shape=(jax.ShapeDtypeStruct((8, 3)...  124 us
    pallas_call x1, Pallas kernels, open_units(): pl.pallas_call(open_units_kernel, out_shape=(rows, rows, rows, jax.ShapeD...  100 us
    pallas_call x1, Pallas kernels, close_heads(): pl.pallas_call(close_heads_kernel, out_shape=(jax.ShapeDtypeStruct((8, ro...  95.1 us
    pallas_call x1, Pallas kernels, open_heads(): pl.pallas_call(open_heads_kernel, out_shape=(jax.ShapeDtypeStruct((4, 8,...  86.9 us
    pallas_call x1, Pallas kernels, turn(): pl.pallas_call(turn_kernel, out_shape=(jax.ShapeDtypeStruct((own, width),...  81.2 us
    dot_general x5, matrix products, contract_first(): lax.dot_general(left_side, right_side, (((0,), (0,)), ((), ())), preferre...  30.2 us
    dot_general x3, matrix products, dot(): return jnp.dot(left_side, right_side, preferred_element_type=jnp.float32)  21.2 us
    dot_general x4, matrix products, contract_last(): lax.dot_general(left_side, right_side, (((1,), (1,)), ((), ())), preferre...  18.6 us

profile of v9, /device:TPU:11, one launch (start us, length us, event | category | flops | bytes accessed | tf_op | source)
XLA Modules:
  0.0 602.7 jit_solution(973765854144138682)
XLA Ops:
  0.7 0.7 maximum_convert_fusion
  1.5 0.7 convert_element_type.86
  3.1 2.6 reshape.156
  6.7 0.9 maximum_bitcast_fusion
  7.6 1.7 reshape.157.qkv_in
  9.3 0.9 copy.96
  10.5 1.3 copy.95
  11.8 86.9 %open_heads.1 = (bf16[4,8,64,768]{3,2,1,0:T(8,128)(2,1)}, bf16[1,4,2,2,2,64,768]{6,5,4,3,2,1,0:T(8,128)(2,1)}, bf16[4,64,2048]{2,1,0:T(8,128)(2,1)}, bf16[8,128,2048]{2,1,0:T(8,128)(2,1)}, f32[4,8,8,128]{3,2,1,0:T(8,128)}) custom-call(bf16[8,64,768]{2,1,0:T(8,128)(2,1)} %reshape.157.qkv_in, bf16[8,1,64,768]{3,2,1,0:T(8,128)(2,1)} %bitcast.167, ...), custom_call_target="tpu_custom_call" | custom-call | tf_op jit(solution)/shard_map/open_heads/pallas_call | solution.py:527
  98.7 0.9 copy.97
  99.6 0.9 reshape_reshape.6
  100.9 0.7 unstack.51.shift
  101.6 0.7 unstack.41.gain
  102.3 0.7 unstack.49.gain
  102.9 0.7 unstack.43.shift
  104.3 0.6 slice_bitcast_fusion.7
  104.9 1.0 copy.62.start_query
  105.9 1.9 fusion.13
  107.8 1.0 pad_maximum_fusion.1.sine
  108.8 1.0 pad_maximum_fusion.cosine
  109.8 100.1 %open_units.1 = (bf16[4,256,256]{2,1,0:T(8,128)(2,1)}, bf16[4,256,256]{2,1,0:T(8,128)(2,1)}, bf16[4,256,256]{2,1,0:T(8,128)(2,1)}, f32[4,2,256,256]{3,2,1,0:T(8,...) custom-call(bf16[8,128,2048]{2,1,0:T(8,128)(2,1)} %get-tuple-element, ...), custom_call_target="tpu_custom_call" | custom-call | tf_op jit(solution)/shard_map/open_units/pallas_call | solution.py:555
  210.0 6.3 %fusion.19 = f32[1024,768]{1,0:T(8,128)S(1)} fusion(bf16[1024,2048]{1,0:T(8,128)(2,1)} %bitcast.193, bf16[2048,768]{1,0:T(8,128)(2,1)} %bitcast.199), kind=kOutput, calls=%fused_computation.69 | convolution fusion | flops 3221225472 | bytes 10485760 | tf_op jit(solution)/shard_map/dot_general | solution.py:39
  216.3 0.7 fusion.17
  217.1 1.0 copy-done.18
  218.1 3.5 copy-done.13
  221.6 5.3 multiply_convert_fusion.1
  226.8 5.1 convolution_convert_fusion.1
  231.9 81.2 %turn.1 = (bf16[128,2048]{1,0:T(8,128)(2,1)}, f32[128,2048]{1,0:T(8,128)}, bf16[8,128,2048]{2,1,0:T(8,128)(2,1)}, f32[2,8,2048]{2,1,0:T(8,128)}) custom-call(bf16[8,128,2048]{2,1,0:T(8,128)(2,1)} %bitcast.160, bf16[128,2048]{1,0:T(8,128)(2,1)} %get-tuple-element.46.normed, bf16[128,2048]{1,0:T(8,128)(2,1)} %bitcast.182, f32[1,2048]{1,0:T(1,128)} %unstack.49.gain, ...), custom_call_target="tpu_custom_call" | custom-call | tf_op jit(solution)/shard_map/turn/pallas_call | solution.py:861
  313.1 9.7 %multiply_convert_fusion = (bf16[1024,768]{1,0:T(8,128)(2,1)S(1)}, bf16[1024,768]{1,0:T(8,128)(2,1)}) fusion(f32[1024,768]{1,0:T(8,128)} %get-tuple-element.105, f32[1024,768]{1,0:T(8,128)} %copy-done.18, f32[1024,768]{1,0:T(8,128)} %get-tuple-element.132, bf16[1024,2048]{1,0:T(8,128)(2,1)} %bitcast.197, bf16[2048,768]{1,0:T(8,128)(2,1)} %bitcast.174), kind=kOutput, calls=%fused_computation.17 | convolution fusion | flops 3231449088 | bytes 19922944 | tf_op jit(solution)/shard_map/dot_general | solution.py:39
  322.8 5.0 convolution_convert_fusion.2
  327.9 7.6 %convolution_convert_fusion.3 = bf16[2048,768]{1,0:T(8,128)(2,1)} fusion(bf16[1024,2048]{1,0:T(8,128)(2,1)} %bitcast.194, bf16[1024,768]{1,0:T(8,128)(2,1)S(1)} %get-tuple-element.108), kind=kOutput, calls=%fused_computation.6 | convolution fusion | flops 3222798336 | bytes 8912896 | tf_op jit(solution)/shard_map/dot_general | solution.py:33
  335.5 4.9 convolution_convert_fusion.4
  340.4 3.4 fusion.20
  343.9 5.1 add_convert_fusion
  348.9 123.8 %close_units.1 = (bf16[8,3,64,768]{3,2,1,0:T(8,128)(2,1)}, bf16[8,128,2048]{2,1,0:T(8,128)(2,1)}, bf16[8,128,768]{2,1,0:T(8,128)(2,1)}, f32[128,2048]{1,0:T(8,128)}, f32[2,8,2048]{2,1,0:T(8,128)}) custom-call(bf16[4,2,2,2,64,768]{5,4,3,2,1,0:T(8,128)(2,1)} %bitcast.165, bf16[4,2,2,2,64,768]{5,4,3,2,1,0:T(8,128)(2,1)} %bitcast.164, ...), custom_call_target="tpu_custom_call" | custom-call | tf_op jit(solution)/shard_map/close_units/pallas_call | solution.py:1084
  472.8 8.1 %bitcast_convert_fusion = bf16[2048,768]{1,0:T(8,128)(2,1)} fusion(bf16[8,128,2048]{2,1,0:T(8,128)(2,1)} %get-tuple-element.39.x_all, bf16[8,128,768]{2,1,0:T(8,128)(2,1)} %get-tuple-element.57), kind=kOutput, calls=%fused_computation.1 | convolution fusion | flops 3222798336 | bytes 8912896 | tf_op jit(solution)/shard_map/dot_general | solution.py:33
  481.2 0.7 pad.19.small_in
  481.8 4.6 fusion.8
  486.4 5.0 convolution_convert_fusion
  491.4 95.1 %close_heads.1 = (bf16[8,64,768]{2,1,0:T(8,128)(2,1)}, bf16[64,2048]{1,0:T(8,128)(2,1)}, f32[8,128]{1,0:T(8,128)}, f32[128,2048]{1,0:T(8,128)}) custom-call(bf16[4,8,64,768]{3,2,1,0:T(8,128)(2,1)} %bitcast.166, bf16[4,64,2048]{2,1,0:T(8,128)(2,1)} %bitcast.162, f32[8,4,8,128]{3,2,1,0:T(8,128)} %pad.19.small_in, bf16[8,128,2048]{2,1,0:T(8,128)(2,1)} %bitcast.161), custom_call_target="tpu_custom_call" | custom-call | tf_op jit(solution)/shard_map/close_heads/pallas_call | solution.py:1342
  586.5 2.5 add_convert_fusion.1
  589.1 0.7 slice.89
  590.4 1.8 convert_element_type.102
  592.9 0.9 convert_bitcast_fusion
  593.8 1.2 copy.69
  595.0 2.4 reshape.189
  597.4 1.9 copy.85
  599.3 2.1 fusion.10
  601.5 0.8 copy.100
  (71 shorter events, 4.9 us)
Async XLA Ops:
  6.2 3.1 copy-start.7
  6.6 3.6 copy-start.8
  6.7 3.6 copy-start.9
  210.0 6.3 %copy-start = (bf16[2,4,2,2,2,64,768]{6,5,4,3,2,1,0:T(8,128)(2,1)S(1)}, bf16[2,4,2,2,2,64,768]{6,5,4,3,2,1,0:T(8,128)(2,1)}, u32[]{:S(2)}) copy-start(bf16[2,4,2,2,2,64,768]{6,5,4,3,2,1,0:T(8,128)(2,1)} %get-tuple-element.45) | copy-start | bytes 18874372
  216.3 1.8 copy-start.18
  216.3 5.3 copy-start.13
  217.1 9.8 %copy-start.2 = (bf16[1,4,2,2,2,64,768]{6,5,4,3,2,1,0:T(8,128)(2,1)}, bf16[1,4,2,2,2,64,768]{6,5,4,3,2,1,0:T(8,128)(2,1)S(1)}, u32[]{:S(2)}) copy-start(bf16[1,4,2,2,2,64,768]{6,5,4,3,2,1,0:T(8,128)(2,1)S(1)} %get-tuple-element.107) | copy-start | bytes 9437188
  217.1 9.8 %copy-start.4 = (bf16[1,4,2,2,2,64,768]{6,5,4,3,2,1,0:T(8,128)(2,1)}, bf16[1,4,2,2,2,64,768]{6,5,4,3,2,1,0:T(8,128)(2,1)S(1)}, u32[]{:S(2)}) copy-start(bf16[1,4,2,2,2,64,768]{6,5,4,3,2,1,0:T(8,128)(2,1)S(1)} %get-tuple-element.106) | copy-start | bytes 9437188
  226.8 5.1 copy-start.20
  313.1 9.7 %copy-start.15 = (bf16[8,128,2048]{2,1,0:T(8,128)(2,1)S(1)}, bf16[8,128,2048]{2,1,0:T(8,128)(2,1)}, u32[]{:S(2)}) copy-start(bf16[8,128,2048]{2,1,0:T(8,128)(2,1)} %get-tuple-element.48) | copy-start | bytes 12582916
  313.1 9.7 %copy-start.21 = (bf16[1024,768]{1,0:T(8,128)(2,1)S(1)}, bf16[1024,768]{1,0:T(8,128)(2,1)}, u32[]{:S(2)}) copy-start(bf16[1024,768]{1,0:T(8,128)(2,1)} %copy-done.20) | copy-start | bytes 4718596
  322.8 5.0 copy-start.12
  327.8 7.6 %copy-start.14 = (bf16[8,128,2048]{2,1,0:T(8,128)(2,1)S(1)}, bf16[8,128,2048]{2,1,0:T(8,128)(2,1)}, u32[]{:S(2)}) copy-start(bf16[8,128,2048]{2,1,0:T(8,128)(2,1)} %get-tuple-element.43) | copy-start | bytes 12582916
  327.9 7.6 %copy-start.19 = (bf16[1024,768]{1,0:T(8,128)(2,1)S(1)}, bf16[1024,768]{1,0:T(8,128)(2,1)}, u32[]{:S(2)}) copy-start(bf16[1024,768]{1,0:T(8,128)(2,1)} %get-tuple-element.109) | copy-start | bytes 4718596
  335.5 4.9 copy-start.16
  340.4 3.5 copy-start.3
  472.7 8.1 %copy-start.11 = (f32[2,8,2048]{2,1,0:T(8,128)S(1)}, f32[2,8,2048]{2,1,0:T(8,128)}, u32[]{:S(2)}) copy-start(f32[2,8,2048]{2,1,0:T(8,128)} %get-tuple-element.60) | copy-start | bytes 393220
  472.8 9.1 %copy-start.5 = (bf16[8,128,256]{2,1,0:T(8,128)(2,1)S(1)}, bf16[8,128,256]{2,1,0:T(8,128)(2,1)}, u32[]{:S(2)}) copy-start(bf16[8,128,256]{2,1,0:T(8,128)(2,1)} %get-tuple-element.58) | copy-start | bytes 1572868
  481.8 4.6 copy-start.1
  481.8 4.6 copy-start.17
  586.5 5.6 copy-start.6
  599.3 2.1 copy-start.10

commit v10 on v9

--- a/solution.py
+++ b/solution.py
@@ -123,6 +123,11 @@
 
     def send_to_slot(self, key, source, target, device, slot, span, when):
         copy = self.copy(key, source, target, device, slot, span)
+        pl.when(when)(copy.start)
+        self.sent.append((copy, when))
+
+    def send_between(self, key, receive, slot, source, target, device, when):
+        copy = self.copy(key, source, target, device, slot, recv=receive)
         pl.when(when)(copy.start)
         self.sent.append((copy, when))
 
@@ -1061,12 +1066,11 @@
     ffn_last(4)
     for _ in spread:
         pass
+    ffn_last(5)
     pull()
-    ffn_last(5)
-    attend_back(0, 2)
     ffn_last(6)
-    attend_back(2, 4)
     ffn_last(7)
+    attend_back(0, 4)
     own_total.wait()
     for step in steps:
         if step:
@@ -1149,12 +1153,6 @@
     )
     next(scatter)
 
-    def add(*terms):
-        whole = terms[0].astype(jnp.float32)
-        for term in terms[1:]:
-            whole = whole + term.astype(jnp.float32)
-        return whole.astype(jnp.bfloat16)
-
     for delta in range(1, 8):
         device, other = at.plane(delta)
         wire.send(("s", delta), small_in.at[other], small_plane.at[at.rank], device)
@@ -1182,6 +1180,10 @@
     wide = 8 // pieces
     up, down = at.line(jnp.minimum(at.zi + 1, 3)), at.line(jnp.maximum(at.zi - 1, 0))
 
+    def add_ranks(piece, out, *terms):
+        for rank in range(piece * wide, piece * wide + wide):
+            add_rows(out.at[rank], *(term.at[rank] for term in terms))
+
     def qkv_rise(goal, piece, low_z, high_z):
         part = pl.ds(piece * wide, wide)
         here = (at.zi >= low_z) & (at.zi <= high_z)
@@ -1189,7 +1191,7 @@
 
         def climb():
             wire.arrive(("u", goal, piece), up_in.at[goal, part], down)
-            up_sum[goal, part] = add(qkv_in[goal, part], up_in[goal, part])
+            add_ranks(piece, up_sum.at[goal], qkv_in.at[goal], up_in.at[goal])
 
         key = "u", goal, piece
         if low_z == 0:
@@ -1207,7 +1209,7 @@
 
         def descend():
             wire.arrive(("d", goal, piece), down_in.at[goal, part], up)
-            down_sum[goal, part] = add(qkv_in[goal, part], down_in[goal, part])
+            add_ranks(piece, down_sum.at[goal], qkv_in.at[goal], down_in.at[goal])
 
         key = "d", goal, piece
         if high_z == 3:
@@ -1285,14 +1287,24 @@
 
             @pl.when(at.zi == goal)
             def _():
-                terms = [qkv_in[goal, part]]
+                terms = [qkv_in.at[goal]]
                 if goal > 0:
                     wire.arrive(("u", goal, piece), up_in.at[goal, part], down)
-                    terms.append(up_in[goal, part])
+                    terms.append(up_in.at[goal])
                 if goal < 3:
                     wire.arrive(("d", goal, piece), down_in.at[goal, part], up)
-                    terms.append(down_in[goal, part])
-                qkv_total[part] = add(*terms)
+                    terms.append(down_in.at[goal])
+                add_ranks(piece, qkv_total, *terms)
+
+    def qkv_owner(piece):
+        for core in range(wide):
+            rank = piece * wide + core
+            target = (at.zo, at.zi, rank // 4, rank // 2 % 2, rank % 2)
+            source, place = qkv_total.at[rank], qkv_out.at[at.rank]
+            wire.number("qr", 8)
+            wire.send_between(("q", rank), "qr", at.rank, source, place, target, at.rank != rank)
+            own = pltpu.make_async_copy(source, place, own_sems.at[1])
+            pl.when(at.rank == rank)(own.start)
 
     for piece in range(pieces):
         qkv_rise(3, piece, 0, 1)
@@ -1317,17 +1329,11 @@
     proj_last()
     for piece in range(pieces):
         qkv_last(piece)
-    own_qkv = pltpu.make_async_copy(
-        qkv_total.at[at.rank], qkv_out.at[at.rank], own_sems.at[1]
-    )
-    own_qkv.start()
+        qkv_owner(piece)
+    pltpu.make_async_copy(qkv_total.at[at.rank], qkv_out.at[at.rank], own_sems.at[1]).wait()
     for delta in range(1, 8):
         device, other = at.plane(delta)
-        wire.send(("q", delta), qkv_total.at[other], qkv_out.at[at.rank], device)
-    own_qkv.wait()
-    for delta in range(1, 8):
-        device, other = at.plane(delta)
-        wire.arrive(("q", delta), qkv_out.at[other], device)
+        wire.arrive_slot("qr", qkv_out.at[other], device, other, 8, at.rank != other)
     small_last()
     wire.arrive("o", proj_out, holder_device, at.rank != holder)
     wire.drain()
@@ -1435,11 +1441,6 @@
         values = values.reshape((x_size, chunk_count, micro_count, pos_count) + inner)
         return jnp.swapaxes(values, 1, 2).reshape((x_size * micro_count, row_length) + inner)
 
-    def from_rows(values):
-        inner = values.shape[2:]
-        values = values.reshape((x_size, micro_count, chunk_count, pos_count) + inner)
-        return jnp.swapaxes(values, 1, 2).reshape((head_ways * own,) + inner)
-
     row_marks = to_rows(marks.reshape(head_ways * own, 3))
     cosine, sine = rotary_tables(row_marks[..., 2])
     tables = (

time: 612 us -> 604 us (0.987)
  Pallas kernels: 487 us -> 480 us
where the time goes in v10:
time: 604 us; the launch traced here: 595 us
  Pallas kernels  480 us (79%)
  matrix products  70 us (12%)
  local copies, waits for them, and re-layouts  29.6 us (5%)
  other arithmetic  14.4 us (2%)
    pallas_call x1, Pallas kernels, close_units(): pl.pallas_call(close_units_kernel, out_shape=(jax.ShapeDtypeStruct((8, 3)...  120 us
    pallas_call x1, Pallas kernels, open_units(): pl.pallas_call(open_units_kernel, out_shape=(rows, rows, rows, jax.ShapeD...  100 us
    pallas_call x1, Pallas kernels, close_heads(): pl.pallas_call(close_heads_kernel, out_shape=(jax.ShapeDtypeStruct((8, ro...  91.8 us
    pallas_call x1, Pallas kernels, open_heads(): pl.pallas_call(open_heads_kernel, out_shape=(jax.ShapeDtypeStruct((4, 8,...  86.9 us
    pallas_call x1, Pallas kernels, turn(): pl.pallas_call(turn_kernel, out_shape=(jax.ShapeDtypeStruct((own, width),...  81.2 us
    dot_general x5, matrix products, contract_first(): lax.dot_general(left_side, right_side, (((0,), (0,)), ((), ())), preferre...  30.2 us
    dot_general x3, matrix products, dot(): return jnp.dot(left_side, right_side, preferred_element_type=jnp.float32)  21.2 us
    dot_general x4, matrix products, contract_last(): lax.dot_general(left_side, right_side, (((1,), (1,)), ((), ())), preferre...  18.6 us

profile of v10, /device:TPU:11, one launch (start us, length us, event | category | flops | bytes accessed | tf_op | source)
XLA Modules:
  0.0 595.5 jit_solution(13802366000830699141)
XLA Ops:
  0.7 0.7 maximum_convert_fusion
  1.5 0.7 convert_element_type.86
  3.1 2.6 reshape.156
  6.7 0.9 maximum_bitcast_fusion
  7.6 1.7 reshape.157.qkv_in
  9.3 0.9 copy.96
  10.5 1.3 copy.95
  11.8 86.9 %open_heads.1 = (bf16[4,8,64,768]{3,2,1,0:T(8,128)(2,1)}, bf16[1,4,2,2,2,64,768]{6,5,4,3,2,1,0:T(8,128)(2,1)}, bf16[4,64,2048]{2,1,0:T(8,128)(2,1)}, bf16[8,128,2048]{2,1,0:T(8,128)(2,1)}, f32[4,8,8,128]{3,2,1,0:T(8,128)}) custom-call(bf16[8,64,768]{2,1,0:T(8,128)(2,1)} %reshape.157.qkv_in, bf16[8,1,64,768]{3,2,1,0:T(8,128)(2,1)} %bitcast.167, ...), custom_call_target="tpu_custom_call" | custom-call | tf_op jit(solution)/shard_map/open_heads/pallas_call | solution.py:532
  98.7 0.9 copy.97
  99.6 0.9 reshape_reshape.6
  100.9 0.7 unstack.51.shift
  101.6 0.7 unstack.41.gain
  102.3 0.7 unstack.49.gain
  102.9 0.7 unstack.43.shift
  104.3 0.6 slice_bitcast_fusion.7
  104.9 1.0 copy.62.start_query
  105.9 1.9 fusion.13
  107.8 1.0 pad_maximum_fusion.1.sine
  108.8 1.0 pad_maximum_fusion.cosine
  109.8 100.1 %open_units.1 = (bf16[4,256,256]{2,1,0:T(8,128)(2,1)}, bf16[4,256,256]{2,1,0:T(8,128)(2,1)}, bf16[4,256,256]{2,1,0:T(8,128)(2,1)}, f32[4,2,256,256]{3,2,1,0:T(8,...) custom-call(bf16[8,128,2048]{2,1,0:T(8,128)(2,1)} %get-tuple-element, ...), custom_call_target="tpu_custom_call" | custom-call | tf_op jit(solution)/shard_map/open_units/pallas_call | solution.py:560
  210.0 6.3 %fusion.19 = f32[1024,768]{1,0:T(8,128)S(1)} fusion(bf16[1024,2048]{1,0:T(8,128)(2,1)} %bitcast.193, bf16[2048,768]{1,0:T(8,128)(2,1)} %bitcast.199), kind=kOutput, calls=%fused_computation.69 | convolution fusion | flops 3221225472 | bytes 10485760 | tf_op jit(solution)/shard_map/dot_general | solution.py:39
  216.3 0.7 fusion.17
  217.1 1.0 copy-done.18
  218.1 3.5 copy-done.13
  221.6 5.3 multiply_convert_fusion.1
  226.8 5.1 convolution_convert_fusion.1
  231.9 81.2 %turn.1 = (bf16[128,2048]{1,0:T(8,128)(2,1)}, f32[128,2048]{1,0:T(8,128)}, bf16[8,128,2048]{2,1,0:T(8,128)(2,1)}, f32[2,8,2048]{2,1,0:T(8,128)}) custom-call(bf16[8,128,2048]{2,1,0:T(8,128)(2,1)} %bitcast.160, bf16[128,2048]{1,0:T(8,128)(2,1)} %get-tuple-element.46.normed, bf16[128,2048]{1,0:T(8,128)(2,1)} %bitcast.182, f32[1,2048]{1,0:T(1,128)} %unstack.49.gain, ...), custom_call_target="tpu_custom_call" | custom-call | tf_op jit(solution)/shard_map/turn/pallas_call | solution.py:866
  313.1 9.7 %multiply_convert_fusion = (bf16[1024,768]{1,0:T(8,128)(2,1)S(1)}, bf16[1024,768]{1,0:T(8,128)(2,1)}) fusion(f32[1024,768]{1,0:T(8,128)} %get-tuple-element.105, f32[1024,768]{1,0:T(8,128)} %copy-done.18, f32[1024,768]{1,0:T(8,128)} %get-tuple-element.132, bf16[1024,2048]{1,0:T(8,128)(2,1)} %bitcast.197, bf16[2048,768]{1,0:T(8,128)(2,1)} %bitcast.174), kind=kOutput, calls=%fused_computation.17 | convolution fusion | flops 3231449088 | bytes 19922944 | tf_op jit(solution)/shard_map/dot_general | solution.py:39
  322.8 5.0 convolution_convert_fusion.2
  327.9 7.6 %convolution_convert_fusion.3 = bf16[2048,768]{1,0:T(8,128)(2,1)} fusion(bf16[1024,2048]{1,0:T(8,128)(2,1)} %bitcast.194, bf16[1024,768]{1,0:T(8,128)(2,1)S(1)} %get-tuple-element.108), kind=kOutput, calls=%fused_computation.6 | convolution fusion | flops 3222798336 | bytes 8912896 | tf_op jit(solution)/shard_map/dot_general | solution.py:33
  335.5 4.9 convolution_convert_fusion.4
  340.4 3.4 fusion.20
  343.9 5.1 add_convert_fusion
  348.9 119.9 %close_units.1 = (bf16[8,3,64,768]{3,2,1,0:T(8,128)(2,1)}, bf16[8,128,2048]{2,1,0:T(8,128)(2,1)}, bf16[8,128,768]{2,1,0:T(8,128)(2,1)}, f32[128,2048]{1,0:T(8,128)}, f32[2,8,2048]{2,1,0:T(8,128)}) custom-call(bf16[4,2,2,2,64,768]{5,4,3,2,1,0:T(8,128)(2,1)} %bitcast.165, bf16[4,2,2,2,64,768]{5,4,3,2,1,0:T(8,128)(2,1)} %bitcast.164, ...), custom_call_target="tpu_custom_call" | custom-call | tf_op jit(solution)/shard_map/close_units/pallas_call | solution.py:1088
  468.9 8.1 %bitcast_convert_fusion = bf16[2048,768]{1,0:T(8,128)(2,1)} fusion(bf16[8,128,2048]{2,1,0:T(8,128)(2,1)} %get-tuple-element.39.x_all, bf16[8,128,768]{2,1,0:T(8,128)(2,1)} %get-tuple-element.57), kind=kOutput, calls=%fused_computation.1 | convolution fusion | flops 3222798336 | bytes 8912896 | tf_op jit(solution)/shard_map/dot_general | solution.py:33
  477.2 0.7 pad.19.small_in
  477.9 4.6 fusion.8
  482.5 5.0 convolution_convert_fusion
  487.5 91.8 %close_heads.1 = (bf16[8,64,768]{2,1,0:T(8,128)(2,1)}, bf16[64,2048]{1,0:T(8,128)(2,1)}, f32[8,128]{1,0:T(8,128)}, f32[128,2048]{1,0:T(8,128)}) custom-call(bf16[4,8,64,768]{3,2,1,0:T(8,128)(2,1)} %bitcast.166, bf16[4,64,2048]{2,1,0:T(8,128)(2,1)} %bitcast.162, f32[8,4,8,128]{3,2,1,0:T(8,128)} %pad.19.small_in, bf16[8,128,2048]{2,1,0:T(8,128)(2,1)} %bitcast.161), custom_call_target="tpu_custom_call" | custom-call | tf_op jit(solution)/shard_map/close_heads/pallas_call | solution.py:1348
  579.3 2.5 add_convert_fusion.1
  581.9 0.7 slice.89
  583.2 1.8 convert_element_type.102
  585.7 0.9 convert_bitcast_fusion
  586.6 1.2 copy.69
  587.8 2.4 reshape.189
  590.2 1.9 copy.85
  592.1 2.1 fusion.10
  594.3 0.8 copy.100
  (71 shorter events, 4.9 us)
Async XLA Ops:
  6.2 3.1 copy-start.7
  6.6 3.6 copy-start.8
  6.7 3.6 copy-start.9
  210.0 6.3 %copy-start = (bf16[2,4,2,2,2,64,768]{6,5,4,3,2,1,0:T(8,128)(2,1)S(1)}, bf16[2,4,2,2,2,64,768]{6,5,4,3,2,1,0:T(8,128)(2,1)}, u32[]{:S(2)}) copy-start(bf16[2,4,2,2,2,64,768]{6,5,4,3,2,1,0:T(8,128)(2,1)} %get-tuple-element.45) | copy-start | bytes 18874372
  216.3 1.8 copy-start.18
  216.3 5.3 copy-start.13
  217.1 9.8 %copy-start.2 = (bf16[1,4,2,2,2,64,768]{6,5,4,3,2,1,0:T(8,128)(2,1)}, bf16[1,4,2,2,2,64,768]{6,5,4,3,2,1,0:T(8,128)(2,1)S(1)}, u32[]{:S(2)}) copy-start(bf16[1,4,2,2,2,64,768]{6,5,4,3,2,1,0:T(8,128)(2,1)S(1)} %get-tuple-element.107) | copy-start | bytes 9437188
  217.1 9.8 %copy-start.4 = (bf16[1,4,2,2,2,64,768]{6,5,4,3,2,1,0:T(8,128)(2,1)}, bf16[1,4,2,2,2,64,768]{6,5,4,3,2,1,0:T(8,128)(2,1)S(1)}, u32[]{:S(2)}) copy-start(bf16[1,4,2,2,2,64,768]{6,5,4,3,2,1,0:T(8,128)(2,1)S(1)} %get-tuple-element.106) | copy-start | bytes 9437188
  226.8 5.1 copy-start.20
  313.1 9.7 %copy-start.15 = (bf16[8,128,2048]{2,1,0:T(8,128)(2,1)S(1)}, bf16[8,128,2048]{2,1,0:T(8,128)(2,1)}, u32[]{:S(2)}) copy-start(bf16[8,128,2048]{2,1,0:T(8,128)(2,1)} %get-tuple-element.48) | copy-start | bytes 12582916
  313.1 9.7 %copy-start.21 = (bf16[1024,768]{1,0:T(8,128)(2,1)S(1)}, bf16[1024,768]{1,0:T(8,128)(2,1)}, u32[]{:S(2)}) copy-start(bf16[1024,768]{1,0:T(8,128)(2,1)} %copy-done.20) | copy-start | bytes 4718596
  322.8 5.0 copy-start.12
  327.8 7.6 %copy-start.14 = (bf16[8,128,2048]{2,1,0:T(8,128)(2,1)S(1)}, bf16[8,128,2048]{2,1,0:T(8,128)(2,1)}, u32[]{:S(2)}) copy-start(bf16[8,128,2048]{2,1,0:T(8,128)(2,1)} %get-tuple-element.43) | copy-start | bytes 12582916
  327.9 7.6 %copy-start.19 = (bf16[1024,768]{1,0:T(8,128)(2,1)S(1)}, bf16[1024,768]{1,0:T(8,128)(2,1)}, u32[]{:S(2)}) copy-start(bf16[1024,768]{1,0:T(8,128)(2,1)} %get-tuple-element.109) | copy-start | bytes 4718596
  335.5 4.9 copy-start.16
  340.4 3.5 copy-start.3
  468.8 8.1 %copy-start.11 = (f32[2,8,2048]{2,1,0:T(8,128)S(1)}, f32[2,8,2048]{2,1,0:T(8,128)}, u32[]{:S(2)}) copy-start(f32[2,8,2048]{2,1,0:T(8,128)} %get-tuple-element.60) | copy-start | bytes 393220
  468.9 9.1 %copy-start.5 = (bf16[8,128,256]{2,1,0:T(8,128)(2,1)S(1)}, bf16[8,128,256]{2,1,0:T(8,128)(2,1)}, u32[]{:S(2)}) copy-start(bf16[8,128,256]{2,1,0:T(8,128)(2,1)} %get-tuple-element.58) | copy-start | bytes 1572868
  477.9 4.6 copy-start.1
  477.9 4.6 copy-start.17
  579.3 5.6 copy-start.6
  592.1 2.1 copy-start.10

commit v11 on v10

--- a/solution.py
+++ b/solution.py
@@ -491,6 +491,7 @@
     next(units)
     next(units)
     project()
+    next(units)
     next(units)
     attend()
     next(units)

time: 604 us -> 599 us (level)
  no operation moved by 1% of the time
where the time goes in v11:
time: 599 us; the launch traced here: 590 us
  Pallas kernels  474 us (79%)
  matrix products  70 us (12%)
  local copies, waits for them, and re-layouts  29.6 us (5%)
  other arithmetic  14.4 us (2%)
    pallas_call x1, Pallas kernels, close_units(): pl.pallas_call(close_units_kernel, out_shape=(jax.ShapeDtypeStruct((8, 3)...  119 us
    pallas_call x1, Pallas kernels, open_units(): pl.pallas_call(open_units_kernel, out_shape=(rows, rows, rows, jax.ShapeD...  99.4 us
    pallas_call x1, Pallas kernels, close_heads(): pl.pallas_call(close_heads_kernel, out_shape=(jax.ShapeDtypeStruct((8, ro...  91.2 us
    pallas_call x1, Pallas kernels, open_heads(): pl.pallas_call(open_heads_kernel, out_shape=(jax.ShapeDtypeStruct((4, 8,...  86.9 us
    pallas_call x1, Pallas kernels, turn(): pl.pallas_call(turn_kernel, out_shape=(jax.ShapeDtypeStruct((own, width),...  77.8 us
    dot_general x5, matrix products, contract_first(): lax.dot_general(left_side, right_side, (((0,), (0,)), ((), ())), preferre...  30.2 us
    dot_general x3, matrix products, dot(): return jnp.dot(left_side, right_side, preferred_element_type=jnp.float32)  21.2 us
    dot_general x4, matrix products, contract_last(): lax.dot_general(left_side, right_side, (((1,), (1,)), ((), ())), preferre...  18.6 us

profile of v11, /device:TPU:11, one launch (start us, length us, event | category | flops | bytes accessed | tf_op | source)
XLA Modules:
  0.0 589.7 jit_solution(15211418317799696952)
XLA Ops:
  0.7 0.7 maximum_convert_fusion
  1.5 0.7 convert_element_type.86
  3.1 2.6 reshape.156
  6.7 0.9 maximum_bitcast_fusion
  7.6 1.7 reshape.157.qkv_in
  9.3 0.9 copy.96
  10.5 1.3 copy.95
  11.8 86.9 %open_heads.1 = (bf16[4,8,64,768]{3,2,1,0:T(8,128)(2,1)}, bf16[1,4,2,2,2,64,768]{6,5,4,3,2,1,0:T(8,128)(2,1)}, bf16[4,64,2048]{2,1,0:T(8,128)(2,1)}, bf16[8,128,2048]{2,1,0:T(8,128)(2,1)}, f32[4,8,8,128]{3,2,1,0:T(8,128)}) custom-call(bf16[8,64,768]{2,1,0:T(8,128)(2,1)} %reshape.157.qkv_in, bf16[8,1,64,768]{3,2,1,0:T(8,128)(2,1)} %bitcast.167, ...), custom_call_target="tpu_custom_call" | custom-call | tf_op jit(solution)/shard_map/open_heads/pallas_call | solution.py:533
  98.7 0.9 copy.97
  99.6 0.9 reshape_reshape.6
  100.9 0.7 unstack.51.shift
  101.6 0.7 unstack.41.gain
  102.3 0.7 unstack.49.gain
  102.9 0.7 unstack.43.shift
  104.3 0.6 slice_bitcast_fusion.7
  104.9 1.0 copy.62.start_query
  105.9 1.9 fusion.13
  107.8 1.0 pad_maximum_fusion.1.sine
  108.8 1.0 pad_maximum_fusion.cosine
  109.8 99.4 %open_units.1 = (bf16[4,256,256]{2,1,0:T(8,128)(2,1)}, bf16[4,256,256]{2,1,0:T(8,128)(2,1)}, bf16[4,256,256]{2,1,0:T(8,128)(2,1)}, f32[4,2,256,256]{3,2,1,0:T(8,...) custom-call(bf16[8,128,2048]{2,1,0:T(8,128)(2,1)} %get-tuple-element, ...), custom_call_target="tpu_custom_call" | custom-call | tf_op jit(solution)/shard_map/open_units/pallas_call | solution.py:561
  209.2 6.3 %fusion.19 = f32[1024,768]{1,0:T(8,128)S(1)} fusion(bf16[1024,2048]{1,0:T(8,128)(2,1)} %bitcast.193, bf16[2048,768]{1,0:T(8,128)(2,1)} %bitcast.199), kind=kOutput, calls=%fused_computation.69 | convolution fusion | flops 3221225472 | bytes 10485760 | tf_op jit(solution)/shard_map/dot_general | solution.py:39
  215.6 0.7 fusion.17
  216.3 1.0 copy-done.18
  217.3 3.5 copy-done.13
  220.8 5.3 multiply_convert_fusion.1
  226.1 5.1 convolution_convert_fusion.1
  231.1 77.8 %turn.1 = (bf16[128,2048]{1,0:T(8,128)(2,1)}, f32[128,2048]{1,0:T(8,128)}, bf16[8,128,2048]{2,1,0:T(8,128)(2,1)}, f32[2,8,2048]{2,1,0:T(8,128)}) custom-call(bf16[8,128,2048]{2,1,0:T(8,128)(2,1)} %bitcast.160, bf16[128,2048]{1,0:T(8,128)(2,1)} %get-tuple-element.46.normed, bf16[128,2048]{1,0:T(8,128)(2,1)} %bitcast.182, f32[1,2048]{1,0:T(1,128)} %unstack.49.gain, ...), custom_call_target="tpu_custom_call" | custom-call | tf_op jit(solution)/shard_map/turn/pallas_call | solution.py:867
  308.9 9.7 %multiply_convert_fusion = (bf16[1024,768]{1,0:T(8,128)(2,1)S(1)}, bf16[1024,768]{1,0:T(8,128)(2,1)}) fusion(f32[1024,768]{1,0:T(8,128)} %get-tuple-element.105, f32[1024,768]{1,0:T(8,128)} %copy-done.18, f32[1024,768]{1,0:T(8,128)} %get-tuple-element.132, bf16[1024,2048]{1,0:T(8,128)(2,1)} %bitcast.197, bf16[2048,768]{1,0:T(8,128)(2,1)} %bitcast.174), kind=kOutput, calls=%fused_computation.17 | convolution fusion | flops 3231449088 | bytes 19922944 | tf_op jit(solution)/shard_map/dot_general | solution.py:39
  318.6 5.0 convolution_convert_fusion.2
  323.7 7.6 %convolution_convert_fusion.3 = bf16[2048,768]{1,0:T(8,128)(2,1)} fusion(bf16[1024,2048]{1,0:T(8,128)(2,1)} %bitcast.194, bf16[1024,768]{1,0:T(8,128)(2,1)S(1)} %get-tuple-element.108), kind=kOutput, calls=%fused_computation.6 | convolution fusion | flops 3222798336 | bytes 8912896 | tf_op jit(solution)/shard_map/dot_general | solution.py:33
  331.4 4.9 convolution_convert_fusion.4
  336.3 3.4 fusion.20
  339.7 5.1 add_convert_fusion
  344.8 118.8 %close_units.1 = (bf16[8,3,64,768]{3,2,1,0:T(8,128)(2,1)}, bf16[8,128,2048]{2,1,0:T(8,128)(2,1)}, bf16[8,128,768]{2,1,0:T(8,128)(2,1)}, f32[128,2048]{1,0:T(8,128)}, f32[2,8,2048]{2,1,0:T(8,128)}) custom-call(bf16[4,2,2,2,64,768]{5,4,3,2,1,0:T(8,128)(2,1)} %bitcast.165, bf16[4,2,2,2,64,768]{5,4,3,2,1,0:T(8,128)(2,1)} %bitcast.164, ...), custom_call_target="tpu_custom_call" | custom-call | tf_op jit(solution)/shard_map/close_units/pallas_call | solution.py:1089
  463.6 8.0 %bitcast_convert_fusion = bf16[2048,768]{1,0:T(8,128)(2,1)} fusion(bf16[8,128,2048]{2,1,0:T(8,128)(2,1)} %get-tuple-element.39.x_all, bf16[8,128,768]{2,1,0:T(8,128)(2,1)} %get-tuple-element.57), kind=kOutput, calls=%fused_computation.1 | convolution fusion | flops 3222798336 | bytes 8912896 | tf_op jit(solution)/shard_map/dot_general | solution.py:33
  472.0 0.7 pad.19.small_in
  472.7 4.6 fusion.8
  477.3 5.0 convolution_convert_fusion
  482.3 91.2 %close_heads.1 = (bf16[8,64,768]{2,1,0:T(8,128)(2,1)}, bf16[64,2048]{1,0:T(8,128)(2,1)}, f32[8,128]{1,0:T(8,128)}, f32[128,2048]{1,0:T(8,128)}) custom-call(bf16[4,8,64,768]{3,2,1,0:T(8,128)(2,1)} %bitcast.166, bf16[4,64,2048]{2,1,0:T(8,128)(2,1)} %bitcast.162, f32[8,4,8,128]{3,2,1,0:T(8,128)} %pad.19.small_in, bf16[8,128,2048]{2,1,0:T(8,128)(2,1)} %bitcast.161), custom_call_target="tpu_custom_call" | custom-call | tf_op jit(solution)/shard_map/close_heads/pallas_call | solution.py:1349
  573.5 2.5 add_convert_fusion.1
  576.1 0.7 slice.89
  577.4 1.8 convert_element_type.102
  579.9 0.9 convert_bitcast_fusion
  580.8 1.2 copy.69
  582.0 2.4 reshape.189
  584.4 1.9 copy.85
  586.3 2.1 fusion.10
  588.5 0.8 copy.100
  (71 shorter events, 4.9 us)
Async XLA Ops:
  6.2 3.1 copy-start.7
  6.6 3.6 copy-start.8
  6.7 3.6 copy-start.9
  209.2 6.3 %copy-start = (bf16[2,4,2,2,2,64,768]{6,5,4,3,2,1,0:T(8,128)(2,1)S(1)}, bf16[2,4,2,2,2,64,768]{6,5,4,3,2,1,0:T(8,128)(2,1)}, u32[]{:S(2)}) copy-start(bf16[2,4,2,2,2,64,768]{6,5,4,3,2,1,0:T(8,128)(2,1)} %get-tuple-element.45) | copy-start | bytes 18874372
  215.5 1.8 copy-start.18
  215.5 5.3 copy-start.13
  216.3 9.8 %copy-start.2 = (bf16[1,4,2,2,2,64,768]{6,5,4,3,2,1,0:T(8,128)(2,1)}, bf16[1,4,2,2,2,64,768]{6,5,4,3,2,1,0:T(8,128)(2,1)S(1)}, u32[]{:S(2)}) copy-start(bf16[1,4,2,2,2,64,768]{6,5,4,3,2,1,0:T(8,128)(2,1)S(1)} %get-tuple-element.107) | copy-start | bytes 9437188
  216.3 9.8 %copy-start.4 = (bf16[1,4,2,2,2,64,768]{6,5,4,3,2,1,0:T(8,128)(2,1)}, bf16[1,4,2,2,2,64,768]{6,5,4,3,2,1,0:T(8,128)(2,1)S(1)}, u32[]{:S(2)}) copy-start(bf16[1,4,2,2,2,64,768]{6,5,4,3,2,1,0:T(8,128)(2,1)S(1)} %get-tuple-element.106) | copy-start | bytes 9437188
  226.1 5.1 copy-start.20
  308.9 9.7 %copy-start.15 = (bf16[8,128,2048]{2,1,0:T(8,128)(2,1)S(1)}, bf16[8,128,2048]{2,1,0:T(8,128)(2,1)}, u32[]{:S(2)}) copy-start(bf16[8,128,2048]{2,1,0:T(8,128)(2,1)} %get-tuple-element.48) | copy-start | bytes 12582916
  308.9 9.7 %copy-start.21 = (bf16[1024,768]{1,0:T(8,128)(2,1)S(1)}, bf16[1024,768]{1,0:T(8,128)(2,1)}, u32[]{:S(2)}) copy-start(bf16[1024,768]{1,0:T(8,128)(2,1)} %copy-done.20) | copy-start | bytes 4718596
  318.6 5.0 copy-start.12
  323.7 7.6 %copy-start.14 = (bf16[8,128,2048]{2,1,0:T(8,128)(2,1)S(1)}, bf16[8,128,2048]{2,1,0:T(8,128)(2,1)}, u32[]{:S(2)}) copy-start(bf16[8,128,2048]{2,1,0:T(8,128)(2,1)} %get-tuple-element.43) | copy-start | bytes 12582916
  323.7 7.6 %copy-start.19 = (bf16[1024,768]{1,0:T(8,128)(2,1)S(1)}, bf16[1024,768]{1,0:T(8,128)(2,1)}, u32[]{:S(2)}) copy-start(bf16[1024,768]{1,0:T(8,128)(2,1)} %get-tuple-element.109) | copy-start | bytes 4718596
  331.3 4.9 copy-start.16
  336.3 3.5 copy-start.3
  463.6 8.1 %copy-start.11 = (f32[2,8,2048]{2,1,0:T(8,128)S(1)}, f32[2,8,2048]{2,1,0:T(8,128)}, u32[]{:S(2)}) copy-start(f32[2,8,2048]{2,1,0:T(8,128)} %get-tuple-element.60) | copy-start | bytes 393220
  463.6 9.1 %copy-start.5 = (bf16[8,128,256]{2,1,0:T(8,128)(2,1)S(1)}, bf16[8,128,256]{2,1,0:T(8,128)(2,1)}, u32[]{:S(2)}) copy-start(bf16[8,128,256]{2,1,0:T(8,128)(2,1)} %get-tuple-element.58) | copy-start | bytes 1572868
  472.7 4.6 copy-start.1
  472.7 4.6 copy-start.17
  573.5 5.6 copy-start.6
  586.3 2.1 copy-start.10
